TPU v7x, 128 devices: a whole 4x4x4 slice. The times are simulated.
128 devices in a mesh: lat: 32 (over x, z, core), lev: 4 (over y).
Axes of the slice: x: 4, y: 4, z: 4, core: 2. Of those that a mesh axis runs over, the one named last changes fastest.
Arguments:
- tracer_dyn: bfloat16 [64, 72, 64, 1024], P(None, 'lev', 'lat'), may hold values from 0.19921875 to 5
- courant_lat: bfloat16 [72, 64, 1024], P('lev', 'lat'), may hold values from -0.44921875 to 0.44921875
- courant_lon: bfloat16 [72, 64, 1024], P('lev', 'lat'), may hold values from -0.44921875 to 0.44921875
- conv_matrix: bfloat16 [72, 72, 65536], P(None, None, ('lat', 'lev'))
- conv_mask: int32 [65536], P(('lat', 'lev')), may hold values from 0 to 1, as said below
- column_order: int32 [65536], P(('lat', 'lev')), may hold values from 0 to 511, as said below
- rain: bfloat16 [72, 65536], P(None, ('lat', 'lev')), may hold values from 0.019897461 to 1
- scav_rate: float32 [64], replicated, may hold values from 0.05 to 2
- pair_flag: int32 [64], replicated, may hold values from 0 to 1
Outputs:
- tracer_phys: bfloat16 [64, 72, 65536], P(None, None, ('lat', 'lev'))
Inputs may be any that keep to these rules, and one draw needn't show every extreme that they name: `conv_mask`: in each aligned block of 512 entries (one span) at most 256 are 1, and some block has exactly 256. `column_order`: each aligned block of 512 entries holds every number of 0 to 511 once.
All inputs are finite; a program needn't handle non-finite values.
Results may differ from a plain program's by a relative error of at most 0.005.
Values may be sent and summed in bfloat16 or wider, within the bound.
No kernel may reach another device: no remote copies, remote signals or barrier semaphores. Data moves between devices by JAX's collectives and lax.ppermute only.
A program may use at most 128 MiB of HBM per device.

v0:
```python
import jax
import jax.numpy as jnp
from jax import lax
from jax.sharding import PartitionSpec as P


def padded_2(block, sides, width):
    for axis, dim in sides:
        count = lax.axis_size(axis)
        forward = [(i, i + 1) for i in range(count - 1)]
        backward = [(target, source) for source, target in forward]
        low = lax.ppermute(
            lax.slice_in_dim(block, block.shape[dim] - width, None, axis=dim), axis, forward
        )
        high = lax.ppermute(lax.slice_in_dim(block, 0, width, axis=dim), axis, backward)
        block = jnp.concatenate([low, block, high], axis=dim)
    return block


def shifted(value, axis, steps):
    count = lax.axis_size(axis)
    initial, last = (max(0, -steps), min(count, count - steps))
    return lax.ppermute(value, axis, [(source, source + steps) for source in range(initial, last)])


def swapped(shard, axis, apart):
    return lax.ppermute(shard, axis, [(i, i ^ 1 << apart) for i in range(lax.axis_size(axis))])


def advect_block(center, south_side, north_side, south_face, north_face, west_face):
    east_face = jnp.roll(west_face, -1, axis=-1)
    south_flux = south_face * jnp.where(south_face > 0, south_side, center)
    north_flux = north_face * jnp.where(north_face > 0, center, north_side)
    west_flux = west_face * jnp.where(west_face > 0, jnp.roll(center, 1, axis=-1), center)
    east_flux = east_face * jnp.where(east_face > 0, center, jnp.roll(center, -1, axis=-1))
    return center - (north_flux - south_flux) - (east_flux - west_flux)


def convect(matrix, tracers_bf):
    return jnp.einsum("kec,tec->tkc", matrix, tracers_bf, preferred_element_type=jnp.float32)


def local(
    tracer_dyn,
    courant_lat,
    courant_lon,
    conv_matrix,
    conv_mask,
    column_order,
    rain,
    scav_rate,
    pair_flag,
):
    n_lat = lax.axis_size("lat")
    n_lev = lax.axis_size("lev")
    tracers, lev_group, lat_dev, lon_all = tracer_dyn.shape
    lon_block = lon_all // n_lev
    padded = padded_2(tracer_dyn, (("lat", 2),), 1)
    center = tracer_dyn.astype(jnp.float32)
    south_side = padded[:, :, :-2].astype(jnp.float32)
    north_side = padded[:, :, 2:].astype(jnp.float32)
    south_face = courant_lat.astype(jnp.float32)
    above_face = shifted(courant_lat[:, :1], "lat", -1)
    north_face = jnp.concatenate([south_face[:, 1:], above_face.astype(jnp.float32)], axis=1)
    west_face = courant_lon.astype(jnp.float32)
    advected = advect_block(
        center, south_side, north_side, south_face, north_face, west_face
    ).astype(jnp.bfloat16)
    sectioned = advected.reshape(tracers, 1, lev_group, lat_dev, n_lev, lon_block)
    arrived = lax.all_to_all(sectioned, "lev", split_axis=4, concat_axis=1, tiled=True)
    physics = arrived.reshape(tracers, lev_group * n_lev, lat_dev * lon_block)
    levels = physics.shape[1]
    columns = physics.shape[2]
    placing = (jnp.arange(columns, dtype=jnp.int32)[:, None] == column_order[None, :]).astype(
        jnp.bfloat16
    )
    ordered = jnp.dot(
        physics.reshape(tracers * levels, columns), placing, preferred_element_type=jnp.float32
    )
    ordered = ordered.astype(jnp.bfloat16).reshape(tracers, levels, columns)
    ordered_f = ordered.astype(jnp.float32)
    moved = convect(conv_matrix, ordered)
    convected = jnp.where(conv_mask[None, None, :] > 0, moved, ordered_f)
    washed = (
        convected * jnp.exp(-scav_rate[:, None, None] * rain.astype(jnp.float32)[None])
    ).astype(jnp.bfloat16)
    top_bit = n_lat.bit_length() - 2
    partner = swapped(washed, "lat", top_bit)
    pair_index = lax.axis_index("lat") % (n_lat // 2) * n_lev + lax.axis_index("lev")
    flag_value = pair_flag[pair_index]
    return jnp.where(flag_value > 0, partner, washed)


def solution(mesh):
    placed = (
        P(None, "lev", "lat", None),
        P("lev", "lat", None),
        P("lev", "lat", None),
        P(None, None, ("lat", "lev")),
        P(("lat", "lev")),
        P(("lat", "lev")),
        P(None, ("lat", "lev")),
        P(),
        P(),
    )
    return jax.shard_map(
        local, mesh=mesh, in_specs=placed, out_specs=P(None, None, ("lat", "lev")), check_vma=False
    )
```

profile of v0, /device:TPU:97, one launch (start us, length us, event | category | flops | bytes accessed | tf_op | source)
XLA Modules:
  0.0 371.5 jit_solution(9625130969221222224)
XLA Ops:
  0.0 0.0 slice-start
  0.0 0.0 slice-start.1
  0.0 2.8 collective-permute-start
  2.8 9.9 %fusion.11 = (bf16[64,18,1,1024]{3,2,1,0:T(2,128)(2,1)S(1)}, bf16[64,18,1,1024]{3,2,1,0:T(2,128)(2,1)S(1)}) fusion(bf16[64,18,2,1024]{3,2,1,0:T(2,128)(2,1)} %param.9), kind=kLoop, calls=%fused_computation.29 | loop fusion | bytes 9437184 | tf_op jit(solution)/shard_map/slice | solution.py:15
  12.7 0.0 copy-start
  12.7 1.3 copy.50
  14.0 5.1 %collective-permute-start.2 = (bf16[64,18,1,1024]{3,0,2,1:T(8,128)(2,1)S(1)}, bf16[64,18,1,1024]{3,0,2,1:T(8,128)(2,1)}, u32[]{:S(2)}, u32[]{:S(2)}) collective-permute-start(bf16[64,18,1,1024]{3,0,2,1:T(8,128)(2,1)S(1)} %copy.50), channel_id=1, source_target_pairs={{0,4},{4,8},{8,12},{12,16},{16,20},{20,24},{24,28},{28,32},{32,36}... | collective-permute-start | bytes 7077896 | tf_op jit(solution)/shard_map/ppermute | solution.py:12
  19.1 2.7 copy.49
  21.9 2.1 collective-permute-start.1
  24.0 0.0 slice-done
  24.0 0.0 slice-done.1
  24.0 2.6 fusion.13
  26.6 0.0 copy-done
  26.6 0.1 slice.57
  26.7 0.9 broadcast_compare_fusion.1
  27.6 0.0 copy-start.1
  27.6 14.0 %fusion.12 = (f32[64,18,2,1023]{3,2,1,0:T(2,128)}, f32[64,18,2,1023]{3,2,1,0:T(2,128)}) fusion(bf16[64,18,2,1024]{3,2,1,0:T(2,128)(2,1)S(1)} %bitcast.20), kind=kLoop, calls=%fused_computation.30 | loop fusion | bytes 37711872 | tf_op jit(solution)/shard_map/jit(_roll_static)/slice | solution.py:35
  41.6 0.0 copy-done.1
  41.6 0.7 broadcast_compare_fusion.2
  42.4 0.1 slice.56
  42.4 0.1 convert_element_type.39
  42.5 0.1 convert_element_type.35
  42.6 0.0 collective-permute-done
  42.6 0.1 convert_element_type.36
  42.6 0.2 broadcast_compare_fusion.3
  42.8 0.8 pad_maximum_fusion.2
  43.6 1.3 collective-permute-done.2
  44.9 7.5 %copy.36 = bf16[64,18,1,1024]{3,2,1,0:T(2,128)(2,1)} copy(bf16[64,18,1,1024]{3,0,2,1:T(8,128)(2,1)} %collective-permute-done.2) | data formatting | bytes 4718592 | tf_op jit(solution)/shard_map/ppermute | solution.py:12
  52.4 2.1 collective-permute-done.1
  54.5 7.5 %copy.34 = bf16[64,18,1,1024]{3,2,1,0:T(2,128)(2,1)} copy(bf16[64,18,1,1024]{3,0,2,1:T(8,128)(2,1)} %collective-permute-done.1) | data formatting | bytes 4718592 | tf_op jit(solution)/shard_map/ppermute | solution.py:15
  62.0 46.9 %fusion.9 = bf16[64,18,2,1024]{3,2,1,0:T(2,128)(2,1)} fusion(f32[64,18,2,1023]{3,2,1,0:T(2,128)} %get-tuple-element.10, f32[64,18,2,1]{3,2,1,0:T(2,128)} %get-tuple-element.12, pred[18,2,1024]{2,1,0:T(4,128)(4,1)} %get-tuple-element.13, f32[64,18,2,1]{3,2,1,0:T(2,128)} %get-tuple-element.11, f32[64,18,2,1023]{3,2,1,0:T(2,128)} %get-tuple-element.9, ...), kind=kLoop, calls=%fused_computation.15 | loop fusion | flops 56623104 | bytes 33767424 | tf_op jit(solution)/shard_map/convert_element_type | solution.py:68
  108.8 8.6 %reshape.21 = bf16[64,1,18,2,4,256]{5,4,3,2,0,1:T(4,128)(2,1)} reshape(bf16[64,18,2,1024]{3,2,1,0:T(2,128)(2,1)} %fusion.9) | data formatting | bytes 9437184 | tf_op jit(solution)/shard_map/reshape | solution.py:69
  117.4 8.1 %copy.38 = bf16[64,1,18,2,4,256]{5,3,2,0,1,4:T(2,128)(2,1)} copy(bf16[64,1,18,2,4,256]{5,4,3,2,0,1:T(4,128)(2,1)} %reshape.21) | data formatting | bytes 9437184 | tf_op jit(solution)/shard_map/reshape | solution.py:69
  125.5 5.2 %all-to-all-start = ((bf16[64,1,18,2,4,256]{5,3,2,0,1,4:T(2,128)(2,1)}), bf16[64,1,18,2,4,256]{5,3,2,0,1,4:T(2,128)(2,1)}, u32[]{:S(2)}, u32[]{:S(2)}) async-start(bf16[64,1,18,2,4,256]{5,3,2,0,1,4:T(2,128)(2,1)} %copy.38), calls=%async_computation | async-start | bytes 9437184 | tf_op jit(solution)/shard_map/all_to_all | solution.py:70
  130.7 0.0 copy-start.2
  130.7 0.0 copy-start.5
  130.8 0.0 copy-start.3
  130.8 11.6 %copy.41 = bf16[72,72,512]{1,0,2:T(8,128)(2,1)} copy(bf16[72,72,512]{2,1,0:T(8,128)(2,1)} %param.12) | data formatting | bytes 10616832 | tf_op args[3]
  142.3 0.0 copy-done.2
  142.3 0.1 copy.43
  142.4 0.0 copy-done.5
  142.5 0.0 copy-done.3
  142.5 40.6 %all-to-all-done = bf16[64,1,18,2,4,256]{5,3,2,0,1,4:T(2,128)(2,1)} async-done(((bf16[64,1,18,2,4,256]{5,3,2,0,1,4:T(2,128)(2,1)}), bf16[64,1,18,2,4,256]{5,3,2,0,1,4:T(2,128)(2,1)}, u32[]{:S(2)}, u32[]{:S(2)}) %all-to-all-start) | async-done | bytes 4718624 | tf_op jit(solution)/shard_map/all_to_all | solution.py:70
  183.0 0.0 copy-start.4
  183.0 7.8 %copy.39 = bf16[64,4,1,18,2,1,256]{6,4,3,1,0,5,2:T(2,128)(2,1)} copy(bf16[64,4,1,18,2,1,256]{6,4,3,0,1,5,2:T(2,128)(2,1)} %bitcast.2) | data formatting | bytes 9437184 | tf_op jit(solution)/shard_map/all_to_all | solution.py:70
  190.8 3.1 copy.51
  193.9 0.0 copy-done.4
  194.0 4.4 %convolution_convert_fusion = bf16[4608,512]{1,0:T(8,128)(2,1)} fusion(bf16[4608,512]{1,0:T(8,128)(2,1)S(1)} %bitcast.23, s32[512]{0:T(512)S(1)} %copy-done.4), kind=kOutput, calls=%fused_computation.17 | convolution fusion | flops 2418540544 | bytes 9439232 | tf_op jit(solution)/shard_map/dot_general | solution.py:77
  198.3 11.2 %copy.40 = bf16[64,72,512]{1,0,2:T(8,128)(2,1)} copy(bf16[64,72,512]{2,1,0:T(8,128)(2,1)} %bitcast.22) | data formatting | bytes 9437184 | tf_op jit(solution)/shard_map/reshape | solution.py:80
  209.5 16.7 %fusion.1 = bf16[64,72,512]{1,0,2:T(8,128)(2,1)} fusion(bf16[64,72,512]{1,0,2:T(8,128)(2,1)} %copy.40, bf16[72,72,512]{1,0,2:T(8,128)(2,1)} %copy.41, f32[72,512]{0,1:T(8,128)S(1)} %copy.43, f32[64]{0:T(128)S(1)} %neg.4, pred[512]{0:T(512)(128)(4,1)S(1)} %broadcast_compare_fusion.4), kind=kOutput, calls=%fused_computation.2 | convolution fusion | flops 351535104 | bytes 14893824 | tf_op jit(solution)/shard_map/kec,tec->tkc/dot_general | solution.py:40
  226.2 0.0 copy-start.6
  226.2 11.4 %copy.44 = bf16[64,72,512]{2,1,0:T(8,128)(2,1)} copy(bf16[64,72,512]{1,0,2:T(8,128)(2,1)} %fusion.1) | data formatting | bytes 9437184 | tf_op jit(solution)/shard_map/convert_element_type | solution.py:86
  237.6 2.7 collective-permute-start.3
  240.3 0.0 copy-done.6
  240.3 0.6 dynamic_slice.3
  241.7 100.0 %collective-permute-done.3 = bf16[64,72,512]{2,1,0:T(8,128)(2,1)} collective-permute-done((bf16[64,72,512]{2,1,0:T(8,128)(2,1)}, bf16[64,72,512]{2,1,0:T(8,128)(2,1)}, u32[]{:S(2)}, u32[]{:S(2)}) %collective-permute-start.3) | collective-permute-done | bytes 4718624 | tf_op jit(solution)/shard_map/ppermute | solution.py:27
  341.7 11.2 %copy.45 = bf16[64,72,512]{1,0,2:T(8,128)(2,1)} copy(bf16[64,72,512]{2,1,0:T(8,128)(2,1)} %collective-permute-done.3) | data formatting | bytes 9437184 | tf_op jit(solution)/shard_map/ppermute | solution.py:27
  352.9 7.2 %broadcast_select_fusion = bf16[64,72,512]{1,0,2:T(8,128)(2,1)} fusion(bf16[64,72,512]{1,0,2:T(8,128)(2,1)} %copy.45, bf16[64,72,512]{1,0,2:T(8,128)(2,1)} %fusion.1, pred[]{:T(512)} %bitcast), kind=kLoop, calls=%fused_computation.16 | loop fusion | flops 2359296 | bytes 14155777 | tf_op jit(solution)/shard_map/jit(_where)/select_n | solution.py:91
  360.1 11.4 %copy.46 = bf16[64,72,512]{2,1,0:T(8,128)(2,1)} copy(bf16[64,72,512]{1,0,2:T(8,128)(2,1)} %broadcast_select_fusion) | data formatting | bytes 9437184 | tf_op jit(solution)/shard_map/jit(_where)/select_n | solution.py:91
  (4 shorter events, 0.0 us)
Async XLA Ops:
  0.0 24.0 %slice-start = ((s8[4718592]{0:T(1024)(128)(4,1)}), s8[4194304]{0:T(1024)(128)(4,1)S(1)}, s32[]{:S(2)}) async-start(s8[4718592]{0:T(1024)(128)(4,1)} %bitcast.19), calls=%async_computation.1 | async-start | bytes 8388608
  0.0 24.0 %slice-start.1 = ((s8[4718592]{0:T(1024)(128)(4,1)}), s8[524288]{0:T(1024)(128)(4,1)S(1)}, s32[]{:S(2)}) async-start(s8[4718592]{0:T(1024)(128)(4,1)} %bitcast.19), calls=%async_computation.2 | async-start | bytes 1048576
  0.0 42.6 %collective-permute-start = (bf16[18,1,1024]{2,1,0:T(2,128)(2,1)}, bf16[18,1,1024]{2,1,0:T(2,128)(2,1)S(1)}, u32[]{:S(2)}, u32[]{:S(2)}) collective-permute-start(bf16[18,1,1024]{2,1,0:T(2,128)(2,1)} %bitcast.24), channel_id=1, source_target_pairs={{4,0},{8,4},{12,8},{16,12},{20,16},{24,20},{28,24},{32,28},{36,32}... | collective-permute-start | bytes 110600 | tf_op jit(solution)/shard_map/ppermute | solution.py:23
  12.7 13.8 %copy-start = (bf16[18,2,1024]{2,1,0:T(2,128)(2,1)S(1)}, bf16[18,2,1024]{2,1,0:T(2,128)(2,1)}, u32[]{:S(2)}) copy-start(bf16[18,2,1024]{2,1,0:T(2,128)(2,1)} %param.11) | copy-start | bytes 221188
  14.0 30.9 %collective-permute-start.2 = (bf16[64,18,1,1024]{3,0,2,1:T(8,128)(2,1)S(1)}, bf16[64,18,1,1024]{3,0,2,1:T(8,128)(2,1)}, u32[]{:S(2)}, u32[]{:S(2)}) collective-permute-start(bf16[64,18,1,1024]{3,0,2,1:T(8,128)(2,1)S(1)} %copy.50), channel_id=1, source_target_pairs={{0,4},{4,8},{8,12},{12,16},{16,20},{20,24},{24,28},{28,32},{32,36}... | collective-permute-start | bytes 7077896 | tf_op jit(solution)/shard_map/ppermute | solution.py:12
  21.9 32.6 %collective-permute-start.1 = (bf16[64,18,1,1024]{3,0,2,1:T(8,128)(2,1)}, bf16[64,18,1,1024]{3,0,2,1:T(8,128)(2,1)}, u32[]{:S(2)}, u32[]{:S(2)}) collective-permute-start(bf16[64,18,1,1024]{3,0,2,1:T(8,128)(2,1)} %copy.49), channel_id=1, source_target_pairs={{4,0},{8,4},{12,8},{16,12},{20,16},{24,20},{28,24},{32,28},{36,32}... | collective-permute-start | bytes 7077896 | tf_op jit(solution)/shard_map/ppermute | solution.py:15
  27.6 14.0 %copy-start.1 = (bf16[18,2,1024]{2,1,0:T(2,128)(2,1)S(1)}, bf16[18,2,1024]{2,1,0:T(2,128)(2,1)}, u32[]{:S(2)}) copy-start(bf16[18,2,1024]{2,1,0:T(2,128)(2,1)} %param.10) | copy-start | bytes 221188
  125.5 57.5 %all-to-all-start = ((bf16[64,1,18,2,4,256]{5,3,2,0,1,4:T(2,128)(2,1)}), bf16[64,1,18,2,4,256]{5,3,2,0,1,4:T(2,128)(2,1)}, u32[]{:S(2)}, u32[]{:S(2)}) async-start(bf16[64,1,18,2,4,256]{5,3,2,0,1,4:T(2,128)(2,1)} %copy.38), calls=%async_computation | async-start | bytes 9437184 | tf_op jit(solution)/shard_map/all_to_all | solution.py:70
  130.7 11.6 %copy-start.2 = (bf16[72,512]{1,0:T(8,128)(2,1)S(1)}, bf16[72,512]{1,0:T(8,128)(2,1)}, u32[]{:S(2)}) copy-start(bf16[72,512]{1,0:T(8,128)(2,1)} %param.15) | copy-start | bytes 221188
  130.7 11.7 %copy-start.5 = (f32[64]{0:T(128)S(1)}, f32[64]{0:T(128)}, u32[]{:S(2)}) copy-start(f32[64]{0:T(128)} %param.16) | copy-start | bytes 772
  130.8 11.7 %copy-start.3 = (s32[512]{0:T(512)S(1)}, s32[512]{0:T(512)}, u32[]{:S(2)}) copy-start(s32[512]{0:T(512)} %param.13) | copy-start | bytes 6148
  183.0 10.9 %copy-start.4 = (s32[512]{0:T(512)S(1)}, s32[512]{0:T(512)}, u32[]{:S(2)}) copy-start(s32[512]{0:T(512)} %param.14) | copy-start | bytes 6148
  226.2 14.2 %copy-start.6 = (s32[64]{0:T(128)S(1)}, s32[64]{0:T(128)}, u32[]{:S(2)}) copy-start(s32[64]{0:T(128)} %param.17) | copy-start | bytes 772
  237.6 104.1 %collective-permute-start.3 = (bf16[64,72,512]{2,1,0:T(8,128)(2,1)}, bf16[64,72,512]{2,1,0:T(8,128)(2,1)}, u32[]{:S(2)}, u32[]{:S(2)}) collective-permute-start(bf16[64,72,512]{2,1,0:T(8,128)(2,1)} %copy.44), channel_id=1, source_target_pairs={{0,64},{4,68},{8,72},{12,76},{16,80},{20,84},{24,88},{28,92},{32,9... | collective-permute-start | bytes 14155784 | tf_op jit(solution)/shard_map/ppermute | solution.py:27
where the time goes:
time: 373 us; the launch traced here: 371 us
  waiting for transfers between devices  144 us (39%)
  local copies, waits for them, and re-layouts  131 us (35%)
  other arithmetic  56.8 us (15%)
  matrix products  21 us (6%)
  starting transfers between devices  18 us (5%)
    ppermute x1, waiting for transfers between devices, swapped(): lax.ppermute(shard, axis, [(i, i ^ 1 << apart) for i in range(lax.axis_si...  100 us
    convert_element_type x1, other arithmetic, local(): advected = advect_block(center, south_side, north_side, south_face, north...  46.9 us
    all_to_all x1, waiting for transfers between devices, local(): lax.all_to_all(sectioned, 'lev', split_axis=4, concat_axis=1, tiled=True)  40.6 us
    unnamed x22, local copies, waits for them, and re-layouts  18.8 us
    dot_general x1, matrix products, convect(): jnp.einsum('kec,tec->tkc', matrix, tracers_bf, preferred_element_type=jnp...  16.7 us
    reshape x2, local copies, waits for them, and re-layouts, local(): advected.reshape(tracers, 1, lev_group, lat_dev, n_lev, lon_block)  16.7 us
    slice x2, local copies, waits for them, and re-layouts, advect_block(): jnp.roll(center, -1, axis=-1)  16.6 us
    convert_element_type x1, local copies, waits for them, and re-layouts, local(): washed = (convected * jnp.exp(-scav_rate[:, None, None] * rain.astype(jnp...  11.4 us
  transfers between devices with their start and end apart: 5, of which 4 were waited for; matrix products, arithmetic and copies ran while one was open for 14% of the time, Pallas kernels for 0%

commit v1 on v0

v1 whole, which is shorter than its diff:
```python
import functools

import jax
import jax.numpy as jnp
from jax import lax
from jax.experimental import pallas as pl
from jax.experimental.pallas import tpu as pltpu
from jax.sharding import PartitionSpec as P

GROUP = 8
CHUNKS = (1, 1, 2, 2, 2)
CAP = 256
K_BLOCK = 8
F32 = jnp.float32
BF16 = jnp.bfloat16


def odd_rows(rows):
    return lax.broadcasted_iota(jnp.int32, (rows, 128), 0) % 2 == 1


def extract_kernel(q_ref, north_ref, south_ref):
    levels = q_ref.shape[1]
    odd = odd_rows(16)

    def level(k, carry):
        for pair in range(GROUP // 2):
            a = q_ref[2 * pair, k].astype(F32)
            b = q_ref[2 * pair + 1, k].astype(F32)
            north_ref[0, k, pair] = jnp.where(odd, a, pltpu.roll(b, 15, 0)).astype(BF16)
            south_ref[0, k, pair] = jnp.where(odd, pltpu.roll(b, 1, 0), a).astype(BF16)
        return carry

    lax.fori_loop(0, levels, level, 0)


def extract(q, first, groups):
    levels = q.shape[1]
    shape = jax.ShapeDtypeStruct((groups, levels, GROUP // 2, 16, 128), BF16)
    block = pl.BlockSpec((1, levels, GROUP // 2, 16, 128), lambda g: (g, 0, 0, 0, 0))
    return pl.pallas_call(
        extract_kernel,
        grid=(groups,),
        in_specs=[pl.BlockSpec((GROUP, levels, 16, 128), lambda g: (g + first, 0, 0, 0))],
        out_specs=[block, block],
        out_shape=[shape, shape],
        cost_estimate=pl.CostEstimate(
            flops=groups * 10**6, bytes_accessed=groups * 1200000, transcendentals=0
        ),
        compiler_params=pltpu.CompilerParams(vmem_limit_bytes=16 << 20),
        name="extract",
    )(q)


def lane_shift(x, lane, toward_east):
    if toward_east:
        turned = pltpu.roll(x, 127, 1)
        return jnp.where(lane == 127, pltpu.roll(turned, 14, 0), turned)
    turned = pltpu.roll(x, 1, 1)
    return jnp.where(lane == 0, pltpu.roll(turned, 2, 0), turned)


def advect_kernel(place_ref, q_ref, low_ref, high_ref, lat_ref, lon_ref, above_ref, *refs):
    outs, held = refs[:-1], refs[-1]
    levels = q_ref.shape[1]
    rows = levels * GROUP
    odd = odd_rows(16)
    lane = lax.broadcasted_iota(jnp.int32, (16, 128), 1)

    def level(k, carry):
        south = lat_ref[k].astype(F32)
        north = jnp.where(
            odd, pltpu.roll(above_ref[k].astype(F32), 1, 0), pltpu.roll(south, 15, 0)
        )
        west = lon_ref[k].astype(F32)
        east = lane_shift(west, lane, True)
        from_south, from_west = jnp.maximum(south, 0.0), jnp.maximum(west, 0.0)
        from_north, from_east = -jnp.minimum(north, 0.0), -jnp.minimum(east, 0.0)
        own = (
            1.0
            - (jnp.maximum(north, 0.0) - jnp.minimum(south, 0.0))
            - (jnp.maximum(east, 0.0) - jnp.minimum(west, 0.0))
        )
        for pair in range(GROUP // 2):
            low = low_ref[0, k, pair].astype(F32)
            high = high_ref[0, k, pair].astype(F32)
            for part in range(2):
                q = q_ref[2 * pair + part, k].astype(F32)
                below = low if part else pltpu.roll(low, 15, 0)
                above = high if part else pltpu.roll(high, 1, 0)
                q_s = jnp.where(odd, pltpu.roll(q, 1, 0), below)
                q_n = jnp.where(odd, above, pltpu.roll(q, 15, 0))
                q_w = lane_shift(q, lane, False)
                q_e = lane_shift(q, lane, True)
                new = (
                    own * q
                    + (from_south * q_s + from_north * q_n)
                    + (from_west * q_w + from_east * q_e)
                )
                start = k * GROUP + (2 * pair + part)
                held[pl.ds(start, 16, stride=rows), :] = new
        return carry

    lax.fori_loop(0, levels, level, 0)
    place = place_ref[0]
    for shift, out in enumerate(outs):
        target = lax.rem(place + shift, 4)
        for lat in range(2):
            for half in range(2):
                base = pl.multiple_of((4 * target + (2 * half + lat)) * rows, 8)
                column = (2 * lat + half) * 128
                out[0, :, column : column + 128] = held[pl.ds(base, rows), :].astype(BF16)


def advect(place, q, low, high, lat, lon, above, first, halo_first, groups):
    levels = q.shape[1]
    rows = levels * GROUP
    halo = pl.BlockSpec(
        (1, levels, GROUP // 2, 16, 128), lambda g, p: (g + halo_first, 0, 0, 0, 0)
    )
    face = pl.BlockSpec((levels, 16, 128), lambda g, p: (0, 0, 0))
    return pl.pallas_call(
        advect_kernel,
        grid_spec=pltpu.PrefetchScalarGridSpec(
            num_scalar_prefetch=1,
            grid=(groups,),
            in_specs=[
                pl.BlockSpec((GROUP, levels, 16, 128), lambda g, p: (g + first, 0, 0, 0)),
                halo,
                halo,
                face,
                face,
                face,
            ],
            out_specs=[pl.BlockSpec((1, rows, 512), lambda g, p: (g, 0, 0))] * 4,
            scratch_shapes=[pltpu.VMEM((16 * rows, 128), F32)],
        ),
        out_shape=[jax.ShapeDtypeStruct((groups, rows, 512), BF16)] * 4,
        cost_estimate=pl.CostEstimate(
            flops=groups * 10**7, bytes_accessed=groups * 2000000, transcendentals=0
        ),
        compiler_params=pltpu.CompilerParams(vmem_limit_bytes=24 << 20),
        name="advect",
    )(place, q, low, high, lat, lon, above)


def table_kernel(
    matrix_ref, mask_ref, order_ref, rain_ref, small_ref, placing_ref, back_ref, wet_ref, all_ref
):
    columns = mask_ref.shape[1]

    @pl.when(pl.program_id(0) == 0)
    def _():
        mask = mask_ref[...]
        order = order_ref[...]
        row = lax.broadcasted_iota(jnp.int32, (columns, columns), 0)
        column = lax.broadcasted_iota(jnp.int32, (columns, columns), 1)
        earlier = jnp.where(row < column, 1.0, 0.0).astype(BF16)
        ones = jnp.where(mask > 0, 1.0, 0.0)
        wide = jnp.broadcast_to(ones, (8, columns)).astype(BF16)
        rank = jnp.dot(wide, earlier, preferred_element_type=F32)[0:1]
        rank = jnp.where(mask > 0, rank, -1.0).astype(jnp.int32)
        slot = lax.broadcasted_iota(jnp.int32, (CAP, columns), 0)
        back = jnp.where(slot == rank, 1.0, 0.0).astype(BF16)
        back_ref[...] = back
        whole = jnp.where(row == order, 1.0, 0.0)
        placing_ref[:, :columns] = jnp.where(mask > 0, 0.0, whole).astype(BF16)
        placing_ref[:, columns:] = lax.dot_general(
            whole.astype(BF16), back, (((1,), (1,)), ((), ())), preferred_element_type=F32
        ).astype(BF16)
        wet = lax.dot_general(
            rain_ref[...], back, (((1,), (1,)), ((), ())), preferred_element_type=F32
        )
        for tile in range(CAP // 128):
            wet_ref[tile] = wet[:, tile * 128 : (tile + 1) * 128]
        for tile in range(columns // 128):
            all_ref[tile] = rain_ref[:, tile * 128 : (tile + 1) * 128].astype(F32)

    small = lax.dot_general(
        matrix_ref[...], back_ref[...], (((1,), (1,)), ((), ())), preferred_element_type=F32
    )
    for tile in range(CAP // 128):
        small_ref[tile] = small[:, tile * 128 : (tile + 1) * 128]


def tables(matrix, mask, order, rain):
    rows, columns = matrix.shape
    levels = rain.shape[0]
    steps = 9
    whole = lambda *shape: pl.BlockSpec(shape, lambda i: (0,) * len(shape))
    return pl.pallas_call(
        table_kernel,
        grid=(steps,),
        in_specs=[
            pl.BlockSpec((rows // steps, columns), lambda i: (i, 0)),
            whole(1, columns),
            whole(1, columns),
            whole(levels, columns),
        ],
        out_specs=[
            pl.BlockSpec((CAP // 128, rows // steps, 128), lambda i: (0, i, 0)),
            whole(columns, columns + CAP),
            whole(CAP, columns),
            whole(CAP // 128, levels, 128),
            whole(columns // 128, levels, 128),
        ],
        out_shape=[
            jax.ShapeDtypeStruct((CAP // 128, rows, 128), F32),
            jax.ShapeDtypeStruct((columns, columns + CAP), BF16),
            jax.ShapeDtypeStruct((CAP, columns), BF16),
            jax.ShapeDtypeStruct((CAP // 128, levels, 128), F32),
            jax.ShapeDtypeStruct((columns // 128, levels, 128), F32),
        ],
        cost_estimate=pl.CostEstimate(
            flops=2 * rows * columns * CAP, bytes_accessed=12 * 10**6, transcendentals=0
        ),
        compiler_params=pltpu.CompilerParams(vmem_limit_bytes=24 << 20),
        name="tables",
    )(matrix, mask, order, rain)


def physics_kernel(
    place_ref,
    part0_ref,
    part1_ref,
    part2_ref,
    part3_ref,
    placing_ref,
    back_ref,
    matrix_ref,
    rain_ref,
    wet_ref,
    rate_ref,
    out_ref,
    dry,
    moist,
    held,
):
    groups, rows, columns = part0_ref.shape
    levels = dry.shape[1] // GROUP
    step = pl.program_id(0)

    @pl.when(step == 0)
    def _():
        for shift, part in enumerate((part0_ref, part1_ref, part2_ref, part3_ref)):
            source = lax.rem(place_ref[0] + (4 - shift), 4)
            base = pl.multiple_of(source * rows, 8)
            for g in range(groups):
                placed = jnp.dot(part[g], placing_ref[...], preferred_element_type=F32)
                dry[g, pl.ds(base, rows), :] = placed[:, :columns]
                moist[g, pl.ds(base, rows), :] = placed[:, columns:]

    first = step * K_BLOCK
    rates = [rate_ref[g] for g in range(groups)]
    washed = [[[None] * 2 for _ in range(K_BLOCK)] for _ in range(groups)]
    for tile in range(CAP // 128):
        lanes = slice(tile * 128, (tile + 1) * 128)

        def source_levels(block, sums, tile=tile, lanes=lanes):
            sums = list(sums)
            for inner in range(8):
                e = block * 8 + inner
                spot = pl.multiple_of(block * (8 * GROUP) + inner * GROUP, GROUP)
                values = [moist[g, pl.ds(spot, GROUP), lanes] for g in range(groups)]
                for k in range(K_BLOCK):
                    weight = matrix_ref[tile, k, pl.ds(e, GROUP, stride=0), :]
                    for g in range(groups):
                        at = g * K_BLOCK + k
                        sums[at] = sums[at] + weight * values[g]
            return tuple(sums)

        zero = jnp.zeros((GROUP, 128), F32)
        sums = lax.fori_loop(
            0, levels // 8, source_levels, (zero,) * (groups * K_BLOCK)
        )
        for k in range(K_BLOCK):
            wet = wet_ref[tile, pl.ds(first + k, GROUP, stride=0), :]
            for g in range(groups):
                washed[g][k][tile] = sums[g * K_BLOCK + k] * jnp.exp(-rates[g] * wet)
    for g in range(groups):
        packed = jnp.concatenate(
            [jnp.concatenate(washed[g][k], axis=1) for k in range(K_BLOCK)], axis=0
        ).astype(BF16)
        spread = jnp.dot(packed, back_ref[...], preferred_element_type=F32)
        for k in range(K_BLOCK):
            spot = pl.multiple_of((first + k) * GROUP, GROUP)
            plain = dry[g, pl.ds(spot, GROUP), :]
            for tile in range(columns // 128):
                lanes = slice(tile * 128, (tile + 1) * 128)
                wet = rain_ref[tile, pl.ds(first + k, GROUP, stride=0), :]
                held[tile, pl.ds(g * GROUP * levels + first + k, GROUP, stride=levels), :] = (
                    spread[k * GROUP : (k + 1) * GROUP, lanes]
                    + plain[:, lanes] * jnp.exp(-rates[g] * wet)
                )

    @pl.when(step == pl.num_programs(0) - 1)
    def _():
        for tile in range(columns // 128):
            out_ref[:, tile * 128 : (tile + 1) * 128] = held[tile].astype(BF16)


def physics(place, parts, placing, back, matrix, rain, wet, rates, first, groups):
    rows, columns = parts[0].shape[1:]
    levels = rain.shape[1]
    whole = lambda *shape: pl.BlockSpec(shape, lambda i, p: (0,) * len(shape))
    flops = groups * 2 * GROUP * levels * (columns * (columns + 2 * CAP) + levels * CAP * 20)
    return pl.pallas_call(
        physics_kernel,
        grid_spec=pltpu.PrefetchScalarGridSpec(
            num_scalar_prefetch=1,
            grid=(levels // K_BLOCK,),
            in_specs=[whole(groups, rows, columns)] * 4
            + [
                whole(columns, columns + CAP),
                whole(CAP, columns),
                pl.BlockSpec((CAP // 128, K_BLOCK, levels, 128), lambda i, p: (0, i, 0, 0)),
                whole(columns // 128, levels, 128),
                whole(CAP // 128, levels, 128),
                pl.BlockSpec((groups, GROUP, 128), lambda i, p: (first // groups, 0, 0)),
            ],
            out_specs=whole(groups * GROUP * levels, columns),
            scratch_shapes=[
                pltpu.VMEM((groups, levels * GROUP, columns), F32),
                pltpu.VMEM((groups, levels * GROUP, CAP), F32),
                pltpu.VMEM((columns // 128, groups * GROUP * levels, 128), F32),
            ],
        ),
        out_shape=jax.ShapeDtypeStruct((groups * GROUP * levels, columns), BF16),
        cost_estimate=pl.CostEstimate(
            flops=flops, bytes_accessed=groups * 1200000 + 6500000, transcendentals=0
        ),
        compiler_params=pltpu.CompilerParams(vmem_limit_bytes=32 << 20),
        name="physics",
    )(place, *parts, placing, back, matrix, rain, wet, rates)


def choose_kernel(flag_ref, own_ref, partner_ref, *refs):
    out_ref = refs[-1]

    @pl.when(flag_ref[0] > 0)
    def _():
        out_ref[...] = partner_ref[...]

    @pl.when(flag_ref[0] <= 0)
    def _():
        out_ref[...] = own_ref[...]


def choose(flag, own, partner, whole, shape, first, groups):
    rows = shape[0] // (sum(CHUNKS))
    columns = shape[1]
    operands = [own, partner]
    specs = [
        pl.BlockSpec((rows, columns), lambda g, f: (jnp.where(f[0] > 0, 0, g), 0)),
        pl.BlockSpec((rows, columns), lambda g, f: (jnp.where(f[0] > 0, g, 0), 0)),
    ]
    aliases = {}
    if whole is not None:
        operands.append(whole)
        specs.append(pl.BlockSpec(memory_space=pl.ANY))
        aliases = {3: 0}
    return pl.pallas_call(
        choose_kernel,
        grid_spec=pltpu.PrefetchScalarGridSpec(
            num_scalar_prefetch=1,
            grid=(groups,),
            in_specs=specs,
            out_specs=pl.BlockSpec((rows, columns), lambda g, f: (g + first, 0)),
        ),
        out_shape=jax.ShapeDtypeStruct(shape, BF16),
        input_output_aliases=aliases,
        cost_estimate=pl.CostEstimate(
            flops=0, bytes_accessed=groups * 1200000, transcendentals=0
        ),
        compiler_params=pltpu.CompilerParams(vmem_limit_bytes=16 << 20),
        name="choose",
    )(flag, *operands)


def shifted(value, axis, steps):
    count = lax.axis_size(axis)
    pairs = [(i, i + steps) for i in range(count) if 0 <= i + steps < count]
    return lax.ppermute(value, axis, pairs)


def turned(value, axis, steps):
    count = lax.axis_size(axis)
    return lax.ppermute(value, axis, [(i, (i + steps) % count) for i in range(count)])


def paired(value, axis):
    count = lax.axis_size(axis)
    return lax.ppermute(value, axis, [(i, i ^ (count // 2)) for i in range(count)])


def tiled_rows(value):
    lead = value.shape[:-2]
    lats, lons = value.shape[-2:]
    split = value.reshape(*lead, lats, lons // 128, 128)
    return jnp.swapaxes(split, -3, -2).reshape(*lead, lats * lons // 128, 128)


def local(
    tracer_dyn,
    courant_lat,
    courant_lon,
    conv_matrix,
    conv_mask,
    column_order,
    rain,
    scav_rate,
    pair_flag,
):
    n_lat = lax.axis_size("lat")
    n_lev = lax.axis_size("lev")
    tracers = tracer_dyn.shape[0]
    levels, columns = rain.shape
    lev_place = lax.axis_index("lev")
    place = lev_place.astype(jnp.int32).reshape(1)
    pair_index = lax.axis_index("lat") % (n_lat // 2) * n_lev + lev_place
    flag = lax.dynamic_slice_in_dim(pair_flag, pair_index, 1)
    rates = jnp.broadcast_to(
        scav_rate.reshape(tracers // GROUP, GROUP, 1), (tracers // GROUP, GROUP, 128)
    )

    q = tiled_rows(tracer_dyn)
    lat, lon = tiled_rows(courant_lat), tiled_rows(courant_lon)
    above = tiled_rows(shifted(courant_lat, "lat", -1))
    halos = []
    spans = ((0, CHUNKS[0]), (CHUNKS[0], sum(CHUNKS) - CHUNKS[0]))
    for first, groups in spans:
        north, south = extract(q, first, groups)
        halos.append((shifted(north, "lat", 1), shifted(south, "lat", -1)))
    small, placing, back, wet, wet_all = tables(
        conv_matrix.reshape(levels * levels, columns),
        conv_mask.reshape(1, columns),
        column_order.reshape(1, columns),
        rain,
    )
    small = small.reshape(CAP // 128, levels, levels, 128)

    out = None
    first = 0
    for number, groups in enumerate(CHUNKS):
        low, high = halos[min(number, 1)]
        halo_first = first - spans[min(number, 1)][0]
        parts = advect(place, q, low, high, lat, lon, above, first, halo_first, groups)
        parts = [parts[0]] + [turned(parts[s], "lev", s) for s in range(1, n_lev)]
        own = physics(place, parts, placing, back, small, wet_all, wet, rates, first, groups)
        partner = paired(own, "lat")
        out = choose(flag, own, partner, out, (tracers * levels, columns), first, groups)
        first += groups
    return out.reshape(tracers, levels, columns)


def solution(mesh):
    placed = (
        P(None, "lev", "lat", None),
        P("lev", "lat", None),
        P("lev", "lat", None),
        P(None, None, ("lat", "lev")),
        P(("lat", "lev")),
        P(("lat", "lev")),
        P(None, ("lat", "lev")),
        P(),
        P(),
    )
    return jax.shard_map(
        local, mesh=mesh, in_specs=placed, out_specs=P(None, None, ("lat", "lev")), check_vma=False
    )
```

time: 373 us -> 229 us (0.61)
  local copies, waits for them, and re-layouts: 131 us -> 11.8 us
  Pallas kernels: 0 us -> 91.6 us
  waiting for transfers between devices: 144 us -> 86.1 us
  other arithmetic: 56.8 us -> 0.01 us
  matrix products: 21 us -> 0 us
  starting transfers between devices: 18 us -> 38 us
    pallas_call x0 -> x18, Pallas kernels: none -> 91.6 us  [the longest x5 48.8 us: physics(): pl.pallas_call(physics_kernel, grid_spec=pltpu.PrefetchScalarGridSpec(num...]
    convert_element_type x4 -> x0, other arithmetic: 47 us -> none  [the longest x1 46.9 us: local(): advected = advect_block(center, south_side, north_side, south_face, north...]
    all_to_all x1 -> x0, waiting for transfers between devices: 40.6 us -> none  [local(): lax.all_to_all(sectioned, 'lev', split_axis=4, concat_axis=1, tiled=True)]
    reshape x3 -> x0, local copies, waits for them, and re-layouts: 27.8 us -> none  [the longest x2 16.7 us: local(): advected.reshape(tracers, 1, lev_group, lat_dev, n_lev, lon_block)]
    slice x6 -> x0, local copies, waits for them, and re-layouts: 26.7 us -> none  [the longest x2 16.6 us: advect_block(): jnp.roll(center, -1, axis=-1)]
    ppermute x3 -> x0, local copies, waits for them, and re-layouts: 26.2 us -> none  [the longest x1 11.2 us: swapped(): lax.ppermute(shard, axis, [(i, i ^ 1 << apart) for i in range(lax.axis_si...]
    ppermute x4 -> x25, starting transfers between devices: 12.8 us -> 38 us  [the longest x15 15.1 us: turned(): lax.ppermute(value, axis, [(i, (i + steps) % count) for i in range(count)])]
    dot_general x2 -> x0, matrix products: 21 us -> none  [the longest x1 16.7 us: convect(): jnp.einsum('kec,tec->tkc', matrix, tracers_bf, preferred_element_type=jnp...]
  transfers between devices with their start and end apart: 5 -> 25, of which waited for: 4 -> 6; matrix products, arithmetic and copies ran while one was open for 14% -> 0% of each run, Pallas kernels for 0% -> 34%
where the time goes in v1:
time: 229 us; the launch traced here: 228 us
  Pallas kernels  91.6 us (40%)
  waiting for transfers between devices  86.1 us (38%)
  starting transfers between devices  38 us (17%)
  local copies, waits for them, and re-layouts  11.8 us (5%)
    ppermute x5, waiting for transfers between devices, paired(): lax.ppermute(value, axis, [(i, i ^ count // 2) for i in range(count)])  52.2 us
    pallas_call x5, Pallas kernels, physics(): pl.pallas_call(physics_kernel, grid_spec=pltpu.PrefetchScalarGridSpec(num...  48.8 us
    ppermute x5, waiting for transfers between devices, shifted(): return lax.ppermute(value, axis, pairs)  24.3 us
    pallas_call x5, Pallas kernels, advect(): pl.pallas_call(advect_kernel, grid_spec=pltpu.PrefetchScalarGridSpec(num_...  22.4 us
    ppermute x15, starting transfers between devices, turned(): lax.ppermute(value, axis, [(i, (i + steps) % count) for i in range(count)])  15.1 us
    ppermute x5, starting transfers between devices, shifted(): return lax.ppermute(value, axis, pairs)  14.3 us
    pallas_call x5, Pallas kernels, choose(): pl.pallas_call(choose_kernel, grid_spec=pltpu.PrefetchScalarGridSpec(num_...  11.8 us
    unnamed x36, local copies, waits for them, and re-layouts  11 us
  transfers between devices with their start and end apart: 25, of which 6 were waited for; matrix products, arithmetic and copies ran while one was open for 0% of the time, Pallas kernels for 34%

profile of v1, /device:TPU:97, one launch (start us, length us, event | category | flops | bytes accessed | tf_op | source)
XLA Modules:
  0.0 227.7 jit_solution(13298062609903438906)
XLA Ops:
  0.0 2.3 %copy-done = bf16[64,18,2,1024]{3,2,1,0:T(2,128)(2,1)S(1)} copy-done((bf16[64,18,2,1024]{3,2,1,0:T(2,128)(2,1)S(1)}, bf16[64,18,2,1024]{3,2,1,0:T(2,128)(2,1)}, u32[]{:S(2)}) %copy-start) | copy-done | bytes 4718616
  2.3 4.2 %extract.2 = (bf16[7,18,4,16,128]{4,3,2,1,0:T(8,128)(2,1)}, bf16[7,18,4,16,128]{4,3,2,1,0:T(8,128)(2,1)}) custom-call(bf16[64,18,16,128]{3,2,1,0:T(8,128)(2,1)S(1)} %bitcast.26), custom_call_target="tpu_custom_call" | custom-call | flops 7000000 | bytes 8400000 | tf_op jit(solution)/shard_map/extract/pallas_call | solution.py:41
  6.5 2.3 %collective-permute-start = (bf16[7,18,4,16,128]{4,3,2,1,0:T(8,128)(2,1)}, bf16[7,18,4,16,128]{4,3,2,1,0:T(8,128)(2,1)S(1)}, u32[]{:S(2)}, u32[]{:S(2)}) collective-permute-start(bf16[7,18,4,16,128]{4,3,2,1,0:T(8,128)(2,1)} %get-tuple-element.34), channel_id=1, source_target_pairs={{0,4},{4,8},{8,12},{12,16},{16,20},{20,24},{24,28},{28,32},{32,36}... | collective-permute-start | bytes 6193160 | tf_op jit(solution)/shard_map/ppermute | solution.py:383
  8.9 2.2 collective-permute-start.1
  11.1 3.6 %collective-permute-start.2 = (bf16[18,2,1024]{2,1,0:T(2,128)(2,1)S(1)}, bf16[18,2,1024]{2,1,0:T(2,128)(2,1)S(1)}, u32[]{:S(2)}, u32[]{:S(2)}) collective-permute-start(bf16[18,2,1024]{2,1,0:T(2,128)(2,1)S(1)} %copy-done.4), channel_id=1, source_target_pairs={{4,0},{8,4},{12,8},{16,12},{20,16},{24,20},{28,24},{32,28},{36,32}... | collective-permute-start | bytes 221192 | tf_op jit(solution)/shard_map/ppermute | solution.py:383
  14.7 24.2 %collective-permute-done.2 = bf16[18,2,1024]{2,1,0:T(2,128)(2,1)S(1)} collective-permute-done((bf16[18,2,1024]{2,1,0:T(2,128)(2,1)S(1)}, bf16[18,2,1024]{2,1,0:T(2,128)(2,1)S(1)}, u32[]{:S(2)}, u32[]{:S(2)}) %collective-permute-start.2) | collective-permute-done | bytes 73760 | tf_op jit(solution)/shard_map/ppermute | solution.py:383
  39.0 0.0 collective-permute-done.1.high_ref
  39.0 0.0 copy-start.1
  39.0 2.3 %copy-done.1 = bf16[64,18,2,1024]{3,2,1,0:T(2,128)(2,1)S(1)} copy-done((bf16[64,18,2,1024]{3,2,1,0:T(2,128)(2,1)S(1)}, bf16[64,18,2,1024]{3,2,1,0:T(2,128)(2,1)}, u32[]{:S(2)}) %copy-start.1) | copy-done | bytes 4718616
  41.3 6.0 %advect.7 = (bf16[2,144,512]{2,1,0:T(8,128)(2,1)S(1)}, bf16[2,144,512]{2,1,0:T(8,128)(2,1)}, bf16[2,144,512]{2,1,0:T(8,128)(2,1)}, bf16[2,144,512]{2,1,0:T(8,128)(2,1)}) custom-call(s32[1]{0:T(128)} %bitcast.place_ref, bf16[64,18,16,128]{3,2,1,0:T(8,128)(2,1)S(1)} %bitcast.27, bf16[7,18,4,16,128]{4,3,2,1,0:T(8,128)(2,1)S(1)} %collective-permute-done.low_ref, ...), custom_call_target="tpu_custom_call" | custom-call | flops 20000000 | bytes 4000000 | tf_op jit(solution)/shard_map/advect/pallas_call | solution.py:122
  47.3 1.3 collective-permute-start.11
  48.6 2.6 %collective-permute-start.12 = (bf16[2,144,512]{2,1,0:T(8,128)(2,1)}, bf16[2,144,512]{2,1,0:T(8,128)(2,1)}, u32[]{:S(2)}, u32[]{:S(2)}) collective-permute-start(bf16[2,144,512]{2,1,0:T(8,128)(2,1)} %get-tuple-element.51), channel_id=1, source_target_pairs={{0,2},{1,3},{2,0},{3,1},{4,6},{5,7},{6,4},{7,5},{8,10},{9,11},{10,... | collective-permute-start | bytes 884744 | tf_op jit(solution)/shard_map/ppermute | solution.py:388
  51.2 1.1 collective-permute-start.13
  52.3 5.9 %advect.6 = (bf16[2,144,512]{2,1,0:T(8,128)(2,1)S(1)}, bf16[2,144,512]{2,1,0:T(8,128)(2,1)}, bf16[2,144,512]{2,1,0:T(8,128)(2,1)S(1)}, bf16[2,144,512]{2,1,0:T(8,128)(2,1)S(1)}) custom-call(s32[1]{0:T(128)} %bitcast.place_ref, bf16[64,18,16,128]{3,2,1,0:T(8,128)(2,1)S(1)} %bitcast.28, bf16[7,18,4,16,128]{4,3,2,1,0:T(8,128)(2,1)S(1)} %collective-permute-done.low_ref, ...), custom_call_target="tpu_custom_call" | custom-call | flops 20000000 | bytes 4000000 | tf_op jit(solution)/shard_map/advect/pallas_call | solution.py:122
  58.3 0.7 copy-done.11
  59.0 0.7 copy-done.13
  59.7 0.4 collective-permute-start.7
  60.1 0.1 broadcast_in_dim.7
  60.2 2.3 %copy-done.2 = bf16[64,18,2,1024]{3,2,1,0:T(2,128)(2,1)S(1)} copy-done((bf16[64,18,2,1024]{3,2,1,0:T(2,128)(2,1)S(1)}, bf16[64,18,2,1024]{3,2,1,0:T(2,128)(2,1)}, u32[]{:S(2)}) %copy-start.2) | copy-done | bytes 4718616
  62.5 0.0 slice-start.1
  62.5 0.2 extract.3
  62.8 0.9 collective-permute-start.8
  63.7 2.1 collective-permute-start.9
  65.8 2.5 %copy-done.3 = bf16[72,72,512]{2,1,0:T(8,128)(2,1)S(1)} copy-done((bf16[72,72,512]{2,1,0:T(8,128)(2,1)S(1)}, bf16[72,72,512]{2,1,0:T(8,128)(2,1)}, u32[]{:S(2)}) %copy-start.3) | copy-done | bytes 5308440
  68.3 4.1 %tables.1 = (f32[2,5184,128]{2,1,0:T(8,128)S(1)}, bf16[512,768]{1,0:T(8,128)(2,1)S(1)}, bf16[256,512]{1,0:T(8,128)(2,1)S(1)}, f32[2,72,128]{2,1,0:T(8,128)S(1)}, f32[4,72,128]{2,1,0:T(8,128)S(1)}) custom-call(bf16[5184,512]{1,0:T(8,128)(2,1)S(1)} %bitcast.40, s32[1,512]{1,0:T(1,128)S(1)} %bitcast.56, s32[1,512]{1,0:T(1,128)S(1)} %bitcast.57, ...), custom_call_target="tpu_custom_call" | custom-call | flops 1358954496 | bytes 12000000 | tf_op jit(solution)/shard_map/tables/pallas_call | solution.py:191
  72.5 5.3 %advect.5 = (bf16[2,144,512]{2,1,0:T(8,128)(2,1)S(1)}, bf16[2,144,512]{2,1,0:T(8,128)(2,1)S(1)}, bf16[2,144,512]{2,1,0:T(8,128)(2,1)S(1)}, bf16[2,144,512]{2,1,0:T(8,128)(2,1)S(1)}) custom-call(s32[1]{0:T(128)} %bitcast.place_ref, bf16[64,18,16,128]{3,2,1,0:T(8,128)(2,1)S(1)} %bitcast.32, bf16[7,18,4,16,128]{4,3,2,1,0:T(8,128)(2,1)S(1)} %collective-permute-done.low_ref, ...), custom_call_target="tpu_custom_call" | custom-call | flops 20000000 | bytes 4000000 | tf_op jit(solution)/shard_map/advect/pallas_call | solution.py:122
  77.8 0.0 collective-permute-done.12.part2_ref
  77.8 0.1 collective-permute-start.3
  77.9 1.8 collective-permute-start.4
  79.7 0.0 collective-permute-done.7.part1_ref
  79.7 2.0 collective-permute-start.5
  81.7 0.1 broadcast_in_dim.8.rate_ref
  81.7 12.7 %physics.7.own_ref = bf16[1152,512]{1,0:T(8,128)(2,1)} custom-call(s32[1]{0:T(128)} %bitcast.place_ref, bf16[2,144,512]{2,1,0:T(8,128)(2,1)S(1)} %copy-done.7, bf16[2,144,512]{2,1,0:T(8,128)(2,1)} %collective-permute-done.11.part1_ref, bf16[2,144,512]{2,1,0:T(8,128)(2,1)} %collective-permute-done.12.part2_ref, ...), custom_call_target="tpu_custom_call" | custom-call | flops 2057306112 | bytes 8900000 | tf_op jit(solution)/shard_map/physics/pallas_call | solution.py:307
  94.5 0.0 collective-permute-done.8.part2_ref
  94.5 4.3 %collective-permute-start.19 = (bf16[1,18,4,16,128]{4,3,2,1,0:T(8,128)(2,1)S(1)}, bf16[1,18,4,16,128]{4,3,2,1,0:T(8,128)(2,1)S(1)}, u32[]{:S(2)}, u32[]{:S(2)}) collective-permute-start(bf16[1,18,4,16,128]{4,3,2,1,0:T(8,128)(2,1)S(1)} %get-tuple-element.57), channel_id=1, source_target_pairs={{0,4},{4,8},{8,12},{12,16},{16,20},{20,24},{24,28},{28,32},{32,36}... | collective-permute-start | bytes 884744 | tf_op jit(solution)/shard_map/ppermute | solution.py:383
  98.7 0.0 collective-permute-done.9.part3_ref
  98.8 1.9 collective-permute-start.20
  100.7 11.6 %physics.6.own_ref = bf16[1152,512]{1,0:T(8,128)(2,1)} custom-call(s32[1]{0:T(128)} %bitcast.place_ref, bf16[2,144,512]{2,1,0:T(8,128)(2,1)S(1)} %get-tuple-element.45.part0_ref, bf16[2,144,512]{2,1,0:T(8,128)(2,1)S(1)} %collective-permute-done.7.part1_ref, bf16[2,144,512]{2,1,0:T(8,128)(2,1)S(1)} %collective-permute-done.8.part2_ref, ...), custom_call_target="tpu_custom_call" | custom-call | flops 2057306112 | bytes 8900000 | tf_op jit(solution)/shard_map/physics/pallas_call | solution.py:307
  112.3 2.5 %collective-permute-start.10 = (bf16[1152,512]{1,0:T(8,128)(2,1)}, bf16[1152,512]{1,0:T(8,128)(2,1)}, u32[]{:S(2)}, u32[]{:S(2)}) collective-permute-start(bf16[1152,512]{1,0:T(8,128)(2,1)} %physics.6.own_ref), channel_id=1, source_target_pairs={{0,64},{4,68},{8,72},{12,76},{16,80},{20,84},{24,88},{28,92},{32,9... | collective-permute-start | bytes 3538952 | tf_op jit(solution)/shard_map/ppermute | solution.py:393
  114.8 0.4 collective-permute-start.14
  115.3 11.6 %physics.5.own_ref = bf16[1152,512]{1,0:T(8,128)(2,1)} custom-call(s32[1]{0:T(128)} %bitcast.place_ref, bf16[2,144,512]{2,1,0:T(8,128)(2,1)S(1)} %get-tuple-element.36.part0_ref, bf16[2,144,512]{2,1,0:T(8,128)(2,1)S(1)} %collective-permute-done.3.part1_ref, bf16[2,144,512]{2,1,0:T(8,128)(2,1)S(1)} %collective-permute-done.4.part2_ref, ...), custom_call_target="tpu_custom_call" | custom-call | flops 2057306112 | bytes 8900000 | tf_op jit(solution)/shard_map/physics/pallas_call | solution.py:307
  126.9 2.5 %collective-permute-start.6 = (bf16[1152,512]{1,0:T(8,128)(2,1)}, bf16[1152,512]{1,0:T(8,128)(2,1)}, u32[]{:S(2)}, u32[]{:S(2)}) collective-permute-start(bf16[1152,512]{1,0:T(8,128)(2,1)} %physics.5.own_ref), channel_id=1, source_target_pairs={{0,64},{4,68},{8,72},{12,76},{16,80},{20,84},{24,88},{28,92},{32,9... | collective-permute-start | bytes 3538952 | tf_op jit(solution)/shard_map/ppermute | solution.py:393
  129.4 2.1 advect.9
  131.5 0.1 collective-permute-start.21
  131.6 0.9 collective-permute-start.22
  132.6 3.1 %advect.8 = (bf16[1,144,512]{2,1,0:T(8,128)(2,1)S(1)}, bf16[1,144,512]{2,1,0:T(8,128)(2,1)S(1)}, bf16[1,144,512]{2,1,0:T(8,128)(2,1)S(1)}, bf16[1,144,512]{2,1,0:T(8,128)(2,1)S(1)}) custom-call(s32[1]{0:T(128)} %bitcast.place_ref, bf16[64,18,16,128]{3,2,1,0:T(8,128)(2,1)S(1)} %bitcast.34, bf16[7,18,4,16,128]{4,3,2,1,0:T(8,128)(2,1)S(1)} %collective-permute-done.low_ref, ...), custom_call_target="tpu_custom_call" | custom-call | flops 10000000 | bytes 2000000 | tf_op jit(solution)/shard_map/advect/pallas_call | solution.py:122
  135.7 5.4 %collective-permute-done.21.part1_ref = bf16[1,144,512]{2,1,0:T(8,128)(2,1)S(1)} collective-permute-done((bf16[1,144,512]{2,1,0:T(8,128)(2,1)S(1)}, bf16[1,144,512]{2,1,0:T(8,128)(2,1)S(1)}, u32[]{:S(2)}, u32[]{:S(2)}) %collective-permute-start.21) | collective-permute-done | bytes 147488 | tf_op jit(solution)/shard_map/ppermute | solution.py:388
  141.1 0.0 collective-permute-start.23
  141.1 1.5 collective-permute-start.15
  142.5 2.9 %collective-permute-done.23.part3_ref = bf16[1,144,512]{2,1,0:T(8,128)(2,1)S(1)} collective-permute-done((bf16[1,144,512]{2,1,0:T(8,128)(2,1)S(1)}, bf16[1,144,512]{2,1,0:T(8,128)(2,1)S(1)}, u32[]{:S(2)}, u32[]{:S(2)}) %collective-permute-start.23) | collective-permute-done | bytes 147488 | tf_op jit(solution)/shard_map/ppermute | solution.py:388
  145.5 1.2 collective-permute-done.15.part1_ref
  146.7 0.4 collective-permute-start.17
  147.0 6.4 %physics.9.own_ref = bf16[576,512]{1,0:T(8,128)(2,1)S(1)} custom-call(s32[1]{0:T(128)} %bitcast.place_ref, bf16[1,144,512]{2,1,0:T(8,128)(2,1)S(1)} %get-tuple-element.59.part0_ref, bf16[1,144,512]{2,1,0:T(8,128)(2,1)S(1)} %collective-permute-done.21.part1_ref, bf16[1,144,512]{2,1,0:T(8,128)(2,1)S(1)} %collective-permute-done.22.part2_ref, ...), custom_call_target="tpu_custom_call" | custom-call | flops 1028653056 | bytes 7700000 | tf_op jit(solution)/shard_map/physics/pallas_call | solution.py:307
  153.5 0.5 collective-permute-start.24
  154.0 6.4 %physics.8.own_ref = bf16[576,512]{1,0:T(8,128)(2,1)S(1)} custom-call(s32[1]{0:T(128)} %bitcast.place_ref, bf16[1,144,512]{2,1,0:T(8,128)(2,1)S(1)} %get-tuple-element.53.part0_ref, bf16[1,144,512]{2,1,0:T(8,128)(2,1)S(1)} %collective-permute-done.15.part1_ref, bf16[1,144,512]{2,1,0:T(8,128)(2,1)S(1)} %collective-permute-done.16.part2_ref, ...), custom_call_target="tpu_custom_call" | custom-call | flops 1028653056 | bytes 7700000 | tf_op jit(solution)/shard_map/physics/pallas_call | solution.py:307
  160.4 2.6 %collective-permute-start.18 = (bf16[576,512]{1,0:T(8,128)(2,1)S(1)}, bf16[576,512]{1,0:T(8,128)(2,1)S(1)}, u32[]{:S(2)}, u32[]{:S(2)}) collective-permute-start(bf16[576,512]{1,0:T(8,128)(2,1)S(1)} %physics.8.own_ref), channel_id=1, source_target_pairs={{0,64},{4,68},{8,72},{12,76},{16,80},{20,84},{24,88},{28,92},{32,9... | collective-permute-start | bytes 1769480 | tf_op jit(solution)/shard_map/ppermute | solution.py:393
  163.1 0.6 dynamic_slice.3.flag_ref
  163.7 41.1 %collective-permute-done.24.partner_ref = bf16[576,512]{1,0:T(8,128)(2,1)S(1)} collective-permute-done((bf16[576,512]{1,0:T(8,128)(2,1)S(1)}, bf16[576,512]{1,0:T(8,128)(2,1)S(1)}, u32[]{:S(2)}, u32[]{:S(2)}) %collective-permute-start.24) | collective-permute-done | bytes 589856 | tf_op jit(solution)/shard_map/ppermute | solution.py:393
  204.8 1.5 choose.5.refs_0_
  206.3 11.2 %collective-permute-done.18.partner_ref = bf16[576,512]{1,0:T(8,128)(2,1)S(1)} collective-permute-done((bf16[576,512]{1,0:T(8,128)(2,1)S(1)}, bf16[576,512]{1,0:T(8,128)(2,1)S(1)}, u32[]{:S(2)}, u32[]{:S(2)}) %collective-permute-start.18) | collective-permute-done | bytes 589856 | tf_op jit(solution)/shard_map/ppermute | solution.py:393
  217.4 1.5 choose.6.refs_0_
  218.9 2.9 %choose.7.refs_0_ = bf16[4608,512]{1,0:T(8,128)(2,1)} custom-call(s32[1]{0:T(128)} %dynamic_slice.3.flag_ref, bf16[1152,512]{1,0:T(8,128)(2,1)} %physics.7.own_ref, bf16[1152,512]{1,0:T(8,128)(2,1)} %collective-permute-done.14.partner_ref, bf16[4608,512]{1,0:T(8,128)(2,1)} %choose.6.refs_0_), custom_call_target="tpu_custom_call", output_to_operand_aliasing={{}: (3, {})} | custom-call | bytes 2400000 | tf_op jit(solution)/shard_map/choose/pallas_call | solution.py:362
  221.8 2.9 %choose.8.refs_0_ = bf16[4608,512]{1,0:T(8,128)(2,1)} custom-call(s32[1]{0:T(128)} %dynamic_slice.3.flag_ref, bf16[1152,512]{1,0:T(8,128)(2,1)} %physics.6.own_ref, bf16[1152,512]{1,0:T(8,128)(2,1)} %collective-permute-done.10.partner_ref, bf16[4608,512]{1,0:T(8,128)(2,1)} %choose.7.refs_0_), custom_call_target="tpu_custom_call", output_to_operand_aliasing={{}: (3, {})} | custom-call | bytes 2400000 | tf_op jit(solution)/shard_map/choose/pallas_call | solution.py:362
  224.8 2.9 %choose.9 = bf16[4608,512]{1,0:T(8,128)(2,1)} custom-call(s32[1]{0:T(128)} %dynamic_slice.3.flag_ref, bf16[1152,512]{1,0:T(8,128)(2,1)} %physics.5.own_ref, bf16[1152,512]{1,0:T(8,128)(2,1)} %collective-permute-done.6.partner_ref, bf16[4608,512]{1,0:T(8,128)(2,1)} %choose.8.refs_0_), custom_call_target="tpu_custom_call", output_to_operand_aliasing={{}: (3, {})} | custom-call | bytes 2400000 | tf_op jit(solution)/shard_map/choose/pallas_call | solution.py:362
  (44 shorter events, 0.1 us)
Async XLA Ops:
  0.0 2.3 %copy-start = (bf16[64,18,2,1024]{3,2,1,0:T(2,128)(2,1)S(1)}, bf16[64,18,2,1024]{3,2,1,0:T(2,128)(2,1)}, u32[]{:S(2)}) copy-start(bf16[64,18,2,1024]{3,2,1,0:T(2,128)(2,1)} %param.9) | copy-start | bytes 14155780
  2.3 8.7 %copy-start.4 = (bf16[18,2,1024]{2,1,0:T(2,128)(2,1)S(1)}, bf16[18,2,1024]{2,1,0:T(2,128)(2,1)}, u32[]{:S(2)}) copy-start(bf16[18,2,1024]{2,1,0:T(2,128)(2,1)} %param.10) | copy-start | bytes 221188
  2.3 36.6 %copy-start.5 = (bf16[18,2,1024]{2,1,0:T(2,128)(2,1)S(1)}, bf16[18,2,1024]{2,1,0:T(2,128)(2,1)}, u32[]{:S(2)}) copy-start(bf16[18,2,1024]{2,1,0:T(2,128)(2,1)} %param.11) | copy-start | bytes 221188
  6.5 32.4 %collective-permute-start = (bf16[7,18,4,16,128]{4,3,2,1,0:T(8,128)(2,1)}, bf16[7,18,4,16,128]{4,3,2,1,0:T(8,128)(2,1)S(1)}, u32[]{:S(2)}, u32[]{:S(2)}) collective-permute-start(bf16[7,18,4,16,128]{4,3,2,1,0:T(8,128)(2,1)} %get-tuple-element.34), channel_id=1, source_target_pairs={{0,4},{4,8},{8,12},{12,16},{16,20},{20,24},{24,28},{28,32},{32,36}... | collective-permute-start | bytes 6193160 | tf_op jit(solution)/shard_map/ppermute | solution.py:383
  8.9 30.1 %collective-permute-start.1 = (bf16[7,18,4,16,128]{4,3,2,1,0:T(8,128)(2,1)}, bf16[7,18,4,16,128]{4,3,2,1,0:T(8,128)(2,1)}, u32[]{:S(2)}, u32[]{:S(2)}) collective-permute-start(bf16[7,18,4,16,128]{4,3,2,1,0:T(8,128)(2,1)} %get-tuple-element.35), channel_id=1, source_target_pairs={{4,0},{8,4},{12,8},{16,12},{20,16},{24,20},{28,24},{32,28},{36,32}... | collective-permute-start | bytes 6193160 | tf_op jit(solution)/shard_map/ppermute | solution.py:383
  11.1 27.9 %collective-permute-start.2 = (bf16[18,2,1024]{2,1,0:T(2,128)(2,1)S(1)}, bf16[18,2,1024]{2,1,0:T(2,128)(2,1)S(1)}, u32[]{:S(2)}, u32[]{:S(2)}) collective-permute-start(bf16[18,2,1024]{2,1,0:T(2,128)(2,1)S(1)} %copy-done.4), channel_id=1, source_target_pairs={{4,0},{8,4},{12,8},{16,12},{20,16},{24,20},{28,24},{32,28},{36,32}... | collective-permute-start | bytes 221192 | tf_op jit(solution)/shard_map/ppermute | solution.py:383
  39.0 2.3 %copy-start.1 = (bf16[64,18,2,1024]{3,2,1,0:T(2,128)(2,1)S(1)}, bf16[64,18,2,1024]{3,2,1,0:T(2,128)(2,1)}, u32[]{:S(2)}) copy-start(bf16[64,18,2,1024]{3,2,1,0:T(2,128)(2,1)} %param.9) | copy-start | bytes 14155780
  47.3 10.9 %copy-start.6 = (bf16[2,144,512]{2,1,0:T(8,128)(2,1)}, bf16[2,144,512]{2,1,0:T(8,128)(2,1)S(1)}, u32[]{:S(2)}) copy-start(bf16[2,144,512]{2,1,0:T(8,128)(2,1)S(1)} %get-tuple-element.49.part0_ref) | copy-start | bytes 884740
  47.3 16.3 %collective-permute-start.11 = (bf16[2,144,512]{2,1,0:T(8,128)(2,1)}, bf16[2,144,512]{2,1,0:T(8,128)(2,1)}, u32[]{:S(2)}, u32[]{:S(2)}) collective-permute-start(bf16[2,144,512]{2,1,0:T(8,128)(2,1)} %get-tuple-element.50), channel_id=1, source_target_pairs={{0,1},{1,2},{2,3},{3,0},{4,5},{5,6},{6,7},{7,4},{8,9},{9,10},{10,1... | collective-permute-start | bytes 884744 | tf_op jit(solution)/shard_map/ppermute | solution.py:388
  48.6 29.1 %collective-permute-start.12 = (bf16[2,144,512]{2,1,0:T(8,128)(2,1)}, bf16[2,144,512]{2,1,0:T(8,128)(2,1)}, u32[]{:S(2)}, u32[]{:S(2)}) collective-permute-start(bf16[2,144,512]{2,1,0:T(8,128)(2,1)} %get-tuple-element.51), channel_id=1, source_target_pairs={{0,2},{1,3},{2,0},{3,1},{4,6},{5,7},{6,4},{7,5},{8,10},{9,11},{10,... | collective-permute-start | bytes 884744 | tf_op jit(solution)/shard_map/ppermute | solution.py:388
  51.2 8.9 %copy-start.14 = (f32[64]{0:T(128)S(1)}, f32[64]{0:T(128)}, u32[]{:S(2)}) copy-start(f32[64]{0:T(128)} %param.16) | copy-start | bytes 772
  51.2 26.6 %collective-permute-start.13 = (bf16[2,144,512]{2,1,0:T(8,128)(2,1)}, bf16[2,144,512]{2,1,0:T(8,128)(2,1)}, u32[]{:S(2)}, u32[]{:S(2)}) collective-permute-start(bf16[2,144,512]{2,1,0:T(8,128)(2,1)} %get-tuple-element.52), channel_id=1, source_target_pairs={{0,3},{1,0},{2,1},{3,2},{4,7},{5,4},{6,5},{7,6},{8,11},{9,8},{10,9... | collective-permute-start | bytes 884744 | tf_op jit(solution)/shard_map/ppermute | solution.py:388
  52.3 20.1 %slice-start = ((s8[4718592]{0:T(1024)(128)(4,1)}), s8[524288]{0:T(1024)(128)(4,1)S(1)}, s32[]{:S(2)}) async-start(s8[4718592]{0:T(1024)(128)(4,1)} %bitcast.30), calls=%async_computation | async-start | bytes 1048576
  58.3 0.7 copy-start.11
  59.0 0.7 copy-start.13
  59.7 20.0 %collective-permute-start.7 = (bf16[2,144,512]{2,1,0:T(8,128)(2,1)}, bf16[2,144,512]{2,1,0:T(8,128)(2,1)S(1)}, u32[]{:S(2)}, u32[]{:S(2)}) collective-permute-start(bf16[2,144,512]{2,1,0:T(8,128)(2,1)} %get-tuple-element.46), channel_id=1, source_target_pairs={{0,1},{1,2},{2,3},{3,0},{4,5},{5,6},{6,7},{7,4},{8,9},{9,10},{10,1... | collective-permute-start | bytes 884744 | tf_op jit(solution)/shard_map/ppermute | solution.py:388
  60.2 2.3 %copy-start.2 = (bf16[64,18,2,1024]{3,2,1,0:T(2,128)(2,1)S(1)}, bf16[64,18,2,1024]{3,2,1,0:T(2,128)(2,1)}, u32[]{:S(2)}) copy-start(bf16[64,18,2,1024]{3,2,1,0:T(2,128)(2,1)} %param.9) | copy-start | bytes 14155780
  62.5 1.1 copy-start.12
  62.5 3.2 %copy-start.8 = (bf16[72,512]{1,0:T(8,128)(2,1)S(1)}, bf16[72,512]{1,0:T(8,128)(2,1)}, u32[]{:S(2)}) copy-start(bf16[72,512]{1,0:T(8,128)(2,1)} %rain_ref.1) | copy-start | bytes 221188
  62.5 3.2 %copy-start.9 = (s32[512]{0:T(512)S(1)}, s32[512]{0:T(512)}, u32[]{:S(2)}) copy-start(s32[512]{0:T(512)} %param.13) | copy-start | bytes 6148
  62.5 3.2 %copy-start.10 = (s32[512]{0:T(512)S(1)}, s32[512]{0:T(512)}, u32[]{:S(2)}) copy-start(s32[512]{0:T(512)} %param.14) | copy-start | bytes 6148
  62.5 9.9 %slice-start.1 = ((s8[4718592]{0:T(1024)(128)(4,1)}), s8[4194304]{0:T(1024)(128)(4,1)S(1)}, s32[]{:S(2)}) async-start(s8[4718592]{0:T(1024)(128)(4,1)} %bitcast.30), calls=%async_computation.1 | async-start | bytes 8388608
  62.8 31.7 %collective-permute-start.8 = (bf16[2,144,512]{2,1,0:T(8,128)(2,1)}, bf16[2,144,512]{2,1,0:T(8,128)(2,1)S(1)}, u32[]{:S(2)}, u32[]{:S(2)}) collective-permute-start(bf16[2,144,512]{2,1,0:T(8,128)(2,1)} %copy-done.13), channel_id=1, source_target_pairs={{0,2},{1,3},{2,0},{3,1},{4,6},{5,7},{6,4},{7,5},{8,10},{9,11},{10,... | collective-permute-start | bytes 884744 | tf_op jit(solution)/shard_map/ppermute | solution.py:388
  63.7 35.1 %collective-permute-start.9 = (bf16[2,144,512]{2,1,0:T(8,128)(2,1)S(1)}, bf16[2,144,512]{2,1,0:T(8,128)(2,1)S(1)}, u32[]{:S(2)}, u32[]{:S(2)}) collective-permute-start(bf16[2,144,512]{2,1,0:T(8,128)(2,1)S(1)} %copy-done.12), channel_id=1, source_target_pairs={{0,3},{1,0},{2,1},{3,2},{4,7},{5,4},{6,5},{7,6},{8,11},{9,8},{10,9... | collective-permute-start | bytes 884744 | tf_op jit(solution)/shard_map/ppermute | solution.py:388
  65.8 2.5 %copy-start.3 = (bf16[72,72,512]{2,1,0:T(8,128)(2,1)S(1)}, bf16[72,72,512]{2,1,0:T(8,128)(2,1)}, u32[]{:S(2)}) copy-start(bf16[72,72,512]{2,1,0:T(8,128)(2,1)} %param.12) | copy-start | bytes 15925252
  72.5 9.3 %copy-start.7 = (bf16[2,144,512]{2,1,0:T(8,128)(2,1)S(1)}, bf16[2,144,512]{2,1,0:T(8,128)(2,1)}, u32[]{:S(2)}) copy-start(bf16[2,144,512]{2,1,0:T(8,128)(2,1)} %copy-done.6) | copy-start | bytes 884740
  77.8 34.5 %collective-permute-start.3 = (bf16[2,144,512]{2,1,0:T(8,128)(2,1)S(1)}, bf16[2,144,512]{2,1,0:T(8,128)(2,1)S(1)}, u32[]{:S(2)}, u32[]{:S(2)}) collective-permute-start(bf16[2,144,512]{2,1,0:T(8,128)(2,1)S(1)} %get-tuple-element.37), channel_id=1, source_target_pairs={{0,1},{1,2},{2,3},{3,0},{4,5},{5,6},{6,7},{7,4},{8,9},{9,10},{10,1... | collective-permute-start | bytes 884744 | tf_op jit(solution)/shard_map/ppermute | solution.py:388
  77.9 37.0 %collective-permute-start.4 = (bf16[2,144,512]{2,1,0:T(8,128)(2,1)S(1)}, bf16[2,144,512]{2,1,0:T(8,128)(2,1)S(1)}, u32[]{:S(2)}, u32[]{:S(2)}) collective-permute-start(bf16[2,144,512]{2,1,0:T(8,128)(2,1)S(1)} %get-tuple-element.38), channel_id=1, source_target_pairs={{0,2},{1,3},{2,0},{3,1},{4,6},{5,7},{6,4},{7,5},{8,10},{9,11},{10,... | collective-permute-start | bytes 884744 | tf_op jit(solution)/shard_map/ppermute | solution.py:388
  79.7 35.6 %collective-permute-start.5 = (bf16[2,144,512]{2,1,0:T(8,128)(2,1)S(1)}, bf16[2,144,512]{2,1,0:T(8,128)(2,1)S(1)}, u32[]{:S(2)}, u32[]{:S(2)}) collective-permute-start(bf16[2,144,512]{2,1,0:T(8,128)(2,1)S(1)} %get-tuple-element.39), channel_id=1, source_target_pairs={{0,3},{1,0},{2,1},{3,2},{4,7},{5,4},{6,5},{7,6},{8,11},{9,8},{10,9... | collective-permute-start | bytes 884744 | tf_op jit(solution)/shard_map/ppermute | solution.py:388
  94.5 34.9 %collective-permute-start.19 = (bf16[1,18,4,16,128]{4,3,2,1,0:T(8,128)(2,1)S(1)}, bf16[1,18,4,16,128]{4,3,2,1,0:T(8,128)(2,1)S(1)}, u32[]{:S(2)}, u32[]{:S(2)}) collective-permute-start(bf16[1,18,4,16,128]{4,3,2,1,0:T(8,128)(2,1)S(1)} %get-tuple-element.57), channel_id=1, source_target_pairs={{0,4},{4,8},{8,12},{12,16},{16,20},{20,24},{24,28},{28,32},{32,36}... | collective-permute-start | bytes 884744 | tf_op jit(solution)/shard_map/ppermute | solution.py:383
  98.8 30.7 %collective-permute-start.20 = (bf16[1,18,4,16,128]{4,3,2,1,0:T(8,128)(2,1)S(1)}, bf16[1,18,4,16,128]{4,3,2,1,0:T(8,128)(2,1)S(1)}, u32[]{:S(2)}, u32[]{:S(2)}) collective-permute-start(bf16[1,18,4,16,128]{4,3,2,1,0:T(8,128)(2,1)S(1)} %get-tuple-element.58), channel_id=1, source_target_pairs={{4,0},{8,4},{12,8},{16,12},{20,16},{24,20},{28,24},{32,28},{36,32}... | collective-permute-start | bytes 884744 | tf_op jit(solution)/shard_map/ppermute | solution.py:383
  112.3 109.5 %collective-permute-start.10 = (bf16[1152,512]{1,0:T(8,128)(2,1)}, bf16[1152,512]{1,0:T(8,128)(2,1)}, u32[]{:S(2)}, u32[]{:S(2)}) collective-permute-start(bf16[1152,512]{1,0:T(8,128)(2,1)} %physics.6.own_ref), channel_id=1, source_target_pairs={{0,64},{4,68},{8,72},{12,76},{16,80},{20,84},{24,88},{28,92},{32,9... | collective-permute-start | bytes 3538952 | tf_op jit(solution)/shard_map/ppermute | solution.py:393
  114.8 104.1 %collective-permute-start.14 = (bf16[1152,512]{1,0:T(8,128)(2,1)}, bf16[1152,512]{1,0:T(8,128)(2,1)}, u32[]{:S(2)}, u32[]{:S(2)}) collective-permute-start(bf16[1152,512]{1,0:T(8,128)(2,1)} %physics.7.own_ref), channel_id=1, source_target_pairs={{0,64},{4,68},{8,72},{12,76},{16,80},{20,84},{24,88},{28,92},{32,9... | collective-permute-start | bytes 3538952 | tf_op jit(solution)/shard_map/ppermute | solution.py:393
  126.9 97.9 %collective-permute-start.6 = (bf16[1152,512]{1,0:T(8,128)(2,1)}, bf16[1152,512]{1,0:T(8,128)(2,1)}, u32[]{:S(2)}, u32[]{:S(2)}) collective-permute-start(bf16[1152,512]{1,0:T(8,128)(2,1)} %physics.5.own_ref), channel_id=1, source_target_pairs={{0,64},{4,68},{8,72},{12,76},{16,80},{20,84},{24,88},{28,92},{32,9... | collective-permute-start | bytes 3538952 | tf_op jit(solution)/shard_map/ppermute | solution.py:393
  131.5 9.5 %collective-permute-start.21 = (bf16[1,144,512]{2,1,0:T(8,128)(2,1)S(1)}, bf16[1,144,512]{2,1,0:T(8,128)(2,1)S(1)}, u32[]{:S(2)}, u32[]{:S(2)}) collective-permute-start(bf16[1,144,512]{2,1,0:T(8,128)(2,1)S(1)} %get-tuple-element.60), channel_id=1, source_target_pairs={{0,1},{1,2},{2,3},{3,0},{4,5},{5,6},{6,7},{7,4},{8,9},{9,10},{10,1... | collective-permute-start | bytes 442376 | tf_op jit(solution)/shard_map/ppermute | solution.py:388
  131.6 9.4 %collective-permute-start.22 = (bf16[1,144,512]{2,1,0:T(8,128)(2,1)S(1)}, bf16[1,144,512]{2,1,0:T(8,128)(2,1)S(1)}, u32[]{:S(2)}, u32[]{:S(2)}) collective-permute-start(bf16[1,144,512]{2,1,0:T(8,128)(2,1)S(1)} %get-tuple-element.61), channel_id=1, source_target_pairs={{0,2},{1,3},{2,0},{3,1},{4,6},{5,7},{6,4},{7,5},{8,10},{9,11},{10,... | collective-permute-start | bytes 442376 | tf_op jit(solution)/shard_map/ppermute | solution.py:388
  141.1 4.4 %collective-permute-start.23 = (bf16[1,144,512]{2,1,0:T(8,128)(2,1)S(1)}, bf16[1,144,512]{2,1,0:T(8,128)(2,1)S(1)}, u32[]{:S(2)}, u32[]{:S(2)}) collective-permute-start(bf16[1,144,512]{2,1,0:T(8,128)(2,1)S(1)} %get-tuple-element.62), channel_id=1, source_target_pairs={{0,3},{1,0},{2,1},{3,2},{4,7},{5,4},{6,5},{7,6},{8,11},{9,8},{10,9... | collective-permute-start | bytes 442376 | tf_op jit(solution)/shard_map/ppermute | solution.py:388
  141.1 5.6 %collective-permute-start.15 = (bf16[1,144,512]{2,1,0:T(8,128)(2,1)S(1)}, bf16[1,144,512]{2,1,0:T(8,128)(2,1)S(1)}, u32[]{:S(2)}, u32[]{:S(2)}) collective-permute-start(bf16[1,144,512]{2,1,0:T(8,128)(2,1)S(1)} %get-tuple-element.54), channel_id=1, source_target_pairs={{0,1},{1,2},{2,3},{3,0},{4,5},{5,6},{6,7},{7,4},{8,9},{9,10},{10,1... | collective-permute-start | bytes 442376 | tf_op jit(solution)/shard_map/ppermute | solution.py:388
  145.5 8.0 %collective-permute-start.16 = (bf16[1,144,512]{2,1,0:T(8,128)(2,1)S(1)}, bf16[1,144,512]{2,1,0:T(8,128)(2,1)S(1)}, u32[]{:S(2)}, u32[]{:S(2)}) collective-permute-start(bf16[1,144,512]{2,1,0:T(8,128)(2,1)S(1)} %get-tuple-element.55), channel_id=1, source_target_pairs={{0,2},{1,3},{2,0},{3,1},{4,6},{5,7},{6,4},{7,5},{8,10},{9,11},{10,... | collective-permute-start | bytes 442376 | tf_op jit(solution)/shard_map/ppermute | solution.py:388
  146.7 7.3 %collective-permute-start.17 = (bf16[1,144,512]{2,1,0:T(8,128)(2,1)S(1)}, bf16[1,144,512]{2,1,0:T(8,128)(2,1)S(1)}, u32[]{:S(2)}, u32[]{:S(2)}) collective-permute-start(bf16[1,144,512]{2,1,0:T(8,128)(2,1)S(1)} %get-tuple-element.56), channel_id=1, source_target_pairs={{0,3},{1,0},{2,1},{3,2},{4,7},{5,4},{6,5},{7,6},{8,11},{9,8},{10,9... | collective-permute-start | bytes 442376 | tf_op jit(solution)/shard_map/ppermute | solution.py:388
  153.5 51.3 %collective-permute-start.24 = (bf16[576,512]{1,0:T(8,128)(2,1)S(1)}, bf16[576,512]{1,0:T(8,128)(2,1)S(1)}, u32[]{:S(2)}, u32[]{:S(2)}) collective-permute-start(bf16[576,512]{1,0:T(8,128)(2,1)S(1)} %physics.9.own_ref), channel_id=1, source_target_pairs={{0,64},{4,68},{8,72},{12,76},{16,80},{20,84},{24,88},{28,92},{32,9... | collective-permute-start | bytes 1769480 | tf_op jit(solution)/shard_map/ppermute | solution.py:393
  154.0 9.1 %copy-start.15 = (s32[64]{0:T(128)S(1)}, s32[64]{0:T(128)}, u32[]{:S(2)}) copy-start(s32[64]{0:T(128)} %param.17) | copy-start | bytes 772
  160.4 57.0 %collective-permute-start.18 = (bf16[576,512]{1,0:T(8,128)(2,1)S(1)}, bf16[576,512]{1,0:T(8,128)(2,1)S(1)}, u32[]{:S(2)}, u32[]{:S(2)}) collective-permute-start(bf16[576,512]{1,0:T(8,128)(2,1)S(1)} %physics.8.own_ref), channel_id=1, source_target_pairs={{0,64},{4,68},{8,72},{12,76},{16,80},{20,84},{24,88},{28,92},{32,9... | collective-permute-start | bytes 1769480 | tf_op jit(solution)/shard_map/ppermute | solution.py:393

commit v2 on v1

v2 whole, which is shorter than its diff:
```python
import itertools

import jax
import jax.numpy as jnp
import numpy as np
from jax import lax
from jax.experimental import pallas as pl
from jax.experimental.pallas import tpu as pltpu
from jax.sharding import PartitionSpec as P

GROUP = 8
CHUNKS = (1, 1, 2, 2, 2)
SPANS = ((0, 1), (1, 3), (4, 4))
ORDER = (
    ("extract", 0),
    ("extract", 1),
    ("advect", 0),
    ("tables", 0),
    ("advect", 1),
    ("physics", 0),
    ("extract", 2),
    ("advect", 2),
    ("physics", 1),
    ("advect", 3),
    ("physics", 2),
    ("choose", 0),
    ("advect", 4),
    ("physics", 3),
    ("choose", 1),
    ("physics", 4),
    ("choose", 2),
    ("choose", 3),
    ("choose", 4),
)
CAP = 256
K_BLOCK = 8
F32 = jnp.float32
BF16 = jnp.bfloat16


def deinterleave():
    move = np.zeros((256, 256), np.float32)
    for k, a, t, i in itertools.product(range(2), range(2), range(GROUP), range(8)):
        move[((k * 2 + a) * GROUP + t) * 8 + i, ((t * 2 + k) * 8 + i) * 2 + a] = 1
    return jnp.asarray(move, BF16)


def regroup(n_lev):
    move = np.zeros((n_lev, 256, 256), np.float32)
    for j, s, a, h in itertools.product(range(n_lev), range(n_lev), range(2), range(2)):
        tile = 2 * ((j + s) % n_lev) + h
        for k, t in itertools.product(range(2), range(GROUP)):
            row = (((s * 2 + a) * 2 + h) * 2 + k) * GROUP + t
            move[j, row, ((k * 2 + a) * GROUP + t) * 8 + tile] = 1
    return jnp.asarray(move, BF16)


def face_rows(levels):
    rows = levels * 8
    move = np.zeros((2 * rows, 2 * rows), np.float32)
    for a, r in itertools.product(range(2), range(rows)):
        move[a * rows + r, r * 2 + a] = 1
    return jnp.asarray(move, BF16)


def product(a, b):
    return jnp.dot(a, b, preferred_element_type=F32)


def two_levels(q_ref, pair):
    return q_ref[:, pl.ds(2 * pair, 2)].reshape(2 * GROUP * 16, 128)


def extract_kernel(apart_ref, face_move_ref, q_ref, lat_ref, *refs):
    north_ref, south_ref = refs[-2:]
    levels = q_ref.shape[1]
    rows = levels * GROUP * 8

    def body(pair, carry):
        apart = product(apart_ref[...], two_levels(q_ref, pair)).astype(BF16)
        spot = pl.multiple_of(pair * 128, 128)
        south_ref[0, pl.ds(spot, 64), :] = apart[0:64]
        north_ref[0, pl.ds(spot, 64), :] = apart[64:128]
        south_ref[0, pl.ds(spot + 64, 64), :] = apart[128:192]
        north_ref[0, pl.ds(spot + 64, 64), :] = apart[192:256]
        return carry

    lax.fori_loop(0, levels // 2, body, 0)
    if south_ref.shape[1] > rows:
        faces = lat_ref[...].reshape(levels * 16, 128)
        south_ref[0, rows:, :] = product(face_move_ref[: levels * 8], faces).astype(BF16)


def whole_block(*shape):
    return pl.BlockSpec(shape, lambda *_: (0,) * len(shape))


def extract(apart, face_move, q, lat, first, groups, after):
    levels = q.shape[1]
    rows = levels * GROUP * 8
    extra = levels * 8 if first == 0 else 0
    return pl.pallas_call(
        extract_kernel,
        grid=(groups,),
        in_specs=[
            whole_block(*apart.shape),
            whole_block(*face_move.shape),
            pl.BlockSpec((GROUP, levels, 16, 128), lambda g: (g + first, 0, 0, 0)),
            whole_block(*lat.shape),
        ]
        + [pl.BlockSpec(memory_space=pl.ANY)] * len(after),
        out_specs=[
            pl.BlockSpec((1, rows, 128), lambda g: (g, 0, 0)),
            pl.BlockSpec((1, rows + extra, 128), lambda g: (g, 0, 0)),
        ],
        out_shape=[
            jax.ShapeDtypeStruct((groups, rows, 128), BF16),
            jax.ShapeDtypeStruct((groups, rows + extra, 128), BF16),
        ],
        cost_estimate=pl.CostEstimate(
            flops=groups * 10**6, bytes_accessed=groups * 1200000, transcendentals=0
        ),
        compiler_params=pltpu.CompilerParams(vmem_limit_bytes=16 << 20),
        name="extract",
    )(apart, face_move, q, lat, *after)


def beside(x, lane, toward_east):
    if toward_east:
        turned = pltpu.roll(x, 127, 1)
        return jnp.where(lane == 127, pltpu.roll(turned, 7, 0), turned)
    turned = pltpu.roll(x, 1, 1)
    return jnp.where(lane == 0, pltpu.roll(turned, 1, 0), turned)


def advect_kernel(
    place_ref, apart_ref, group_ref, face_move_ref, q_ref, low_ref, high_ref, lat_ref, lon_ref,
    above_ref, *refs
):
    outs, faces = refs[-5:-1], refs[-1]
    levels = q_ref.shape[1]
    lane = lax.broadcasted_iota(jnp.int32, (8, 128), 1)

    @pl.when(pl.program_id(0) == 0)
    def _():
        for at, ref in ((0, lat_ref), (2, lon_ref)):
            both = product(face_move_ref[...], ref[...].reshape(levels * 16, 128))
            faces[at] = both[: levels * 8]
            faces[at + 1] = both[levels * 8 :]
        faces[4] = above_ref[0].astype(F32)

    def body(pair, carry):
        apart = product(apart_ref[...], two_levels(q_ref, pair))
        spot = pl.multiple_of(pair * 128, 128)
        low = low_ref[0, pl.ds(spot, 128), :].astype(F32)
        high = high_ref[0, pl.ds(spot, 128), :].astype(F32)
        results = []
        for k in range(2):
            at = pl.ds(pl.multiple_of((2 * pair + k) * 8, 8), 8)
            edge = [faces[0, at, :], faces[1, at, :], faces[4, at, :]]
            terms = []
            for lat in range(2):
                south, north, west = edge[lat], edge[lat + 1], faces[2 + lat, at, :]
                east = beside(west, lane, True)
                own = (
                    1.0
                    - (jnp.maximum(north, 0.0) - jnp.minimum(south, 0.0))
                    - (jnp.maximum(east, 0.0) - jnp.minimum(west, 0.0))
                )
                terms.append(
                    (
                        own,
                        jnp.maximum(south, 0.0),
                        -jnp.minimum(north, 0.0),
                        jnp.maximum(west, 0.0),
                        -jnp.minimum(east, 0.0),
                    )
                )
            made = [[], []]
            for t in range(GROUP):
                rows = [
                    apart[(k * 2 + lat) * 64 + t * 8 : (k * 2 + lat) * 64 + t * 8 + 8]
                    for lat in range(2)
                ]
                outer = [x[k * 64 + t * 8 : k * 64 + t * 8 + 8] for x in (low, high)]
                column = [outer[0], rows[0], rows[1], outer[1]]
                for lat in range(2):
                    own, from_s, from_n, from_w, from_e = terms[lat]
                    made[lat].append(
                        own * rows[lat]
                        + (from_s * column[lat] + from_n * column[lat + 2])
                        + (
                            from_w * beside(rows[lat], lane, False)
                            + from_e * beside(rows[lat], lane, True)
                        )
                    )
            results += made[0] + made[1]
        sent = product(group_ref[0], jnp.concatenate(results, axis=0).astype(BF16)).astype(BF16)
        spot = pl.multiple_of(pair * 16, 16)
        for shift, out in enumerate(outs):
            for quarter in range(4):
                row = (shift * 4 + quarter) * 16
                out[0, pl.ds(spot, 16), quarter * 128 : (quarter + 1) * 128] = sent[row : row + 16]
        return carry

    lax.fori_loop(0, levels // 2, body, 0)


def advect(
    place, apart, group, face_move, q, low, high, lat, lon, above, first, halo_first, groups, after
):
    levels = q.shape[1]
    rows = levels * GROUP
    halo = pl.BlockSpec((1, rows * 8, 128), lambda g, p: (g + halo_first, 0, 0))
    return pl.pallas_call(
        advect_kernel,
        grid_spec=pltpu.PrefetchScalarGridSpec(
            num_scalar_prefetch=1,
            grid=(groups,),
            in_specs=[
                whole_block(*apart.shape),
                pl.BlockSpec((1, 256, 256), lambda g, p: (p[0], 0, 0)),
                whole_block(*face_move.shape),
                pl.BlockSpec((GROUP, levels, 16, 128), lambda g, p: (g + first, 0, 0, 0)),
                halo,
                halo,
                whole_block(*lat.shape),
                whole_block(*lon.shape),
                pl.BlockSpec((1, levels * 8, 128), lambda g, p: (0, GROUP, 0)),
            ]
            + [pl.BlockSpec(memory_space=pl.ANY)] * len(after),
            out_specs=[pl.BlockSpec((1, rows, 512), lambda g, p: (g, 0, 0))] * 4,
            scratch_shapes=[pltpu.VMEM((5, levels * 8, 128), F32)],
        ),
        out_shape=[jax.ShapeDtypeStruct((groups, rows, 512), BF16)] * 4,
        cost_estimate=pl.CostEstimate(
            flops=groups * 10**7, bytes_accessed=groups * 2000000, transcendentals=0
        ),
        compiler_params=pltpu.CompilerParams(vmem_limit_bytes=24 << 20),
        name="advect",
    )(place, apart, group, face_move, q, low, high, lat, lon, above, *after)


def table_kernel(matrix_ref, mask_ref, order_ref, rain_ref, *refs):
    small_ref, placing_ref, back_ref, wet_ref, all_ref = refs[-5:]
    columns = mask_ref.shape[1]

    @pl.when(pl.program_id(0) == 0)
    def _():
        mask = mask_ref[...]
        order = order_ref[...]
        row = lax.broadcasted_iota(jnp.int32, (columns, columns), 0)
        column = lax.broadcasted_iota(jnp.int32, (columns, columns), 1)
        earlier = jnp.where(row < column, 1.0, 0.0).astype(BF16)
        ones = jnp.where(mask > 0, 1.0, 0.0)
        wide = jnp.broadcast_to(ones, (8, columns)).astype(BF16)
        rank = jnp.dot(wide, earlier, preferred_element_type=F32)[0:1]
        rank = jnp.where(mask > 0, rank, -1.0).astype(jnp.int32)
        slot = lax.broadcasted_iota(jnp.int32, (CAP, columns), 0)
        back = jnp.where(slot == rank, 1.0, 0.0).astype(BF16)
        back_ref[...] = back
        whole = jnp.where(row == order, 1.0, 0.0)
        placing_ref[:, :columns] = jnp.where(mask > 0, 0.0, whole).astype(BF16)
        placing_ref[:, columns:] = lax.dot_general(
            whole.astype(BF16), back, (((1,), (1,)), ((), ())), preferred_element_type=F32
        ).astype(BF16)
        wet = lax.dot_general(
            rain_ref[...], back, (((1,), (1,)), ((), ())), preferred_element_type=F32
        )
        for tile in range(CAP // 128):
            wet_ref[tile] = wet[:, tile * 128 : (tile + 1) * 128]
        for tile in range(columns // 128):
            all_ref[tile] = rain_ref[:, tile * 128 : (tile + 1) * 128].astype(F32)

    small = lax.dot_general(
        matrix_ref[...], back_ref[...], (((1,), (1,)), ((), ())), preferred_element_type=F32
    )
    for tile in range(CAP // 128):
        small_ref[tile] = small[:, tile * 128 : (tile + 1) * 128]


def tables(matrix, mask, order, rain, after):
    rows, columns = matrix.shape
    levels = rain.shape[0]
    steps = 9
    whole = lambda *shape: pl.BlockSpec(shape, lambda i: (0,) * len(shape))
    return pl.pallas_call(
        table_kernel,
        grid=(steps,),
        in_specs=[
            pl.BlockSpec((rows // steps, columns), lambda i: (i, 0)),
            whole(1, columns),
            whole(1, columns),
            whole(levels, columns),
        ]
        + [pl.BlockSpec(memory_space=pl.ANY)] * len(after),
        out_specs=[
            pl.BlockSpec((CAP // 128, rows // steps, 128), lambda i: (0, i, 0)),
            whole(columns, columns + CAP),
            whole(CAP, columns),
            whole(CAP // 128, levels, 128),
            whole(columns // 128, levels, 128),
        ],
        out_shape=[
            jax.ShapeDtypeStruct((CAP // 128, rows, 128), F32),
            jax.ShapeDtypeStruct((columns, columns + CAP), BF16),
            jax.ShapeDtypeStruct((CAP, columns), BF16),
            jax.ShapeDtypeStruct((CAP // 128, levels, 128), F32),
            jax.ShapeDtypeStruct((columns // 128, levels, 128), F32),
        ],
        cost_estimate=pl.CostEstimate(
            flops=2 * rows * columns * CAP, bytes_accessed=12 * 10**6, transcendentals=0
        ),
        compiler_params=pltpu.CompilerParams(vmem_limit_bytes=24 << 20),
        name="tables",
    )(matrix, mask, order, rain, *after)


def physics_kernel(
    place_ref,
    part0_ref,
    part1_ref,
    part2_ref,
    part3_ref,
    placing_ref,
    back_ref,
    matrix_ref,
    rain_ref,
    wet_ref,
    rate_ref,
    *refs,
):
    out_ref, dry, moist, turned, held = refs[-5:]
    groups, rows, columns = part0_ref.shape
    levels = matrix_ref.shape[1]
    tiles = CAP // 128
    rates = [rate_ref[g] for g in range(groups)]

    for shift, part in enumerate((part0_ref, part1_ref, part2_ref, part3_ref)):
        source = lax.rem(place_ref[0] + (4 - shift), 4)
        base = pl.multiple_of(source * rows, 8)
        for g in range(groups):
            placed = product(part[g], placing_ref[...])
            dry[g, pl.ds(base, rows), :] = placed[:, :columns]
            for tile in range(tiles):
                at = columns + tile * 128
                moist[g, tile, pl.ds(base, rows), :] = placed[:, at : at + 128]

    def contract(step, carry):
        block, tile = step // tiles, step % tiles
        first = block * K_BLOCK
        sums = [[jnp.zeros((GROUP, 128), F32)] * K_BLOCK for _ in range(groups)]
        for e in range(levels):
            values = [moist[g, tile, e * GROUP : (e + 1) * GROUP, :] for g in range(groups)]
            for k in range(K_BLOCK):
                weight = matrix_ref[tile, first + k, pl.ds(e, GROUP, stride=0), :]
                for g in range(groups):
                    sums[g][k] = sums[g][k] + weight * values[g]
        wets = [wet_ref[tile, pl.ds(first + k, GROUP, stride=0), :] for k in range(K_BLOCK)]
        spot = pl.multiple_of(first * GROUP, GROUP * K_BLOCK)
        for g in range(groups):
            washed = [sums[g][k] * jnp.exp(-rates[g] * wets[k]) for k in range(K_BLOCK)]
            turned[g, tile, pl.ds(spot, GROUP * K_BLOCK), :] = jnp.concatenate(
                washed, axis=0
            ).astype(BF16)
        return carry

    lax.fori_loop(0, levels // K_BLOCK * tiles, contract, 0)

    some = 24

    def finish(block, carry):
        first = block * some
        spot = pl.multiple_of(first * GROUP, GROUP * some)
        for g in range(groups):
            spread = sum(
                product(
                    turned[g, tile, pl.ds(spot, GROUP * some), :],
                    back_ref[tile * 128 : (tile + 1) * 128],
                )
                for tile in range(tiles)
            )
            for k in range(some):
                for tile in range(columns // 128):
                    lanes = slice(tile * 128, (tile + 1) * 128)
                    wet = rain_ref[tile, pl.ds(first + k, GROUP, stride=0), :]
                    plain = dry[g, pl.ds(spot + k * GROUP, GROUP), lanes]
                    held[tile, pl.ds(g * GROUP * levels + first + k, GROUP, stride=levels), :] = (
                        spread[k * GROUP : (k + 1) * GROUP, lanes] + plain * jnp.exp(-rates[g] * wet)
                    )
        return carry

    lax.fori_loop(0, levels // some, finish, 0)
    for tile in range(columns // 128):
        out_ref[:, tile * 128 : (tile + 1) * 128] = held[tile].astype(BF16)


def physics(place, parts, placing, back, matrix, rain, wet, rates, first, groups, after):
    rows, columns = parts[0].shape[1:]
    levels = rain.shape[1]
    flops = groups * 2 * GROUP * levels * (columns * (columns + 2 * CAP) + levels * CAP * 20)
    return pl.pallas_call(
        physics_kernel,
        grid_spec=pltpu.PrefetchScalarGridSpec(
            num_scalar_prefetch=1,
            grid=(1,),
            in_specs=[whole_block(groups, rows, columns)] * 4
            + [whole_block(*x.shape) for x in (placing, back, matrix, rain, wet)]
            + [pl.BlockSpec((groups, GROUP, 128), lambda i, p: (first // groups, 0, 0))]
            + [pl.BlockSpec(memory_space=pl.ANY)] * len(after),
            out_specs=whole_block(groups * GROUP * levels, columns),
            scratch_shapes=[
                pltpu.VMEM((groups, levels * GROUP, columns), F32),
                pltpu.VMEM((groups, CAP // 128, levels * GROUP, 128), F32),
                pltpu.VMEM((groups, CAP // 128, levels * GROUP, 128), BF16),
                pltpu.VMEM((columns // 128, groups * GROUP * levels, 128), F32),
            ],
        ),
        out_shape=jax.ShapeDtypeStruct((groups * GROUP * levels, columns), BF16),
        cost_estimate=pl.CostEstimate(
            flops=flops, bytes_accessed=groups * 1200000 + 6500000, transcendentals=0
        ),
        compiler_params=pltpu.CompilerParams(vmem_limit_bytes=32 << 20),
        name="physics",
    )(place, *parts, placing, back, matrix, rain, wet, rates, *after)


def choose_kernel(flag_ref, own_ref, partner_ref, *refs):
    out_ref = refs[-1]

    @pl.when(flag_ref[0] > 0)
    def _():
        out_ref[...] = partner_ref[...]

    @pl.when(flag_ref[0] <= 0)
    def _():
        out_ref[...] = own_ref[...]


def choose(flag, own, partner, whole, shape, first, groups, after):
    rows = shape[0] // (2 * sum(CHUNKS))
    columns = shape[1]
    operands = [own, partner]
    specs = [
        pl.BlockSpec((rows, columns), lambda g, f: (jnp.where(f[0] > 0, 0, g), 0)),
        pl.BlockSpec((rows, columns), lambda g, f: (jnp.where(f[0] > 0, g, 0), 0)),
    ]
    aliases = {}
    if whole is not None:
        operands.append(whole)
        specs.append(pl.BlockSpec(memory_space=pl.ANY))
        aliases = {3: 0}
    operands += after
    specs += [pl.BlockSpec(memory_space=pl.ANY)] * len(after)
    return pl.pallas_call(
        choose_kernel,
        grid_spec=pltpu.PrefetchScalarGridSpec(
            num_scalar_prefetch=1,
            grid=(2 * groups,),
            in_specs=specs,
            out_specs=pl.BlockSpec((rows, columns), lambda g, f: (g + 2 * first, 0)),
        ),
        out_shape=jax.ShapeDtypeStruct(shape, BF16),
        input_output_aliases=aliases,
        cost_estimate=pl.CostEstimate(
            flops=0, bytes_accessed=groups * 1200000, transcendentals=0
        ),
        compiler_params=pltpu.CompilerParams(vmem_limit_bytes=16 << 20),
        name="choose",
    )(flag, *operands)


def shifted(value, axis, steps):
    count = lax.axis_size(axis)
    pairs = [(i, i + steps) for i in range(count) if 0 <= i + steps < count]
    return lax.ppermute(value, axis, pairs)


def turned(value, axis, steps):
    count = lax.axis_size(axis)
    return lax.ppermute(value, axis, [(i, (i + steps) % count) for i in range(count)])


def paired(value, axis):
    count = lax.axis_size(axis)
    return lax.ppermute(value, axis, [(i, i ^ (count // 2)) for i in range(count)])


def tiled_rows(value):
    lead = value.shape[:-2]
    lats, lons = value.shape[-2:]
    split = value.reshape(*lead, lats, lons // 128, 128)
    return jnp.swapaxes(split, -3, -2).reshape(*lead, lats * lons // 128, 128)


def local(
    tracer_dyn,
    courant_lat,
    courant_lon,
    conv_matrix,
    conv_mask,
    column_order,
    rain,
    scav_rate,
    pair_flag,
):
    n_lat = lax.axis_size("lat")
    n_lev = lax.axis_size("lev")
    tracers = tracer_dyn.shape[0]
    levels, columns = rain.shape
    lev_place = lax.axis_index("lev")
    place = lev_place.astype(jnp.int32).reshape(1)
    pair_index = lax.axis_index("lat") % (n_lat // 2) * n_lev + lev_place
    flag = lax.dynamic_slice_in_dim(pair_flag, pair_index, 1)
    rates = jnp.broadcast_to(
        scav_rate.reshape(tracers // GROUP, GROUP, 1), (tracers // GROUP, GROUP, 128)
    )

    q = pltpu.with_memory_space_constraint(tiled_rows(tracer_dyn), pltpu.HBM)
    lat, lon = tiled_rows(courant_lat), tiled_rows(courant_lon)
    apart, group, face_move = deinterleave(), regroup(n_lev), face_rows(lat.shape[0])
    firsts = [sum(CHUNKS[:number]) for number in range(len(CHUNKS))]
    halos, sections, owns, partners, made = {}, {}, {}, {}, {}
    out = last = None
    for kind, number in ORDER:
        after = [] if last is None else [last]
        if kind == "extract":
            north, south = extract(apart, face_move, q, lat, *SPANS[number], after)
            last = north
            halos[number] = (shifted(north, "lat", 1), shifted(south, "lat", -1))
        elif kind == "tables":
            made = tables(
                conv_matrix.reshape(levels * levels, columns),
                conv_mask.reshape(1, columns),
                column_order.reshape(1, columns),
                rain,
                after,
            )
            last = made[2]
        elif kind == "advect":
            first, groups = firsts[number], CHUNKS[number]
            span = max(i for i in range(len(SPANS)) if SPANS[i][0] <= first)
            parts = advect(
                place, apart, group, face_move, q, *halos[span], lat, lon, halos[0][1],
                first, first - SPANS[span][0], groups, after,
            )
            last = parts[0]
            sections[number] = [parts[0]] + [turned(parts[s], "lev", s) for s in range(1, n_lev)]
        elif kind == "physics":
            small, placing, back, wet, wet_all = made
            small = small.reshape(CAP // 128, levels, levels, 128)
            own = physics(
                place, sections[number], placing, back, small, wet_all, wet, rates,
                firsts[number], CHUNKS[number], after,
            )
            last = owns[number] = own
            partners[number] = paired(own, "lat")
        else:
            out = choose(
                flag, owns[number], partners[number], out, (tracers * levels, columns),
                firsts[number], CHUNKS[number], after,
            )
    return out.reshape(tracers, levels, columns)


def solution(mesh):
    placed = (
        P(None, "lev", "lat", None),
        P("lev", "lat", None),
        P("lev", "lat", None),
        P(None, None, ("lat", "lev")),
        P(("lat", "lev")),
        P(("lat", "lev")),
        P(None, ("lat", "lev")),
        P(),
        P(),
    )
    return jax.shard_map(
        local, mesh=mesh, in_specs=placed, out_specs=P(None, None, ("lat", "lev")), check_vma=False
    )
```

time: 229 us -> 266 us (1.16)
  Pallas kernels: 91.6 us -> 125 us
  starting transfers between devices: 38 us -> 52.9 us
  waiting for transfers between devices: 86.1 us -> 77.4 us
  local copies, waits for them, and re-layouts: 11.8 us -> 7.72 us
    ppermute x5, waiting for transfers between devices: 52.2 us -> 71.6 us  [paired(): lax.ppermute(value, axis, [(i, i ^ count // 2) for i in range(count)])]
    pallas_call x5, Pallas kernels: 22.4 us -> 40.9 us  [advect(): pl.pallas_call(advect_kernel, grid_spec=pltpu.PrefetchScalarGridSpec(num_...]
    ppermute x5 -> x6, waiting for transfers between devices: 24.3 us -> 5.76 us  [shifted(): return lax.ppermute(value, axis, pairs)]
    pallas_call x2 -> x3, Pallas kernels: 4.44 us -> 17.8 us  [extract(): pl.pallas_call(extract_kernel, grid=(groups,), in_specs=[whole_block(*apa...]
    ppermute x5 -> x6, starting transfers between devices: 14.3 us -> 24.6 us  [shifted(): return lax.ppermute(value, axis, pairs)]
    ppermute x15, waiting for transfers between devices: 9.57 us -> 0.04 us  [turned(): lax.ppermute(value, axis, [(i, (i + steps) % count) for i in range(count)])]
    pallas_call x5, Pallas kernels: 11.8 us -> 17 us  [choose(): pl.pallas_call(choose_kernel, grid_spec=pltpu.PrefetchScalarGridSpec(num_...]
    ppermute x15, starting transfers between devices: 15.1 us -> 19.5 us  [turned(): lax.ppermute(value, axis, [(i, (i + steps) % count) for i in range(count)])]
  transfers between devices with their start and end apart: 25 -> 26, of which waited for: 6 -> 3; matrix products, arithmetic and copies ran while one was open for 0% -> 0% of each run, Pallas kernels for 34% -> 36%
where the time goes in v2:
time: 266 us; the launch traced here: 263 us
  Pallas kernels  125 us (47%)
  waiting for transfers between devices  77.4 us (29%)
  starting transfers between devices  52.9 us (20%)
  local copies, waits for them, and re-layouts  7.72 us (3%)
    ppermute x5, waiting for transfers between devices, paired(): lax.ppermute(value, axis, [(i, i ^ count // 2) for i in range(count)])  71.6 us
    pallas_call x5, Pallas kernels, physics(): pl.pallas_call(physics_kernel, grid_spec=pltpu.PrefetchScalarGridSpec(num...  45.1 us
    pallas_call x5, Pallas kernels, advect(): pl.pallas_call(advect_kernel, grid_spec=pltpu.PrefetchScalarGridSpec(num_...  40.9 us
    ppermute x6, starting transfers between devices, shifted(): return lax.ppermute(value, axis, pairs)  24.6 us
    ppermute x15, starting transfers between devices, turned(): lax.ppermute(value, axis, [(i, (i + steps) % count) for i in range(count)])  19.5 us
    pallas_call x3, Pallas kernels, extract(): pl.pallas_call(extract_kernel, grid=(groups,), in_specs=[whole_block(*apa...  17.8 us
    pallas_call x5, Pallas kernels, choose(): pl.pallas_call(choose_kernel, grid_spec=pltpu.PrefetchScalarGridSpec(num_...  17 us
    ppermute x5, starting transfers between devices, paired(): lax.ppermute(value, axis, [(i, i ^ count // 2) for i in range(count)])  8.84 us
  transfers between devices with their start and end apart: 26, of which 3 were waited for; matrix products, arithmetic and copies ran while one was open for 0% of the time, Pallas kernels for 36%

profile of v2, /device:TPU:97, one launch (start us, length us, event | category | flops | bytes accessed | tf_op | source)
XLA Modules:
  0.0 263.4 jit_solution(215391695535173160)
XLA Ops:
  0.0 0.9 copy-done
  0.9 0.9 copy-done.3
  1.8 0.9 copy-done.6
  2.7 3.5 %extract.3 = (bf16[1,1152,128]{2,1,0:T(8,128)(2,1)}, bf16[1,1296,128]{2,1,0:T(8,128)(2,1)}) custom-call(bf16[256,256]{1,0:T(8,128)(2,1)S(1)} %copy-done.3, bf16[288,288]{1,0:T(8,128)(2,1)S(1)} %copy-done, bf16[64,18,16,128]{3,2,1,0:T(8,128)(2,1)} %bitcast.42, bf16[18,16,128]{2,1,0:T(8,128)(2,1)S(1)} %bitcast.27), custom_call_target="tpu_custom_call" | custom-call | flops 1000000 | bytes 1200000 | tf_op jit(solution)/shard_map/extract/pallas_call | solution.py:102
  6.3 0.0 copy-start.8
  6.3 6.8 %extract.4 = (bf16[3,1152,128]{2,1,0:T(8,128)(2,1)}, bf16[3,1152,128]{2,1,0:T(8,128)(2,1)}) custom-call(bf16[256,256]{1,0:T(8,128)(2,1)S(1)} %copy-done.3, bf16[288,288]{1,0:T(8,128)(2,1)S(1)} %copy-done, bf16[64,18,16,128]{3,2,1,0:T(8,128)(2,1)} %bitcast.43, bf16[18,16,128]{2,1,0:T(8,128)(2,1)S(1)} %bitcast.28, bf16[1,1152,128]{2,1,0:T(8,128)(2,1)} %get-tuple-element.36.refs_0_), custom_call_target="tpu_custom_call" | custom-call | flops 3000000 | bytes 3600000 | tf_op jit(solution)/shard_map/extract/pallas_call | solution.py:102
  13.1 2.6 collective-permute-start.6
  15.7 5.1 %collective-permute-start.5 = (bf16[3,1152,128]{2,1,0:T(8,128)(2,1)}, bf16[3,1152,128]{2,1,0:T(8,128)(2,1)S(1)}, u32[]{:S(2)}, u32[]{:S(2)}) collective-permute-start(bf16[3,1152,128]{2,1,0:T(8,128)(2,1)} %get-tuple-element.38.refs_0_), channel_id=1, source_target_pairs={{0,4},{4,8},{8,12},{12,16},{16,20},{20,24},{24,28},{28,32},{32,36}... | collective-permute-start | bytes 2654216 | tf_op jit(solution)/shard_map/ppermute | solution.py:476
  20.8 1.9 collective-permute-start.1
  22.7 5.8 %collective-permute-start = (bf16[1,1152,128]{2,1,0:T(8,128)(2,1)}, bf16[1,1152,128]{2,1,0:T(8,128)(2,1)S(1)}, u32[]{:S(2)}, u32[]{:S(2)}) collective-permute-start(bf16[1,1152,128]{2,1,0:T(8,128)(2,1)} %get-tuple-element.36.refs_0_), channel_id=1, source_target_pairs={{0,4},{4,8},{8,12},{12,16},{16,20},{20,24},{24,28},{28,32},{32,36}... | collective-permute-start | bytes 884744 | tf_op jit(solution)/shard_map/ppermute | solution.py:476
  28.5 5.7 %collective-permute-done.low_ref = bf16[1,1152,128]{2,1,0:T(8,128)(2,1)S(1)} collective-permute-done((bf16[1,1152,128]{2,1,0:T(8,128)(2,1)}, bf16[1,1152,128]{2,1,0:T(8,128)(2,1)S(1)}, u32[]{:S(2)}, u32[]{:S(2)}) %collective-permute-start) | collective-permute-done | bytes 294944 | tf_op jit(solution)/shard_map/ppermute | solution.py:476
  34.2 0.8 copy-done.10
  35.0 1.0 copy-done.11
  36.0 6.3 %advect.5 = (bf16[1,144,512]{2,1,0:T(8,128)(2,1)S(1)}, bf16[1,144,512]{2,1,0:T(8,128)(2,1)}, bf16[1,144,512]{2,1,0:T(8,128)(2,1)}, bf16[1,144,512]{2,1,0:T(8,128)(2,1)}) custom-call(s32[1]{0:T(128)} %bitcast.place_ref, bf16[256,256]{1,0:T(8,128)(2,1)S(1)} %copy-done.4, bf16[4,256,256]{2,1,0:T(8,128)(2,1)S(1)} %copy-done.2, bf16[288,288]{1,0:T(8,128)(2,1)S(1)} %copy-done.1, ...), custom_call_target="tpu_custom_call" | custom-call | flops 10000000 | bytes 2000000 | tf_op jit(solution)/shard_map/advect/pallas_call | solution.py:215
  42.3 1.3 collective-permute-start.2
  43.6 2.6 collective-permute-start.3
  46.2 1.1 collective-permute-start.4
  47.3 0.1 broadcast_in_dim.7
  47.4 0.0 copy-start.5
  47.4 2.5 copy-done.5
  49.9 4.1 %tables.1 = (f32[2,5184,128]{2,1,0:T(8,128)S(1)}, bf16[512,768]{1,0:T(8,128)(2,1)S(1)}, bf16[256,512]{1,0:T(8,128)(2,1)S(1)}, f32[2,72,128]{2,1,0:T(8,128)S(1)}, f32[4,72,128]{2,1,0:T(8,128)S(1)}) custom-call(bf16[5184,512]{1,0:T(8,128)(2,1)S(1)} %bitcast.26, s32[1,512]{1,0:T(1,128)S(1)} %bitcast.40, s32[1,512]{1,0:T(1,128)S(1)} %bitcast.41, ...), custom_call_target="tpu_custom_call" | custom-call | flops 1358954496 | bytes 12000000 | tf_op jit(solution)/shard_map/tables/pallas_call | solution.py:287
  54.0 5.5 %advect.6 = (bf16[1,144,512]{2,1,0:T(8,128)(2,1)S(1)}, bf16[1,144,512]{2,1,0:T(8,128)(2,1)S(1)}, bf16[1,144,512]{2,1,0:T(8,128)(2,1)S(1)}, bf16[1,144,512]{2,1,0:T(8,128)(2,1)S(1)}) custom-call(s32[1]{0:T(128)} %bitcast.place_ref, bf16[256,256]{1,0:T(8,128)(2,1)S(1)} %copy-done.4, bf16[4,256,256]{2,1,0:T(8,128)(2,1)S(1)} %copy-done.2, ...), custom_call_target="tpu_custom_call" | custom-call | flops 10000000 | bytes 2000000 | tf_op jit(solution)/shard_map/advect/pallas_call | solution.py:215
  59.6 0.0 collective-permute-done.3.part2_ref
  59.6 0.0 collective-permute-done.4.part3_ref
  59.6 0.1 broadcast_in_dim.8.rate_ref
  59.6 7.6 %physics.5.refs_0_.own_ref = bf16[576,512]{1,0:T(8,128)(2,1)} custom-call(s32[1]{0:T(128)} %bitcast.place_ref, bf16[1,144,512]{2,1,0:T(8,128)(2,1)S(1)} %get-tuple-element.39.refs_0_.part0_ref, bf16[1,144,512]{2,1,0:T(8,128)(2,1)S(1)} %collective-permute-done.2.part1_ref, bf16[1,144,512]{2,1,0:T(8,128)(2,1)} %collective-permute-done.3.part2_ref, ...), custom_call_target="tpu_custom_call" | custom-call | flops 1028653056 | bytes 7700000 | tf_op jit(solution)/shard_map/physics/pallas_call | solution.py:402
  67.2 7.5 %extract.5 = (bf16[4,1152,128]{2,1,0:T(8,128)(2,1)S(1)}, bf16[4,1152,128]{2,1,0:T(8,128)(2,1)S(1)}) custom-call(bf16[256,256]{1,0:T(8,128)(2,1)S(1)} %copy-done.4, bf16[288,288]{1,0:T(8,128)(2,1)S(1)} %copy-done.1, bf16[64,18,16,128]{3,2,1,0:T(8,128)(2,1)} %bitcast.46, bf16[18,16,128]{2,1,0:T(8,128)(2,1)S(1)} %bitcast.31, ...), custom_call_target="tpu_custom_call" | custom-call | flops 4000000 | bytes 4800000 | tf_op jit(solution)/shard_map/extract/pallas_call | solution.py:102
  74.8 2.0 collective-permute-start.8
  76.8 7.2 %collective-permute-start.7 = (bf16[4,1152,128]{2,1,0:T(8,128)(2,1)S(1)}, bf16[4,1152,128]{2,1,0:T(8,128)(2,1)S(1)}, u32[]{:S(2)}, u32[]{:S(2)}) collective-permute-start(bf16[4,1152,128]{2,1,0:T(8,128)(2,1)S(1)} %get-tuple-element.50.refs_0_), channel_id=1, source_target_pairs={{0,4},{4,8},{8,12},{12,16},{16,20},{20,24},{24,28},{28,32},{32,36}... | collective-permute-start | bytes 3538952 | tf_op jit(solution)/shard_map/ppermute | solution.py:476
  84.0 0.5 collective-permute-start.12
  84.5 0.4 collective-permute-start.13
  84.9 2.0 collective-permute-start.14
  86.9 9.7 %advect.7 = (bf16[2,144,512]{2,1,0:T(8,128)(2,1)S(1)}, bf16[2,144,512]{2,1,0:T(8,128)(2,1)S(1)}, bf16[2,144,512]{2,1,0:T(8,128)(2,1)S(1)}, bf16[2,144,512]{2,1,0:T(8,128)(2,1)S(1)}) custom-call(s32[1]{0:T(128)} %bitcast.place_ref, bf16[256,256]{1,0:T(8,128)(2,1)S(1)} %copy-done.4, bf16[4,256,256]{2,1,0:T(8,128)(2,1)S(1)} %copy-done.2, ...), custom_call_target="tpu_custom_call" | custom-call | flops 20000000 | bytes 4000000 | tf_op jit(solution)/shard_map/advect/pallas_call | solution.py:215
  96.7 0.4 collective-permute-start.9
  97.1 0.0 collective-permute-done.13.part2_ref
  97.1 1.9 collective-permute-start.10
  99.0 2.0 collective-permute-start.11
  101.0 6.6 %physics.6.refs_0_.own_ref = bf16[576,512]{1,0:T(8,128)(2,1)} custom-call(s32[1]{0:T(128)} %bitcast.place_ref, bf16[1,144,512]{2,1,0:T(8,128)(2,1)S(1)} %get-tuple-element.49.refs_0_.part0_ref, bf16[1,144,512]{2,1,0:T(8,128)(2,1)S(1)} %collective-permute-done.12.part1_ref, bf16[1,144,512]{2,1,0:T(8,128)(2,1)S(1)} %collective-permute-done.13.part2_ref, ...), custom_call_target="tpu_custom_call" | custom-call | flops 1028653056 | bytes 7700000 | tf_op jit(solution)/shard_map/physics/pallas_call | solution.py:402
  107.6 9.7 %advect.8 = (bf16[2,144,512]{2,1,0:T(8,128)(2,1)S(1)}, bf16[2,144,512]{2,1,0:T(8,128)(2,1)S(1)}, bf16[2,144,512]{2,1,0:T(8,128)(2,1)S(1)}, bf16[2,144,512]{2,1,0:T(8,128)(2,1)S(1)}) custom-call(s32[1]{0:T(128)} %bitcast.place_ref, bf16[256,256]{1,0:T(8,128)(2,1)S(1)} %copy-done.4, bf16[4,256,256]{2,1,0:T(8,128)(2,1)S(1)} %copy-done.2, ...), custom_call_target="tpu_custom_call" | custom-call | flops 20000000 | bytes 4000000 | tf_op jit(solution)/shard_map/advect/pallas_call | solution.py:215
  117.3 0.1 collective-permute-start.18
  117.4 1.2 collective-permute-start.19
  118.6 1.7 collective-permute-start.20
  120.3 0.0 collective-permute-done.10.part2_ref
  120.3 10.3 %physics.7.refs_0_.own_ref = bf16[1152,512]{1,0:T(8,128)(2,1)S(1)} custom-call(s32[1]{0:T(128)} %bitcast.place_ref, bf16[2,144,512]{2,1,0:T(8,128)(2,1)S(1)} %get-tuple-element.52.refs_0_.part0_ref, bf16[2,144,512]{2,1,0:T(8,128)(2,1)S(1)} %collective-permute-done.9.part1_ref, bf16[2,144,512]{2,1,0:T(8,128)(2,1)S(1)} %collective-permute-done.10.part2_ref, ...), custom_call_target="tpu_custom_call" | custom-call | flops 2057306112 | bytes 8900000 | tf_op jit(solution)/shard_map/physics/pallas_call | solution.py:402
  130.6 9.7 %advect.9 = (bf16[2,144,512]{2,1,0:T(8,128)(2,1)S(1)}, bf16[2,144,512]{2,1,0:T(8,128)(2,1)S(1)}, bf16[2,144,512]{2,1,0:T(8,128)(2,1)S(1)}, bf16[2,144,512]{2,1,0:T(8,128)(2,1)S(1)}) custom-call(s32[1]{0:T(128)} %bitcast.place_ref, bf16[256,256]{1,0:T(8,128)(2,1)S(1)} %copy-done.4, bf16[4,256,256]{2,1,0:T(8,128)(2,1)S(1)} %copy-done.2, ...), custom_call_target="tpu_custom_call" | custom-call | flops 20000000 | bytes 4000000 | tf_op jit(solution)/shard_map/advect/pallas_call | solution.py:215
  140.4 0.5 collective-permute-start.15
  140.8 1.9 collective-permute-start.16
  142.7 2.0 collective-permute-start.17
  144.7 2.7 %collective-permute-start.23 = (bf16[1152,512]{1,0:T(8,128)(2,1)S(1)}, bf16[1152,512]{1,0:T(8,128)(2,1)}, u32[]{:S(2)}, u32[]{:S(2)}) collective-permute-start(bf16[1152,512]{1,0:T(8,128)(2,1)S(1)} %physics.7.refs_0_.own_ref), channel_id=1, source_target_pairs={{0,64},{4,68},{8,72},{12,76},{16,80},{20,84},{24,88},{28,92},{32,9... | collective-permute-start | bytes 3538952 | tf_op jit(solution)/shard_map/ppermute | solution.py:486
  147.4 10.3 %physics.8.refs_0_.refs_1_.own_ref = bf16[1152,512]{1,0:T(8,128)(2,1)S(1)} custom-call(s32[1]{0:T(128)} %bitcast.place_ref, bf16[2,144,512]{2,1,0:T(8,128)(2,1)S(1)} %get-tuple-element.59.refs_0_.part0_ref, bf16[2,144,512]{2,1,0:T(8,128)(2,1)S(1)} %collective-permute-done.18.part1_ref, bf16[2,144,512]{2,1,0:T(8,128)(2,1)S(1)} %collective-permute-done.19.part2_ref, ...), custom_call_target="tpu_custom_call" | custom-call | flops 2057306112 | bytes 8900000 | tf_op jit(solution)/shard_map/physics/pallas_call | solution.py:402
  157.7 0.0 copy-start.16
  157.7 0.3 collective-permute-start.22
  158.0 10.3 %physics.9.refs_1_.own_ref = bf16[1152,512]{1,0:T(8,128)(2,1)S(1)} custom-call(s32[1]{0:T(128)} %bitcast.place_ref, bf16[2,144,512]{2,1,0:T(8,128)(2,1)S(1)} %get-tuple-element.60.refs_0_.part0_ref, bf16[2,144,512]{2,1,0:T(8,128)(2,1)S(1)} %collective-permute-done.15.part1_ref, bf16[2,144,512]{2,1,0:T(8,128)(2,1)S(1)} %collective-permute-done.16.part2_ref, ...), custom_call_target="tpu_custom_call" | custom-call | flops 2057306112 | bytes 8900000 | tf_op jit(solution)/shard_map/physics/pallas_call | solution.py:402
  168.4 2.8 %collective-permute-start.21 = (bf16[1152,512]{1,0:T(8,128)(2,1)S(1)}, bf16[1152,512]{1,0:T(8,128)(2,1)}, u32[]{:S(2)}, u32[]{:S(2)}) collective-permute-start(bf16[1152,512]{1,0:T(8,128)(2,1)S(1)} %physics.9.refs_1_.own_ref), channel_id=1, source_target_pairs={{0,64},{4,68},{8,72},{12,76},{16,80},{20,84},{24,88},{28,92},{32,9... | collective-permute-start | bytes 3538952 | tf_op jit(solution)/shard_map/ppermute | solution.py:486
  171.2 0.2 collective-permute-start.25
  171.4 2.7 %collective-permute-start.24 = (bf16[576,512]{1,0:T(8,128)(2,1)}, bf16[576,512]{1,0:T(8,128)(2,1)}, u32[]{:S(2)}, u32[]{:S(2)}) collective-permute-start(bf16[576,512]{1,0:T(8,128)(2,1)} %physics.6.refs_0_.own_ref), channel_id=1, source_target_pairs={{0,64},{4,68},{8,72},{12,76},{16,80},{20,84},{24,88},{28,92},{32,9... | collective-permute-start | bytes 1769480 | tf_op jit(solution)/shard_map/ppermute | solution.py:486
  174.2 0.6 dynamic_slice.3.flag_ref
  174.8 62.7 %collective-permute-done.25.partner_ref = bf16[576,512]{1,0:T(8,128)(2,1)} collective-permute-done((bf16[576,512]{1,0:T(8,128)(2,1)}, bf16[576,512]{1,0:T(8,128)(2,1)}, u32[]{:S(2)}, u32[]{:S(2)}) %collective-permute-start.25) | collective-permute-done | bytes 589856 | tf_op jit(solution)/shard_map/ppermute | solution.py:486
  237.5 2.5 choose.5.refs_0_
  239.9 8.9 %collective-permute-done.24.partner_ref = bf16[576,512]{1,0:T(8,128)(2,1)} collective-permute-done((bf16[576,512]{1,0:T(8,128)(2,1)}, bf16[576,512]{1,0:T(8,128)(2,1)}, u32[]{:S(2)}, u32[]{:S(2)}) %collective-permute-start.24) | collective-permute-done | bytes 589856 | tf_op jit(solution)/shard_map/ppermute | solution.py:486
  248.8 2.5 choose.6.refs_0_
  251.3 4.0 %choose.7.refs_0_ = bf16[4608,512]{1,0:T(8,128)(2,1)} custom-call(s32[1]{0:T(128)} %dynamic_slice.3.flag_ref, bf16[1152,512]{1,0:T(8,128)(2,1)S(1)} %physics.7.refs_0_.own_ref, bf16[1152,512]{1,0:T(8,128)(2,1)} %collective-permute-done.23.partner_ref, bf16[4608,512]{1,0:T(8,128)(2,1)} %choose.6.refs_0_, ...), custom_call_target="tpu_custom_call", output_to_operand_aliasing={{}: (3, {})} | custom-call | bytes 2400000 | tf_op jit(solution)/shard_map/choose/pallas_call | solution.py:455
  255.3 4.0 %choose.8.refs_0_ = bf16[4608,512]{1,0:T(8,128)(2,1)} custom-call(s32[1]{0:T(128)} %dynamic_slice.3.flag_ref, bf16[1152,512]{1,0:T(8,128)(2,1)S(1)} %physics.8.refs_0_.refs_1_.own_ref, bf16[1152,512]{1,0:T(8,128)(2,1)} %collective-permute-done.22.partner_ref, bf16[4608,512]{1,0:T(8,128)(2,1)} %choose.7.refs_0_, ...), custom_call_target="tpu_custom_call", output_to_operand_aliasing={{}: (3, {})} | custom-call | bytes 2400000 | tf_op jit(solution)/shard_map/choose/pallas_call | solution.py:455
  259.4 4.0 %choose.9 = bf16[4608,512]{1,0:T(8,128)(2,1)} custom-call(s32[1]{0:T(128)} %dynamic_slice.3.flag_ref, bf16[1152,512]{1,0:T(8,128)(2,1)S(1)} %physics.9.refs_1_.own_ref, bf16[1152,512]{1,0:T(8,128)(2,1)} %collective-permute-done.21.partner_ref, bf16[4608,512]{1,0:T(8,128)(2,1)} %choose.8.refs_0_, ...), custom_call_target="tpu_custom_call", output_to_operand_aliasing={{}: (3, {})} | custom-call | bytes 2400000 | tf_op jit(solution)/shard_map/choose/pallas_call | solution.py:455
  (44 shorter events, 0.1 us)
Async XLA Ops:
  0.0 0.9 copy-start
  0.9 0.9 copy-start.3
  1.8 0.9 copy-start.6
  6.3 28.7 %copy-start.1 = (bf16[288,288]{1,0:T(8,128)(2,1)S(1)}, bf16[288,288]{1,0:T(8,128)(2,1)}, u32[]{:S(2)}) copy-start(bf16[288,288]{1,0:T(8,128)(2,1)} %constant.35.clone.face_move_ref) | copy-start | bytes 497668
  6.3 28.7 %copy-start.2 = (bf16[4,256,256]{2,1,0:T(8,128)(2,1)S(1)}, bf16[4,256,256]{2,1,0:T(8,128)(2,1)}, u32[]{:S(2)}) copy-start(bf16[4,256,256]{2,1,0:T(8,128)(2,1)} %constant.34.clone.group_ref) | copy-start | bytes 1572868
  6.3 28.7 %copy-start.4 = (bf16[256,256]{1,0:T(8,128)(2,1)S(1)}, bf16[256,256]{1,0:T(8,128)(2,1)}, u32[]{:S(2)}) copy-start(bf16[256,256]{1,0:T(8,128)(2,1)} %constant.33.clone.apart_ref) | copy-start | bytes 393220
  6.3 28.7 %copy-start.7 = (bf16[18,2,1024]{2,1,0:T(2,128)(2,1)S(1)}, bf16[18,2,1024]{2,1,0:T(2,128)(2,1)}, u32[]{:S(2)}) copy-start(bf16[18,2,1024]{2,1,0:T(2,128)(2,1)} %param.13) | copy-start | bytes 221188
  6.3 28.7 %copy-start.8 = (bf16[18,2,1024]{2,1,0:T(2,128)(2,1)S(1)}, bf16[18,2,1024]{2,1,0:T(2,128)(2,1)}, u32[]{:S(2)}) copy-start(bf16[18,2,1024]{2,1,0:T(2,128)(2,1)} %param.14) | copy-start | bytes 221188
  13.1 40.9 %collective-permute-start.6 = (bf16[3,1152,128]{2,1,0:T(8,128)(2,1)}, bf16[3,1152,128]{2,1,0:T(8,128)(2,1)S(1)}, u32[]{:S(2)}, u32[]{:S(2)}) collective-permute-start(bf16[3,1152,128]{2,1,0:T(8,128)(2,1)} %get-tuple-element.48), channel_id=1, source_target_pairs={{4,0},{8,4},{12,8},{16,12},{20,16},{24,20},{28,24},{32,28},{36,32}... | collective-permute-start | bytes 2654216 | tf_op jit(solution)/shard_map/ppermute | solution.py:476
  15.7 38.4 %collective-permute-start.5 = (bf16[3,1152,128]{2,1,0:T(8,128)(2,1)}, bf16[3,1152,128]{2,1,0:T(8,128)(2,1)S(1)}, u32[]{:S(2)}, u32[]{:S(2)}) collective-permute-start(bf16[3,1152,128]{2,1,0:T(8,128)(2,1)} %get-tuple-element.38.refs_0_), channel_id=1, source_target_pairs={{0,4},{4,8},{8,12},{12,16},{16,20},{20,24},{24,28},{28,32},{32,36}... | collective-permute-start | bytes 2654216 | tf_op jit(solution)/shard_map/ppermute | solution.py:476
  20.8 14.2 %collective-permute-start.1 = (bf16[1,1296,128]{2,1,0:T(8,128)(2,1)}, bf16[1,1296,128]{2,1,0:T(8,128)(2,1)S(1)}, u32[]{:S(2)}, u32[]{:S(2)}) collective-permute-start(bf16[1,1296,128]{2,1,0:T(8,128)(2,1)} %get-tuple-element.37), channel_id=1, source_target_pairs={{4,0},{8,4},{12,8},{16,12},{20,16},{24,20},{28,24},{32,28},{36,32}... | collective-permute-start | bytes 995336 | tf_op jit(solution)/shard_map/ppermute | solution.py:476
  22.7 11.5 %collective-permute-start = (bf16[1,1152,128]{2,1,0:T(8,128)(2,1)}, bf16[1,1152,128]{2,1,0:T(8,128)(2,1)S(1)}, u32[]{:S(2)}, u32[]{:S(2)}) collective-permute-start(bf16[1,1152,128]{2,1,0:T(8,128)(2,1)} %get-tuple-element.36.refs_0_), channel_id=1, source_target_pairs={{0,4},{4,8},{8,12},{12,16},{16,20},{20,24},{24,28},{28,32},{32,36}... | collective-permute-start | bytes 884744 | tf_op jit(solution)/shard_map/ppermute | solution.py:476
  34.2 0.8 copy-start.10
  35.0 1.0 copy-start.11
  36.0 11.3 %copy-start.15 = (f32[64]{0:T(128)S(1)}, f32[64]{0:T(128)}, u32[]{:S(2)}) copy-start(f32[64]{0:T(128)} %param.19) | copy-start | bytes 772
  36.0 11.4 %copy-start.12 = (bf16[72,512]{1,0:T(8,128)(2,1)S(1)}, bf16[72,512]{1,0:T(8,128)(2,1)}, u32[]{:S(2)}) copy-start(bf16[72,512]{1,0:T(8,128)(2,1)} %rain_ref.1) | copy-start | bytes 221188
  36.0 11.4 %copy-start.13 = (s32[512]{0:T(512)S(1)}, s32[512]{0:T(512)}, u32[]{:S(2)}) copy-start(s32[512]{0:T(512)} %param.16) | copy-start | bytes 6148
  36.0 11.4 %copy-start.14 = (s32[512]{0:T(512)S(1)}, s32[512]{0:T(512)}, u32[]{:S(2)}) copy-start(s32[512]{0:T(512)} %param.17) | copy-start | bytes 6148
  42.3 17.3 %collective-permute-start.2 = (bf16[1,144,512]{2,1,0:T(8,128)(2,1)}, bf16[1,144,512]{2,1,0:T(8,128)(2,1)S(1)}, u32[]{:S(2)}, u32[]{:S(2)}) collective-permute-start(bf16[1,144,512]{2,1,0:T(8,128)(2,1)} %get-tuple-element.40), channel_id=1, source_target_pairs={{0,1},{1,2},{2,3},{3,0},{4,5},{5,6},{6,7},{7,4},{8,9},{9,10},{10,1... | collective-permute-start | bytes 442376 | tf_op jit(solution)/shard_map/ppermute | solution.py:481
  43.6 16.0 %collective-permute-start.3 = (bf16[1,144,512]{2,1,0:T(8,128)(2,1)}, bf16[1,144,512]{2,1,0:T(8,128)(2,1)}, u32[]{:S(2)}, u32[]{:S(2)}) collective-permute-start(bf16[1,144,512]{2,1,0:T(8,128)(2,1)} %get-tuple-element.41), channel_id=1, source_target_pairs={{0,2},{1,3},{2,0},{3,1},{4,6},{5,7},{6,4},{7,5},{8,10},{9,11},{10,... | collective-permute-start | bytes 442376 | tf_op jit(solution)/shard_map/ppermute | solution.py:481
  46.2 13.4 %collective-permute-start.4 = (bf16[1,144,512]{2,1,0:T(8,128)(2,1)}, bf16[1,144,512]{2,1,0:T(8,128)(2,1)}, u32[]{:S(2)}, u32[]{:S(2)}) collective-permute-start(bf16[1,144,512]{2,1,0:T(8,128)(2,1)} %get-tuple-element.42), channel_id=1, source_target_pairs={{0,3},{1,0},{2,1},{3,2},{4,7},{5,4},{6,5},{7,6},{8,11},{9,8},{10,9... | collective-permute-start | bytes 442376 | tf_op jit(solution)/shard_map/ppermute | solution.py:481
  47.4 2.5 copy-start.5
  74.8 32.9 %collective-permute-start.8 = (bf16[4,1152,128]{2,1,0:T(8,128)(2,1)S(1)}, bf16[4,1152,128]{2,1,0:T(8,128)(2,1)S(1)}, u32[]{:S(2)}, u32[]{:S(2)}) collective-permute-start(bf16[4,1152,128]{2,1,0:T(8,128)(2,1)S(1)} %get-tuple-element.51), channel_id=1, source_target_pairs={{4,0},{8,4},{12,8},{16,12},{20,16},{24,20},{28,24},{32,28},{36,32}... | collective-permute-start | bytes 3538952 | tf_op jit(solution)/shard_map/ppermute | solution.py:476
  76.8 30.8 %collective-permute-start.7 = (bf16[4,1152,128]{2,1,0:T(8,128)(2,1)S(1)}, bf16[4,1152,128]{2,1,0:T(8,128)(2,1)S(1)}, u32[]{:S(2)}, u32[]{:S(2)}) collective-permute-start(bf16[4,1152,128]{2,1,0:T(8,128)(2,1)S(1)} %get-tuple-element.50.refs_0_), channel_id=1, source_target_pairs={{0,4},{4,8},{8,12},{12,16},{16,20},{20,24},{24,28},{28,32},{32,36}... | collective-permute-start | bytes 3538952 | tf_op jit(solution)/shard_map/ppermute | solution.py:476
  84.0 12.7 %collective-permute-start.12 = (bf16[1,144,512]{2,1,0:T(8,128)(2,1)S(1)}, bf16[1,144,512]{2,1,0:T(8,128)(2,1)S(1)}, u32[]{:S(2)}, u32[]{:S(2)}) collective-permute-start(bf16[1,144,512]{2,1,0:T(8,128)(2,1)S(1)} %get-tuple-element.56), channel_id=1, source_target_pairs={{0,1},{1,2},{2,3},{3,0},{4,5},{5,6},{6,7},{7,4},{8,9},{9,10},{10,1... | collective-permute-start | bytes 442376 | tf_op jit(solution)/shard_map/ppermute | solution.py:481
  84.5 12.7 %collective-permute-start.13 = (bf16[1,144,512]{2,1,0:T(8,128)(2,1)S(1)}, bf16[1,144,512]{2,1,0:T(8,128)(2,1)S(1)}, u32[]{:S(2)}, u32[]{:S(2)}) collective-permute-start(bf16[1,144,512]{2,1,0:T(8,128)(2,1)S(1)} %get-tuple-element.57), channel_id=1, source_target_pairs={{0,2},{1,3},{2,0},{3,1},{4,6},{5,7},{6,4},{7,5},{8,10},{9,11},{10,... | collective-permute-start | bytes 442376 | tf_op jit(solution)/shard_map/ppermute | solution.py:481
  84.9 14.1 %collective-permute-start.14 = (bf16[1,144,512]{2,1,0:T(8,128)(2,1)S(1)}, bf16[1,144,512]{2,1,0:T(8,128)(2,1)S(1)}, u32[]{:S(2)}, u32[]{:S(2)}) collective-permute-start(bf16[1,144,512]{2,1,0:T(8,128)(2,1)S(1)} %get-tuple-element.58), channel_id=1, source_target_pairs={{0,3},{1,0},{2,1},{3,2},{4,7},{5,4},{6,5},{7,6},{8,11},{9,8},{10,9... | collective-permute-start | bytes 442376 | tf_op jit(solution)/shard_map/ppermute | solution.py:481
  96.7 21.9 %collective-permute-start.9 = (bf16[2,144,512]{2,1,0:T(8,128)(2,1)S(1)}, bf16[2,144,512]{2,1,0:T(8,128)(2,1)S(1)}, u32[]{:S(2)}, u32[]{:S(2)}) collective-permute-start(bf16[2,144,512]{2,1,0:T(8,128)(2,1)S(1)} %get-tuple-element.53), channel_id=1, source_target_pairs={{0,1},{1,2},{2,3},{3,0},{4,5},{5,6},{6,7},{7,4},{8,9},{9,10},{10,1... | collective-permute-start | bytes 884744 | tf_op jit(solution)/shard_map/ppermute | solution.py:481
  97.1 23.2 %collective-permute-start.10 = (bf16[2,144,512]{2,1,0:T(8,128)(2,1)S(1)}, bf16[2,144,512]{2,1,0:T(8,128)(2,1)S(1)}, u32[]{:S(2)}, u32[]{:S(2)}) collective-permute-start(bf16[2,144,512]{2,1,0:T(8,128)(2,1)S(1)} %get-tuple-element.54), channel_id=1, source_target_pairs={{0,2},{1,3},{2,0},{3,1},{4,6},{5,7},{6,4},{7,5},{8,10},{9,11},{10,... | collective-permute-start | bytes 884744 | tf_op jit(solution)/shard_map/ppermute | solution.py:481
  99.0 21.3 %collective-permute-start.11 = (bf16[2,144,512]{2,1,0:T(8,128)(2,1)S(1)}, bf16[2,144,512]{2,1,0:T(8,128)(2,1)S(1)}, u32[]{:S(2)}, u32[]{:S(2)}) collective-permute-start(bf16[2,144,512]{2,1,0:T(8,128)(2,1)S(1)} %get-tuple-element.55), channel_id=1, source_target_pairs={{0,3},{1,0},{2,1},{3,2},{4,7},{5,4},{6,5},{7,6},{8,11},{9,8},{10,9... | collective-permute-start | bytes 884744 | tf_op jit(solution)/shard_map/ppermute | solution.py:481
  117.3 25.4 %collective-permute-start.18 = (bf16[2,144,512]{2,1,0:T(8,128)(2,1)S(1)}, bf16[2,144,512]{2,1,0:T(8,128)(2,1)S(1)}, u32[]{:S(2)}, u32[]{:S(2)}) collective-permute-start(bf16[2,144,512]{2,1,0:T(8,128)(2,1)S(1)} %get-tuple-element.64), channel_id=1, source_target_pairs={{0,1},{1,2},{2,3},{3,0},{4,5},{5,6},{6,7},{7,4},{8,9},{9,10},{10,1... | collective-permute-start | bytes 884744 | tf_op jit(solution)/shard_map/ppermute | solution.py:481
  117.4 27.3 %collective-permute-start.19 = (bf16[2,144,512]{2,1,0:T(8,128)(2,1)S(1)}, bf16[2,144,512]{2,1,0:T(8,128)(2,1)S(1)}, u32[]{:S(2)}, u32[]{:S(2)}) collective-permute-start(bf16[2,144,512]{2,1,0:T(8,128)(2,1)S(1)} %get-tuple-element.65), channel_id=1, source_target_pairs={{0,2},{1,3},{2,0},{3,1},{4,6},{5,7},{6,4},{7,5},{8,10},{9,11},{10,... | collective-permute-start | bytes 884744 | tf_op jit(solution)/shard_map/ppermute | solution.py:481
  118.6 28.8 %collective-permute-start.20 = (bf16[2,144,512]{2,1,0:T(8,128)(2,1)S(1)}, bf16[2,144,512]{2,1,0:T(8,128)(2,1)S(1)}, u32[]{:S(2)}, u32[]{:S(2)}) collective-permute-start(bf16[2,144,512]{2,1,0:T(8,128)(2,1)S(1)} %get-tuple-element.66), channel_id=1, source_target_pairs={{0,3},{1,0},{2,1},{3,2},{4,7},{5,4},{6,5},{7,6},{8,11},{9,8},{10,9... | collective-permute-start | bytes 884744 | tf_op jit(solution)/shard_map/ppermute | solution.py:481
  120.3 10.3 %copy-start.9 = (bf16[18,2,1024]{2,1,0:T(2,128)(2,1)S(1)}, bf16[18,2,1024]{2,1,0:T(2,128)(2,1)}, u32[]{:S(2)}) copy-start(bf16[18,2,1024]{2,1,0:T(2,128)(2,1)} %param.14) | copy-start | bytes 221188
  140.4 17.7 %collective-permute-start.15 = (bf16[2,144,512]{2,1,0:T(8,128)(2,1)S(1)}, bf16[2,144,512]{2,1,0:T(8,128)(2,1)S(1)}, u32[]{:S(2)}, u32[]{:S(2)}) collective-permute-start(bf16[2,144,512]{2,1,0:T(8,128)(2,1)S(1)} %get-tuple-element.61), channel_id=1, source_target_pairs={{0,1},{1,2},{2,3},{3,0},{4,5},{5,6},{6,7},{7,4},{8,9},{9,10},{10,1... | collective-permute-start | bytes 884744 | tf_op jit(solution)/shard_map/ppermute | solution.py:481
  140.8 17.2 %collective-permute-start.16 = (bf16[2,144,512]{2,1,0:T(8,128)(2,1)S(1)}, bf16[2,144,512]{2,1,0:T(8,128)(2,1)S(1)}, u32[]{:S(2)}, u32[]{:S(2)}) collective-permute-start(bf16[2,144,512]{2,1,0:T(8,128)(2,1)S(1)} %get-tuple-element.62), channel_id=1, source_target_pairs={{0,2},{1,3},{2,0},{3,1},{4,6},{5,7},{6,4},{7,5},{8,10},{9,11},{10,... | collective-permute-start | bytes 884744 | tf_op jit(solution)/shard_map/ppermute | solution.py:481
  142.7 15.4 %collective-permute-start.17 = (bf16[2,144,512]{2,1,0:T(8,128)(2,1)S(1)}, bf16[2,144,512]{2,1,0:T(8,128)(2,1)S(1)}, u32[]{:S(2)}, u32[]{:S(2)}) collective-permute-start(bf16[2,144,512]{2,1,0:T(8,128)(2,1)S(1)} %get-tuple-element.63), channel_id=1, source_target_pairs={{0,3},{1,0},{2,1},{3,2},{4,7},{5,4},{6,5},{7,6},{8,11},{9,8},{10,9... | collective-permute-start | bytes 884744 | tf_op jit(solution)/shard_map/ppermute | solution.py:481
  144.7 106.7 %collective-permute-start.23 = (bf16[1152,512]{1,0:T(8,128)(2,1)S(1)}, bf16[1152,512]{1,0:T(8,128)(2,1)}, u32[]{:S(2)}, u32[]{:S(2)}) collective-permute-start(bf16[1152,512]{1,0:T(8,128)(2,1)S(1)} %physics.7.refs_0_.own_ref), channel_id=1, source_target_pairs={{0,64},{4,68},{8,72},{12,76},{16,80},{20,84},{24,88},{28,92},{32,9... | collective-permute-start | bytes 3538952 | tf_op jit(solution)/shard_map/ppermute | solution.py:486
  157.7 16.4 %copy-start.16 = (s32[64]{0:T(128)S(1)}, s32[64]{0:T(128)}, u32[]{:S(2)}) copy-start(s32[64]{0:T(128)} %param.20) | copy-start | bytes 772
  157.7 97.6 %collective-permute-start.22 = (bf16[1152,512]{1,0:T(8,128)(2,1)S(1)}, bf16[1152,512]{1,0:T(8,128)(2,1)}, u32[]{:S(2)}, u32[]{:S(2)}) collective-permute-start(bf16[1152,512]{1,0:T(8,128)(2,1)S(1)} %physics.8.refs_0_.refs_1_.own_ref), channel_id=1, source_target_pairs={{0,64},{4,68},{8,72},{12,76},{16,80},{20,84},{24,88},{28,92},{32,9... | collective-permute-start | bytes 3538952 | tf_op jit(solution)/shard_map/ppermute | solution.py:486
  168.4 91.0 %collective-permute-start.21 = (bf16[1152,512]{1,0:T(8,128)(2,1)S(1)}, bf16[1152,512]{1,0:T(8,128)(2,1)}, u32[]{:S(2)}, u32[]{:S(2)}) collective-permute-start(bf16[1152,512]{1,0:T(8,128)(2,1)S(1)} %physics.9.refs_1_.own_ref), channel_id=1, source_target_pairs={{0,64},{4,68},{8,72},{12,76},{16,80},{20,84},{24,88},{28,92},{32,9... | collective-permute-start | bytes 3538952 | tf_op jit(solution)/shard_map/ppermute | solution.py:486
  171.2 66.3 %collective-permute-start.25 = (bf16[576,512]{1,0:T(8,128)(2,1)}, bf16[576,512]{1,0:T(8,128)(2,1)}, u32[]{:S(2)}, u32[]{:S(2)}) collective-permute-start(bf16[576,512]{1,0:T(8,128)(2,1)} %physics.5.refs_0_.own_ref), channel_id=1, source_target_pairs={{0,64},{4,68},{8,72},{12,76},{16,80},{20,84},{24,88},{28,92},{32,9... | collective-permute-start | bytes 1769480 | tf_op jit(solution)/shard_map/ppermute | solution.py:486
  171.4 77.4 %collective-permute-start.24 = (bf16[576,512]{1,0:T(8,128)(2,1)}, bf16[576,512]{1,0:T(8,128)(2,1)}, u32[]{:S(2)}, u32[]{:S(2)}) collective-permute-start(bf16[576,512]{1,0:T(8,128)(2,1)} %physics.6.refs_0_.own_ref), channel_id=1, source_target_pairs={{0,64},{4,68},{8,72},{12,76},{16,80},{20,84},{24,88},{28,92},{32,9... | collective-permute-start | bytes 1769480 | tf_op jit(solution)/shard_map/ppermute | solution.py:486

commit v3 on v2

--- a/solution.py
+++ b/solution.py
@@ -1,12 +1,12 @@
-import itertools
+import functools
 
 import jax
 import jax.numpy as jnp
-import numpy as np
 from jax import lax
 from jax.experimental import pallas as pl
 from jax.experimental.pallas import tpu as pltpu
 from jax.sharding import PartitionSpec as P
+
 
 GROUP = 8
 CHUNKS = (1, 1, 2, 2, 2)
@@ -23,11 +23,11 @@
     ("physics", 1),
     ("advect", 3),
     ("physics", 2),
-    ("choose", 0),
     ("advect", 4),
     ("physics", 3),
+    ("physics", 4),
+    ("choose", 0),
     ("choose", 1),
-    ("physics", 4),
     ("choose", 2),
     ("choose", 3),
     ("choose", 4),
@@ -38,29 +38,28 @@
 BF16 = jnp.bfloat16
 
 
+def ones_where(row_target, columns):
+    column = lax.broadcasted_iota(jnp.int32, (row_target.shape[0], columns), 1)
+    return jnp.where(column == row_target, 1.0, 0.0).astype(BF16)
+
+
 def deinterleave():
-    move = np.zeros((256, 256), np.float32)
-    for k, a, t, i in itertools.product(range(2), range(2), range(GROUP), range(8)):
-        move[((k * 2 + a) * GROUP + t) * 8 + i, ((t * 2 + k) * 8 + i) * 2 + a] = 1
-    return jnp.asarray(move, BF16)
-
-
-def regroup(n_lev):
-    move = np.zeros((n_lev, 256, 256), np.float32)
-    for j, s, a, h in itertools.product(range(n_lev), range(n_lev), range(2), range(2)):
-        tile = 2 * ((j + s) % n_lev) + h
-        for k, t in itertools.product(range(2), range(GROUP)):
-            row = (((s * 2 + a) * 2 + h) * 2 + k) * GROUP + t
-            move[j, row, ((k * 2 + a) * GROUP + t) * 8 + tile] = 1
-    return jnp.asarray(move, BF16)
-
-
-def face_rows(levels):
-    rows = levels * 8
-    move = np.zeros((2 * rows, 2 * rows), np.float32)
-    for a, r in itertools.product(range(2), range(rows)):
-        move[a * rows + r, r * 2 + a] = 1
-    return jnp.asarray(move, BF16)
+    row = lax.broadcasted_iota(jnp.int32, (256, 256), 0)
+    level, lat, tracer, tile = row >> 7, (row >> 6) & 1, (row >> 3) & 7, row & 7
+    return ones_where((((tracer * 2 + level) * 8) + tile) * 2 + lat, 256)
+
+
+def regroup(place):
+    row = lax.broadcasted_iota(jnp.int32, (256, 256), 0)
+    target = ((row >> 6) + place) & 3
+    lat, half, level, tracer = (row >> 5) & 1, (row >> 4) & 1, (row >> 3) & 1, row & 7
+    return ones_where(((level * 2 + lat) * 8 + tracer) * 8 + 2 * target + half, 256)
+
+
+def face_rows(rows, lats):
+    row = lax.broadcasted_iota(jnp.int32, (lats * rows, 2 * rows), 0)
+    lat = (row >= rows).astype(jnp.int32)
+    return ones_where(2 * (row - lat * rows) + lat, 2 * rows)
 
 
 def product(a, b):
@@ -71,31 +70,31 @@
     return q_ref[:, pl.ds(2 * pair, 2)].reshape(2 * GROUP * 16, 128)
 
 
-def extract_kernel(apart_ref, face_move_ref, q_ref, lat_ref, *refs):
-    north_ref, south_ref = refs[-2:]
+def extract_kernel(q_ref, lat_ref, *refs):
+    north_ref, south_ref, apart_ref = refs[-3:]
     levels = q_ref.shape[1]
     rows = levels * GROUP * 8
 
-    def body(pair, carry):
+    @pl.when(pl.program_id(0) == 0)
+    def _():
+        apart_ref[...] = deinterleave()
+
+    for pair in range(levels // 2):
         apart = product(apart_ref[...], two_levels(q_ref, pair)).astype(BF16)
-        spot = pl.multiple_of(pair * 128, 128)
-        south_ref[0, pl.ds(spot, 64), :] = apart[0:64]
-        north_ref[0, pl.ds(spot, 64), :] = apart[64:128]
-        south_ref[0, pl.ds(spot + 64, 64), :] = apart[128:192]
-        north_ref[0, pl.ds(spot + 64, 64), :] = apart[192:256]
-        return carry
-
-    lax.fori_loop(0, levels // 2, body, 0)
+        for k in range(2):
+            spot = pair * 128 + k * 64
+            south_ref[0, spot : spot + 64, :] = apart[k * 128 : k * 128 + 64]
+            north_ref[0, spot : spot + 64, :] = apart[k * 128 + 64 : k * 128 + 128]
     if south_ref.shape[1] > rows:
         faces = lat_ref[...].reshape(levels * 16, 128)
-        south_ref[0, rows:, :] = product(face_move_ref[: levels * 8], faces).astype(BF16)
+        south_ref[0, rows:, :] = product(face_rows(levels * 8, 1), faces).astype(BF16)
 
 
 def whole_block(*shape):
     return pl.BlockSpec(shape, lambda *_: (0,) * len(shape))
 
 
-def extract(apart, face_move, q, lat, first, groups, after):
+def extract(q, lat, first, groups, after):
     levels = q.shape[1]
     rows = levels * GROUP * 8
     extra = levels * 8 if first == 0 else 0
@@ -103,8 +102,6 @@
         extract_kernel,
         grid=(groups,),
         in_specs=[
-            whole_block(*apart.shape),
-            whole_block(*face_move.shape),
             pl.BlockSpec((GROUP, levels, 16, 128), lambda g: (g + first, 0, 0, 0)),
             whole_block(*lat.shape),
         ]
@@ -113,6 +110,7 @@
             pl.BlockSpec((1, rows, 128), lambda g: (g, 0, 0)),
             pl.BlockSpec((1, rows + extra, 128), lambda g: (g, 0, 0)),
         ],
+        scratch_shapes=[pltpu.VMEM((256, 256), BF16)],
         out_shape=[
             jax.ShapeDtypeStruct((groups, rows, 128), BF16),
             jax.ShapeDtypeStruct((groups, rows + extra, 128), BF16),
@@ -122,7 +120,7 @@
         ),
         compiler_params=pltpu.CompilerParams(vmem_limit_bytes=16 << 20),
         name="extract",
-    )(apart, face_move, q, lat, *after)
+    )(q, lat, *after)
 
 
 def beside(x, lane, toward_east):
@@ -134,27 +132,30 @@
 
 
 def advect_kernel(
-    place_ref, apart_ref, group_ref, face_move_ref, q_ref, low_ref, high_ref, lat_ref, lon_ref,
-    above_ref, *refs
+    place_ref, q_ref, low_ref, high_ref, lat_ref, lon_ref, above_ref, *refs
 ):
-    outs, faces = refs[-5:-1], refs[-1]
+    outs = refs[-10:-6]
+    faces, apart_ref, group_ref, apart, made, edges = refs[-6:]
     levels = q_ref.shape[1]
     lane = lax.broadcasted_iota(jnp.int32, (8, 128), 1)
 
     @pl.when(pl.program_id(0) == 0)
     def _():
+        apart_ref[...] = deinterleave()
+        group_ref[...] = regroup(place_ref[0])
+        move = face_rows(levels * 8, 2)
         for at, ref in ((0, lat_ref), (2, lon_ref)):
-            both = product(face_move_ref[...], ref[...].reshape(levels * 16, 128))
+            both = product(move, ref[...].reshape(levels * 16, 128))
             faces[at] = both[: levels * 8]
             faces[at + 1] = both[levels * 8 :]
         faces[4] = above_ref[0].astype(F32)
 
+    for pair in range(levels // 2):
+        apart[pair] = product(apart_ref[...], two_levels(q_ref, pair))
+    edges[0] = low_ref[0].astype(F32)
+    edges[1] = high_ref[0].astype(F32)
+
     def body(pair, carry):
-        apart = product(apart_ref[...], two_levels(q_ref, pair))
-        spot = pl.multiple_of(pair * 128, 128)
-        low = low_ref[0, pl.ds(spot, 128), :].astype(F32)
-        high = high_ref[0, pl.ds(spot, 128), :].astype(F32)
-        results = []
         for k in range(2):
             at = pl.ds(pl.multiple_of((2 * pair + k) * 8, 8), 8)
             edge = [faces[0, at, :], faces[1, at, :], faces[4, at, :]]
@@ -176,17 +177,17 @@
                         -jnp.minimum(east, 0.0),
                     )
                 )
-            made = [[], []]
+            results = [[], []]
             for t in range(GROUP):
                 rows = [
-                    apart[(k * 2 + lat) * 64 + t * 8 : (k * 2 + lat) * 64 + t * 8 + 8]
+                    apart[pair, (k * 2 + lat) * 64 + t * 8 : (k * 2 + lat) * 64 + t * 8 + 8, :]
                     for lat in range(2)
                 ]
-                outer = [x[k * 64 + t * 8 : k * 64 + t * 8 + 8] for x in (low, high)]
-                column = [outer[0], rows[0], rows[1], outer[1]]
+                spot = pl.multiple_of(pair * 128 + (k * 64 + t * 8), 8)
+                column = [edges[0, pl.ds(spot, 8), :], *rows, edges[1, pl.ds(spot, 8), :]]
                 for lat in range(2):
                     own, from_s, from_n, from_w, from_e = terms[lat]
-                    made[lat].append(
+                    results[lat].append(
                         own * rows[lat]
                         + (from_s * column[lat] + from_n * column[lat + 2])
                         + (
@@ -194,20 +195,23 @@
                             + from_e * beside(rows[lat], lane, True)
                         )
                     )
-            results += made[0] + made[1]
-        sent = product(group_ref[0], jnp.concatenate(results, axis=0).astype(BF16)).astype(BF16)
-        spot = pl.multiple_of(pair * 16, 16)
+            for lat in range(2):
+                row = (k * 2 + lat) * 64
+                made[pair, row : row + 64, :] = jnp.concatenate(results[lat], axis=0).astype(BF16)
+        return carry
+
+    lax.fori_loop(0, levels // 2, body, 0)
+    for pair in range(levels // 2):
+        sent = product(group_ref[...], made[pair]).astype(BF16)
         for shift, out in enumerate(outs):
             for quarter in range(4):
                 row = (shift * 4 + quarter) * 16
-                out[0, pl.ds(spot, 16), quarter * 128 : (quarter + 1) * 128] = sent[row : row + 16]
-        return carry
-
-    lax.fori_loop(0, levels // 2, body, 0)
+                lanes = slice(quarter * 128, (quarter + 1) * 128)
+                out[0, pair * 16 : pair * 16 + 16, lanes] = sent[row : row + 16]
 
 
 def advect(
-    place, apart, group, face_move, q, low, high, lat, lon, above, first, halo_first, groups, after
+    place, q, low, high, lat, lon, above, first, halo_first, groups, after
 ):
     levels = q.shape[1]
     rows = levels * GROUP
@@ -218,9 +222,6 @@
             num_scalar_prefetch=1,
             grid=(groups,),
             in_specs=[
-                whole_block(*apart.shape),
-                pl.BlockSpec((1, 256, 256), lambda g, p: (p[0], 0, 0)),
-                whole_block(*face_move.shape),
                 pl.BlockSpec((GROUP, levels, 16, 128), lambda g, p: (g + first, 0, 0, 0)),
                 halo,
                 halo,
@@ -230,7 +231,14 @@
             ]
             + [pl.BlockSpec(memory_space=pl.ANY)] * len(after),
             out_specs=[pl.BlockSpec((1, rows, 512), lambda g, p: (g, 0, 0))] * 4,
-            scratch_shapes=[pltpu.VMEM((5, levels * 8, 128), F32)],
+            scratch_shapes=[
+                pltpu.VMEM((5, levels * 8, 128), F32),
+                pltpu.VMEM((256, 256), BF16),
+                pltpu.VMEM((256, 256), BF16),
+                pltpu.VMEM((levels // 2, 256, 128), F32),
+                pltpu.VMEM((levels // 2, 256, 128), BF16),
+                pltpu.VMEM((2, rows * 8, 128), F32),
+            ],
         ),
         out_shape=[jax.ShapeDtypeStruct((groups, rows, 512), BF16)] * 4,
         cost_estimate=pl.CostEstimate(
@@ -238,7 +246,7 @@
         ),
         compiler_params=pltpu.CompilerParams(vmem_limit_bytes=24 << 20),
         name="advect",
-    )(place, apart, group, face_move, q, low, high, lat, lon, above, *after)
+    )(place, q, low, high, lat, lon, above, *after)
 
 
 def table_kernel(matrix_ref, mask_ref, order_ref, rain_ref, *refs):
@@ -516,24 +524,26 @@
         scav_rate.reshape(tracers // GROUP, GROUP, 1), (tracers // GROUP, GROUP, 128)
     )
 
-    q = pltpu.with_memory_space_constraint(tiled_rows(tracer_dyn), pltpu.HBM)
-    lat, lon = tiled_rows(courant_lat), tiled_rows(courant_lon)
-    apart, group, face_move = deinterleave(), regroup(n_lev), face_rows(lat.shape[0])
+    in_hbm = functools.partial(pltpu.with_memory_space_constraint, memory_space=pltpu.HBM)
+    q = in_hbm(tiled_rows(tracer_dyn))
+    lat, lon = in_hbm(tiled_rows(courant_lat)), in_hbm(tiled_rows(courant_lon))
     firsts = [sum(CHUNKS[:number]) for number in range(len(CHUNKS))]
     halos, sections, owns, partners, made = {}, {}, {}, {}, {}
     out = last = None
     for kind, number in ORDER:
         after = [] if last is None else [last]
         if kind == "extract":
-            north, south = extract(apart, face_move, q, lat, *SPANS[number], after)
+            north, south = extract(q, lat, *SPANS[number], after)
             last = north
-            halos[number] = (shifted(north, "lat", 1), shifted(south, "lat", -1))
+            high = shifted(south, "lat", -1)
+            low = shifted(north, "lat", 1)
+            halos[number] = (low, high)
         elif kind == "tables":
             made = tables(
-                conv_matrix.reshape(levels * levels, columns),
-                conv_mask.reshape(1, columns),
-                column_order.reshape(1, columns),
-                rain,
+                in_hbm(conv_matrix.reshape(levels * levels, columns)),
+                in_hbm(conv_mask.reshape(1, columns)),
+                in_hbm(column_order.reshape(1, columns)),
+                in_hbm(rain),
                 after,
             )
             last = made[2]
@@ -541,11 +551,14 @@
             first, groups = firsts[number], CHUNKS[number]
             span = max(i for i in range(len(SPANS)) if SPANS[i][0] <= first)
             parts = advect(
-                place, apart, group, face_move, q, *halos[span], lat, lon, halos[0][1],
+                place, q, *halos[span], lat, lon, halos[0][1],
                 first, first - SPANS[span][0], groups, after,
             )
+            parts = list(parts)
             last = parts[0]
-            sections[number] = [parts[0]] + [turned(parts[s], "lev", s) for s in range(1, n_lev)]
+            for s in (2, 1, 3):
+                parts[s] = turned(parts[s], "lev", s)
+            sections[number] = parts
         elif kind == "physics":
             small, placing, back, wet, wet_all = made
             small = small.reshape(CAP // 128, levels, levels, 128)
@@ -575,6 +588,7 @@
         P(),
         P(),
     )
+
     return jax.shard_map(
         local, mesh=mesh, in_specs=placed, out_specs=P(None, None, ("lat", "lev")), check_vma=False
     )

time: 266 us -> 236 us (0.89)
  Pallas kernels: 125 us -> 107 us
  starting transfers between devices: 52.9 us -> 43.6 us
  local copies, waits for them, and re-layouts: 7.72 us -> 0.81 us
  waiting for transfers between devices: 77.4 us -> 80.3 us
    pallas_call x5, Pallas kernels: 40.9 us -> 26.5 us  [advect(): pl.pallas_call(advect_kernel, grid_spec=pltpu.PrefetchScalarGridSpec(num_...]
    pallas_call x3, Pallas kernels: 17.8 us -> 9.9 us  [extract(): pl.pallas_call(extract_kernel, grid=(groups,), in_specs=[pl.BlockSpec((GR...]
    ppermute x6, starting transfers between devices: 24.6 us -> 16.8 us  [shifted(): return lax.ppermute(value, axis, pairs)]
    unnamed x34 -> x4, local copies, waits for them, and re-layouts: 6.98 us -> 0.01 us
    ppermute x6, waiting for transfers between devices: 5.76 us -> 10.4 us  [shifted(): return lax.ppermute(value, axis, pairs)]
    pallas_call x1, Pallas kernels: 4.15 us -> 8.1 us  [tables(): pl.pallas_call(table_kernel, grid=(steps,), in_specs=[pl.BlockSpec((rows...]
  transfers between devices with their start and end apart: 26 -> 26, of which waited for: 3 -> 5; matrix products, arithmetic and copies ran while one was open for 0% -> 0% of each run, Pallas kernels for 36% -> 37%
where the time goes in v3:
time: 236 us; the launch traced here: 232 us
  Pallas kernels  107 us (45%)
  waiting for transfers between devices  80.3 us (34%)
  starting transfers between devices  43.6 us (18%)
    ppermute x5, waiting for transfers between devices, paired(): lax.ppermute(value, axis, [(i, i ^ count // 2) for i in range(count)])  69.1 us
    pallas_call x5, Pallas kernels, physics(): pl.pallas_call(physics_kernel, grid_spec=pltpu.PrefetchScalarGridSpec(num...  45.1 us
    pallas_call x5, Pallas kernels, advect(): pl.pallas_call(advect_kernel, grid_spec=pltpu.PrefetchScalarGridSpec(num_...  26.5 us
    ppermute x15, starting transfers between devices, turned(): lax.ppermute(value, axis, [(i, (i + steps) % count) for i in range(count)])  18.1 us
    pallas_call x5, Pallas kernels, choose(): pl.pallas_call(choose_kernel, grid_spec=pltpu.PrefetchScalarGridSpec(num_...  17.3 us
    ppermute x6, starting transfers between devices, shifted(): return lax.ppermute(value, axis, pairs)  16.8 us
    ppermute x6, waiting for transfers between devices, shifted(): return lax.ppermute(value, axis, pairs)  10.4 us
    pallas_call x3, Pallas kernels, extract(): pl.pallas_call(extract_kernel, grid=(groups,), in_specs=[pl.BlockSpec((GR...  9.9 us
  transfers between devices with their start and end apart: 26, of which 5 were waited for; matrix products, arithmetic and copies ran while one was open for 0% of the time, Pallas kernels for 37%

profile of v3, /device:TPU:97, one launch (start us, length us, event | category | flops | bytes accessed | tf_op | source)
XLA Modules:
  0.0 231.8 jit_solution(15619747911645579460)
XLA Ops:
  0.0 2.3 extract.3
  2.3 3.9 %extract.4 = (bf16[3,1152,128]{2,1,0:T(8,128)(2,1)S(1)}, bf16[3,1152,128]{2,1,0:T(8,128)(2,1)}) custom-call(bf16[64,18,16,128]{3,2,1,0:T(8,128)(2,1)} %bitcast.27, bf16[18,16,128]{2,1,0:T(8,128)(2,1)} %bitcast.36, bf16[1,1152,128]{2,1,0:T(8,128)(2,1)S(1)} %get-tuple-element.36.refs_0_), custom_call_target="tpu_custom_call" | custom-call | flops 3000000 | bytes 3600000 | tf_op jit(solution)/shard_map/extract/pallas_call | solution.py:101
  6.2 2.3 collective-permute-start.5
  8.5 2.2 collective-permute-start.6
  10.7 3.6 %collective-permute-start.1 = (bf16[1,1296,128]{2,1,0:T(8,128)(2,1)}, bf16[1,1296,128]{2,1,0:T(8,128)(2,1)S(1)}, u32[]{:S(2)}, u32[]{:S(2)}) collective-permute-start(bf16[1,1296,128]{2,1,0:T(8,128)(2,1)} %get-tuple-element.37), channel_id=1, source_target_pairs={{4,0},{8,4},{12,8},{16,12},{20,16},{24,20},{28,24},{32,28},{36,32}... | collective-permute-start | bytes 995336 | tf_op jit(solution)/shard_map/ppermute | solution.py:484
  14.4 4.0 %collective-permute-start = (bf16[1,1152,128]{2,1,0:T(8,128)(2,1)S(1)}, bf16[1,1152,128]{2,1,0:T(8,128)(2,1)}, u32[]{:S(2)}, u32[]{:S(2)}) collective-permute-start(bf16[1,1152,128]{2,1,0:T(8,128)(2,1)S(1)} %get-tuple-element.36.refs_0_), channel_id=1, source_target_pairs={{0,4},{4,8},{8,12},{12,16},{16,20},{20,24},{24,28},{28,32},{32,36}... | collective-permute-start | bytes 884744 | tf_op jit(solution)/shard_map/ppermute | solution.py:484
  18.4 3.6 %collective-permute-done.low_ref = bf16[1,1152,128]{2,1,0:T(8,128)(2,1)} collective-permute-done((bf16[1,1152,128]{2,1,0:T(8,128)(2,1)S(1)}, bf16[1,1152,128]{2,1,0:T(8,128)(2,1)}, u32[]{:S(2)}, u32[]{:S(2)}) %collective-permute-start) | collective-permute-done | bytes 294944 | tf_op jit(solution)/shard_map/ppermute | solution.py:484
  22.1 6.7 %collective-permute-done.1.high_ref.above_ref = bf16[1,1296,128]{2,1,0:T(8,128)(2,1)S(1)} collective-permute-done((bf16[1,1296,128]{2,1,0:T(8,128)(2,1)}, bf16[1,1296,128]{2,1,0:T(8,128)(2,1)S(1)}, u32[]{:S(2)}, u32[]{:S(2)}) %collective-permute-start.1) | collective-permute-done | bytes 331808 | tf_op jit(solution)/shard_map/ppermute | solution.py:484
  28.8 4.5 %advect.5 = (bf16[1,144,512]{2,1,0:T(8,128)(2,1)S(1)}, bf16[1,144,512]{2,1,0:T(8,128)(2,1)}, bf16[1,144,512]{2,1,0:T(8,128)(2,1)}, bf16[1,144,512]{2,1,0:T(8,128)(2,1)}) custom-call(s32[1]{0:T(128)} %bitcast.place_ref, bf16[64,18,16,128]{3,2,1,0:T(8,128)(2,1)} %bitcast.28, bf16[1,1152,128]{2,1,0:T(8,128)(2,1)} %collective-permute-done.low_ref, ...), custom_call_target="tpu_custom_call" | custom-call | flops 10000000 | bytes 2000000 | tf_op jit(solution)/shard_map/advect/pallas_call | solution.py:219
  33.2 1.3 collective-permute-start.2
  34.5 2.6 %collective-permute-start.3 = (bf16[1,144,512]{2,1,0:T(8,128)(2,1)}, bf16[1,144,512]{2,1,0:T(8,128)(2,1)S(1)}, u32[]{:S(2)}, u32[]{:S(2)}) collective-permute-start(bf16[1,144,512]{2,1,0:T(8,128)(2,1)} %get-tuple-element.41), channel_id=1, source_target_pairs={{0,2},{1,3},{2,0},{3,1},{4,6},{5,7},{6,4},{7,5},{8,10},{9,11},{10,... | collective-permute-start | bytes 442376 | tf_op jit(solution)/shard_map/ppermute | solution.py:489
  37.2 1.1 collective-permute-start.4
  38.2 0.1 broadcast_in_dim.7
  38.3 8.1 %tables.1 = (f32[2,5184,128]{2,1,0:T(8,128)S(1)}, bf16[512,768]{1,0:T(8,128)(2,1)S(1)}, bf16[256,512]{1,0:T(8,128)(2,1)S(1)}, f32[2,72,128]{2,1,0:T(8,128)S(1)}, f32[4,72,128]{2,1,0:T(8,128)S(1)}) custom-call(bf16[5184,512]{1,0:T(8,128)(2,1)} %bitcast.34, s32[1,512]{1,0:T(1,128)} %bitcast.48, s32[1,512]{1,0:T(1,128)} %bitcast.49, bf16[72,512]{1,0:T(8,128)(2,1)} %rain_ref.1, ...), custom_call_target="tpu_custom_call" | custom-call | flops 1358954496 | bytes 12000000 | tf_op jit(solution)/shard_map/tables/pallas_call | solution.py:295
  46.4 0.0 collective-permute-done.6.high_ref
  46.4 3.6 %advect.6 = (bf16[1,144,512]{2,1,0:T(8,128)(2,1)S(1)}, bf16[1,144,512]{2,1,0:T(8,128)(2,1)S(1)}, bf16[1,144,512]{2,1,0:T(8,128)(2,1)S(1)}, bf16[1,144,512]{2,1,0:T(8,128)(2,1)S(1)}) custom-call(s32[1]{0:T(128)} %bitcast.place_ref, bf16[64,18,16,128]{3,2,1,0:T(8,128)(2,1)} %bitcast.29, bf16[3,1152,128]{2,1,0:T(8,128)(2,1)S(1)} %collective-permute-done.5.low_ref, ...), custom_call_target="tpu_custom_call" | custom-call | flops 10000000 | bytes 2000000 | tf_op jit(solution)/shard_map/advect/pallas_call | solution.py:219
  50.1 0.0 collective-permute-done.2.part1_ref
  50.1 0.0 collective-permute-done.4.part3_ref
  50.1 0.1 broadcast_in_dim.8.rate_ref
  50.2 7.5 %physics.5.refs_0_.own_ref = bf16[576,512]{1,0:T(8,128)(2,1)} custom-call(s32[1]{0:T(128)} %bitcast.place_ref, bf16[1,144,512]{2,1,0:T(8,128)(2,1)S(1)} %get-tuple-element.39.refs_0_.part0_ref, bf16[1,144,512]{2,1,0:T(8,128)(2,1)S(1)} %collective-permute-done.2.part1_ref, bf16[1,144,512]{2,1,0:T(8,128)(2,1)S(1)} %collective-permute-done.3.part2_ref, ...), custom_call_target="tpu_custom_call" | custom-call | flops 1028653056 | bytes 7700000 | tf_op jit(solution)/shard_map/physics/pallas_call | solution.py:410
  57.7 3.7 %extract.5 = (bf16[4,1152,128]{2,1,0:T(8,128)(2,1)S(1)}, bf16[4,1152,128]{2,1,0:T(8,128)(2,1)S(1)}) custom-call(bf16[64,18,16,128]{3,2,1,0:T(8,128)(2,1)} %bitcast.30, bf16[18,16,128]{2,1,0:T(8,128)(2,1)} %bitcast.39, bf16[576,512]{1,0:T(8,128)(2,1)} %physics.5.refs_0_.own_ref), custom_call_target="tpu_custom_call" | custom-call | flops 4000000 | bytes 4800000 | tf_op jit(solution)/shard_map/extract/pallas_call | solution.py:101
  61.4 2.7 %collective-permute-start.7 = (bf16[4,1152,128]{2,1,0:T(8,128)(2,1)S(1)}, bf16[4,1152,128]{2,1,0:T(8,128)(2,1)S(1)}, u32[]{:S(2)}, u32[]{:S(2)}) collective-permute-start(bf16[4,1152,128]{2,1,0:T(8,128)(2,1)S(1)} %get-tuple-element.50.refs_0_), channel_id=1, source_target_pairs={{0,4},{4,8},{8,12},{12,16},{16,20},{20,24},{24,28},{28,32},{32,36}... | collective-permute-start | bytes 3538952 | tf_op jit(solution)/shard_map/ppermute | solution.py:484
  64.1 1.9 collective-permute-start.8
  66.0 0.5 collective-permute-start.12
  66.5 0.5 collective-permute-start.13
  67.0 2.0 collective-permute-start.14
  69.0 6.1 %advect.7 = (bf16[2,144,512]{2,1,0:T(8,128)(2,1)S(1)}, bf16[2,144,512]{2,1,0:T(8,128)(2,1)S(1)}, bf16[2,144,512]{2,1,0:T(8,128)(2,1)S(1)}, bf16[2,144,512]{2,1,0:T(8,128)(2,1)S(1)}) custom-call(s32[1]{0:T(128)} %bitcast.place_ref, bf16[64,18,16,128]{3,2,1,0:T(8,128)(2,1)} %bitcast.31, bf16[3,1152,128]{2,1,0:T(8,128)(2,1)S(1)} %collective-permute-done.5.low_ref, ...), custom_call_target="tpu_custom_call" | custom-call | flops 20000000 | bytes 4000000 | tf_op jit(solution)/shard_map/advect/pallas_call | solution.py:219
  75.1 0.8 collective-permute-done.12.part1_ref
  75.9 1.4 collective-permute-start.10
  77.3 0.6 collective-permute-start.11
  77.9 0.0 collective-permute-done.14.part3_ref
  77.9 0.9 collective-permute-start.9
  78.8 6.6 %physics.6.refs_0_.own_ref = bf16[576,512]{1,0:T(8,128)(2,1)} custom-call(s32[1]{0:T(128)} %bitcast.place_ref, bf16[1,144,512]{2,1,0:T(8,128)(2,1)S(1)} %get-tuple-element.49.refs_0_.part0_ref, bf16[1,144,512]{2,1,0:T(8,128)(2,1)S(1)} %collective-permute-done.12.part1_ref, bf16[1,144,512]{2,1,0:T(8,128)(2,1)S(1)} %collective-permute-done.13.part2_ref, ...), custom_call_target="tpu_custom_call" | custom-call | flops 1028653056 | bytes 7700000 | tf_op jit(solution)/shard_map/physics/pallas_call | solution.py:410
  85.4 6.1 %advect.8 = (bf16[2,144,512]{2,1,0:T(8,128)(2,1)S(1)}, bf16[2,144,512]{2,1,0:T(8,128)(2,1)S(1)}, bf16[2,144,512]{2,1,0:T(8,128)(2,1)S(1)}, bf16[2,144,512]{2,1,0:T(8,128)(2,1)S(1)}) custom-call(s32[1]{0:T(128)} %bitcast.place_ref, bf16[64,18,16,128]{3,2,1,0:T(8,128)(2,1)} %bitcast.32, bf16[4,1152,128]{2,1,0:T(8,128)(2,1)S(1)} %collective-permute-done.7.low_ref, ...), custom_call_target="tpu_custom_call" | custom-call | flops 20000000 | bytes 4000000 | tf_op jit(solution)/shard_map/advect/pallas_call | solution.py:219
  91.6 0.1 collective-permute-start.18
  91.7 3.0 %collective-permute-start.19 = (bf16[2,144,512]{2,1,0:T(8,128)(2,1)S(1)}, bf16[2,144,512]{2,1,0:T(8,128)(2,1)S(1)}, u32[]{:S(2)}, u32[]{:S(2)}) collective-permute-start(bf16[2,144,512]{2,1,0:T(8,128)(2,1)S(1)} %get-tuple-element.65), channel_id=1, source_target_pairs={{0,2},{1,3},{2,0},{3,1},{4,6},{5,7},{6,4},{7,5},{8,10},{9,11},{10,... | collective-permute-start | bytes 884744 | tf_op jit(solution)/shard_map/ppermute | solution.py:489
  94.7 0.6 collective-permute-start.20
  95.3 10.3 %physics.7.refs_0_.own_ref = bf16[1152,512]{1,0:T(8,128)(2,1)S(1)} custom-call(s32[1]{0:T(128)} %bitcast.place_ref, bf16[2,144,512]{2,1,0:T(8,128)(2,1)S(1)} %get-tuple-element.52.refs_0_.part0_ref, bf16[2,144,512]{2,1,0:T(8,128)(2,1)S(1)} %collective-permute-done.9.part1_ref, bf16[2,144,512]{2,1,0:T(8,128)(2,1)S(1)} %collective-permute-done.10.part2_ref, ...), custom_call_target="tpu_custom_call" | custom-call | flops 2057306112 | bytes 8900000 | tf_op jit(solution)/shard_map/physics/pallas_call | solution.py:410
  105.6 6.2 %advect.9 = (bf16[2,144,512]{2,1,0:T(8,128)(2,1)S(1)}, bf16[2,144,512]{2,1,0:T(8,128)(2,1)S(1)}, bf16[2,144,512]{2,1,0:T(8,128)(2,1)S(1)}, bf16[2,144,512]{2,1,0:T(8,128)(2,1)S(1)}) custom-call(s32[1]{0:T(128)} %bitcast.place_ref, bf16[64,18,16,128]{3,2,1,0:T(8,128)(2,1)} %bitcast.33, bf16[4,1152,128]{2,1,0:T(8,128)(2,1)S(1)} %collective-permute-done.7.low_ref, ...), custom_call_target="tpu_custom_call" | custom-call | flops 20000000 | bytes 4000000 | tf_op jit(solution)/shard_map/advect/pallas_call | solution.py:219
  111.8 0.9 collective-permute-start.15
  112.7 0.7 collective-permute-start.16
  113.4 0.0 collective-permute-done.18.part1_ref
  113.4 2.0 collective-permute-start.17
  115.3 2.5 %collective-permute-start.23 = (bf16[1152,512]{1,0:T(8,128)(2,1)S(1)}, bf16[1152,512]{1,0:T(8,128)(2,1)}, u32[]{:S(2)}, u32[]{:S(2)}) collective-permute-start(bf16[1152,512]{1,0:T(8,128)(2,1)S(1)} %physics.7.refs_0_.own_ref), channel_id=1, source_target_pairs={{0,64},{4,68},{8,72},{12,76},{16,80},{20,84},{24,88},{28,92},{32,9... | collective-permute-start | bytes 3538952 | tf_op jit(solution)/shard_map/ppermute | solution.py:494
  117.8 0.0 collective-permute-done.20.part3_ref
  117.8 10.3 %physics.8.refs_0_.own_ref = bf16[1152,512]{1,0:T(8,128)(2,1)S(1)} custom-call(s32[1]{0:T(128)} %bitcast.place_ref, bf16[2,144,512]{2,1,0:T(8,128)(2,1)S(1)} %get-tuple-element.59.refs_0_.part0_ref, bf16[2,144,512]{2,1,0:T(8,128)(2,1)S(1)} %collective-permute-done.18.part1_ref, bf16[2,144,512]{2,1,0:T(8,128)(2,1)S(1)} %collective-permute-done.19.part2_ref, ...), custom_call_target="tpu_custom_call" | custom-call | flops 2057306112 | bytes 8900000 | tf_op jit(solution)/shard_map/physics/pallas_call | solution.py:410
  128.1 0.0 copy-start.1
  128.1 0.8 collective-permute-start.22
  129.0 0.0 collective-permute-done.15.part1_ref
  129.0 0.0 collective-permute-done.16.part2_ref
  129.0 0.0 collective-permute-done.17.part3_ref
  129.0 10.3 %physics.9.refs_0_.refs_1_.own_ref = bf16[1152,512]{1,0:T(8,128)(2,1)S(1)} custom-call(s32[1]{0:T(128)} %bitcast.place_ref, bf16[2,144,512]{2,1,0:T(8,128)(2,1)S(1)} %get-tuple-element.60.refs_0_.part0_ref, bf16[2,144,512]{2,1,0:T(8,128)(2,1)S(1)} %collective-permute-done.15.part1_ref, bf16[2,144,512]{2,1,0:T(8,128)(2,1)S(1)} %collective-permute-done.16.part2_ref, ...), custom_call_target="tpu_custom_call" | custom-call | flops 2057306112 | bytes 8900000 | tf_op jit(solution)/shard_map/physics/pallas_call | solution.py:410
  139.3 2.5 %collective-permute-start.21 = (bf16[1152,512]{1,0:T(8,128)(2,1)S(1)}, bf16[1152,512]{1,0:T(8,128)(2,1)}, u32[]{:S(2)}, u32[]{:S(2)}) collective-permute-start(bf16[1152,512]{1,0:T(8,128)(2,1)S(1)} %physics.9.refs_0_.refs_1_.own_ref), channel_id=1, source_target_pairs={{0,64},{4,68},{8,72},{12,76},{16,80},{20,84},{24,88},{28,92},{32,9... | collective-permute-start | bytes 3538952 | tf_op jit(solution)/shard_map/ppermute | solution.py:494
  141.8 0.5 collective-permute-start.25
  142.3 2.5 %collective-permute-start.24 = (bf16[576,512]{1,0:T(8,128)(2,1)}, bf16[576,512]{1,0:T(8,128)(2,1)}, u32[]{:S(2)}, u32[]{:S(2)}) collective-permute-start(bf16[576,512]{1,0:T(8,128)(2,1)} %physics.6.refs_0_.own_ref), channel_id=1, source_target_pairs={{0,64},{4,68},{8,72},{12,76},{16,80},{20,84},{24,88},{28,92},{32,9... | collective-permute-start | bytes 1769480 | tf_op jit(solution)/shard_map/ppermute | solution.py:494
  144.8 0.6 dynamic_slice.3.flag_ref
  145.4 59.0 %collective-permute-done.25.partner_ref = bf16[576,512]{1,0:T(8,128)(2,1)} collective-permute-done((bf16[576,512]{1,0:T(8,128)(2,1)}, bf16[576,512]{1,0:T(8,128)(2,1)}, u32[]{:S(2)}, u32[]{:S(2)}) %collective-permute-start.25) | collective-permute-done | bytes 589856 | tf_op jit(solution)/shard_map/ppermute | solution.py:494
  204.4 2.5 %choose.5.refs_0_ = bf16[4608,512]{1,0:T(8,128)(2,1)} custom-call(s32[1]{0:T(128)} %dynamic_slice.3.flag_ref, bf16[576,512]{1,0:T(8,128)(2,1)} %physics.5.refs_0_.own_ref, bf16[576,512]{1,0:T(8,128)(2,1)} %collective-permute-done.25.partner_ref, bf16[1152,512]{1,0:T(8,128)(2,1)S(1)} %physics.9.refs_0_.refs_1_.own_ref), custom_call_target="tpu_custom_call" | custom-call | bytes 1200000 | tf_op jit(solution)/shard_map/choose/pallas_call | solution.py:463
  207.0 10.1 %collective-permute-done.24.partner_ref = bf16[576,512]{1,0:T(8,128)(2,1)} collective-permute-done((bf16[576,512]{1,0:T(8,128)(2,1)}, bf16[576,512]{1,0:T(8,128)(2,1)}, u32[]{:S(2)}, u32[]{:S(2)}) %collective-permute-start.24) | collective-permute-done | bytes 589856 | tf_op jit(solution)/shard_map/ppermute | solution.py:494
  217.1 2.5 %choose.6.refs_0_ = bf16[4608,512]{1,0:T(8,128)(2,1)} custom-call(s32[1]{0:T(128)} %dynamic_slice.3.flag_ref, bf16[576,512]{1,0:T(8,128)(2,1)} %physics.6.refs_0_.own_ref, bf16[576,512]{1,0:T(8,128)(2,1)} %collective-permute-done.24.partner_ref, bf16[4608,512]{1,0:T(8,128)(2,1)} %choose.5.refs_0_, ...), custom_call_target="tpu_custom_call", output_to_operand_aliasing={{}: (3, {})} | custom-call | bytes 1200000 | tf_op jit(solution)/shard_map/choose/pallas_call | solution.py:463
  219.6 0.0 collective-permute-done.23.partner_ref
  219.6 4.1 %choose.7.refs_0_ = bf16[4608,512]{1,0:T(8,128)(2,1)} custom-call(s32[1]{0:T(128)} %dynamic_slice.3.flag_ref, bf16[1152,512]{1,0:T(8,128)(2,1)S(1)} %physics.7.refs_0_.own_ref, bf16[1152,512]{1,0:T(8,128)(2,1)} %collective-permute-done.23.partner_ref, bf16[4608,512]{1,0:T(8,128)(2,1)} %choose.6.refs_0_, ...), custom_call_target="tpu_custom_call", output_to_operand_aliasing={{}: (3, {})} | custom-call | bytes 2400000 | tf_op jit(solution)/shard_map/choose/pallas_call | solution.py:463
  223.7 4.1 %choose.8.refs_0_ = bf16[4608,512]{1,0:T(8,128)(2,1)} custom-call(s32[1]{0:T(128)} %dynamic_slice.3.flag_ref, bf16[1152,512]{1,0:T(8,128)(2,1)S(1)} %physics.8.refs_0_.own_ref, bf16[1152,512]{1,0:T(8,128)(2,1)} %collective-permute-done.22.partner_ref, bf16[4608,512]{1,0:T(8,128)(2,1)} %choose.7.refs_0_, ...), custom_call_target="tpu_custom_call", output_to_operand_aliasing={{}: (3, {})} | custom-call | bytes 2400000 | tf_op jit(solution)/shard_map/choose/pallas_call | solution.py:463
  227.7 4.1 %choose.9 = bf16[4608,512]{1,0:T(8,128)(2,1)} custom-call(s32[1]{0:T(128)} %dynamic_slice.3.flag_ref, bf16[1152,512]{1,0:T(8,128)(2,1)S(1)} %physics.9.refs_0_.refs_1_.own_ref, bf16[1152,512]{1,0:T(8,128)(2,1)} %collective-permute-done.21.partner_ref, bf16[4608,512]{1,0:T(8,128)(2,1)} %choose.8.refs_0_, ...), custom_call_target="tpu_custom_call", output_to_operand_aliasing={{}: (3, {})} | custom-call | bytes 2400000 | tf_op jit(solution)/shard_map/choose/pallas_call | solution.py:463
  (14 shorter events, 0.0 us)
Async XLA Ops:
  6.2 40.2 %collective-permute-start.5 = (bf16[3,1152,128]{2,1,0:T(8,128)(2,1)S(1)}, bf16[3,1152,128]{2,1,0:T(8,128)(2,1)S(1)}, u32[]{:S(2)}, u32[]{:S(2)}) collective-permute-start(bf16[3,1152,128]{2,1,0:T(8,128)(2,1)S(1)} %get-tuple-element.38.refs_0_), channel_id=1, source_target_pairs={{0,4},{4,8},{8,12},{12,16},{16,20},{20,24},{24,28},{28,32},{32,36}... | collective-permute-start | bytes 2654216 | tf_op jit(solution)/shard_map/ppermute | solution.py:484
  8.5 37.9 %collective-permute-start.6 = (bf16[3,1152,128]{2,1,0:T(8,128)(2,1)}, bf16[3,1152,128]{2,1,0:T(8,128)(2,1)S(1)}, u32[]{:S(2)}, u32[]{:S(2)}) collective-permute-start(bf16[3,1152,128]{2,1,0:T(8,128)(2,1)} %get-tuple-element.48), channel_id=1, source_target_pairs={{4,0},{8,4},{12,8},{16,12},{20,16},{24,20},{28,24},{32,28},{36,32}... | collective-permute-start | bytes 2654216 | tf_op jit(solution)/shard_map/ppermute | solution.py:484
  10.7 18.0 %collective-permute-start.1 = (bf16[1,1296,128]{2,1,0:T(8,128)(2,1)}, bf16[1,1296,128]{2,1,0:T(8,128)(2,1)S(1)}, u32[]{:S(2)}, u32[]{:S(2)}) collective-permute-start(bf16[1,1296,128]{2,1,0:T(8,128)(2,1)} %get-tuple-element.37), channel_id=1, source_target_pairs={{4,0},{8,4},{12,8},{16,12},{20,16},{24,20},{28,24},{32,28},{36,32}... | collective-permute-start | bytes 995336 | tf_op jit(solution)/shard_map/ppermute | solution.py:484
  14.4 7.7 %collective-permute-start = (bf16[1,1152,128]{2,1,0:T(8,128)(2,1)S(1)}, bf16[1,1152,128]{2,1,0:T(8,128)(2,1)}, u32[]{:S(2)}, u32[]{:S(2)}) collective-permute-start(bf16[1,1152,128]{2,1,0:T(8,128)(2,1)S(1)} %get-tuple-element.36.refs_0_), channel_id=1, source_target_pairs={{0,4},{4,8},{8,12},{12,16},{16,20},{20,24},{24,28},{28,32},{32,36}... | collective-permute-start | bytes 884744 | tf_op jit(solution)/shard_map/ppermute | solution.py:484
  28.8 9.5 %copy-start = (f32[64]{0:T(128)S(1)}, f32[64]{0:T(128)}, u32[]{:S(2)}) copy-start(f32[64]{0:T(128)} %param.16) | copy-start | bytes 772
  33.2 16.8 %collective-permute-start.2 = (bf16[1,144,512]{2,1,0:T(8,128)(2,1)}, bf16[1,144,512]{2,1,0:T(8,128)(2,1)S(1)}, u32[]{:S(2)}, u32[]{:S(2)}) collective-permute-start(bf16[1,144,512]{2,1,0:T(8,128)(2,1)} %get-tuple-element.40), channel_id=1, source_target_pairs={{0,1},{1,2},{2,3},{3,0},{4,5},{5,6},{6,7},{7,4},{8,9},{9,10},{10,1... | collective-permute-start | bytes 442376 | tf_op jit(solution)/shard_map/ppermute | solution.py:489
  34.5 15.5 %collective-permute-start.3 = (bf16[1,144,512]{2,1,0:T(8,128)(2,1)}, bf16[1,144,512]{2,1,0:T(8,128)(2,1)S(1)}, u32[]{:S(2)}, u32[]{:S(2)}) collective-permute-start(bf16[1,144,512]{2,1,0:T(8,128)(2,1)} %get-tuple-element.41), channel_id=1, source_target_pairs={{0,2},{1,3},{2,0},{3,1},{4,6},{5,7},{6,4},{7,5},{8,10},{9,11},{10,... | collective-permute-start | bytes 442376 | tf_op jit(solution)/shard_map/ppermute | solution.py:489
  37.2 12.9 %collective-permute-start.4 = (bf16[1,144,512]{2,1,0:T(8,128)(2,1)}, bf16[1,144,512]{2,1,0:T(8,128)(2,1)}, u32[]{:S(2)}, u32[]{:S(2)}) collective-permute-start(bf16[1,144,512]{2,1,0:T(8,128)(2,1)} %get-tuple-element.42), channel_id=1, source_target_pairs={{0,3},{1,0},{2,1},{3,2},{4,7},{5,4},{6,5},{7,6},{8,11},{9,8},{10,9... | collective-permute-start | bytes 442376 | tf_op jit(solution)/shard_map/ppermute | solution.py:489
  61.4 24.1 %collective-permute-start.7 = (bf16[4,1152,128]{2,1,0:T(8,128)(2,1)S(1)}, bf16[4,1152,128]{2,1,0:T(8,128)(2,1)S(1)}, u32[]{:S(2)}, u32[]{:S(2)}) collective-permute-start(bf16[4,1152,128]{2,1,0:T(8,128)(2,1)S(1)} %get-tuple-element.50.refs_0_), channel_id=1, source_target_pairs={{0,4},{4,8},{8,12},{12,16},{16,20},{20,24},{24,28},{28,32},{32,36}... | collective-permute-start | bytes 3538952 | tf_op jit(solution)/shard_map/ppermute | solution.py:484
  64.1 21.4 %collective-permute-start.8 = (bf16[4,1152,128]{2,1,0:T(8,128)(2,1)S(1)}, bf16[4,1152,128]{2,1,0:T(8,128)(2,1)S(1)}, u32[]{:S(2)}, u32[]{:S(2)}) collective-permute-start(bf16[4,1152,128]{2,1,0:T(8,128)(2,1)S(1)} %get-tuple-element.51), channel_id=1, source_target_pairs={{4,0},{8,4},{12,8},{16,12},{20,16},{24,20},{28,24},{32,28},{36,32}... | collective-permute-start | bytes 3538952 | tf_op jit(solution)/shard_map/ppermute | solution.py:484
  66.0 9.9 %collective-permute-start.12 = (bf16[1,144,512]{2,1,0:T(8,128)(2,1)S(1)}, bf16[1,144,512]{2,1,0:T(8,128)(2,1)S(1)}, u32[]{:S(2)}, u32[]{:S(2)}) collective-permute-start(bf16[1,144,512]{2,1,0:T(8,128)(2,1)S(1)} %get-tuple-element.56), channel_id=1, source_target_pairs={{0,1},{1,2},{2,3},{3,0},{4,5},{5,6},{6,7},{7,4},{8,9},{9,10},{10,1... | collective-permute-start | bytes 442376 | tf_op jit(solution)/shard_map/ppermute | solution.py:489
  66.5 10.9 %collective-permute-start.13 = (bf16[1,144,512]{2,1,0:T(8,128)(2,1)S(1)}, bf16[1,144,512]{2,1,0:T(8,128)(2,1)S(1)}, u32[]{:S(2)}, u32[]{:S(2)}) collective-permute-start(bf16[1,144,512]{2,1,0:T(8,128)(2,1)S(1)} %get-tuple-element.57), channel_id=1, source_target_pairs={{0,2},{1,3},{2,0},{3,1},{4,6},{5,7},{6,4},{7,5},{8,10},{9,11},{10,... | collective-permute-start | bytes 442376 | tf_op jit(solution)/shard_map/ppermute | solution.py:489
  67.0 11.0 %collective-permute-start.14 = (bf16[1,144,512]{2,1,0:T(8,128)(2,1)S(1)}, bf16[1,144,512]{2,1,0:T(8,128)(2,1)S(1)}, u32[]{:S(2)}, u32[]{:S(2)}) collective-permute-start(bf16[1,144,512]{2,1,0:T(8,128)(2,1)S(1)} %get-tuple-element.58), channel_id=1, source_target_pairs={{0,3},{1,0},{2,1},{3,2},{4,7},{5,4},{6,5},{7,6},{8,11},{9,8},{10,9... | collective-permute-start | bytes 442376 | tf_op jit(solution)/shard_map/ppermute | solution.py:489
  75.9 18.7 %collective-permute-start.10 = (bf16[2,144,512]{2,1,0:T(8,128)(2,1)S(1)}, bf16[2,144,512]{2,1,0:T(8,128)(2,1)S(1)}, u32[]{:S(2)}, u32[]{:S(2)}) collective-permute-start(bf16[2,144,512]{2,1,0:T(8,128)(2,1)S(1)} %get-tuple-element.54), channel_id=1, source_target_pairs={{0,2},{1,3},{2,0},{3,1},{4,6},{5,7},{6,4},{7,5},{8,10},{9,11},{10,... | collective-permute-start | bytes 884744 | tf_op jit(solution)/shard_map/ppermute | solution.py:489
  77.3 18.0 %collective-permute-start.11 = (bf16[2,144,512]{2,1,0:T(8,128)(2,1)S(1)}, bf16[2,144,512]{2,1,0:T(8,128)(2,1)S(1)}, u32[]{:S(2)}, u32[]{:S(2)}) collective-permute-start(bf16[2,144,512]{2,1,0:T(8,128)(2,1)S(1)} %get-tuple-element.55), channel_id=1, source_target_pairs={{0,3},{1,0},{2,1},{3,2},{4,7},{5,4},{6,5},{7,6},{8,11},{9,8},{10,9... | collective-permute-start | bytes 884744 | tf_op jit(solution)/shard_map/ppermute | solution.py:489
  77.9 17.4 %collective-permute-start.9 = (bf16[2,144,512]{2,1,0:T(8,128)(2,1)S(1)}, bf16[2,144,512]{2,1,0:T(8,128)(2,1)S(1)}, u32[]{:S(2)}, u32[]{:S(2)}) collective-permute-start(bf16[2,144,512]{2,1,0:T(8,128)(2,1)S(1)} %get-tuple-element.53), channel_id=1, source_target_pairs={{0,1},{1,2},{2,3},{3,0},{4,5},{5,6},{6,7},{7,4},{8,9},{9,10},{10,1... | collective-permute-start | bytes 884744 | tf_op jit(solution)/shard_map/ppermute | solution.py:489
  91.6 21.8 %collective-permute-start.18 = (bf16[2,144,512]{2,1,0:T(8,128)(2,1)S(1)}, bf16[2,144,512]{2,1,0:T(8,128)(2,1)S(1)}, u32[]{:S(2)}, u32[]{:S(2)}) collective-permute-start(bf16[2,144,512]{2,1,0:T(8,128)(2,1)S(1)} %get-tuple-element.64), channel_id=1, source_target_pairs={{0,1},{1,2},{2,3},{3,0},{4,5},{5,6},{6,7},{7,4},{8,9},{9,10},{10,1... | collective-permute-start | bytes 884744 | tf_op jit(solution)/shard_map/ppermute | solution.py:489
  91.7 23.7 %collective-permute-start.19 = (bf16[2,144,512]{2,1,0:T(8,128)(2,1)S(1)}, bf16[2,144,512]{2,1,0:T(8,128)(2,1)S(1)}, u32[]{:S(2)}, u32[]{:S(2)}) collective-permute-start(bf16[2,144,512]{2,1,0:T(8,128)(2,1)S(1)} %get-tuple-element.65), channel_id=1, source_target_pairs={{0,2},{1,3},{2,0},{3,1},{4,6},{5,7},{6,4},{7,5},{8,10},{9,11},{10,... | collective-permute-start | bytes 884744 | tf_op jit(solution)/shard_map/ppermute | solution.py:489
  94.7 23.1 %collective-permute-start.20 = (bf16[2,144,512]{2,1,0:T(8,128)(2,1)S(1)}, bf16[2,144,512]{2,1,0:T(8,128)(2,1)S(1)}, u32[]{:S(2)}, u32[]{:S(2)}) collective-permute-start(bf16[2,144,512]{2,1,0:T(8,128)(2,1)S(1)} %get-tuple-element.66), channel_id=1, source_target_pairs={{0,3},{1,0},{2,1},{3,2},{4,7},{5,4},{6,5},{7,6},{8,11},{9,8},{10,9... | collective-permute-start | bytes 884744 | tf_op jit(solution)/shard_map/ppermute | solution.py:489
  111.8 17.2 %collective-permute-start.15 = (bf16[2,144,512]{2,1,0:T(8,128)(2,1)S(1)}, bf16[2,144,512]{2,1,0:T(8,128)(2,1)S(1)}, u32[]{:S(2)}, u32[]{:S(2)}) collective-permute-start(bf16[2,144,512]{2,1,0:T(8,128)(2,1)S(1)} %get-tuple-element.61), channel_id=1, source_target_pairs={{0,1},{1,2},{2,3},{3,0},{4,5},{5,6},{6,7},{7,4},{8,9},{9,10},{10,1... | collective-permute-start | bytes 884744 | tf_op jit(solution)/shard_map/ppermute | solution.py:489
  112.7 16.3 %collective-permute-start.16 = (bf16[2,144,512]{2,1,0:T(8,128)(2,1)S(1)}, bf16[2,144,512]{2,1,0:T(8,128)(2,1)S(1)}, u32[]{:S(2)}, u32[]{:S(2)}) collective-permute-start(bf16[2,144,512]{2,1,0:T(8,128)(2,1)S(1)} %get-tuple-element.62), channel_id=1, source_target_pairs={{0,2},{1,3},{2,0},{3,1},{4,6},{5,7},{6,4},{7,5},{8,10},{9,11},{10,... | collective-permute-start | bytes 884744 | tf_op jit(solution)/shard_map/ppermute | solution.py:489
  113.4 15.6 %collective-permute-start.17 = (bf16[2,144,512]{2,1,0:T(8,128)(2,1)S(1)}, bf16[2,144,512]{2,1,0:T(8,128)(2,1)S(1)}, u32[]{:S(2)}, u32[]{:S(2)}) collective-permute-start(bf16[2,144,512]{2,1,0:T(8,128)(2,1)S(1)} %get-tuple-element.63), channel_id=1, source_target_pairs={{0,3},{1,0},{2,1},{3,2},{4,7},{5,4},{6,5},{7,6},{8,11},{9,8},{10,9... | collective-permute-start | bytes 884744 | tf_op jit(solution)/shard_map/ppermute | solution.py:489
  115.3 104.3 %collective-permute-start.23 = (bf16[1152,512]{1,0:T(8,128)(2,1)S(1)}, bf16[1152,512]{1,0:T(8,128)(2,1)}, u32[]{:S(2)}, u32[]{:S(2)}) collective-permute-start(bf16[1152,512]{1,0:T(8,128)(2,1)S(1)} %physics.7.refs_0_.own_ref), channel_id=1, source_target_pairs={{0,64},{4,68},{8,72},{12,76},{16,80},{20,84},{24,88},{28,92},{32,9... | collective-permute-start | bytes 3538952 | tf_op jit(solution)/shard_map/ppermute | solution.py:494
  128.1 16.7 %copy-start.1 = (s32[64]{0:T(128)S(1)}, s32[64]{0:T(128)}, u32[]{:S(2)}) copy-start(s32[64]{0:T(128)} %param.17) | copy-start | bytes 772
  128.1 95.5 %collective-permute-start.22 = (bf16[1152,512]{1,0:T(8,128)(2,1)S(1)}, bf16[1152,512]{1,0:T(8,128)(2,1)}, u32[]{:S(2)}, u32[]{:S(2)}) collective-permute-start(bf16[1152,512]{1,0:T(8,128)(2,1)S(1)} %physics.8.refs_0_.own_ref), channel_id=1, source_target_pairs={{0,64},{4,68},{8,72},{12,76},{16,80},{20,84},{24,88},{28,92},{32,9... | collective-permute-start | bytes 3538952 | tf_op jit(solution)/shard_map/ppermute | solution.py:494
  139.3 88.5 %collective-permute-start.21 = (bf16[1152,512]{1,0:T(8,128)(2,1)S(1)}, bf16[1152,512]{1,0:T(8,128)(2,1)}, u32[]{:S(2)}, u32[]{:S(2)}) collective-permute-start(bf16[1152,512]{1,0:T(8,128)(2,1)S(1)} %physics.9.refs_0_.refs_1_.own_ref), channel_id=1, source_target_pairs={{0,64},{4,68},{8,72},{12,76},{16,80},{20,84},{24,88},{28,92},{32,9... | collective-permute-start | bytes 3538952 | tf_op jit(solution)/shard_map/ppermute | solution.py:494
  141.8 62.6 %collective-permute-start.25 = (bf16[576,512]{1,0:T(8,128)(2,1)}, bf16[576,512]{1,0:T(8,128)(2,1)}, u32[]{:S(2)}, u32[]{:S(2)}) collective-permute-start(bf16[576,512]{1,0:T(8,128)(2,1)} %physics.5.refs_0_.own_ref), channel_id=1, source_target_pairs={{0,64},{4,68},{8,72},{12,76},{16,80},{20,84},{24,88},{28,92},{32,9... | collective-permute-start | bytes 1769480 | tf_op jit(solution)/shard_map/ppermute | solution.py:494
  142.3 74.7 %collective-permute-start.24 = (bf16[576,512]{1,0:T(8,128)(2,1)}, bf16[576,512]{1,0:T(8,128)(2,1)}, u32[]{:S(2)}, u32[]{:S(2)}) collective-permute-start(bf16[576,512]{1,0:T(8,128)(2,1)} %physics.6.refs_0_.own_ref), channel_id=1, source_target_pairs={{0,64},{4,68},{8,72},{12,76},{16,80},{20,84},{24,88},{28,92},{32,9... | collective-permute-start | bytes 1769480 | tf_op jit(solution)/shard_map/ppermute | solution.py:494

commit v4 on v2

--- a/solution.py
+++ b/solution.py
@@ -1,3 +1,4 @@
+import functools
 import itertools
 
 import jax
@@ -8,8 +9,9 @@
 from jax.experimental.pallas import tpu as pltpu
 from jax.sharding import PartitionSpec as P
 
+
 GROUP = 8
-CHUNKS = (1, 1, 2, 2, 2)
+CHUNKS = (1, 1, 2, 2, 1, 1)
 SPANS = ((0, 1), (1, 3), (4, 4))
 ORDER = (
     ("extract", 0),
@@ -23,14 +25,17 @@
     ("physics", 1),
     ("advect", 3),
     ("physics", 2),
-    ("choose", 0),
     ("advect", 4),
     ("physics", 3),
+    ("advect", 5),
+    ("physics", 4),
+    ("physics", 5),
+    ("choose", 0),
     ("choose", 1),
-    ("physics", 4),
     ("choose", 2),
     ("choose", 3),
     ("choose", 4),
+    ("choose", 5),
 )
 CAP = 256
 K_BLOCK = 8
@@ -68,24 +73,28 @@
 
 
 def two_levels(q_ref, pair):
-    return q_ref[:, pl.ds(2 * pair, 2)].reshape(2 * GROUP * 16, 128)
+    return q_ref[:, 2 * pair : 2 * pair + 2].reshape(2 * GROUP * 16, 128)
+
+
+def moved_rows(move, blocks):
+    moved = []
+    for at in range(0, len(blocks), 2):
+        some = blocks[at : at + 2]
+        both = product(move, jnp.concatenate(some, axis=1))
+        moved += [both[:, i * 128 : (i + 1) * 128] for i in range(len(some))]
+    return moved
 
 
 def extract_kernel(apart_ref, face_move_ref, q_ref, lat_ref, *refs):
     north_ref, south_ref = refs[-2:]
     levels = q_ref.shape[1]
     rows = levels * GROUP * 8
-
-    def body(pair, carry):
-        apart = product(apart_ref[...], two_levels(q_ref, pair)).astype(BF16)
-        spot = pl.multiple_of(pair * 128, 128)
-        south_ref[0, pl.ds(spot, 64), :] = apart[0:64]
-        north_ref[0, pl.ds(spot, 64), :] = apart[64:128]
-        south_ref[0, pl.ds(spot + 64, 64), :] = apart[128:192]
-        north_ref[0, pl.ds(spot + 64, 64), :] = apart[192:256]
-        return carry
-
-    lax.fori_loop(0, levels // 2, body, 0)
+    blocks = [two_levels(q_ref, pair) for pair in range(levels // 2)]
+    for pair, apart in enumerate(moved_rows(apart_ref[...], blocks)):
+        for k in range(2):
+            spot = pair * 128 + k * 64
+            south_ref[0, spot : spot + 64, :] = apart[k * 128 : k * 128 + 64].astype(BF16)
+            north_ref[0, spot : spot + 64, :] = apart[k * 128 + 64 : k * 128 + 128].astype(BF16)
     if south_ref.shape[1] > rows:
         faces = lat_ref[...].reshape(levels * 16, 128)
         south_ref[0, rows:, :] = product(face_move_ref[: levels * 8], faces).astype(BF16)
@@ -137,56 +146,57 @@
     place_ref, apart_ref, group_ref, face_move_ref, q_ref, low_ref, high_ref, lat_ref, lon_ref,
     above_ref, *refs
 ):
-    outs, faces = refs[-5:-1], refs[-1]
+    outs = refs[-7:-3]
+    faces, apart, made = refs[-3:]
     levels = q_ref.shape[1]
     lane = lax.broadcasted_iota(jnp.int32, (8, 128), 1)
 
     @pl.when(pl.program_id(0) == 0)
     def _():
-        for at, ref in ((0, lat_ref), (2, lon_ref)):
-            both = product(face_move_ref[...], ref[...].reshape(levels * 16, 128))
-            faces[at] = both[: levels * 8]
-            faces[at + 1] = both[levels * 8 :]
+        blocks = [ref[...].reshape(levels * 16, 128) for ref in (lat_ref, lon_ref)]
+        for at, both in enumerate(moved_rows(face_move_ref[...], blocks)):
+            faces[2 * at] = both[: levels * 8]
+            faces[2 * at + 1] = both[levels * 8 :]
         faces[4] = above_ref[0].astype(F32)
 
-    def body(pair, carry):
-        apart = product(apart_ref[...], two_levels(q_ref, pair))
-        spot = pl.multiple_of(pair * 128, 128)
-        low = low_ref[0, pl.ds(spot, 128), :].astype(F32)
-        high = high_ref[0, pl.ds(spot, 128), :].astype(F32)
-        results = []
-        for k in range(2):
-            at = pl.ds(pl.multiple_of((2 * pair + k) * 8, 8), 8)
-            edge = [faces[0, at, :], faces[1, at, :], faces[4, at, :]]
-            terms = []
-            for lat in range(2):
-                south, north, west = edge[lat], edge[lat + 1], faces[2 + lat, at, :]
-                east = beside(west, lane, True)
-                own = (
-                    1.0
-                    - (jnp.maximum(north, 0.0) - jnp.minimum(south, 0.0))
-                    - (jnp.maximum(east, 0.0) - jnp.minimum(west, 0.0))
+    blocks = [two_levels(q_ref, pair) for pair in range(levels // 2)]
+    for pair, rows in enumerate(moved_rows(apart_ref[...], blocks)):
+        apart[2 * pair] = rows[:128]
+        apart[2 * pair + 1] = rows[128:]
+
+    def body(k, carry):
+        at = pl.ds(pl.multiple_of(k * 8, 8), 8)
+        edge = [faces[0, at, :], faces[1, at, :], faces[4, at, :]]
+        terms = []
+        for lat in range(2):
+            south, north, west = edge[lat], edge[lat + 1], faces[2 + lat, at, :]
+            east = beside(west, lane, True)
+            own = (
+                1.0
+                - (jnp.maximum(north, 0.0) - jnp.minimum(south, 0.0))
+                - (jnp.maximum(east, 0.0) - jnp.minimum(west, 0.0))
+            )
+            terms.append(
+                (
+                    own,
+                    jnp.maximum(south, 0.0),
+                    -jnp.minimum(north, 0.0),
+                    jnp.maximum(west, 0.0),
+                    -jnp.minimum(east, 0.0),
                 )
-                terms.append(
-                    (
-                        own,
-                        jnp.maximum(south, 0.0),
-                        -jnp.minimum(north, 0.0),
-                        jnp.maximum(west, 0.0),
-                        -jnp.minimum(east, 0.0),
-                    )
-                )
-            made = [[], []]
-            for t in range(GROUP):
-                rows = [
-                    apart[(k * 2 + lat) * 64 + t * 8 : (k * 2 + lat) * 64 + t * 8 + 8]
-                    for lat in range(2)
-                ]
-                outer = [x[k * 64 + t * 8 : k * 64 + t * 8 + 8] for x in (low, high)]
-                column = [outer[0], rows[0], rows[1], outer[1]]
+            )
+        for t in range(0, GROUP, 2):
+            spot = pl.multiple_of(k * 64 + t * 8, 16)
+            outer = [ref[0, pl.ds(spot, 16), :].astype(F32) for ref in (low_ref, high_ref)]
+            results = [[], []]
+            for part in range(2):
+                row = (t + part) * 8
+                rows = [apart[k, lat * 64 + row : lat * 64 + row + 8, :] for lat in range(2)]
+                beyond = [x[part * 8 : part * 8 + 8] for x in outer]
+                column = [beyond[0], *rows, beyond[1]]
                 for lat in range(2):
                     own, from_s, from_n, from_w, from_e = terms[lat]
-                    made[lat].append(
+                    results[lat].append(
                         own * rows[lat]
                         + (from_s * column[lat] + from_n * column[lat + 2])
                         + (
@@ -194,16 +204,19 @@
                             + from_e * beside(rows[lat], lane, True)
                         )
                     )
-            results += made[0] + made[1]
-        sent = product(group_ref[0], jnp.concatenate(results, axis=0).astype(BF16)).astype(BF16)
-        spot = pl.multiple_of(pair * 16, 16)
+            for lat in range(2):
+                row = lat * 64 + t * 8
+                made[k, row : row + 16, :] = jnp.concatenate(results[lat], axis=0).astype(BF16)
+        return carry
+
+    lax.fori_loop(0, levels, body, 0)
+    blocks = [made[2 * pair : 2 * pair + 2].reshape(256, 128) for pair in range(levels // 2)]
+    for pair, sent in enumerate(moved_rows(group_ref[0], blocks)):
         for shift, out in enumerate(outs):
             for quarter in range(4):
                 row = (shift * 4 + quarter) * 16
-                out[0, pl.ds(spot, 16), quarter * 128 : (quarter + 1) * 128] = sent[row : row + 16]
-        return carry
-
-    lax.fori_loop(0, levels // 2, body, 0)
+                lanes = slice(quarter * 128, (quarter + 1) * 128)
+                out[0, pair * 16 : pair * 16 + 16, lanes] = sent[row : row + 16].astype(BF16)
 
 
 def advect(
@@ -230,7 +243,11 @@
             ]
             + [pl.BlockSpec(memory_space=pl.ANY)] * len(after),
             out_specs=[pl.BlockSpec((1, rows, 512), lambda g, p: (g, 0, 0))] * 4,
-            scratch_shapes=[pltpu.VMEM((5, levels * 8, 128), F32)],
+            scratch_shapes=[
+                pltpu.VMEM((5, levels * 8, 128), F32),
+                pltpu.VMEM((levels, 128, 128), F32),
+                pltpu.VMEM((levels, 128, 128), BF16),
+            ],
         ),
         out_shape=[jax.ShapeDtypeStruct((groups, rows, 512), BF16)] * 4,
         cost_estimate=pl.CostEstimate(
@@ -242,71 +259,73 @@
 
 
 def table_kernel(matrix_ref, mask_ref, order_ref, rain_ref, *refs):
-    small_ref, placing_ref, back_ref, wet_ref, all_ref = refs[-5:]
+    small_ref, placing_ref, back_ref, wet_ref, all_ref, held, sems = refs[-7:]
     columns = mask_ref.shape[1]
-
-    @pl.when(pl.program_id(0) == 0)
-    def _():
-        mask = mask_ref[...]
-        order = order_ref[...]
-        row = lax.broadcasted_iota(jnp.int32, (columns, columns), 0)
-        column = lax.broadcasted_iota(jnp.int32, (columns, columns), 1)
-        earlier = jnp.where(row < column, 1.0, 0.0).astype(BF16)
-        ones = jnp.where(mask > 0, 1.0, 0.0)
-        wide = jnp.broadcast_to(ones, (8, columns)).astype(BF16)
-        rank = jnp.dot(wide, earlier, preferred_element_type=F32)[0:1]
-        rank = jnp.where(mask > 0, rank, -1.0).astype(jnp.int32)
-        slot = lax.broadcasted_iota(jnp.int32, (CAP, columns), 0)
-        back = jnp.where(slot == rank, 1.0, 0.0).astype(BF16)
-        back_ref[...] = back
-        whole = jnp.where(row == order, 1.0, 0.0)
-        placing_ref[:, :columns] = jnp.where(mask > 0, 0.0, whole).astype(BF16)
-        placing_ref[:, columns:] = lax.dot_general(
-            whole.astype(BF16), back, (((1,), (1,)), ((), ())), preferred_element_type=F32
-        ).astype(BF16)
-        wet = lax.dot_general(
-            rain_ref[...], back, (((1,), (1,)), ((), ())), preferred_element_type=F32
-        )
+    pieces, rows = held.shape[:2]
+    copies = [
+        pltpu.make_async_copy(matrix_ref.at[pl.ds(i * rows, rows)], held.at[i], sems.at[i])
+        for i in range(pieces)
+    ]
+    for copy in copies:
+        copy.start()
+
+    mask = mask_ref[...]
+    order = order_ref[...]
+    row = lax.broadcasted_iota(jnp.int32, (columns, columns), 0)
+    column = lax.broadcasted_iota(jnp.int32, (columns, columns), 1)
+    earlier = jnp.where(row < column, 1.0, 0.0).astype(BF16)
+    ones = jnp.where(mask > 0, 1.0, 0.0)
+    wide = jnp.broadcast_to(ones, (8, columns)).astype(BF16)
+    rank = product(wide, earlier)[0:1]
+    rank = jnp.where(mask > 0, rank, -1.0).astype(jnp.int32)
+    slot = lax.broadcasted_iota(jnp.int32, (CAP, columns), 0)
+    back = jnp.where(slot == rank, 1.0, 0.0).astype(BF16)
+    back_ref[...] = back
+    whole = jnp.where(row == order, 1.0, 0.0)
+    placing_ref[:, :columns] = jnp.where(mask > 0, 0.0, whole).astype(BF16)
+    placing_ref[:, columns:] = crossed(whole.astype(BF16), back).astype(BF16)
+    wet = crossed(rain_ref[...], back)
+    for tile in range(CAP // 128):
+        wet_ref[tile] = wet[:, tile * 128 : (tile + 1) * 128]
+    for tile in range(columns // 128):
+        all_ref[tile] = rain_ref[:, tile * 128 : (tile + 1) * 128].astype(F32)
+    for i in range(pieces):
+        copies[i].wait()
+        small = crossed(held[i], back_ref[...])
         for tile in range(CAP // 128):
-            wet_ref[tile] = wet[:, tile * 128 : (tile + 1) * 128]
-        for tile in range(columns // 128):
-            all_ref[tile] = rain_ref[:, tile * 128 : (tile + 1) * 128].astype(F32)
-
-    small = lax.dot_general(
-        matrix_ref[...], back_ref[...], (((1,), (1,)), ((), ())), preferred_element_type=F32
-    )
-    for tile in range(CAP // 128):
-        small_ref[tile] = small[:, tile * 128 : (tile + 1) * 128]
+            small_ref[tile, i * rows : (i + 1) * rows, :] = small[:, tile * 128 : (tile + 1) * 128]
+
+
+def crossed(a, b):
+    return lax.dot_general(a, b, (((1,), (1,)), ((), ())), preferred_element_type=F32)
 
 
 def tables(matrix, mask, order, rain, after):
     rows, columns = matrix.shape
     levels = rain.shape[0]
-    steps = 9
-    whole = lambda *shape: pl.BlockSpec(shape, lambda i: (0,) * len(shape))
+    pieces = 9
+    shapes = [
+        ((CAP // 128, rows, 128), F32),
+        ((columns, columns + CAP), BF16),
+        ((CAP, columns), BF16),
+        ((CAP // 128, levels, 128), F32),
+        ((columns // 128, levels, 128), F32),
+    ]
     return pl.pallas_call(
         table_kernel,
-        grid=(steps,),
+        grid=(1,),
         in_specs=[
-            pl.BlockSpec((rows // steps, columns), lambda i: (i, 0)),
-            whole(1, columns),
-            whole(1, columns),
-            whole(levels, columns),
+            pl.BlockSpec(memory_space=pl.ANY),
+            whole_block(1, columns),
+            whole_block(1, columns),
+            whole_block(levels, columns),
         ]
         + [pl.BlockSpec(memory_space=pl.ANY)] * len(after),
-        out_specs=[
-            pl.BlockSpec((CAP // 128, rows // steps, 128), lambda i: (0, i, 0)),
-            whole(columns, columns + CAP),
-            whole(CAP, columns),
-            whole(CAP // 128, levels, 128),
-            whole(columns // 128, levels, 128),
-        ],
-        out_shape=[
-            jax.ShapeDtypeStruct((CAP // 128, rows, 128), F32),
-            jax.ShapeDtypeStruct((columns, columns + CAP), BF16),
-            jax.ShapeDtypeStruct((CAP, columns), BF16),
-            jax.ShapeDtypeStruct((CAP // 128, levels, 128), F32),
-            jax.ShapeDtypeStruct((columns // 128, levels, 128), F32),
+        out_specs=[whole_block(*shape) for shape, _ in shapes],
+        out_shape=[jax.ShapeDtypeStruct(*x) for x in shapes],
+        scratch_shapes=[
+            pltpu.VMEM((pieces, rows // pieces, columns), BF16),
+            pltpu.SemaphoreType.DMA((pieces,)),
         ],
         cost_estimate=pl.CostEstimate(
             flops=2 * rows * columns * CAP, bytes_accessed=12 * 10**6, transcendentals=0
@@ -425,47 +444,63 @@
     )(place, *parts, placing, back, matrix, rain, wet, rates, *after)
 
 
-def choose_kernel(flag_ref, own_ref, partner_ref, *refs):
-    out_ref = refs[-1]
+def choose_kernel(flag_ref, own_ref, partner_ref, *refs, first):
+    out_ref, held, in_sems, out_sems = refs[-4:]
+    pieces, rows = held.shape[:2]
+
+    def copied_from(source):
+        ins = [
+            pltpu.make_async_copy(source.at[pl.ds(i * rows, rows)], held.at[i], in_sems.at[i])
+            for i in range(pieces)
+        ]
+        outs = [
+            pltpu.make_async_copy(
+                held.at[i], out_ref.at[pl.ds(first + i * rows, rows)], out_sems.at[i]
+            )
+            for i in range(pieces)
+        ]
+        for copy in ins:
+            copy.start()
+        for i in range(pieces):
+            ins[i].wait()
+            outs[i].start()
+        for copy in outs:
+            copy.wait()
 
     @pl.when(flag_ref[0] > 0)
     def _():
-        out_ref[...] = partner_ref[...]
+        copied_from(partner_ref)
 
     @pl.when(flag_ref[0] <= 0)
     def _():
-        out_ref[...] = own_ref[...]
+        copied_from(own_ref)
 
 
 def choose(flag, own, partner, whole, shape, first, groups, after):
-    rows = shape[0] // (2 * sum(CHUNKS))
-    columns = shape[1]
+    rows = shape[0] // sum(CHUNKS)
+    pieces = 4 * groups
     operands = [own, partner]
-    specs = [
-        pl.BlockSpec((rows, columns), lambda g, f: (jnp.where(f[0] > 0, 0, g), 0)),
-        pl.BlockSpec((rows, columns), lambda g, f: (jnp.where(f[0] > 0, g, 0), 0)),
-    ]
     aliases = {}
     if whole is not None:
         operands.append(whole)
-        specs.append(pl.BlockSpec(memory_space=pl.ANY))
         aliases = {3: 0}
     operands += after
-    specs += [pl.BlockSpec(memory_space=pl.ANY)] * len(after)
+    anywhere = pl.BlockSpec(memory_space=pl.ANY)
     return pl.pallas_call(
-        choose_kernel,
-        grid_spec=pltpu.PrefetchScalarGridSpec(
-            num_scalar_prefetch=1,
-            grid=(2 * groups,),
-            in_specs=specs,
-            out_specs=pl.BlockSpec((rows, columns), lambda g, f: (g + 2 * first, 0)),
-        ),
+        functools.partial(choose_kernel, first=first * rows),
+        in_specs=[pl.BlockSpec(memory_space=pltpu.SMEM)] + [anywhere] * len(operands),
+        out_specs=anywhere,
+        scratch_shapes=[
+            pltpu.VMEM((pieces, rows * groups // pieces, shape[1]), BF16),
+            pltpu.SemaphoreType.DMA((pieces,)),
+            pltpu.SemaphoreType.DMA((pieces,)),
+        ],
         out_shape=jax.ShapeDtypeStruct(shape, BF16),
         input_output_aliases=aliases,
         cost_estimate=pl.CostEstimate(
             flops=0, bytes_accessed=groups * 1200000, transcendentals=0
         ),
-        compiler_params=pltpu.CompilerParams(vmem_limit_bytes=16 << 20),
+        compiler_params=pltpu.CompilerParams(vmem_limit_bytes=8 << 20),
         name="choose",
     )(flag, *operands)
 
@@ -516,10 +551,13 @@
         scav_rate.reshape(tracers // GROUP, GROUP, 1), (tracers // GROUP, GROUP, 128)
     )
 
-    q = pltpu.with_memory_space_constraint(tiled_rows(tracer_dyn), pltpu.HBM)
-    lat, lon = tiled_rows(courant_lat), tiled_rows(courant_lon)
-    apart, group, face_move = deinterleave(), regroup(n_lev), face_rows(lat.shape[0])
+    in_hbm = functools.partial(pltpu.with_memory_space_constraint, memory_space=pltpu.HBM)
+    q = in_hbm(tiled_rows(tracer_dyn))
+    lat, lon = in_hbm(tiled_rows(courant_lat)), in_hbm(tiled_rows(courant_lon))
     firsts = [sum(CHUNKS[:number]) for number in range(len(CHUNKS))]
+    apart, group, face_move = (
+        in_hbm(x) for x in (deinterleave(), regroup(n_lev), face_rows(lat.shape[0]))
+    )
     halos, sections, owns, partners, made = {}, {}, {}, {}, {}
     out = last = None
     for kind, number in ORDER:
@@ -527,13 +565,15 @@
         if kind == "extract":
             north, south = extract(apart, face_move, q, lat, *SPANS[number], after)
             last = north
-            halos[number] = (shifted(north, "lat", 1), shifted(south, "lat", -1))
+            high = shifted(south, "lat", -1)
+            low = shifted(north, "lat", 1)
+            halos[number] = (low, high)
         elif kind == "tables":
             made = tables(
-                conv_matrix.reshape(levels * levels, columns),
-                conv_mask.reshape(1, columns),
-                column_order.reshape(1, columns),
-                rain,
+                in_hbm(conv_matrix.reshape(levels * levels, columns)),
+                in_hbm(conv_mask.reshape(1, columns)),
+                in_hbm(column_order.reshape(1, columns)),
+                in_hbm(rain),
                 after,
             )
             last = made[2]
@@ -544,8 +584,11 @@
                 place, apart, group, face_move, q, *halos[span], lat, lon, halos[0][1],
                 first, first - SPANS[span][0], groups, after,
             )
+            parts = list(parts)
             last = parts[0]
-            sections[number] = [parts[0]] + [turned(parts[s], "lev", s) for s in range(1, n_lev)]
+            for s in (2, 1, 3):
+                parts[s] = turned(parts[s], "lev", s)
+            sections[number] = parts
         elif kind == "physics":
             small, placing, back, wet, wet_all = made
             small = small.reshape(CAP // 128, levels, levels, 128)
@@ -575,6 +618,7 @@
         P(),
         P(),
     )
+
     return jax.shard_map(
         local, mesh=mesh, in_specs=placed, out_specs=P(None, None, ("lat", "lev")), check_vma=False
     )

time: 266 us -> 214 us (0.80)
  waiting for transfers between devices: 77.4 us -> 48.7 us
  Pallas kernels: 125 us -> 108 us
  local copies, waits for them, and re-layouts: 7.72 us -> 3.72 us
  starting transfers between devices: 52.9 us -> 50.2 us
    ppermute x5 -> x6, waiting for transfers between devices: 71.6 us -> 34 us  [paired(): lax.ppermute(value, axis, [(i, i ^ count // 2) for i in range(count)])]
    pallas_call x5 -> x6, Pallas kernels: 40.9 us -> 31.1 us  [advect(): pl.pallas_call(advect_kernel, grid_spec=pltpu.PrefetchScalarGridSpec(num_...]
    pallas_call x3, Pallas kernels: 17.8 us -> 9.78 us  [extract(): pl.pallas_call(extract_kernel, grid=(groups,), in_specs=[whole_block(*apa...]
    ppermute x6, starting transfers between devices: 24.6 us -> 16.9 us  [shifted(): return lax.ppermute(value, axis, pairs)]
    ppermute x6, waiting for transfers between devices: 5.76 us -> 10.4 us  [shifted(): return lax.ppermute(value, axis, pairs)]
    ppermute x15 -> x18, waiting for transfers between devices: 0.04 us -> 4.34 us  [turned(): lax.ppermute(value, axis, [(i, (i + steps) % count) for i in range(count)])]
    unnamed x34 -> x12, local copies, waits for them, and re-layouts: 6.98 us -> 3 us
    ppermute x15 -> x18, starting transfers between devices: 19.5 us -> 22.6 us  [turned(): lax.ppermute(value, axis, [(i, (i + steps) % count) for i in range(count)])]
  transfers between devices with their start and end apart: 26 -> 30, of which waited for: 3 -> 8; matrix products, arithmetic and copies ran while one was open for 0% -> 0% of each run, Pallas kernels for 36% -> 42%
where the time goes in v4:
time: 214 us; the launch traced here: 211 us
  Pallas kernels  108 us (50%)
  starting transfers between devices  50.2 us (23%)
  waiting for transfers between devices  48.7 us (23%)
  local copies, waits for them, and re-layouts  3.72 us (2%)
    pallas_call x6, Pallas kernels, physics(): pl.pallas_call(physics_kernel, grid_spec=pltpu.PrefetchScalarGridSpec(num...  45.5 us
    ppermute x6, waiting for transfers between devices, paired(): lax.ppermute(value, axis, [(i, i ^ count // 2) for i in range(count)])  34 us
    pallas_call x6, Pallas kernels, advect(): pl.pallas_call(advect_kernel, grid_spec=pltpu.PrefetchScalarGridSpec(num_...  31.1 us
    ppermute x18, starting transfers between devices, turned(): lax.ppermute(value, axis, [(i, (i + steps) % count) for i in range(count)])  22.6 us
    ppermute x6, starting transfers between devices, shifted(): return lax.ppermute(value, axis, pairs)  16.9 us
    pallas_call x6, Pallas kernels, choose(): pl.pallas_call(functools.partial(choose_kernel, first=first * rows), in_s...  14.9 us
    ppermute x6, starting transfers between devices, paired(): lax.ppermute(value, axis, [(i, i ^ count // 2) for i in range(count)])  10.7 us
    ppermute x6, waiting for transfers between devices, shifted(): return lax.ppermute(value, axis, pairs)  10.4 us
  transfers between devices with their start and end apart: 30, of which 8 were waited for; matrix products, arithmetic and copies ran while one was open for 0% of the time, Pallas kernels for 42%

profile of v4, /device:TPU:97, one launch (start us, length us, event | category | flops | bytes accessed | tf_op | source)
XLA Modules:
  0.0 210.9 jit_solution(13288010065224265474)
XLA Ops:
  0.0 2.5 %extract.3 = (bf16[1,1152,128]{2,1,0:T(8,128)(2,1)}, bf16[1,1296,128]{2,1,0:T(8,128)(2,1)}) custom-call(bf16[256,256]{1,0:T(8,128)(2,1)} %constant.33.clone.apart_ref, bf16[288,288]{1,0:T(8,128)(2,1)} %constant.35.clone.face_move_ref, bf16[64,18,16,128]{3,2,1,0:T(8,128)(2,1)} %bitcast.27, bf16[18,16,128]{2,1,0:T(8,128)(2,1)} %bitcast.36), custom_call_target="tpu_custom_call" | custom-call | flops 1000000 | bytes 1200000 | tf_op jit(solution)/shard_map/extract/pallas_call | solution.py:111
  2.5 3.7 %extract.4 = (bf16[3,1152,128]{2,1,0:T(8,128)(2,1)S(1)}, bf16[3,1152,128]{2,1,0:T(8,128)(2,1)}) custom-call(bf16[256,256]{1,0:T(8,128)(2,1)} %constant.33.clone.apart_ref, bf16[288,288]{1,0:T(8,128)(2,1)} %constant.35.clone.face_move_ref, bf16[64,18,16,128]{3,2,1,0:T(8,128)(2,1)} %bitcast.28, bf16[18,16,128]{2,1,0:T(8,128)(2,1)} %bitcast.37, ...), custom_call_target="tpu_custom_call" | custom-call | flops 3000000 | bytes 3600000 | tf_op jit(solution)/shard_map/extract/pallas_call | solution.py:111
  6.2 2.4 %collective-permute-start.5 = (bf16[3,1152,128]{2,1,0:T(8,128)(2,1)S(1)}, bf16[3,1152,128]{2,1,0:T(8,128)(2,1)S(1)}, u32[]{:S(2)}, u32[]{:S(2)}) collective-permute-start(bf16[3,1152,128]{2,1,0:T(8,128)(2,1)S(1)} %get-tuple-element.42.refs_0_), channel_id=1, source_target_pairs={{0,4},{4,8},{8,12},{12,16},{16,20},{20,24},{24,28},{28,32},{32,36}... | collective-permute-start | bytes 2654216 | tf_op jit(solution)/shard_map/ppermute | solution.py:511
  8.6 2.2 %collective-permute-start.6 = (bf16[3,1152,128]{2,1,0:T(8,128)(2,1)}, bf16[3,1152,128]{2,1,0:T(8,128)(2,1)S(1)}, u32[]{:S(2)}, u32[]{:S(2)}) collective-permute-start(bf16[3,1152,128]{2,1,0:T(8,128)(2,1)} %get-tuple-element.52), channel_id=1, source_target_pairs={{4,0},{8,4},{12,8},{16,12},{20,16},{24,20},{28,24},{32,28},{36,32}... | collective-permute-start | bytes 2654216 | tf_op jit(solution)/shard_map/ppermute | solution.py:511
  10.8 3.6 %collective-permute-start.1 = (bf16[1,1296,128]{2,1,0:T(8,128)(2,1)}, bf16[1,1296,128]{2,1,0:T(8,128)(2,1)S(1)}, u32[]{:S(2)}, u32[]{:S(2)}) collective-permute-start(bf16[1,1296,128]{2,1,0:T(8,128)(2,1)} %get-tuple-element.41), channel_id=1, source_target_pairs={{4,0},{8,4},{12,8},{16,12},{20,16},{24,20},{28,24},{32,28},{36,32}... | collective-permute-start | bytes 995336 | tf_op jit(solution)/shard_map/ppermute | solution.py:511
  14.5 4.0 %collective-permute-start = (bf16[1,1152,128]{2,1,0:T(8,128)(2,1)}, bf16[1,1152,128]{2,1,0:T(8,128)(2,1)S(1)}, u32[]{:S(2)}, u32[]{:S(2)}) collective-permute-start(bf16[1,1152,128]{2,1,0:T(8,128)(2,1)} %get-tuple-element.40.refs_0_), channel_id=1, source_target_pairs={{0,4},{4,8},{8,12},{12,16},{16,20},{20,24},{24,28},{28,32},{32,36}... | collective-permute-start | bytes 884744 | tf_op jit(solution)/shard_map/ppermute | solution.py:511
  18.5 4.0 %collective-permute-done.low_ref = bf16[1,1152,128]{2,1,0:T(8,128)(2,1)S(1)} collective-permute-done((bf16[1,1152,128]{2,1,0:T(8,128)(2,1)}, bf16[1,1152,128]{2,1,0:T(8,128)(2,1)S(1)}, u32[]{:S(2)}, u32[]{:S(2)}) %collective-permute-start) | collective-permute-done | bytes 294944 | tf_op jit(solution)/shard_map/ppermute | solution.py:511
  22.5 6.4 %collective-permute-done.1.high_ref.above_ref = bf16[1,1296,128]{2,1,0:T(8,128)(2,1)S(1)} collective-permute-done((bf16[1,1296,128]{2,1,0:T(8,128)(2,1)}, bf16[1,1296,128]{2,1,0:T(8,128)(2,1)S(1)}, u32[]{:S(2)}, u32[]{:S(2)}) %collective-permute-start.1) | collective-permute-done | bytes 331808 | tf_op jit(solution)/shard_map/ppermute | solution.py:511
  28.9 4.8 %advect.6 = (bf16[1,144,512]{2,1,0:T(8,128)(2,1)S(1)}, bf16[1,144,512]{2,1,0:T(8,128)(2,1)}, bf16[1,144,512]{2,1,0:T(8,128)(2,1)}, bf16[1,144,512]{2,1,0:T(8,128)(2,1)}) custom-call(s32[1]{0:T(128)} %bitcast.place_ref, bf16[256,256]{1,0:T(8,128)(2,1)} %constant.33.clone.apart_ref, bf16[4,256,256]{2,1,0:T(8,128)(2,1)} %constant.34.clone.group_ref, ...), custom_call_target="tpu_custom_call" | custom-call | flops 10000000 | bytes 2000000 | tf_op jit(solution)/shard_map/advect/pallas_call | solution.py:228
  33.7 1.3 collective-permute-start.2
  35.0 2.6 %collective-permute-start.3 = (bf16[1,144,512]{2,1,0:T(8,128)(2,1)}, bf16[1,144,512]{2,1,0:T(8,128)(2,1)S(1)}, u32[]{:S(2)}, u32[]{:S(2)}) collective-permute-start(bf16[1,144,512]{2,1,0:T(8,128)(2,1)} %get-tuple-element.45), channel_id=1, source_target_pairs={{0,2},{1,3},{2,0},{3,1},{4,6},{5,7},{6,4},{7,5},{8,10},{9,11},{10,... | collective-permute-start | bytes 442376 | tf_op jit(solution)/shard_map/ppermute | solution.py:516
  37.6 1.1 collective-permute-start.4
  38.7 0.1 broadcast_in_dim.7
  38.7 6.4 %tables.1 = (f32[2,5184,128]{2,1,0:T(8,128)S(1)}, bf16[512,768]{1,0:T(8,128)(2,1)S(1)}, bf16[256,512]{1,0:T(8,128)(2,1)S(1)}, f32[2,72,128]{2,1,0:T(8,128)S(1)}, f32[4,72,128]{2,1,0:T(8,128)S(1)}) custom-call(bf16[5184,512]{1,0:T(8,128)(2,1)} %bitcast.45, s32[1,512]{1,0:T(1,128)} %bitcast.52, s32[1,512]{1,0:T(1,128)} %bitcast.53, bf16[72,512]{1,0:T(8,128)(2,1)} %rain_ref.1, ...), custom_call_target="tpu_custom_call" | custom-call | flops 1358954496 | bytes 12000000 | tf_op jit(solution)/shard_map/tables/pallas_call | solution.py:314
  45.2 4.1 %advect.7 = (bf16[1,144,512]{2,1,0:T(8,128)(2,1)S(1)}, bf16[1,144,512]{2,1,0:T(8,128)(2,1)S(1)}, bf16[1,144,512]{2,1,0:T(8,128)(2,1)S(1)}, bf16[1,144,512]{2,1,0:T(8,128)(2,1)S(1)}) custom-call(s32[1]{0:T(128)} %bitcast.place_ref, bf16[256,256]{1,0:T(8,128)(2,1)} %constant.33.clone.apart_ref, bf16[4,256,256]{2,1,0:T(8,128)(2,1)} %constant.34.clone.group_ref, ...), custom_call_target="tpu_custom_call" | custom-call | flops 10000000 | bytes 2000000 | tf_op jit(solution)/shard_map/advect/pallas_call | solution.py:228
  49.3 0.1 broadcast_in_dim.8.rate_ref
  49.3 6.7 %physics.6.refs_0_.own_ref = bf16[576,512]{1,0:T(8,128)(2,1)S(1)} custom-call(s32[1]{0:T(128)} %bitcast.place_ref, bf16[1,144,512]{2,1,0:T(8,128)(2,1)S(1)} %get-tuple-element.43.refs_0_.part0_ref, bf16[1,144,512]{2,1,0:T(8,128)(2,1)S(1)} %collective-permute-done.2.part1_ref, bf16[1,144,512]{2,1,0:T(8,128)(2,1)S(1)} %collective-permute-done.3.part2_ref, ...), custom_call_target="tpu_custom_call" | custom-call | flops 1028653056 | bytes 7700000 | tf_op jit(solution)/shard_map/physics/pallas_call | solution.py:421
  56.1 0.0 copy-start
  56.1 3.6 %extract.5 = (bf16[4,1152,128]{2,1,0:T(8,128)(2,1)S(1)}, bf16[4,1152,128]{2,1,0:T(8,128)(2,1)S(1)}) custom-call(bf16[256,256]{1,0:T(8,128)(2,1)} %constant.33.clone.apart_ref, bf16[288,288]{1,0:T(8,128)(2,1)} %constant.35.clone.face_move_ref, bf16[64,18,16,128]{3,2,1,0:T(8,128)(2,1)} %bitcast.31, bf16[18,16,128]{2,1,0:T(8,128)(2,1)} %bitcast.40, ...), custom_call_target="tpu_custom_call" | custom-call | flops 4000000 | bytes 4800000 | tf_op jit(solution)/shard_map/extract/pallas_call | solution.py:111
  59.7 2.7 %collective-permute-start.7 = (bf16[4,1152,128]{2,1,0:T(8,128)(2,1)S(1)}, bf16[4,1152,128]{2,1,0:T(8,128)(2,1)S(1)}, u32[]{:S(2)}, u32[]{:S(2)}) collective-permute-start(bf16[4,1152,128]{2,1,0:T(8,128)(2,1)S(1)} %get-tuple-element.54.refs_0_), channel_id=1, source_target_pairs={{0,4},{4,8},{8,12},{12,16},{16,20},{20,24},{24,28},{28,32},{32,36}... | collective-permute-start | bytes 3538952 | tf_op jit(solution)/shard_map/ppermute | solution.py:511
  62.4 1.9 collective-permute-start.8
  64.3 0.1 collective-permute-start.10
  64.4 2.7 %collective-permute-start.11 = (bf16[1,144,512]{2,1,0:T(8,128)(2,1)S(1)}, bf16[1,144,512]{2,1,0:T(8,128)(2,1)S(1)}, u32[]{:S(2)}, u32[]{:S(2)}) collective-permute-start(bf16[1,144,512]{2,1,0:T(8,128)(2,1)S(1)} %get-tuple-element.58), channel_id=1, source_target_pairs={{0,3},{1,0},{2,1},{3,2},{4,7},{5,4},{6,5},{7,6},{8,11},{9,8},{10,9... | collective-permute-start | bytes 442376 | tf_op jit(solution)/shard_map/ppermute | solution.py:516
  67.2 7.0 %advect.8 = (bf16[2,144,512]{2,1,0:T(8,128)(2,1)S(1)}, bf16[2,144,512]{2,1,0:T(8,128)(2,1)S(1)}, bf16[2,144,512]{2,1,0:T(8,128)(2,1)S(1)}, bf16[2,144,512]{2,1,0:T(8,128)(2,1)S(1)}) custom-call(s32[1]{0:T(128)} %bitcast.place_ref, bf16[256,256]{1,0:T(8,128)(2,1)} %constant.33.clone.apart_ref, bf16[4,256,256]{2,1,0:T(8,128)(2,1)} %constant.34.clone.group_ref, ...), custom_call_target="tpu_custom_call" | custom-call | flops 20000000 | bytes 4000000 | tf_op jit(solution)/shard_map/advect/pallas_call | solution.py:228
  74.2 0.1 collective-permute-start.15
  74.3 3.8 %collective-permute-start.16 = (bf16[2,144,512]{2,1,0:T(8,128)(2,1)S(1)}, bf16[2,144,512]{2,1,0:T(8,128)(2,1)S(1)}, u32[]{:S(2)}, u32[]{:S(2)}) collective-permute-start(bf16[2,144,512]{2,1,0:T(8,128)(2,1)S(1)} %get-tuple-element.65), channel_id=1, source_target_pairs={{0,2},{1,3},{2,0},{3,1},{4,6},{5,7},{6,4},{7,5},{8,10},{9,11},{10,... | collective-permute-start | bytes 884744 | tf_op jit(solution)/shard_map/ppermute | solution.py:516
  78.2 5.8 %physics.7.refs_0_.own_ref = bf16[576,512]{1,0:T(8,128)(2,1)S(1)} custom-call(s32[1]{0:T(128)} %bitcast.place_ref, bf16[1,144,512]{2,1,0:T(8,128)(2,1)S(1)} %get-tuple-element.53.refs_0_.part0_ref, bf16[1,144,512]{2,1,0:T(8,128)(2,1)S(1)} %collective-permute-done.9.part1_ref, bf16[1,144,512]{2,1,0:T(8,128)(2,1)S(1)} %collective-permute-done.10.part2_ref, ...), custom_call_target="tpu_custom_call" | custom-call | flops 1028653056 | bytes 7700000 | tf_op jit(solution)/shard_map/physics/pallas_call | solution.py:421
  84.0 7.1 %advect.9 = (bf16[2,144,512]{2,1,0:T(8,128)(2,1)S(1)}, bf16[2,144,512]{2,1,0:T(8,128)(2,1)S(1)}, bf16[2,144,512]{2,1,0:T(8,128)(2,1)S(1)}, bf16[2,144,512]{2,1,0:T(8,128)(2,1)S(1)}) custom-call(s32[1]{0:T(128)} %bitcast.place_ref, bf16[256,256]{1,0:T(8,128)(2,1)} %constant.33.clone.apart_ref, bf16[4,256,256]{2,1,0:T(8,128)(2,1)} %constant.34.clone.group_ref, ...), custom_call_target="tpu_custom_call" | custom-call | flops 20000000 | bytes 4000000 | tf_op jit(solution)/shard_map/advect/pallas_call | solution.py:228
  91.1 1.5 collective-permute-start.12
  92.6 0.3 collective-permute-start.13
  92.8 2.2 %collective-permute-start.14 = (bf16[2,144,512]{2,1,0:T(8,128)(2,1)S(1)}, bf16[2,144,512]{2,1,0:T(8,128)(2,1)S(1)}, u32[]{:S(2)}, u32[]{:S(2)}) collective-permute-start(bf16[2,144,512]{2,1,0:T(8,128)(2,1)S(1)} %get-tuple-element.63), channel_id=1, source_target_pairs={{0,3},{1,0},{2,1},{3,2},{4,7},{5,4},{6,5},{7,6},{8,11},{9,8},{10,9... | collective-permute-start | bytes 884744 | tf_op jit(solution)/shard_map/ppermute | solution.py:516
  95.1 10.3 %physics.8.refs_0_.own_ref = bf16[1152,512]{1,0:T(8,128)(2,1)S(1)} custom-call(s32[1]{0:T(128)} %bitcast.place_ref, bf16[2,144,512]{2,1,0:T(8,128)(2,1)S(1)} %get-tuple-element.59.refs_0_.part0_ref, bf16[2,144,512]{2,1,0:T(8,128)(2,1)S(1)} %collective-permute-done.15.part1_ref, bf16[2,144,512]{2,1,0:T(8,128)(2,1)S(1)} %collective-permute-done.16.part2_ref, ...), custom_call_target="tpu_custom_call" | custom-call | flops 2057306112 | bytes 8900000 | tf_op jit(solution)/shard_map/physics/pallas_call | solution.py:421
  105.4 2.5 %collective-permute-start.27 = (bf16[1152,512]{1,0:T(8,128)(2,1)S(1)}, bf16[1152,512]{1,0:T(8,128)(2,1)}, u32[]{:S(2)}, u32[]{:S(2)}) collective-permute-start(bf16[1152,512]{1,0:T(8,128)(2,1)S(1)} %physics.8.refs_0_.own_ref), channel_id=1, source_target_pairs={{0,64},{4,68},{8,72},{12,76},{16,80},{20,84},{24,88},{28,92},{32,9... | collective-permute-start | bytes 3538952 | tf_op jit(solution)/shard_map/ppermute | solution.py:521
  107.9 4.1 %advect.10 = (bf16[1,144,512]{2,1,0:T(8,128)(2,1)S(1)}, bf16[1,144,512]{2,1,0:T(8,128)(2,1)S(1)}, bf16[1,144,512]{2,1,0:T(8,128)(2,1)S(1)}, bf16[1,144,512]{2,1,0:T(8,128)(2,1)S(1)}) custom-call(s32[1]{0:T(128)} %bitcast.place_ref, bf16[256,256]{1,0:T(8,128)(2,1)} %constant.33.clone.apart_ref, bf16[4,256,256]{2,1,0:T(8,128)(2,1)} %constant.34.clone.group_ref, ...), custom_call_target="tpu_custom_call" | custom-call | flops 10000000 | bytes 2000000 | tf_op jit(solution)/shard_map/advect/pallas_call | solution.py:228
  112.0 10.3 %physics.9.refs_0_.own_ref = bf16[1152,512]{1,0:T(8,128)(2,1)S(1)} custom-call(s32[1]{0:T(128)} %bitcast.place_ref, bf16[2,144,512]{2,1,0:T(8,128)(2,1)S(1)} %get-tuple-element.60.refs_0_.part0_ref, bf16[2,144,512]{2,1,0:T(8,128)(2,1)S(1)} %collective-permute-done.12.part1_ref, bf16[2,144,512]{2,1,0:T(8,128)(2,1)S(1)} %collective-permute-done.13.part2_ref, ...), custom_call_target="tpu_custom_call" | custom-call | flops 2057306112 | bytes 8900000 | tf_op jit(solution)/shard_map/physics/pallas_call | solution.py:421
  122.4 0.6 collective-permute-start.26
  123.0 2.5 %collective-permute-start.29 = (bf16[576,512]{1,0:T(8,128)(2,1)S(1)}, bf16[576,512]{1,0:T(8,128)(2,1)S(1)}, u32[]{:S(2)}, u32[]{:S(2)}) collective-permute-start(bf16[576,512]{1,0:T(8,128)(2,1)S(1)} %physics.6.refs_0_.own_ref), channel_id=1, source_target_pairs={{0,64},{4,68},{8,72},{12,76},{16,80},{20,84},{24,88},{28,92},{32,9... | collective-permute-start | bytes 1769480 | tf_op jit(solution)/shard_map/ppermute | solution.py:521
  125.4 1.9 collective-permute-start.22
  127.3 4.1 %advect.11 = (bf16[1,144,512]{2,1,0:T(8,128)(2,1)S(1)}, bf16[1,144,512]{2,1,0:T(8,128)(2,1)S(1)}, bf16[1,144,512]{2,1,0:T(8,128)(2,1)S(1)}, bf16[1,144,512]{2,1,0:T(8,128)(2,1)S(1)}) custom-call(s32[1]{0:T(128)} %bitcast.place_ref, bf16[256,256]{1,0:T(8,128)(2,1)} %constant.33.clone.apart_ref, bf16[4,256,256]{2,1,0:T(8,128)(2,1)} %constant.34.clone.group_ref, ...), custom_call_target="tpu_custom_call" | custom-call | flops 10000000 | bytes 2000000 | tf_op jit(solution)/shard_map/advect/pallas_call | solution.py:228
  131.4 1.2 collective-permute-done.21.part1_ref
  132.6 0.1 collective-permute-start.23
  132.7 1.3 collective-permute-start.18
  134.1 3.1 %collective-permute-done.23.part3_ref = bf16[1,144,512]{2,1,0:T(8,128)(2,1)S(1)} collective-permute-done((bf16[1,144,512]{2,1,0:T(8,128)(2,1)S(1)}, bf16[1,144,512]{2,1,0:T(8,128)(2,1)S(1)}, u32[]{:S(2)}, u32[]{:S(2)}) %collective-permute-start.23) | collective-permute-done | bytes 147488 | tf_op jit(solution)/shard_map/ppermute | solution.py:516
  137.2 1.2 collective-permute-start.19
  138.4 2.2 %collective-permute-start.20 = (bf16[1,144,512]{2,1,0:T(8,128)(2,1)S(1)}, bf16[1,144,512]{2,1,0:T(8,128)(2,1)S(1)}, u32[]{:S(2)}, u32[]{:S(2)}) collective-permute-start(bf16[1,144,512]{2,1,0:T(8,128)(2,1)S(1)} %get-tuple-element.71), channel_id=1, source_target_pairs={{0,3},{1,0},{2,1},{3,2},{4,7},{5,4},{6,5},{7,6},{8,11},{9,8},{10,9... | collective-permute-start | bytes 442376 | tf_op jit(solution)/shard_map/ppermute | solution.py:516
  140.6 6.6 %physics.10.refs_0_.own_ref = bf16[576,512]{1,0:T(8,128)(2,1)} custom-call(s32[1]{0:T(128)} %bitcast.place_ref, bf16[1,144,512]{2,1,0:T(8,128)(2,1)S(1)} %get-tuple-element.67.refs_0_.part0_ref, bf16[1,144,512]{2,1,0:T(8,128)(2,1)S(1)} %collective-permute-done.21.part1_ref, bf16[1,144,512]{2,1,0:T(8,128)(2,1)S(1)} %collective-permute-done.22.part2_ref, ...), custom_call_target="tpu_custom_call" | custom-call | flops 1028653056 | bytes 7700000 | tf_op jit(solution)/shard_map/physics/pallas_call | solution.py:421
  147.2 0.2 collective-permute-start.28
  147.5 2.7 %collective-permute-start.25 = (bf16[576,512]{1,0:T(8,128)(2,1)}, bf16[576,512]{1,0:T(8,128)(2,1)}, u32[]{:S(2)}, u32[]{:S(2)}) collective-permute-start(bf16[576,512]{1,0:T(8,128)(2,1)} %physics.10.refs_0_.own_ref), channel_id=1, source_target_pairs={{0,64},{4,68},{8,72},{12,76},{16,80},{20,84},{24,88},{28,92},{32,9... | collective-permute-start | bytes 1769480 | tf_op jit(solution)/shard_map/ppermute | solution.py:521
  150.2 5.8 %physics.11.refs_0_.refs_1_.own_ref = bf16[576,512]{1,0:T(8,128)(2,1)S(1)} custom-call(s32[1]{0:T(128)} %bitcast.place_ref, bf16[1,144,512]{2,1,0:T(8,128)(2,1)S(1)} %get-tuple-element.68.refs_0_.part0_ref, bf16[1,144,512]{2,1,0:T(8,128)(2,1)S(1)} %collective-permute-done.18.part1_ref, bf16[1,144,512]{2,1,0:T(8,128)(2,1)S(1)} %collective-permute-done.19.part2_ref, ...), custom_call_target="tpu_custom_call" | custom-call | flops 1028653056 | bytes 7700000 | tf_op jit(solution)/shard_map/physics/pallas_call | solution.py:421
  156.0 14.3 %collective-permute-done.29.partner_ref = bf16[576,512]{1,0:T(8,128)(2,1)S(1)} collective-permute-done((bf16[576,512]{1,0:T(8,128)(2,1)S(1)}, bf16[576,512]{1,0:T(8,128)(2,1)S(1)}, u32[]{:S(2)}, u32[]{:S(2)}) %collective-permute-start.29) | collective-permute-done | bytes 589856 | tf_op jit(solution)/shard_map/ppermute | solution.py:521
  170.3 0.9 copy-done.2
  171.1 2.2 %collective-permute-start.24 = (bf16[576,512]{1,0:T(8,128)(2,1)S(1)}, bf16[576,512]{1,0:T(8,128)(2,1)}, u32[]{:S(2)}, u32[]{:S(2)}) collective-permute-start(bf16[576,512]{1,0:T(8,128)(2,1)S(1)} %physics.11.refs_0_.refs_1_.own_ref), channel_id=1, source_target_pairs={{0,64},{4,68},{8,72},{12,76},{16,80},{20,84},{24,88},{28,92},{32,9... | collective-permute-start | bytes 1769480 | tf_op jit(solution)/shard_map/ppermute | solution.py:521
  173.3 0.6 dynamic_slice.3.flag_ref
  173.9 1.1 copy-done.1
  174.9 1.1 copy-done.3
  176.0 2.2 %choose.6.refs_0_ = bf16[4608,512]{1,0:T(8,128)(2,1)} custom-call(s32[1]{0:T(128)} %dynamic_slice.3.flag_ref, bf16[576,512]{1,0:T(8,128)(2,1)S(1)} %copy-done.1, bf16[576,512]{1,0:T(8,128)(2,1)S(1)} %copy-done.3, bf16[576,512]{1,0:T(8,128)(2,1)S(1)} %physics.11.refs_0_.refs_1_.own_ref), custom_call_target="tpu_custom_call" | custom-call | bytes 1200000 | tf_op jit(solution)/shard_map/choose/pallas_call | solution.py:489
  178.2 4.8 %collective-permute-done.28.partner_ref = bf16[576,512]{1,0:T(8,128)(2,1)} collective-permute-done((bf16[576,512]{1,0:T(8,128)(2,1)S(1)}, bf16[576,512]{1,0:T(8,128)(2,1)}, u32[]{:S(2)}, u32[]{:S(2)}) %collective-permute-start.28) | collective-permute-done | bytes 589856 | tf_op jit(solution)/shard_map/ppermute | solution.py:521
  183.0 2.4 %choose.7.refs_0_ = bf16[4608,512]{1,0:T(8,128)(2,1)} custom-call(s32[1]{0:T(128)} %dynamic_slice.3.flag_ref, bf16[576,512]{1,0:T(8,128)(2,1)S(1)} %physics.7.refs_0_.own_ref, bf16[576,512]{1,0:T(8,128)(2,1)} %collective-permute-done.28.partner_ref, bf16[4608,512]{1,0:T(8,128)(2,1)} %choose.6.refs_0_, ...), custom_call_target="tpu_custom_call", output_to_operand_aliasing={{}: (3, {})} | custom-call | bytes 1200000 | tf_op jit(solution)/shard_map/choose/pallas_call | solution.py:489
  185.5 2.7 %choose.8.refs_0_ = bf16[4608,512]{1,0:T(8,128)(2,1)} custom-call(s32[1]{0:T(128)} %dynamic_slice.3.flag_ref, bf16[1152,512]{1,0:T(8,128)(2,1)S(1)} %physics.8.refs_0_.own_ref, bf16[1152,512]{1,0:T(8,128)(2,1)} %collective-permute-done.27.partner_ref, bf16[4608,512]{1,0:T(8,128)(2,1)} %choose.7.refs_0_, ...), custom_call_target="tpu_custom_call", output_to_operand_aliasing={{}: (3, {})} | custom-call | bytes 2400000 | tf_op jit(solution)/shard_map/choose/pallas_call | solution.py:489
  188.2 2.7 %choose.9.refs_0_ = bf16[4608,512]{1,0:T(8,128)(2,1)} custom-call(s32[1]{0:T(128)} %dynamic_slice.3.flag_ref, bf16[1152,512]{1,0:T(8,128)(2,1)S(1)} %physics.9.refs_0_.own_ref, bf16[1152,512]{1,0:T(8,128)(2,1)} %collective-permute-done.26.partner_ref, bf16[4608,512]{1,0:T(8,128)(2,1)} %choose.8.refs_0_, ...), custom_call_target="tpu_custom_call", output_to_operand_aliasing={{}: (3, {})} | custom-call | bytes 2400000 | tf_op jit(solution)/shard_map/choose/pallas_call | solution.py:489
  190.9 4.7 %collective-permute-done.25.partner_ref = bf16[576,512]{1,0:T(8,128)(2,1)} collective-permute-done((bf16[576,512]{1,0:T(8,128)(2,1)}, bf16[576,512]{1,0:T(8,128)(2,1)}, u32[]{:S(2)}, u32[]{:S(2)}) %collective-permute-start.25) | collective-permute-done | bytes 589856 | tf_op jit(solution)/shard_map/ppermute | solution.py:521
  195.7 2.4 %choose.10.refs_0_ = bf16[4608,512]{1,0:T(8,128)(2,1)} custom-call(s32[1]{0:T(128)} %dynamic_slice.3.flag_ref, bf16[576,512]{1,0:T(8,128)(2,1)} %physics.10.refs_0_.own_ref, bf16[576,512]{1,0:T(8,128)(2,1)} %collective-permute-done.25.partner_ref, bf16[4608,512]{1,0:T(8,128)(2,1)} %choose.9.refs_0_, ...), custom_call_target="tpu_custom_call", output_to_operand_aliasing={{}: (3, {})} | custom-call | bytes 1200000 | tf_op jit(solution)/shard_map/choose/pallas_call | solution.py:489
  198.1 10.2 %collective-permute-done.24.partner_ref = bf16[576,512]{1,0:T(8,128)(2,1)} collective-permute-done((bf16[576,512]{1,0:T(8,128)(2,1)S(1)}, bf16[576,512]{1,0:T(8,128)(2,1)}, u32[]{:S(2)}, u32[]{:S(2)}) %collective-permute-start.24) | collective-permute-done | bytes 589856 | tf_op jit(solution)/shard_map/ppermute | solution.py:521
  208.3 2.4 %choose.11 = bf16[4608,512]{1,0:T(8,128)(2,1)} custom-call(s32[1]{0:T(128)} %dynamic_slice.3.flag_ref, bf16[576,512]{1,0:T(8,128)(2,1)S(1)} %physics.11.refs_0_.refs_1_.own_ref, bf16[576,512]{1,0:T(8,128)(2,1)} %collective-permute-done.24.partner_ref, bf16[4608,512]{1,0:T(8,128)(2,1)} %choose.10.refs_0_, ...), custom_call_target="tpu_custom_call", output_to_operand_aliasing={{}: (3, {})} | custom-call | bytes 1200000 | tf_op jit(solution)/shard_map/choose/pallas_call | solution.py:489
  (33 shorter events, 0.1 us)
Async XLA Ops:
  6.2 32.5 %copy-start.4 = (f32[64]{0:T(128)S(1)}, f32[64]{0:T(128)}, u32[]{:S(2)}) copy-start(f32[64]{0:T(128)} %param.19) | copy-start | bytes 772
  6.2 38.9 %collective-permute-start.5 = (bf16[3,1152,128]{2,1,0:T(8,128)(2,1)S(1)}, bf16[3,1152,128]{2,1,0:T(8,128)(2,1)S(1)}, u32[]{:S(2)}, u32[]{:S(2)}) collective-permute-start(bf16[3,1152,128]{2,1,0:T(8,128)(2,1)S(1)} %get-tuple-element.42.refs_0_), channel_id=1, source_target_pairs={{0,4},{4,8},{8,12},{12,16},{16,20},{20,24},{24,28},{28,32},{32,36}... | collective-permute-start | bytes 2654216 | tf_op jit(solution)/shard_map/ppermute | solution.py:511
  8.6 36.5 %collective-permute-start.6 = (bf16[3,1152,128]{2,1,0:T(8,128)(2,1)}, bf16[3,1152,128]{2,1,0:T(8,128)(2,1)S(1)}, u32[]{:S(2)}, u32[]{:S(2)}) collective-permute-start(bf16[3,1152,128]{2,1,0:T(8,128)(2,1)} %get-tuple-element.52), channel_id=1, source_target_pairs={{4,0},{8,4},{12,8},{16,12},{20,16},{24,20},{28,24},{32,28},{36,32}... | collective-permute-start | bytes 2654216 | tf_op jit(solution)/shard_map/ppermute | solution.py:511
  10.8 18.0 %collective-permute-start.1 = (bf16[1,1296,128]{2,1,0:T(8,128)(2,1)}, bf16[1,1296,128]{2,1,0:T(8,128)(2,1)S(1)}, u32[]{:S(2)}, u32[]{:S(2)}) collective-permute-start(bf16[1,1296,128]{2,1,0:T(8,128)(2,1)} %get-tuple-element.41), channel_id=1, source_target_pairs={{4,0},{8,4},{12,8},{16,12},{20,16},{24,20},{28,24},{32,28},{36,32}... | collective-permute-start | bytes 995336 | tf_op jit(solution)/shard_map/ppermute | solution.py:511
  14.5 8.0 %collective-permute-start = (bf16[1,1152,128]{2,1,0:T(8,128)(2,1)}, bf16[1,1152,128]{2,1,0:T(8,128)(2,1)S(1)}, u32[]{:S(2)}, u32[]{:S(2)}) collective-permute-start(bf16[1,1152,128]{2,1,0:T(8,128)(2,1)} %get-tuple-element.40.refs_0_), channel_id=1, source_target_pairs={{0,4},{4,8},{8,12},{12,16},{16,20},{20,24},{24,28},{28,32},{32,36}... | collective-permute-start | bytes 884744 | tf_op jit(solution)/shard_map/ppermute | solution.py:511
  33.7 15.6 %collective-permute-start.2 = (bf16[1,144,512]{2,1,0:T(8,128)(2,1)}, bf16[1,144,512]{2,1,0:T(8,128)(2,1)S(1)}, u32[]{:S(2)}, u32[]{:S(2)}) collective-permute-start(bf16[1,144,512]{2,1,0:T(8,128)(2,1)} %get-tuple-element.44), channel_id=1, source_target_pairs={{0,1},{1,2},{2,3},{3,0},{4,5},{5,6},{6,7},{7,4},{8,9},{9,10},{10,1... | collective-permute-start | bytes 442376 | tf_op jit(solution)/shard_map/ppermute | solution.py:516
  35.0 14.3 %collective-permute-start.3 = (bf16[1,144,512]{2,1,0:T(8,128)(2,1)}, bf16[1,144,512]{2,1,0:T(8,128)(2,1)S(1)}, u32[]{:S(2)}, u32[]{:S(2)}) collective-permute-start(bf16[1,144,512]{2,1,0:T(8,128)(2,1)} %get-tuple-element.45), channel_id=1, source_target_pairs={{0,2},{1,3},{2,0},{3,1},{4,6},{5,7},{6,4},{7,5},{8,10},{9,11},{10,... | collective-permute-start | bytes 442376 | tf_op jit(solution)/shard_map/ppermute | solution.py:516
  37.6 11.7 %collective-permute-start.4 = (bf16[1,144,512]{2,1,0:T(8,128)(2,1)}, bf16[1,144,512]{2,1,0:T(8,128)(2,1)}, u32[]{:S(2)}, u32[]{:S(2)}) collective-permute-start(bf16[1,144,512]{2,1,0:T(8,128)(2,1)} %get-tuple-element.46), channel_id=1, source_target_pairs={{0,3},{1,0},{2,1},{3,2},{4,7},{5,4},{6,5},{7,6},{8,11},{9,8},{10,9... | collective-permute-start | bytes 442376 | tf_op jit(solution)/shard_map/ppermute | solution.py:516
  56.1 66.9 %copy-start = (bf16[576,512]{1,0:T(8,128)(2,1)}, bf16[576,512]{1,0:T(8,128)(2,1)S(1)}, u32[]{:S(2)}) copy-start(bf16[576,512]{1,0:T(8,128)(2,1)S(1)} %physics.6.refs_0_.own_ref) | copy-start | bytes 1769476
  59.7 24.3 %collective-permute-start.7 = (bf16[4,1152,128]{2,1,0:T(8,128)(2,1)S(1)}, bf16[4,1152,128]{2,1,0:T(8,128)(2,1)S(1)}, u32[]{:S(2)}, u32[]{:S(2)}) collective-permute-start(bf16[4,1152,128]{2,1,0:T(8,128)(2,1)S(1)} %get-tuple-element.54.refs_0_), channel_id=1, source_target_pairs={{0,4},{4,8},{8,12},{12,16},{16,20},{20,24},{24,28},{28,32},{32,36}... | collective-permute-start | bytes 3538952 | tf_op jit(solution)/shard_map/ppermute | solution.py:511
  62.4 21.6 %collective-permute-start.8 = (bf16[4,1152,128]{2,1,0:T(8,128)(2,1)S(1)}, bf16[4,1152,128]{2,1,0:T(8,128)(2,1)S(1)}, u32[]{:S(2)}, u32[]{:S(2)}) collective-permute-start(bf16[4,1152,128]{2,1,0:T(8,128)(2,1)S(1)} %get-tuple-element.55), channel_id=1, source_target_pairs={{4,0},{8,4},{12,8},{16,12},{20,16},{24,20},{28,24},{32,28},{36,32}... | collective-permute-start | bytes 3538952 | tf_op jit(solution)/shard_map/ppermute | solution.py:511
  64.3 9.9 %collective-permute-start.10 = (bf16[1,144,512]{2,1,0:T(8,128)(2,1)S(1)}, bf16[1,144,512]{2,1,0:T(8,128)(2,1)S(1)}, u32[]{:S(2)}, u32[]{:S(2)}) collective-permute-start(bf16[1,144,512]{2,1,0:T(8,128)(2,1)S(1)} %get-tuple-element.57), channel_id=1, source_target_pairs={{0,2},{1,3},{2,0},{3,1},{4,6},{5,7},{6,4},{7,5},{8,10},{9,11},{10,... | collective-permute-start | bytes 442376 | tf_op jit(solution)/shard_map/ppermute | solution.py:516
  64.4 9.9 %collective-permute-start.11 = (bf16[1,144,512]{2,1,0:T(8,128)(2,1)S(1)}, bf16[1,144,512]{2,1,0:T(8,128)(2,1)S(1)}, u32[]{:S(2)}, u32[]{:S(2)}) collective-permute-start(bf16[1,144,512]{2,1,0:T(8,128)(2,1)S(1)} %get-tuple-element.58), channel_id=1, source_target_pairs={{0,3},{1,0},{2,1},{3,2},{4,7},{5,4},{6,5},{7,6},{8,11},{9,8},{10,9... | collective-permute-start | bytes 442376 | tf_op jit(solution)/shard_map/ppermute | solution.py:516
  67.2 11.0 %collective-permute-start.9 = (bf16[1,144,512]{2,1,0:T(8,128)(2,1)S(1)}, bf16[1,144,512]{2,1,0:T(8,128)(2,1)S(1)}, u32[]{:S(2)}, u32[]{:S(2)}) collective-permute-start(bf16[1,144,512]{2,1,0:T(8,128)(2,1)S(1)} %get-tuple-element.56), channel_id=1, source_target_pairs={{0,1},{1,2},{2,3},{3,0},{4,5},{5,6},{6,7},{7,4},{8,9},{9,10},{10,1... | collective-permute-start | bytes 442376 | tf_op jit(solution)/shard_map/ppermute | solution.py:516
  74.2 18.6 %collective-permute-start.15 = (bf16[2,144,512]{2,1,0:T(8,128)(2,1)S(1)}, bf16[2,144,512]{2,1,0:T(8,128)(2,1)S(1)}, u32[]{:S(2)}, u32[]{:S(2)}) collective-permute-start(bf16[2,144,512]{2,1,0:T(8,128)(2,1)S(1)} %get-tuple-element.64), channel_id=1, source_target_pairs={{0,1},{1,2},{2,3},{3,0},{4,5},{5,6},{6,7},{7,4},{8,9},{9,10},{10,1... | collective-permute-start | bytes 884744 | tf_op jit(solution)/shard_map/ppermute | solution.py:516
  74.3 20.8 %collective-permute-start.16 = (bf16[2,144,512]{2,1,0:T(8,128)(2,1)S(1)}, bf16[2,144,512]{2,1,0:T(8,128)(2,1)S(1)}, u32[]{:S(2)}, u32[]{:S(2)}) collective-permute-start(bf16[2,144,512]{2,1,0:T(8,128)(2,1)S(1)} %get-tuple-element.65), channel_id=1, source_target_pairs={{0,2},{1,3},{2,0},{3,1},{4,6},{5,7},{6,4},{7,5},{8,10},{9,11},{10,... | collective-permute-start | bytes 884744 | tf_op jit(solution)/shard_map/ppermute | solution.py:516
  78.2 16.9 %collective-permute-start.17 = (bf16[2,144,512]{2,1,0:T(8,128)(2,1)S(1)}, bf16[2,144,512]{2,1,0:T(8,128)(2,1)S(1)}, u32[]{:S(2)}, u32[]{:S(2)}) collective-permute-start(bf16[2,144,512]{2,1,0:T(8,128)(2,1)S(1)} %get-tuple-element.66), channel_id=1, source_target_pairs={{0,3},{1,0},{2,1},{3,2},{4,7},{5,4},{6,5},{7,6},{8,11},{9,8},{10,9... | collective-permute-start | bytes 884744 | tf_op jit(solution)/shard_map/ppermute | solution.py:516
  91.1 21.0 %collective-permute-start.12 = (bf16[2,144,512]{2,1,0:T(8,128)(2,1)S(1)}, bf16[2,144,512]{2,1,0:T(8,128)(2,1)S(1)}, u32[]{:S(2)}, u32[]{:S(2)}) collective-permute-start(bf16[2,144,512]{2,1,0:T(8,128)(2,1)S(1)} %get-tuple-element.61), channel_id=1, source_target_pairs={{0,1},{1,2},{2,3},{3,0},{4,5},{5,6},{6,7},{7,4},{8,9},{9,10},{10,1... | collective-permute-start | bytes 884744 | tf_op jit(solution)/shard_map/ppermute | solution.py:516
  92.6 19.4 %collective-permute-start.13 = (bf16[2,144,512]{2,1,0:T(8,128)(2,1)S(1)}, bf16[2,144,512]{2,1,0:T(8,128)(2,1)S(1)}, u32[]{:S(2)}, u32[]{:S(2)}) collective-permute-start(bf16[2,144,512]{2,1,0:T(8,128)(2,1)S(1)} %get-tuple-element.62), channel_id=1, source_target_pairs={{0,2},{1,3},{2,0},{3,1},{4,6},{5,7},{6,4},{7,5},{8,10},{9,11},{10,... | collective-permute-start | bytes 884744 | tf_op jit(solution)/shard_map/ppermute | solution.py:516
  92.8 19.2 %collective-permute-start.14 = (bf16[2,144,512]{2,1,0:T(8,128)(2,1)S(1)}, bf16[2,144,512]{2,1,0:T(8,128)(2,1)S(1)}, u32[]{:S(2)}, u32[]{:S(2)}) collective-permute-start(bf16[2,144,512]{2,1,0:T(8,128)(2,1)S(1)} %get-tuple-element.63), channel_id=1, source_target_pairs={{0,3},{1,0},{2,1},{3,2},{4,7},{5,4},{6,5},{7,6},{8,11},{9,8},{10,9... | collective-permute-start | bytes 884744 | tf_op jit(solution)/shard_map/ppermute | solution.py:516
  105.4 80.1 %collective-permute-start.27 = (bf16[1152,512]{1,0:T(8,128)(2,1)S(1)}, bf16[1152,512]{1,0:T(8,128)(2,1)}, u32[]{:S(2)}, u32[]{:S(2)}) collective-permute-start(bf16[1152,512]{1,0:T(8,128)(2,1)S(1)} %physics.8.refs_0_.own_ref), channel_id=1, source_target_pairs={{0,64},{4,68},{8,72},{12,76},{16,80},{20,84},{24,88},{28,92},{32,9... | collective-permute-start | bytes 3538952 | tf_op jit(solution)/shard_map/ppermute | solution.py:521
  122.4 65.8 %collective-permute-start.26 = (bf16[1152,512]{1,0:T(8,128)(2,1)S(1)}, bf16[1152,512]{1,0:T(8,128)(2,1)}, u32[]{:S(2)}, u32[]{:S(2)}) collective-permute-start(bf16[1152,512]{1,0:T(8,128)(2,1)S(1)} %physics.9.refs_0_.own_ref), channel_id=1, source_target_pairs={{0,64},{4,68},{8,72},{12,76},{16,80},{20,84},{24,88},{28,92},{32,9... | collective-permute-start | bytes 3538952 | tf_op jit(solution)/shard_map/ppermute | solution.py:521
  123.0 47.3 %collective-permute-start.29 = (bf16[576,512]{1,0:T(8,128)(2,1)S(1)}, bf16[576,512]{1,0:T(8,128)(2,1)S(1)}, u32[]{:S(2)}, u32[]{:S(2)}) collective-permute-start(bf16[576,512]{1,0:T(8,128)(2,1)S(1)} %physics.6.refs_0_.own_ref), channel_id=1, source_target_pairs={{0,64},{4,68},{8,72},{12,76},{16,80},{20,84},{24,88},{28,92},{32,9... | collective-permute-start | bytes 1769480 | tf_op jit(solution)/shard_map/ppermute | solution.py:521
  125.4 7.2 %collective-permute-start.21 = (bf16[1,144,512]{2,1,0:T(8,128)(2,1)S(1)}, bf16[1,144,512]{2,1,0:T(8,128)(2,1)S(1)}, u32[]{:S(2)}, u32[]{:S(2)}) collective-permute-start(bf16[1,144,512]{2,1,0:T(8,128)(2,1)S(1)} %get-tuple-element.72), channel_id=1, source_target_pairs={{0,1},{1,2},{2,3},{3,0},{4,5},{5,6},{6,7},{7,4},{8,9},{9,10},{10,1... | collective-permute-start | bytes 442376 | tf_op jit(solution)/shard_map/ppermute | solution.py:516
  125.4 7.3 %collective-permute-start.22 = (bf16[1,144,512]{2,1,0:T(8,128)(2,1)S(1)}, bf16[1,144,512]{2,1,0:T(8,128)(2,1)S(1)}, u32[]{:S(2)}, u32[]{:S(2)}) collective-permute-start(bf16[1,144,512]{2,1,0:T(8,128)(2,1)S(1)} %get-tuple-element.73), channel_id=1, source_target_pairs={{0,2},{1,3},{2,0},{3,1},{4,6},{5,7},{6,4},{7,5},{8,10},{9,11},{10,... | collective-permute-start | bytes 442376 | tf_op jit(solution)/shard_map/ppermute | solution.py:516
  132.6 4.6 %collective-permute-start.23 = (bf16[1,144,512]{2,1,0:T(8,128)(2,1)S(1)}, bf16[1,144,512]{2,1,0:T(8,128)(2,1)S(1)}, u32[]{:S(2)}, u32[]{:S(2)}) collective-permute-start(bf16[1,144,512]{2,1,0:T(8,128)(2,1)S(1)} %get-tuple-element.74), channel_id=1, source_target_pairs={{0,3},{1,0},{2,1},{3,2},{4,7},{5,4},{6,5},{7,6},{8,11},{9,8},{10,9... | collective-permute-start | bytes 442376 | tf_op jit(solution)/shard_map/ppermute | solution.py:516
  132.7 5.7 %collective-permute-start.18 = (bf16[1,144,512]{2,1,0:T(8,128)(2,1)S(1)}, bf16[1,144,512]{2,1,0:T(8,128)(2,1)S(1)}, u32[]{:S(2)}, u32[]{:S(2)}) collective-permute-start(bf16[1,144,512]{2,1,0:T(8,128)(2,1)S(1)} %get-tuple-element.69), channel_id=1, source_target_pairs={{0,1},{1,2},{2,3},{3,0},{4,5},{5,6},{6,7},{7,4},{8,9},{9,10},{10,1... | collective-permute-start | bytes 442376 | tf_op jit(solution)/shard_map/ppermute | solution.py:516
  137.2 10.0 %collective-permute-start.19 = (bf16[1,144,512]{2,1,0:T(8,128)(2,1)S(1)}, bf16[1,144,512]{2,1,0:T(8,128)(2,1)S(1)}, u32[]{:S(2)}, u32[]{:S(2)}) collective-permute-start(bf16[1,144,512]{2,1,0:T(8,128)(2,1)S(1)} %get-tuple-element.70), channel_id=1, source_target_pairs={{0,2},{1,3},{2,0},{3,1},{4,6},{5,7},{6,4},{7,5},{8,10},{9,11},{10,... | collective-permute-start | bytes 442376 | tf_op jit(solution)/shard_map/ppermute | solution.py:516
  138.4 9.1 %collective-permute-start.20 = (bf16[1,144,512]{2,1,0:T(8,128)(2,1)S(1)}, bf16[1,144,512]{2,1,0:T(8,128)(2,1)S(1)}, u32[]{:S(2)}, u32[]{:S(2)}) collective-permute-start(bf16[1,144,512]{2,1,0:T(8,128)(2,1)S(1)} %get-tuple-element.71), channel_id=1, source_target_pairs={{0,3},{1,0},{2,1},{3,2},{4,7},{5,4},{6,5},{7,6},{8,11},{9,8},{10,9... | collective-permute-start | bytes 442376 | tf_op jit(solution)/shard_map/ppermute | solution.py:516
  147.2 26.1 %copy-start.5 = (s32[64]{0:T(128)S(1)}, s32[64]{0:T(128)}, u32[]{:S(2)}) copy-start(s32[64]{0:T(128)} %param.20) | copy-start | bytes 772
  147.2 35.8 %collective-permute-start.28 = (bf16[576,512]{1,0:T(8,128)(2,1)S(1)}, bf16[576,512]{1,0:T(8,128)(2,1)}, u32[]{:S(2)}, u32[]{:S(2)}) collective-permute-start(bf16[576,512]{1,0:T(8,128)(2,1)S(1)} %physics.7.refs_0_.own_ref), channel_id=1, source_target_pairs={{0,64},{4,68},{8,72},{12,76},{16,80},{20,84},{24,88},{28,92},{32,9... | collective-permute-start | bytes 1769480 | tf_op jit(solution)/shard_map/ppermute | solution.py:521
  147.5 48.2 %collective-permute-start.25 = (bf16[576,512]{1,0:T(8,128)(2,1)}, bf16[576,512]{1,0:T(8,128)(2,1)}, u32[]{:S(2)}, u32[]{:S(2)}) collective-permute-start(bf16[576,512]{1,0:T(8,128)(2,1)} %physics.10.refs_0_.own_ref), channel_id=1, source_target_pairs={{0,64},{4,68},{8,72},{12,76},{16,80},{20,84},{24,88},{28,92},{32,9... | collective-permute-start | bytes 1769480 | tf_op jit(solution)/shard_map/ppermute | solution.py:521
  170.3 0.9 copy-start.2
  171.1 37.2 %collective-permute-start.24 = (bf16[576,512]{1,0:T(8,128)(2,1)S(1)}, bf16[576,512]{1,0:T(8,128)(2,1)}, u32[]{:S(2)}, u32[]{:S(2)}) collective-permute-start(bf16[576,512]{1,0:T(8,128)(2,1)S(1)} %physics.11.refs_0_.refs_1_.own_ref), channel_id=1, source_target_pairs={{0,64},{4,68},{8,72},{12,76},{16,80},{20,84},{24,88},{28,92},{32,9... | collective-permute-start | bytes 1769480 | tf_op jit(solution)/shard_map/ppermute | solution.py:521
  173.9 1.1 copy-start.1
  174.9 1.1 copy-start.3

commit v5 on v4

v5 whole, which is shorter than its diff:
```python
import functools
import itertools

import jax
import jax.numpy as jnp
import numpy as np
from jax import lax
from jax.experimental import pallas as pl
from jax.experimental.pallas import tpu as pltpu
from jax.sharding import PartitionSpec as P


GROUP = 8
CHUNKS = (1, 2, 2, 2, 1)
SPANS = ((0, 1), (1, 2), (3, 5))
ORDER = (
    ("extract", 0),
    ("extract", 1),
    ("advect", 0),
    ("tables", 0),
    ("advect", 1),
    ("physics", 0),
    ("extract", 2),
    ("advect", 2),
    ("physics", 1),
    ("advect", 3),
    ("physics", 2),
    ("advect", 4),
    ("physics", 3),
    ("physics", 4),
    ("choose", 0),
    ("choose", 1),
    ("choose", 2),
    ("choose", 3),
    ("choose", 4),
)
CAP = 256
P_BLOCK = 16
F32 = jnp.float32
BF16 = jnp.bfloat16


def deinterleave():
    move = np.zeros((256, 256), np.float32)
    for k, a, t, i in itertools.product(range(2), range(2), range(GROUP), range(8)):
        move[((k * 2 + a) * GROUP + t) * 8 + i, ((t * 2 + k) * 8 + i) * 2 + a] = 1
    return jnp.asarray(move, BF16)


def face_rows(levels):
    rows = levels * 8
    move = np.zeros((2 * rows, 2 * rows), np.float32)
    for a, r in itertools.product(range(2), range(rows)):
        move[a * rows + r, r * 2 + a] = 1
    return jnp.asarray(move, BF16)


def product(a, b):
    return jnp.dot(a, b, preferred_element_type=F32)


def two_levels(q_ref, pair):
    return q_ref[:, 2 * pair : 2 * pair + 2].reshape(2 * GROUP * 16, 128)


def moved_rows(move, blocks):
    moved = []
    for at in range(0, len(blocks), 2):
        some = blocks[at : at + 2]
        both = product(move, jnp.concatenate(some, axis=1))
        moved += [both[:, i * 128 : (i + 1) * 128] for i in range(len(some))]
    return moved


def extract_kernel(apart_ref, face_move_ref, q_ref, lat_ref, lon_ref, *refs, faces_too):
    outs = refs[-3:] if faces_too else refs[-2:]
    north_ref, south_ref = outs[:2]
    levels = q_ref.shape[1]
    rows = levels * GROUP * 8
    blocks = [two_levels(q_ref, pair) for pair in range(levels // 2)]
    for pair, apart in enumerate(moved_rows(apart_ref[...], blocks)):
        for k in range(2):
            spot = pair * 128 + k * 64
            south_ref[0, spot : spot + 64, :] = apart[k * 128 : k * 128 + 64].astype(BF16)
            north_ref[0, spot : spot + 64, :] = apart[k * 128 + 64 : k * 128 + 128].astype(BF16)
    if south_ref.shape[1] > rows:
        faces = lat_ref[...].reshape(levels * 16, 128)
        south_ref[0, rows:, :] = product(face_move_ref[: levels * 8], faces).astype(BF16)
    if faces_too:

        @pl.when(pl.program_id(0) == 0)
        def _():
            blocks = [ref[...].reshape(levels * 16, 128) for ref in (lat_ref, lon_ref)]
            for at, both in enumerate(moved_rows(face_move_ref[...], blocks)):
                outs[2][2 * at] = both[: levels * 8]
                outs[2][2 * at + 1] = both[levels * 8 :]


def whole_block(*shape, once=False):
    mode = {"pipeline_mode": pl.Buffered(1)} if once else {}
    return pl.BlockSpec(shape, lambda *_: (0,) * len(shape), **mode)


def extract(apart, face_move, q, lat, lon, first, groups, faces_too, after):
    levels = q.shape[1]
    rows = levels * GROUP * 8
    extra = levels * 8 if first == 0 else 0
    faces = (4, levels * 8, 128)
    return pl.pallas_call(
        functools.partial(extract_kernel, faces_too=faces_too),
        grid=(groups,),
        in_specs=[
            whole_block(*apart.shape),
            whole_block(*face_move.shape),
            pl.BlockSpec((GROUP, levels, 16, 128), lambda g: (g + first, 0, 0, 0)),
            whole_block(*lat.shape),
            whole_block(*lon.shape),
        ]
        + [pl.BlockSpec(memory_space=pl.ANY)] * len(after),
        out_specs=[
            pl.BlockSpec((1, rows, 128), lambda g: (g, 0, 0)),
            pl.BlockSpec((1, rows + extra, 128), lambda g: (g, 0, 0)),
        ]
        + [whole_block(*faces)] * faces_too,
        out_shape=[
            jax.ShapeDtypeStruct((groups, rows, 128), BF16),
            jax.ShapeDtypeStruct((groups, rows + extra, 128), BF16),
        ]
        + [jax.ShapeDtypeStruct(faces, F32)] * faces_too,
        cost_estimate=pl.CostEstimate(
            flops=groups * 10**6, bytes_accessed=groups * 1200000, transcendentals=0
        ),
        compiler_params=pltpu.CompilerParams(vmem_limit_bytes=7 << 20),
        name="extract",
    )(apart, face_move, q, lat, lon, *after)


def beside(x, lane, toward_east):
    if toward_east:
        turned = pltpu.roll(x, 127, 1)
        return jnp.where(lane == 127, pltpu.roll(turned, 7, 0), turned)
    turned = pltpu.roll(x, 1, 1)
    return jnp.where(lane == 0, pltpu.roll(turned, 1, 0), turned)


def advect_kernel(
    place_ref, south_ref, north_ref, low_ref, high_ref, faces_ref, above_ref, *refs
):
    outs, made = refs[-5:-1], refs[-1]
    levels = faces_ref.shape[1] // 8
    lane = lax.broadcasted_iota(jnp.int32, (8, 128), 1)

    def body(k, carry):
        at = pl.ds(pl.multiple_of(k * 8, 8), 8)
        edge = [faces_ref[0, at, :], faces_ref[1, at, :], above_ref[0, at, :].astype(F32)]
        terms = []
        for lat in range(2):
            south, north, west = edge[lat], edge[lat + 1], faces_ref[2 + lat, at, :]
            east = beside(west, lane, True)
            own = (
                1.0
                - (jnp.maximum(north, 0.0) - jnp.minimum(south, 0.0))
                - (jnp.maximum(east, 0.0) - jnp.minimum(west, 0.0))
            )
            terms.append(
                (
                    own,
                    jnp.maximum(south, 0.0),
                    -jnp.minimum(north, 0.0),
                    jnp.maximum(west, 0.0),
                    -jnp.minimum(east, 0.0),
                )
            )
        for t in range(0, GROUP, 2):
            spot = pl.multiple_of(k * 64 + t * 8, 16)
            columns = [
                ref[0, pl.ds(spot, 16), :].astype(F32)
                for ref in (low_ref, south_ref, north_ref, high_ref)
            ]
            results = [[], []]
            for part in range(2):
                column = [x[part * 8 : part * 8 + 8] for x in columns]
                rows = column[1:3]
                for lat in range(2):
                    own, from_s, from_n, from_w, from_e = terms[lat]
                    results[lat].append(
                        own * rows[lat]
                        + (from_s * column[lat] + from_n * column[lat + 2])
                        + (
                            from_w * beside(rows[lat], lane, False)
                            + from_e * beside(rows[lat], lane, True)
                        )
                    )
            for lat in range(2):
                spot = pl.multiple_of(k * 128 + (lat * 64 + t * 8), 16)
                made[pl.ds(spot, 16), :] = jnp.concatenate(results[lat], axis=0)
        return carry

    lax.fori_loop(0, levels, body, 0)
    for shift, out in enumerate(outs):
        tile = 2 * lax.rem(place_ref[0] + shift, 4)
        for t, lat, half in itertools.product(range(GROUP), range(2), range(2)):
            start = tile + (lat * 64 + t * 8 + half)
            column = (2 * lat + half) * 128
            out[0, t * levels : (t + 1) * levels, column : column + 128] = made[
                pl.ds(start, levels, stride=128), :
            ].astype(BF16)


def advect(place, south, north, low, high, faces, above, halo_first, groups, after):
    levels = faces.shape[1] // 8
    rows = levels * GROUP
    halo = pl.BlockSpec((1, rows * 8, 128), lambda g: (g + halo_first, 0, 0))
    return pl.pallas_call(
        advect_kernel,
        grid=(groups,),
        in_specs=[
            pl.BlockSpec(memory_space=pltpu.SMEM),
            halo,
            halo,
            halo,
            halo,
            whole_block(*faces.shape),
            pl.BlockSpec((1, levels * 8, 128), lambda g: (0, GROUP, 0)),
        ]
        + [pl.BlockSpec(memory_space=pl.ANY)] * len(after),
        out_specs=[pl.BlockSpec((1, rows, 512), lambda g: (g, 0, 0))] * 4,
        scratch_shapes=[pltpu.VMEM((levels * 128, 128), F32)],
        out_shape=[jax.ShapeDtypeStruct((groups, rows, 512), BF16)] * 4,
        cost_estimate=pl.CostEstimate(
            flops=groups * 10**7, bytes_accessed=groups * 2000000, transcendentals=0
        ),
        compiler_params=pltpu.CompilerParams(vmem_limit_bytes=10 << 20),
        name="advect",
    )(place, south, north, low, high, faces, above, *after)


def table_kernel(matrix_ref, mask_ref, order_ref, rain_ref, *refs):
    small_ref, placing_ref, picking_ref, back_ref, wet_ref, all_ref, held, turned, sems = refs[-9:]
    columns = mask_ref.shape[1]
    levels = rain_ref.shape[0]
    pieces, per_piece = held.shape[:2]
    copies = [
        pltpu.make_async_copy(
            matrix_ref.at[pl.ds(i * per_piece, per_piece)], held.at[i], sems.at[i]
        )
        for i in range(pieces)
    ]
    for copy in copies:
        copy.start()

    mask = mask_ref[...]
    order = order_ref[...]
    row = lax.broadcasted_iota(jnp.int32, (columns, columns), 0)
    column = lax.broadcasted_iota(jnp.int32, (columns, columns), 1)
    earlier = jnp.where(row < column, 1.0, 0.0).astype(BF16)
    ones = jnp.where(mask > 0, 1.0, 0.0)
    wide = jnp.broadcast_to(ones, (8, columns)).astype(BF16)
    rank = product(wide, earlier)[0:1]
    rank = jnp.where(mask > 0, rank, -1.0).astype(jnp.int32)
    slot = lax.broadcasted_iota(jnp.int32, (CAP, columns), 0)
    back = jnp.where(slot == rank, 1.0, 0.0).astype(BF16)
    back_ref[...] = back
    whole = jnp.where(row == order, 1.0, 0.0)
    placing_ref[...] = jnp.where(mask > 0, 0.0, whole).astype(BF16)
    picking_ref[...] = crossed(back, whole.astype(BF16)).astype(BF16)
    rain = rain_ref[...]
    all_ref[...] = rain.astype(F32)
    nothing = jnp.zeros((CAP, 128 - levels), F32)
    wet_ref[...] = jnp.concatenate([crossed(back, rain), nothing], axis=1)
    for piece in range(pieces):
        copies[piece].wait()
        for k in range(per_piece):
            picked = crossed(back_ref[...], held[piece, k])
            turned[pl.ds(k, CAP, stride=per_piece), :] = jnp.concatenate([picked, nothing], axis=1)
        spot = piece * per_piece
        small_ref[:, spot : spot + per_piece, :] = (
            turned[...].reshape(CAP, per_piece, 128).astype(BF16)
        )


def crossed(a, b):
    return lax.dot_general(a, b, (((1,), (1,)), ((), ())), preferred_element_type=F32)


def tables(matrix, mask, order, rain, after):
    levels, _, columns = matrix.shape
    per_piece = 8
    shapes = [
        ((CAP, levels, 128), BF16),
        ((columns, columns), BF16),
        ((CAP, columns), BF16),
        ((CAP, columns), BF16),
        ((CAP, 128), F32),
        ((levels, columns), F32),
    ]
    return pl.pallas_call(
        table_kernel,
        grid=(1,),
        in_specs=[
            pl.BlockSpec(memory_space=pl.ANY),
            whole_block(1, columns),
            whole_block(1, columns),
            whole_block(levels, columns),
        ]
        + [pl.BlockSpec(memory_space=pl.ANY)] * len(after),
        out_specs=[whole_block(*shape, once=True) for shape, _ in shapes],
        out_shape=[jax.ShapeDtypeStruct(*x) for x in shapes],
        scratch_shapes=[
            pltpu.VMEM((levels // per_piece, per_piece, levels, columns), BF16),
            pltpu.VMEM((CAP * per_piece, 128), F32),
            pltpu.SemaphoreType.DMA((levels // per_piece,)),
        ],
        cost_estimate=pl.CostEstimate(
            flops=2 * levels * 128 * columns * CAP, bytes_accessed=12 * 10**6, transcendentals=0
        ),
        compiler_params=pltpu.CompilerParams(vmem_limit_bytes=20 << 20),
        name="tables",
    )(matrix, mask, order, rain, *after)


def physics_kernel(
    place_ref, scav_ref, part0, part1, part2, part3, placing_ref, picking_ref, back_ref,
    matrix_ref, rain_ref, wet_ref, rate_ref, *refs, first
):
    out_ref, columns_in, picked, mixed = refs[-4:]
    groups = part0.shape[0]
    levels = rain_ref.shape[0]
    part = part0.shape[1] // GROUP
    tracers = groups * GROUP

    columns_in[:, levels:, :] = jnp.zeros((tracers, 128 - levels, part0.shape[2]), BF16)
    for place in range(4):

        @pl.when(place_ref[0] == place)
        def _(place=place):
            for shift, ref in enumerate((part0, part1, part2, part3)):
                base = (place - shift) % 4 * part
                for g, t in itertools.product(range(groups), range(GROUP)):
                    columns_in[g * GROUP + t, base : base + part, :] = ref[
                        g, t * part : (t + 1) * part, :
                    ]

    for t in range(tracers):
        picked[t * CAP : (t + 1) * CAP, :] = crossed(picking_ref[...], columns_in[t])

    rate = jnp.concatenate([rate_ref[first + g] for g in range(groups)], axis=0)
    nothing = jnp.zeros((128 - levels, 128), BF16)

    def contract(block, carry):
        for inner in range(P_BLOCK):
            p = block * P_BLOCK + inner
            mine = picked[pl.ds(p, tracers, stride=CAP), :].astype(BF16)
            matrix = jnp.concatenate([matrix_ref[p], nothing], axis=0)
            wet = wet_ref[pl.ds(p, tracers, stride=0), :]
            mixed[pl.ds(p, tracers, stride=CAP), :] = crossed(mine, matrix) * jnp.exp(-rate * wet)
        return carry

    lax.fori_loop(0, CAP // P_BLOCK, contract, 0)

    def finish(block, carry):
        for inner in range(2):
            t = block * 2 + inner
            spot = pl.multiple_of(t * CAP, CAP)
            spread = lax.dot_general(
                mixed[pl.ds(spot, CAP), :].astype(BF16),
                back_ref[...],
                (((0,), (0,)), ((), ())),
                preferred_element_type=F32,
            )[:levels]
            plain = product(columns_in[t, :levels], placing_ref[...])
            scav = scav_ref[first * GROUP + t]
            out_ref[t] = (spread + plain * jnp.exp(-scav * rain_ref[...])).astype(BF16)
        return carry

    lax.fori_loop(0, tracers // 2, finish, 0)


def physics(place, scav, parts, made, rates, first, groups, after):
    matrix, placing, picking, back, wet, rain = made
    columns = parts[0].shape[2]
    levels = rain.shape[0]
    tracers = groups * GROUP
    flops = 2 * tracers * levels * columns * (columns + 3 * CAP)
    scalars = pl.BlockSpec(memory_space=pltpu.SMEM)
    operands = (placing, picking, back, matrix, rain, wet)
    return pl.pallas_call(
        functools.partial(physics_kernel, first=first),
        grid=(1,),
        in_specs=[scalars, scalars]
        + [whole_block(*x.shape, once=True) for x in (*parts, *operands)]
        + [whole_block(*rates.shape)]
        + [pl.BlockSpec(memory_space=pl.ANY)] * len(after),
        out_specs=whole_block(tracers, levels, columns, once=True),
        scratch_shapes=[
            pltpu.VMEM((tracers, 128, columns), BF16),
            pltpu.VMEM((tracers * CAP, 128), F32),
            pltpu.VMEM((tracers * CAP, 128), F32),
        ],
        out_shape=jax.ShapeDtypeStruct((tracers, levels, columns), BF16),
        cost_estimate=pl.CostEstimate(
            flops=flops, bytes_accessed=groups * 1200000 + 6500000, transcendentals=0
        ),
        compiler_params=pltpu.CompilerParams(vmem_limit_bytes=(9 + 8 * groups) << 20),
        name="physics",
    )(place, scav, *parts, *operands, rates, *after)


def choose_kernel(flag_ref, own_ref, partner_ref, *refs, first):
    out_ref, held, in_sems, out_sems = refs[-4:]
    pieces, rows = held.shape[:2]

    def copied_from(source):
        ins = [
            pltpu.make_async_copy(source.at[pl.ds(i * rows, rows)], held.at[i], in_sems.at[i])
            for i in range(pieces)
        ]
        outs = [
            pltpu.make_async_copy(
                held.at[i], out_ref.at[pl.ds(first + i * rows, rows)], out_sems.at[i]
            )
            for i in range(pieces)
        ]
        for copy in ins:
            copy.start()
        for i in range(pieces):
            ins[i].wait()
            outs[i].start()
        for copy in outs:
            copy.wait()

    @pl.when(flag_ref[0] > 0)
    def _():
        copied_from(partner_ref)

    @pl.when(flag_ref[0] <= 0)
    def _():
        copied_from(own_ref)


def choose(flag, own, partner, whole, shape, first, groups, after):
    rows = shape[0] // sum(CHUNKS)
    pieces = 4 * groups
    operands = [own, partner]
    aliases = {}
    if whole is not None:
        operands.append(whole)
        aliases = {3: 0}
    operands += after
    anywhere = pl.BlockSpec(memory_space=pl.ANY)
    return pl.pallas_call(
        functools.partial(choose_kernel, first=first * rows),
        in_specs=[pl.BlockSpec(memory_space=pltpu.SMEM)] + [anywhere] * len(operands),
        out_specs=anywhere,
        scratch_shapes=[
            pltpu.VMEM((pieces, rows * groups // pieces, shape[1]), BF16),
            pltpu.SemaphoreType.DMA((pieces,)),
            pltpu.SemaphoreType.DMA((pieces,)),
        ],
        out_shape=jax.ShapeDtypeStruct(shape, BF16),
        input_output_aliases=aliases,
        cost_estimate=pl.CostEstimate(
            flops=0, bytes_accessed=groups * 1200000, transcendentals=0
        ),
        compiler_params=pltpu.CompilerParams(vmem_limit_bytes=8 << 20),
        name="choose",
    )(flag, *operands)


def shifted(value, axis, steps):
    count = lax.axis_size(axis)
    pairs = [(i, i + steps) for i in range(count) if 0 <= i + steps < count]
    return lax.ppermute(value, axis, pairs)


def turned(value, axis, steps):
    count = lax.axis_size(axis)
    return lax.ppermute(value, axis, [(i, (i + steps) % count) for i in range(count)])


def paired(value, axis):
    count = lax.axis_size(axis)
    return lax.ppermute(value, axis, [(i, i ^ (count // 2)) for i in range(count)])


def tiled_rows(value):
    lead = value.shape[:-2]
    lats, lons = value.shape[-2:]
    split = value.reshape(*lead, lats, lons // 128, 128)
    return jnp.swapaxes(split, -3, -2).reshape(*lead, lats * lons // 128, 128)


def local(
    tracer_dyn,
    courant_lat,
    courant_lon,
    conv_matrix,
    conv_mask,
    column_order,
    rain,
    scav_rate,
    pair_flag,
):
    n_lat = lax.axis_size("lat")
    n_lev = lax.axis_size("lev")
    tracers = tracer_dyn.shape[0]
    levels, columns = rain.shape
    lev_place = lax.axis_index("lev")
    pair_index = lax.axis_index("lat") % (n_lat // 2) * n_lev + lev_place
    flag = lax.dynamic_slice_in_dim(pair_flag, pair_index, 1)
    rates = jnp.broadcast_to(
        scav_rate.reshape(tracers // GROUP, GROUP, 1), (tracers // GROUP, GROUP, 128)
    )

    in_hbm = functools.partial(pltpu.with_memory_space_constraint, memory_space=pltpu.HBM)
    q = in_hbm(tiled_rows(tracer_dyn))
    lat, lon = in_hbm(tiled_rows(courant_lat)), in_hbm(tiled_rows(courant_lon))
    firsts = [sum(CHUNKS[:number]) for number in range(len(CHUNKS))]
    apart, face_move = (in_hbm(x) for x in (deinterleave(), face_rows(lat.shape[0])))
    place = lev_place.astype(jnp.int32).reshape(1)
    halos, sections, owns, partners, made = {}, {}, {}, {}, {}
    out = last = None
    for kind, number in ORDER:
        after = [] if last is None else [last]
        if kind == "extract":
            found = extract(
                apart, face_move, q, lat, lon, *SPANS[number], number == 0, after
            )
            north, south = found[:2]
            faces = found[2] if number == 0 else faces
            last = north
            high = shifted(south, "lat", -1)
            low = shifted(north, "lat", 1)
            halos[number] = (south, north, low, high)
        elif kind == "tables":
            made = tables(
                in_hbm(conv_matrix),
                in_hbm(conv_mask.reshape(1, columns)),
                in_hbm(column_order.reshape(1, columns)),
                in_hbm(rain),
                after,
            )
            last = made[2]
        elif kind == "advect":
            first, groups = firsts[number], CHUNKS[number]
            span = max(i for i in range(len(SPANS)) if SPANS[i][0] <= first)
            parts = advect(
                place, *halos[span], faces, halos[0][3], first - SPANS[span][0], groups, after
            )
            parts = list(parts)
            last = parts[0]
            for shift in (2, 1, 3):
                parts[shift] = turned(parts[shift], "lev", shift)
            sections[number] = parts
        elif kind == "physics":
            own = physics(
                place, scav_rate, sections[number], made, rates,
                firsts[number], CHUNKS[number], after,
            )
            own = own.reshape(-1, columns)
            last = owns[number] = own
            partners[number] = paired(own, "lat")
        else:
            out = choose(
                flag, owns[number], partners[number], out, (tracers * levels, columns),
                firsts[number], CHUNKS[number], after,
            )
    return out.reshape(tracers, levels, columns)


def solution(mesh):
    placed = (
        P(None, "lev", "lat", None),
        P("lev", "lat", None),
        P("lev", "lat", None),
        P(None, None, ("lat", "lev")),
        P(("lat", "lev")),
        P(("lat", "lev")),
        P(None, ("lat", "lev")),
        P(),
        P(),
    )

    return jax.shard_map(
        local, mesh=mesh, in_specs=placed, out_specs=P(None, None, ("lat", "lev")), check_vma=False
    )
```

time: 214 us -> 224 us (1.047)
  waiting for transfers between devices: 48.7 us -> 77 us
  starting transfers between devices: 50.2 us -> 40.8 us
  Pallas kernels: 108 us -> 102 us
  local copies, waits for them, and re-layouts: 3.72 us -> 0.81 us
    ppermute x6, waiting for transfers between devices: 10.4 us -> 24.6 us  [shifted(): return lax.ppermute(value, axis, pairs)]
    pallas_call x15 -> x13, Pallas kernels: 86.4 us -> 78.8 us  [the longest x5 47.7 us: physics(): pl.pallas_call(functools.partial(physics_kernel, first=first), grid=(1,),...]
    ppermute x6 -> x5, waiting for transfers between devices: 34 us -> 41 us  [paired(): lax.ppermute(value, axis, [(i, i ^ count // 2) for i in range(count)])]
    ppermute x18 -> x15, waiting for transfers between devices: 4.34 us -> 11.3 us  [turned(): lax.ppermute(value, axis, [(i, (i + steps) % count) for i in range(count)])]
    ppermute x18 -> x15, starting transfers between devices: 22.6 us -> 16.4 us  [turned(): lax.ppermute(value, axis, [(i, (i + steps) % count) for i in range(count)])]
    ppermute x6 -> x5, starting transfers between devices: 10.7 us -> 6.17 us  [paired(): lax.ppermute(value, axis, [(i, i ^ count // 2) for i in range(count)])]
    pallas_call x1, Pallas kernels: 6.38 us -> 9.4 us  [tables(): pl.pallas_call(table_kernel, grid=(1,), in_specs=[pl.BlockSpec(memory_spa...]
    unnamed x12 -> x4, local copies, waits for them, and re-layouts: 3 us -> 0.01 us
  transfers between devices with their start and end apart: 30 -> 26, of which waited for: 8 -> 7; matrix products, arithmetic and copies ran while one was open for 0% -> 0% of each run, Pallas kernels for 42% -> 37%
where the time goes in v5:
time: 224 us; the launch traced here: 221 us
  Pallas kernels  102 us (46%)
  waiting for transfers between devices  77 us (34%)
  starting transfers between devices  40.8 us (18%)
    pallas_call x5, Pallas kernels, physics(): pl.pallas_call(functools.partial(physics_kernel, first=first), grid=(1,),...  47.7 us
    ppermute x5, waiting for transfers between devices, paired(): lax.ppermute(value, axis, [(i, i ^ count // 2) for i in range(count)])  41 us
    ppermute x6, waiting for transfers between devices, shifted(): return lax.ppermute(value, axis, pairs)  24.6 us
    pallas_call x5, Pallas kernels, advect(): pl.pallas_call(advect_kernel, grid=(groups,), in_specs=[pl.BlockSpec(memo...  22.4 us
    ppermute x6, starting transfers between devices, shifted(): return lax.ppermute(value, axis, pairs)  18.2 us
    ppermute x15, starting transfers between devices, turned(): lax.ppermute(value, axis, [(i, (i + steps) % count) for i in range(count)])  16.4 us
    pallas_call x5, Pallas kernels, choose(): pl.pallas_call(functools.partial(choose_kernel, first=first * rows), in_s...  13.3 us
    ppermute x15, waiting for transfers between devices, turned(): lax.ppermute(value, axis, [(i, (i + steps) % count) for i in range(count)])  11.3 us
  transfers between devices with their start and end apart: 26, of which 7 were waited for; matrix products, arithmetic and copies ran while one was open for 0% of the time, Pallas kernels for 37%

profile of v5, /device:TPU:97, one launch (start us, length us, event | category | flops | bytes accessed | tf_op | source)
XLA Modules:
  0.0 220.6 jit_solution(10542133744618949505)
XLA Ops:
  0.0 2.4 %extract.3 = (bf16[1,1152,128]{2,1,0:T(8,128)(2,1)S(1)}, bf16[1,1296,128]{2,1,0:T(8,128)(2,1)}, f32[4,144,128]{2,1,0:T(8,128)S(1)}) custom-call(bf16[256,256]{1,0:T(8,128)(2,1)} %constant.31.clone.apart_ref, bf16[288,288]{1,0:T(8,128)(2,1)} %constant.32.clone.face_move_ref, bf16[64,18,16,128]{3,2,1,0:T(8,128)(2,1)} %bitcast.40, ...), custom_call_target="tpu_custom_call" | custom-call | flops 1000000 | bytes 1200000 | tf_op jit(solution)/shard_map/extract/pallas_call | solution.py:109
  2.4 1.9 extract.4
  4.3 2.3 %collective-permute-start.5 = (bf16[2,1152,128]{2,1,0:T(8,128)(2,1)S(1)}, bf16[2,1152,128]{2,1,0:T(8,128)(2,1)S(1)}, u32[]{:S(2)}, u32[]{:S(2)}) collective-permute-start(bf16[2,1152,128]{2,1,0:T(8,128)(2,1)S(1)} %get-tuple-element.41.refs_0_.north_ref), channel_id=1, source_target_pairs={{0,4},{4,8},{8,12},{12,16},{16,20},{20,24},{24,28},{28,32},{32,36}... | collective-permute-start | bytes 1769480 | tf_op jit(solution)/shard_map/ppermute | solution.py:473
  6.7 2.2 collective-permute-start.6
  8.9 3.6 %collective-permute-start.1 = (bf16[1,1296,128]{2,1,0:T(8,128)(2,1)}, bf16[1,1296,128]{2,1,0:T(8,128)(2,1)S(1)}, u32[]{:S(2)}, u32[]{:S(2)}) collective-permute-start(bf16[1,1296,128]{2,1,0:T(8,128)(2,1)} %get-tuple-element.38.south_ref), channel_id=1, source_target_pairs={{4,0},{8,4},{12,8},{16,12},{20,16},{24,20},{28,24},{32,28},{36,32}... | collective-permute-start | bytes 995336 | tf_op jit(solution)/shard_map/ppermute | solution.py:473
  12.5 4.0 %collective-permute-start = (bf16[1,1152,128]{2,1,0:T(8,128)(2,1)S(1)}, bf16[1,1152,128]{2,1,0:T(8,128)(2,1)}, u32[]{:S(2)}, u32[]{:S(2)}) collective-permute-start(bf16[1,1152,128]{2,1,0:T(8,128)(2,1)S(1)} %get-tuple-element.39.refs_0_.north_ref), channel_id=1, source_target_pairs={{0,4},{4,8},{8,12},{12,16},{16,20},{20,24},{24,28},{28,32},{32,36}... | collective-permute-start | bytes 884744 | tf_op jit(solution)/shard_map/ppermute | solution.py:473
  16.6 0.1 broadcast_in_dim.7
  16.6 3.6 %collective-permute-done.low_ref = bf16[1,1152,128]{2,1,0:T(8,128)(2,1)} collective-permute-done((bf16[1,1152,128]{2,1,0:T(8,128)(2,1)S(1)}, bf16[1,1152,128]{2,1,0:T(8,128)(2,1)}, u32[]{:S(2)}, u32[]{:S(2)}) %collective-permute-start) | collective-permute-done | bytes 294944 | tf_op jit(solution)/shard_map/ppermute | solution.py:473
  20.2 3.3 %collective-permute-done.1.high_ref.above_ref = bf16[1,1296,128]{2,1,0:T(8,128)(2,1)S(1)} collective-permute-done((bf16[1,1296,128]{2,1,0:T(8,128)(2,1)}, bf16[1,1296,128]{2,1,0:T(8,128)(2,1)S(1)}, u32[]{:S(2)}, u32[]{:S(2)}) %collective-permute-start.1) | collective-permute-done | bytes 331808 | tf_op jit(solution)/shard_map/ppermute | solution.py:473
  23.5 3.7 %advect.5 = (bf16[1,144,512]{2,1,0:T(8,128)(2,1)S(1)}, bf16[1,144,512]{2,1,0:T(8,128)(2,1)S(1)}, bf16[1,144,512]{2,1,0:T(8,128)(2,1)S(1)}, bf16[1,144,512]{2,1,0:T(8,128)(2,1)S(1)}) custom-call(s32[1]{0:T(128)} %bitcast.place_ref, bf16[1,1296,128]{2,1,0:T(8,128)(2,1)} %get-tuple-element.38.south_ref, ...), custom_call_target="tpu_custom_call" | custom-call | flops 10000000 | bytes 2000000 | tf_op jit(solution)/shard_map/advect/pallas_call | solution.py:214
  27.2 1.4 collective-permute-start.2
  28.6 2.6 %collective-permute-start.3 = (bf16[1,144,512]{2,1,0:T(8,128)(2,1)S(1)}, bf16[1,144,512]{2,1,0:T(8,128)(2,1)S(1)}, u32[]{:S(2)}, u32[]{:S(2)}) collective-permute-start(bf16[1,144,512]{2,1,0:T(8,128)(2,1)S(1)} %get-tuple-element.44), channel_id=1, source_target_pairs={{0,2},{1,3},{2,0},{3,1},{4,6},{5,7},{6,4},{7,5},{8,10},{9,11},{10,... | collective-permute-start | bytes 442376 | tf_op jit(solution)/shard_map/ppermute | solution.py:478
  31.2 1.1 collective-permute-start.4
  32.3 9.4 %tables.1 = (bf16[256,72,128]{2,1,0:T(8,128)(2,1)S(1)}, bf16[512,512]{1,0:T(8,128)(2,1)S(1)}, bf16[256,512]{1,0:T(8,128)(2,1)S(1)}, bf16[256,512]{1,0:T(8,128)(2...) custom-call(bf16[72,72,512]{2,1,0:T(8,128)(2,1)} %matrix_ref.1, s32[1,512]{1,0:T(1,128)} %bitcast.49, ...), custom_call_target="tpu_custom_call" | custom-call | flops 2415919104 | bytes 12000000 | tf_op jit(solution)/shard_map/tables/pallas_call | solution.py:297
  41.7 0.0 collective-permute-done.5.low_ref
  41.7 0.0 collective-permute-done.6.high_ref
  41.7 5.4 %advect.6 = (bf16[2,144,512]{2,1,0:T(8,128)(2,1)S(1)}, bf16[2,144,512]{2,1,0:T(8,128)(2,1)S(1)}, bf16[2,144,512]{2,1,0:T(8,128)(2,1)S(1)}, bf16[2,144,512]{2,1,0:T(8,128)(2,1)S(1)}) custom-call(s32[1]{0:T(128)} %bitcast.place_ref, bf16[2,1152,128]{2,1,0:T(8,128)(2,1)S(1)} %get-tuple-element.52.south_ref, ...), custom_call_target="tpu_custom_call" | custom-call | flops 20000000 | bytes 4000000 | tf_op jit(solution)/shard_map/advect/pallas_call | solution.py:214
  47.1 0.0 collective-permute-done.2.part1
  47.1 0.0 collective-permute-done.3.part2
  47.1 0.0 collective-permute-done.4.part3
  47.1 0.1 broadcast_in_dim.8.rate_ref
  47.2 7.8 %physics.5 = bf16[8,72,512]{2,1,0:T(8,128)(2,1)S(1)} custom-call(s32[1]{0:T(128)} %bitcast.place_ref, f32[64]{0:T(128)S(1)} %copy-done, bf16[1,144,512]{2,1,0:T(8,128)(2,1)S(1)} %get-tuple-element.42.refs_0_.part0, bf16[1,144,512]{2,1,0:T(8,128)(2,1)S(1)} %collective-permute-done.2.part1, bf16[1,144,512]{2,1,0:T(8,128)(2,1)S(1)} %collective-permute-done.3.part2, ...), custom_call_target="tpu_custom_call" | custom-call | flops 754974720 | bytes 7700000 | tf_op jit(solution)/shard_map/physics/pallas_call | solution.py:387
  55.0 4.4 %extract.5 = (bf16[5,1152,128]{2,1,0:T(8,128)(2,1)S(1)}, bf16[5,1152,128]{2,1,0:T(8,128)(2,1)S(1)}) custom-call(bf16[256,256]{1,0:T(8,128)(2,1)} %constant.31.clone.apart_ref, bf16[288,288]{1,0:T(8,128)(2,1)} %constant.32.clone.face_move_ref, bf16[64,18,16,128]{3,2,1,0:T(8,128)(2,1)} %bitcast.42, bf16[18,16,128]{2,1,0:T(8,128)(2,1)} %bitcast.45, ...), custom_call_target="tpu_custom_call" | custom-call | flops 5000000 | bytes 6000000 | tf_op jit(solution)/shard_map/extract/pallas_call | solution.py:109
  59.4 4.1 %collective-permute-start.7 = (bf16[5,1152,128]{2,1,0:T(8,128)(2,1)S(1)}, bf16[5,1152,128]{2,1,0:T(8,128)(2,1)S(1)}, u32[]{:S(2)}, u32[]{:S(2)}) collective-permute-start(bf16[5,1152,128]{2,1,0:T(8,128)(2,1)S(1)} %get-tuple-element.55.north_ref.refs_0_), channel_id=1, source_target_pairs={{0,4},{4,8},{8,12},{12,16},{16,20},{20,24},{24,28},{28,32},{32,36}... | collective-permute-start | bytes 4423688 | tf_op jit(solution)/shard_map/ppermute | solution.py:473
  63.5 1.9 collective-permute-start.8
  65.5 0.5 collective-permute-start.12
  65.9 0.5 collective-permute-start.13
  66.4 2.2 collective-permute-start.14
  68.6 11.2 %collective-permute-done.7.low_ref = bf16[5,1152,128]{2,1,0:T(8,128)(2,1)S(1)} collective-permute-done((bf16[5,1152,128]{2,1,0:T(8,128)(2,1)S(1)}, bf16[5,1152,128]{2,1,0:T(8,128)(2,1)S(1)}, u32[]{:S(2)}, u32[]{:S(2)}) %collective-permute-start.7) | collective-permute-done | bytes 1474592 | tf_op jit(solution)/shard_map/ppermute | solution.py:473
  79.8 6.5 %collective-permute-done.8.high_ref = bf16[5,1152,128]{2,1,0:T(8,128)(2,1)S(1)} collective-permute-done((bf16[5,1152,128]{2,1,0:T(8,128)(2,1)S(1)}, bf16[5,1152,128]{2,1,0:T(8,128)(2,1)S(1)}, u32[]{:S(2)}, u32[]{:S(2)}) %collective-permute-start.8) | collective-permute-done | bytes 1474592 | tf_op jit(solution)/shard_map/ppermute | solution.py:473
  86.3 5.3 %advect.7 = (bf16[2,144,512]{2,1,0:T(8,128)(2,1)S(1)}, bf16[2,144,512]{2,1,0:T(8,128)(2,1)S(1)}, bf16[2,144,512]{2,1,0:T(8,128)(2,1)S(1)}, bf16[2,144,512]{2,1,0:T(8,128)(2,1)S(1)}) custom-call(s32[1]{0:T(128)} %bitcast.place_ref, bf16[5,1152,128]{2,1,0:T(8,128)(2,1)S(1)} %get-tuple-element.54.south_ref, ...), custom_call_target="tpu_custom_call" | custom-call | flops 20000000 | bytes 4000000 | tf_op jit(solution)/shard_map/advect/pallas_call | solution.py:214
  91.7 0.1 collective-permute-start.10
  91.8 2.7 %collective-permute-start.11 = (bf16[2,144,512]{2,1,0:T(8,128)(2,1)S(1)}, bf16[2,144,512]{2,1,0:T(8,128)(2,1)S(1)}, u32[]{:S(2)}, u32[]{:S(2)}) collective-permute-start(bf16[2,144,512]{2,1,0:T(8,128)(2,1)S(1)} %get-tuple-element.59), channel_id=1, source_target_pairs={{0,3},{1,0},{2,1},{3,2},{4,7},{5,4},{6,5},{7,6},{8,11},{9,8},{10,9... | collective-permute-start | bytes 884744 | tf_op jit(solution)/shard_map/ppermute | solution.py:478
  94.5 0.0 collective-permute-start.9
  94.6 0.0 collective-permute-done.13.part2
  94.6 10.3 %physics.6 = bf16[16,72,512]{2,1,0:T(8,128)(2,1)S(1)} custom-call(s32[1]{0:T(128)} %bitcast.place_ref, f32[64]{0:T(128)S(1)} %copy-done, bf16[2,144,512]{2,1,0:T(8,128)(2,1)S(1)} %get-tuple-element.53.refs_0_.part0, bf16[2,144,512]{2,1,0:T(8,128)(2,1)S(1)} %collective-permute-done.12.part1, bf16[2,144,512]{2,1,0:T(8,128)(2,1)S(1)} %collective-permute-done.13.part2, ...), custom_call_target="tpu_custom_call" | custom-call | flops 1509949440 | bytes 8900000 | tf_op jit(solution)/shard_map/physics/pallas_call | solution.py:387
  104.9 5.4 %advect.8 = (bf16[2,144,512]{2,1,0:T(8,128)(2,1)S(1)}, bf16[2,144,512]{2,1,0:T(8,128)(2,1)S(1)}, bf16[2,144,512]{2,1,0:T(8,128)(2,1)S(1)}, bf16[2,144,512]{2,1,0:T(8,128)(2,1)S(1)}) custom-call(s32[1]{0:T(128)} %bitcast.place_ref, bf16[5,1152,128]{2,1,0:T(8,128)(2,1)S(1)} %get-tuple-element.54.south_ref, ...), custom_call_target="tpu_custom_call" | custom-call | flops 20000000 | bytes 4000000 | tf_op jit(solution)/shard_map/advect/pallas_call | solution.py:214
  110.2 0.1 collective-permute-start.18
  110.3 3.8 %collective-permute-start.19 = (bf16[2,144,512]{2,1,0:T(8,128)(2,1)S(1)}, bf16[2,144,512]{2,1,0:T(8,128)(2,1)S(1)}, u32[]{:S(2)}, u32[]{:S(2)}) collective-permute-start(bf16[2,144,512]{2,1,0:T(8,128)(2,1)S(1)} %get-tuple-element.69), channel_id=1, source_target_pairs={{0,2},{1,3},{2,0},{3,1},{4,6},{5,7},{6,4},{7,5},{8,10},{9,11},{10,... | collective-permute-start | bytes 884744 | tf_op jit(solution)/shard_map/ppermute | solution.py:478
  114.2 2.8 %collective-permute-start.24 = (bf16[1152,512]{1,0:T(8,128)(2,1)S(1)}, bf16[1152,512]{1,0:T(8,128)(2,1)}, u32[]{:S(2)}, u32[]{:S(2)}) collective-permute-start(bf16[1152,512]{1,0:T(8,128)(2,1)S(1)} %bitcast.35), channel_id=1, source_target_pairs={{0,64},{4,68},{8,72},{12,76},{16,80},{20,84},{24,88},{28,92},{32,9... | collective-permute-start | bytes 3538952 | tf_op jit(solution)/shard_map/ppermute | solution.py:483
  117.0 11.3 %physics.7 = bf16[16,72,512]{2,1,0:T(8,128)(2,1)} custom-call(s32[1]{0:T(128)} %bitcast.place_ref, f32[64]{0:T(128)S(1)} %copy-done, bf16[2,144,512]{2,1,0:T(8,128)(2,1)S(1)} %get-tuple-element.56.refs_0_.part0, bf16[2,144,512]{2,1,0:T(8,128)(2,1)S(1)} %collective-permute-done.9.part1, bf16[2,144,512]{2,1,0:T(8,128)(2,1)S(1)} %collective-permute-done.10.part2, ...), custom_call_target="tpu_custom_call" | custom-call | flops 1509949440 | bytes 8900000 | tf_op jit(solution)/shard_map/physics/pallas_call | solution.py:387
  128.3 0.2 collective-permute-start.23
  128.5 2.6 %advect.9 = (bf16[1,144,512]{2,1,0:T(8,128)(2,1)S(1)}, bf16[1,144,512]{2,1,0:T(8,128)(2,1)S(1)}, bf16[1,144,512]{2,1,0:T(8,128)(2,1)S(1)}, bf16[1,144,512]{2,1,0:T(8,128)(2,1)S(1)}) custom-call(s32[1]{0:T(128)} %bitcast.place_ref, bf16[5,1152,128]{2,1,0:T(8,128)(2,1)S(1)} %get-tuple-element.54.south_ref, ...), custom_call_target="tpu_custom_call" | custom-call | flops 10000000 | bytes 2000000 | tf_op jit(solution)/shard_map/advect/pallas_call | solution.py:214
  131.2 0.0 collective-permute-done.18.part1
  131.2 0.0 collective-permute-done.19.part2
  131.2 10.5 %physics.8 = bf16[16,72,512]{2,1,0:T(8,128)(2,1)S(1)} custom-call(s32[1]{0:T(128)} %bitcast.place_ref, f32[64]{0:T(128)S(1)} %copy-done, bf16[2,144,512]{2,1,0:T(8,128)(2,1)S(1)} %get-tuple-element.63.refs_0_.part0, bf16[2,144,512]{2,1,0:T(8,128)(2,1)S(1)} %collective-permute-done.18.part1, bf16[2,144,512]{2,1,0:T(8,128)(2,1)S(1)} %collective-permute-done.19.part2, ...), custom_call_target="tpu_custom_call" | custom-call | flops 1509949440 | bytes 8900000 | tf_op jit(solution)/shard_map/physics/pallas_call | solution.py:387
  141.7 2.8 %collective-permute-start.22 = (bf16[1152,512]{1,0:T(8,128)(2,1)S(1)}, bf16[1152,512]{1,0:T(8,128)(2,1)}, u32[]{:S(2)}, u32[]{:S(2)}) collective-permute-start(bf16[1152,512]{1,0:T(8,128)(2,1)S(1)} %bitcast.31), channel_id=1, source_target_pairs={{0,64},{4,68},{8,72},{12,76},{16,80},{20,84},{24,88},{28,92},{32,9... | collective-permute-start | bytes 3538952 | tf_op jit(solution)/shard_map/ppermute | solution.py:483
  144.6 1.4 collective-permute-start.15
  145.9 0.0 collective-permute-start.16
  146.0 7.1 %collective-permute-done.15.part1 = bf16[1,144,512]{2,1,0:T(8,128)(2,1)S(1)} collective-permute-done((bf16[1,144,512]{2,1,0:T(8,128)(2,1)S(1)}, bf16[1,144,512]{2,1,0:T(8,128)(2,1)S(1)}, u32[]{:S(2)}, u32[]{:S(2)}) %collective-permute-start.15) | collective-permute-done | bytes 147488 | tf_op jit(solution)/shard_map/ppermute | solution.py:478
  153.0 0.0 collective-permute-start.17
  153.0 0.2 collective-permute-start.25
  153.2 4.2 %collective-permute-done.17.part3 = bf16[1,144,512]{2,1,0:T(8,128)(2,1)S(1)} collective-permute-done((bf16[1,144,512]{2,1,0:T(8,128)(2,1)S(1)}, bf16[1,144,512]{2,1,0:T(8,128)(2,1)S(1)}, u32[]{:S(2)}, u32[]{:S(2)}) %collective-permute-start.17) | collective-permute-done | bytes 147488 | tf_op jit(solution)/shard_map/ppermute | solution.py:478
  157.4 7.8 %physics.9 = bf16[8,72,512]{2,1,0:T(8,128)(2,1)S(1)} custom-call(s32[1]{0:T(128)} %bitcast.place_ref, f32[64]{0:T(128)S(1)} %copy-done, bf16[1,144,512]{2,1,0:T(8,128)(2,1)S(1)} %get-tuple-element.64.refs_0_.part0, bf16[1,144,512]{2,1,0:T(8,128)(2,1)S(1)} %collective-permute-done.15.part1, bf16[1,144,512]{2,1,0:T(8,128)(2,1)S(1)} %collective-permute-done.16.part2, ...), custom_call_target="tpu_custom_call" | custom-call | flops 754974720 | bytes 7700000 | tf_op jit(solution)/shard_map/physics/pallas_call | solution.py:387
  165.2 0.2 collective-permute-start.21
  165.4 0.6 dynamic_slice.3.flag_ref
  166.0 41.0 %collective-permute-done.25.partner_ref = bf16[576,512]{1,0:T(8,128)(2,1)} collective-permute-done((bf16[576,512]{1,0:T(8,128)(2,1)S(1)}, bf16[576,512]{1,0:T(8,128)(2,1)}, u32[]{:S(2)}, u32[]{:S(2)}) %collective-permute-start.25) | collective-permute-done | bytes 589856 | tf_op jit(solution)/shard_map/ppermute | solution.py:483
  207.0 2.5 %choose.5.refs_0_ = bf16[4608,512]{1,0:T(8,128)(2,1)} custom-call(s32[1]{0:T(128)} %dynamic_slice.3.flag_ref, bf16[576,512]{1,0:T(8,128)(2,1)S(1)} %bitcast.39, bf16[576,512]{1,0:T(8,128)(2,1)} %collective-permute-done.25.partner_ref, bf16[576,512]{1,0:T(8,128)(2,1)S(1)} %bitcast.25), custom_call_target="tpu_custom_call" | custom-call | bytes 1200000 | tf_op jit(solution)/shard_map/choose/pallas_call | solution.py:451
  209.5 0.0 collective-permute-done.24.partner_ref
  209.5 2.8 %choose.6.refs_0_ = bf16[4608,512]{1,0:T(8,128)(2,1)} custom-call(s32[1]{0:T(128)} %dynamic_slice.3.flag_ref, bf16[1152,512]{1,0:T(8,128)(2,1)S(1)} %bitcast.36, bf16[1152,512]{1,0:T(8,128)(2,1)} %collective-permute-done.24.partner_ref, bf16[4608,512]{1,0:T(8,128)(2,1)} %choose.5.refs_0_, bf16[576,512]{1,0:T(8,128)(2,1)S(1)} %bitcast.26), custom_call_target="tpu_custom_call", output_to_operand_aliasing={{}: (3, {})} | custom-call | bytes 2400000 | tf_op jit(solution)/shard_map/choose/pallas_call | solution.py:451
  212.3 2.8 %choose.7.refs_0_ = bf16[4608,512]{1,0:T(8,128)(2,1)} custom-call(s32[1]{0:T(128)} %dynamic_slice.3.flag_ref, bf16[1152,512]{1,0:T(8,128)(2,1)} %bitcast.20.refs_0_.own_ref, bf16[1152,512]{1,0:T(8,128)(2,1)} %collective-permute-done.23.partner_ref, bf16[4608,512]{1,0:T(8,128)(2,1)} %choose.6.refs_0_, ...), custom_call_target="tpu_custom_call", output_to_operand_aliasing={{}: (3, {})} | custom-call | bytes 2400000 | tf_op jit(solution)/shard_map/choose/pallas_call | solution.py:451
  215.1 2.8 %choose.8.refs_0_ = bf16[4608,512]{1,0:T(8,128)(2,1)} custom-call(s32[1]{0:T(128)} %dynamic_slice.3.flag_ref, bf16[1152,512]{1,0:T(8,128)(2,1)S(1)} %bitcast.33, bf16[1152,512]{1,0:T(8,128)(2,1)} %collective-permute-done.22.partner_ref, bf16[4608,512]{1,0:T(8,128)(2,1)} %choose.7.refs_0_, bf16[576,512]{1,0:T(8,128)(2,1)S(1)} %bitcast.28), custom_call_target="tpu_custom_call", output_to_operand_aliasing={{}: (3, {})} | custom-call | bytes 2400000 | tf_op jit(solution)/shard_map/choose/pallas_call | solution.py:451
  217.9 0.0 collective-permute-done.21.partner_ref
  217.9 2.5 %choose.9 = bf16[4608,512]{1,0:T(8,128)(2,1)} custom-call(s32[1]{0:T(128)} %dynamic_slice.3.flag_ref, bf16[576,512]{1,0:T(8,128)(2,1)S(1)} %bitcast.29, bf16[576,512]{1,0:T(8,128)(2,1)} %collective-permute-done.21.partner_ref, bf16[4608,512]{1,0:T(8,128)(2,1)} %choose.8.refs_0_, bf16[576,512]{1,0:T(8,128)(2,1)S(1)} %bitcast.30), custom_call_target="tpu_custom_call", output_to_operand_aliasing={{}: (3, {})} | custom-call | bytes 1200000 | tf_op jit(solution)/shard_map/choose/pallas_call | solution.py:451
  (14 shorter events, 0.0 us)
Async XLA Ops:
  2.4 14.2 %copy-start = (f32[64]{0:T(128)S(1)}, f32[64]{0:T(128)}, u32[]{:S(2)}) copy-start(f32[64]{0:T(128)} %scav_ref.9) | copy-start | bytes 772
  4.3 37.4 %collective-permute-start.5 = (bf16[2,1152,128]{2,1,0:T(8,128)(2,1)S(1)}, bf16[2,1152,128]{2,1,0:T(8,128)(2,1)S(1)}, u32[]{:S(2)}, u32[]{:S(2)}) collective-permute-start(bf16[2,1152,128]{2,1,0:T(8,128)(2,1)S(1)} %get-tuple-element.41.refs_0_.north_ref), channel_id=1, source_target_pairs={{0,4},{4,8},{8,12},{12,16},{16,20},{20,24},{24,28},{28,32},{32,36}... | collective-permute-start | bytes 1769480 | tf_op jit(solution)/shard_map/ppermute | solution.py:473
  6.7 35.0 %collective-permute-start.6 = (bf16[2,1152,128]{2,1,0:T(8,128)(2,1)S(1)}, bf16[2,1152,128]{2,1,0:T(8,128)(2,1)S(1)}, u32[]{:S(2)}, u32[]{:S(2)}) collective-permute-start(bf16[2,1152,128]{2,1,0:T(8,128)(2,1)S(1)} %get-tuple-element.52.south_ref), channel_id=1, source_target_pairs={{4,0},{8,4},{12,8},{16,12},{20,16},{24,20},{28,24},{32,28},{36,32}... | collective-permute-start | bytes 1769480 | tf_op jit(solution)/shard_map/ppermute | solution.py:473
  8.9 14.7 %collective-permute-start.1 = (bf16[1,1296,128]{2,1,0:T(8,128)(2,1)}, bf16[1,1296,128]{2,1,0:T(8,128)(2,1)S(1)}, u32[]{:S(2)}, u32[]{:S(2)}) collective-permute-start(bf16[1,1296,128]{2,1,0:T(8,128)(2,1)} %get-tuple-element.38.south_ref), channel_id=1, source_target_pairs={{4,0},{8,4},{12,8},{16,12},{20,16},{24,20},{28,24},{32,28},{36,32}... | collective-permute-start | bytes 995336 | tf_op jit(solution)/shard_map/ppermute | solution.py:473
  12.5 7.7 %collective-permute-start = (bf16[1,1152,128]{2,1,0:T(8,128)(2,1)S(1)}, bf16[1,1152,128]{2,1,0:T(8,128)(2,1)}, u32[]{:S(2)}, u32[]{:S(2)}) collective-permute-start(bf16[1,1152,128]{2,1,0:T(8,128)(2,1)S(1)} %get-tuple-element.39.refs_0_.north_ref), channel_id=1, source_target_pairs={{0,4},{4,8},{8,12},{12,16},{16,20},{20,24},{24,28},{28,32},{32,36}... | collective-permute-start | bytes 884744 | tf_op jit(solution)/shard_map/ppermute | solution.py:473
  27.2 19.9 %collective-permute-start.2 = (bf16[1,144,512]{2,1,0:T(8,128)(2,1)S(1)}, bf16[1,144,512]{2,1,0:T(8,128)(2,1)S(1)}, u32[]{:S(2)}, u32[]{:S(2)}) collective-permute-start(bf16[1,144,512]{2,1,0:T(8,128)(2,1)S(1)} %get-tuple-element.43), channel_id=1, source_target_pairs={{0,1},{1,2},{2,3},{3,0},{4,5},{5,6},{6,7},{7,4},{8,9},{9,10},{10,1... | collective-permute-start | bytes 442376 | tf_op jit(solution)/shard_map/ppermute | solution.py:478
  28.6 18.5 %collective-permute-start.3 = (bf16[1,144,512]{2,1,0:T(8,128)(2,1)S(1)}, bf16[1,144,512]{2,1,0:T(8,128)(2,1)S(1)}, u32[]{:S(2)}, u32[]{:S(2)}) collective-permute-start(bf16[1,144,512]{2,1,0:T(8,128)(2,1)S(1)} %get-tuple-element.44), channel_id=1, source_target_pairs={{0,2},{1,3},{2,0},{3,1},{4,6},{5,7},{6,4},{7,5},{8,10},{9,11},{10,... | collective-permute-start | bytes 442376 | tf_op jit(solution)/shard_map/ppermute | solution.py:478
  31.2 15.9 %collective-permute-start.4 = (bf16[1,144,512]{2,1,0:T(8,128)(2,1)S(1)}, bf16[1,144,512]{2,1,0:T(8,128)(2,1)S(1)}, u32[]{:S(2)}, u32[]{:S(2)}) collective-permute-start(bf16[1,144,512]{2,1,0:T(8,128)(2,1)S(1)} %get-tuple-element.45), channel_id=1, source_target_pairs={{0,3},{1,0},{2,1},{3,2},{4,7},{5,4},{6,5},{7,6},{8,11},{9,8},{10,9... | collective-permute-start | bytes 442376 | tf_op jit(solution)/shard_map/ppermute | solution.py:478
  59.4 20.4 %collective-permute-start.7 = (bf16[5,1152,128]{2,1,0:T(8,128)(2,1)S(1)}, bf16[5,1152,128]{2,1,0:T(8,128)(2,1)S(1)}, u32[]{:S(2)}, u32[]{:S(2)}) collective-permute-start(bf16[5,1152,128]{2,1,0:T(8,128)(2,1)S(1)} %get-tuple-element.55.north_ref.refs_0_), channel_id=1, source_target_pairs={{0,4},{4,8},{8,12},{12,16},{16,20},{20,24},{24,28},{28,32},{32,36}... | collective-permute-start | bytes 4423688 | tf_op jit(solution)/shard_map/ppermute | solution.py:473
  63.5 22.8 %collective-permute-start.8 = (bf16[5,1152,128]{2,1,0:T(8,128)(2,1)S(1)}, bf16[5,1152,128]{2,1,0:T(8,128)(2,1)S(1)}, u32[]{:S(2)}, u32[]{:S(2)}) collective-permute-start(bf16[5,1152,128]{2,1,0:T(8,128)(2,1)S(1)} %get-tuple-element.54.south_ref), channel_id=1, source_target_pairs={{4,0},{8,4},{12,8},{16,12},{20,16},{24,20},{28,24},{32,28},{36,32}... | collective-permute-start | bytes 4423688 | tf_op jit(solution)/shard_map/ppermute | solution.py:473
  65.5 29.1 %collective-permute-start.12 = (bf16[2,144,512]{2,1,0:T(8,128)(2,1)S(1)}, bf16[2,144,512]{2,1,0:T(8,128)(2,1)S(1)}, u32[]{:S(2)}, u32[]{:S(2)}) collective-permute-start(bf16[2,144,512]{2,1,0:T(8,128)(2,1)S(1)} %get-tuple-element.60), channel_id=1, source_target_pairs={{0,1},{1,2},{2,3},{3,0},{4,5},{5,6},{6,7},{7,4},{8,9},{9,10},{10,1... | collective-permute-start | bytes 884744 | tf_op jit(solution)/shard_map/ppermute | solution.py:478
  65.9 28.6 %collective-permute-start.13 = (bf16[2,144,512]{2,1,0:T(8,128)(2,1)S(1)}, bf16[2,144,512]{2,1,0:T(8,128)(2,1)S(1)}, u32[]{:S(2)}, u32[]{:S(2)}) collective-permute-start(bf16[2,144,512]{2,1,0:T(8,128)(2,1)S(1)} %get-tuple-element.61), channel_id=1, source_target_pairs={{0,2},{1,3},{2,0},{3,1},{4,6},{5,7},{6,4},{7,5},{8,10},{9,11},{10,... | collective-permute-start | bytes 884744 | tf_op jit(solution)/shard_map/ppermute | solution.py:478
  66.4 28.1 %collective-permute-start.14 = (bf16[2,144,512]{2,1,0:T(8,128)(2,1)S(1)}, bf16[2,144,512]{2,1,0:T(8,128)(2,1)S(1)}, u32[]{:S(2)}, u32[]{:S(2)}) collective-permute-start(bf16[2,144,512]{2,1,0:T(8,128)(2,1)S(1)} %get-tuple-element.62), channel_id=1, source_target_pairs={{0,3},{1,0},{2,1},{3,2},{4,7},{5,4},{6,5},{7,6},{8,11},{9,8},{10,9... | collective-permute-start | bytes 884744 | tf_op jit(solution)/shard_map/ppermute | solution.py:478
  91.7 22.5 %collective-permute-start.10 = (bf16[2,144,512]{2,1,0:T(8,128)(2,1)S(1)}, bf16[2,144,512]{2,1,0:T(8,128)(2,1)S(1)}, u32[]{:S(2)}, u32[]{:S(2)}) collective-permute-start(bf16[2,144,512]{2,1,0:T(8,128)(2,1)S(1)} %get-tuple-element.58), channel_id=1, source_target_pairs={{0,2},{1,3},{2,0},{3,1},{4,6},{5,7},{6,4},{7,5},{8,10},{9,11},{10,... | collective-permute-start | bytes 884744 | tf_op jit(solution)/shard_map/ppermute | solution.py:478
  91.8 22.4 %collective-permute-start.11 = (bf16[2,144,512]{2,1,0:T(8,128)(2,1)S(1)}, bf16[2,144,512]{2,1,0:T(8,128)(2,1)S(1)}, u32[]{:S(2)}, u32[]{:S(2)}) collective-permute-start(bf16[2,144,512]{2,1,0:T(8,128)(2,1)S(1)} %get-tuple-element.59), channel_id=1, source_target_pairs={{0,3},{1,0},{2,1},{3,2},{4,7},{5,4},{6,5},{7,6},{8,11},{9,8},{10,9... | collective-permute-start | bytes 884744 | tf_op jit(solution)/shard_map/ppermute | solution.py:478
  94.5 22.4 %collective-permute-start.9 = (bf16[2,144,512]{2,1,0:T(8,128)(2,1)S(1)}, bf16[2,144,512]{2,1,0:T(8,128)(2,1)S(1)}, u32[]{:S(2)}, u32[]{:S(2)}) collective-permute-start(bf16[2,144,512]{2,1,0:T(8,128)(2,1)S(1)} %get-tuple-element.57), channel_id=1, source_target_pairs={{0,1},{1,2},{2,3},{3,0},{4,5},{5,6},{6,7},{7,4},{8,9},{9,10},{10,1... | collective-permute-start | bytes 884744 | tf_op jit(solution)/shard_map/ppermute | solution.py:478
  110.2 21.0 %collective-permute-start.18 = (bf16[2,144,512]{2,1,0:T(8,128)(2,1)S(1)}, bf16[2,144,512]{2,1,0:T(8,128)(2,1)S(1)}, u32[]{:S(2)}, u32[]{:S(2)}) collective-permute-start(bf16[2,144,512]{2,1,0:T(8,128)(2,1)S(1)} %get-tuple-element.68), channel_id=1, source_target_pairs={{0,1},{1,2},{2,3},{3,0},{4,5},{5,6},{6,7},{7,4},{8,9},{9,10},{10,1... | collective-permute-start | bytes 884744 | tf_op jit(solution)/shard_map/ppermute | solution.py:478
  110.3 20.9 %collective-permute-start.19 = (bf16[2,144,512]{2,1,0:T(8,128)(2,1)S(1)}, bf16[2,144,512]{2,1,0:T(8,128)(2,1)S(1)}, u32[]{:S(2)}, u32[]{:S(2)}) collective-permute-start(bf16[2,144,512]{2,1,0:T(8,128)(2,1)S(1)} %get-tuple-element.69), channel_id=1, source_target_pairs={{0,2},{1,3},{2,0},{3,1},{4,6},{5,7},{6,4},{7,5},{8,10},{9,11},{10,... | collective-permute-start | bytes 884744 | tf_op jit(solution)/shard_map/ppermute | solution.py:478
  114.2 17.1 %collective-permute-start.20 = (bf16[2,144,512]{2,1,0:T(8,128)(2,1)S(1)}, bf16[2,144,512]{2,1,0:T(8,128)(2,1)S(1)}, u32[]{:S(2)}, u32[]{:S(2)}) collective-permute-start(bf16[2,144,512]{2,1,0:T(8,128)(2,1)S(1)} %get-tuple-element.70), channel_id=1, source_target_pairs={{0,3},{1,0},{2,1},{3,2},{4,7},{5,4},{6,5},{7,6},{8,11},{9,8},{10,9... | collective-permute-start | bytes 884744 | tf_op jit(solution)/shard_map/ppermute | solution.py:478
  114.2 95.4 %collective-permute-start.24 = (bf16[1152,512]{1,0:T(8,128)(2,1)S(1)}, bf16[1152,512]{1,0:T(8,128)(2,1)}, u32[]{:S(2)}, u32[]{:S(2)}) collective-permute-start(bf16[1152,512]{1,0:T(8,128)(2,1)S(1)} %bitcast.35), channel_id=1, source_target_pairs={{0,64},{4,68},{8,72},{12,76},{16,80},{20,84},{24,88},{28,92},{32,9... | collective-permute-start | bytes 3538952 | tf_op jit(solution)/shard_map/ppermute | solution.py:483
  128.3 84.0 %collective-permute-start.23 = (bf16[1152,512]{1,0:T(8,128)(2,1)}, bf16[1152,512]{1,0:T(8,128)(2,1)}, u32[]{:S(2)}, u32[]{:S(2)}) collective-permute-start(bf16[1152,512]{1,0:T(8,128)(2,1)} %bitcast.20.refs_0_.own_ref), channel_id=1, source_target_pairs={{0,64},{4,68},{8,72},{12,76},{16,80},{20,84},{24,88},{28,92},{32,9... | collective-permute-start | bytes 3538952 | tf_op jit(solution)/shard_map/ppermute | solution.py:483
  141.7 73.4 %collective-permute-start.22 = (bf16[1152,512]{1,0:T(8,128)(2,1)S(1)}, bf16[1152,512]{1,0:T(8,128)(2,1)}, u32[]{:S(2)}, u32[]{:S(2)}) collective-permute-start(bf16[1152,512]{1,0:T(8,128)(2,1)S(1)} %bitcast.31), channel_id=1, source_target_pairs={{0,64},{4,68},{8,72},{12,76},{16,80},{20,84},{24,88},{28,92},{32,9... | collective-permute-start | bytes 3538952 | tf_op jit(solution)/shard_map/ppermute | solution.py:483
  144.6 8.5 %collective-permute-start.15 = (bf16[1,144,512]{2,1,0:T(8,128)(2,1)S(1)}, bf16[1,144,512]{2,1,0:T(8,128)(2,1)S(1)}, u32[]{:S(2)}, u32[]{:S(2)}) collective-permute-start(bf16[1,144,512]{2,1,0:T(8,128)(2,1)S(1)} %get-tuple-element.65), channel_id=1, source_target_pairs={{0,1},{1,2},{2,3},{3,0},{4,5},{5,6},{6,7},{7,4},{8,9},{9,10},{10,1... | collective-permute-start | bytes 442376 | tf_op jit(solution)/shard_map/ppermute | solution.py:478
  145.9 7.1 %collective-permute-start.16 = (bf16[1,144,512]{2,1,0:T(8,128)(2,1)S(1)}, bf16[1,144,512]{2,1,0:T(8,128)(2,1)S(1)}, u32[]{:S(2)}, u32[]{:S(2)}) collective-permute-start(bf16[1,144,512]{2,1,0:T(8,128)(2,1)S(1)} %get-tuple-element.66), channel_id=1, source_target_pairs={{0,2},{1,3},{2,0},{3,1},{4,6},{5,7},{6,4},{7,5},{8,10},{9,11},{10,... | collective-permute-start | bytes 442376 | tf_op jit(solution)/shard_map/ppermute | solution.py:478
  153.0 12.3 %copy-start.1 = (s32[64]{0:T(128)S(1)}, s32[64]{0:T(128)}, u32[]{:S(2)}) copy-start(s32[64]{0:T(128)} %param.19) | copy-start | bytes 772
  153.0 4.4 %collective-permute-start.17 = (bf16[1,144,512]{2,1,0:T(8,128)(2,1)S(1)}, bf16[1,144,512]{2,1,0:T(8,128)(2,1)S(1)}, u32[]{:S(2)}, u32[]{:S(2)}) collective-permute-start(bf16[1,144,512]{2,1,0:T(8,128)(2,1)S(1)} %get-tuple-element.67), channel_id=1, source_target_pairs={{0,3},{1,0},{2,1},{3,2},{4,7},{5,4},{6,5},{7,6},{8,11},{9,8},{10,9... | collective-permute-start | bytes 442376 | tf_op jit(solution)/shard_map/ppermute | solution.py:478
  153.0 54.0 %collective-permute-start.25 = (bf16[576,512]{1,0:T(8,128)(2,1)S(1)}, bf16[576,512]{1,0:T(8,128)(2,1)}, u32[]{:S(2)}, u32[]{:S(2)}) collective-permute-start(bf16[576,512]{1,0:T(8,128)(2,1)S(1)} %bitcast.38), channel_id=1, source_target_pairs={{0,64},{4,68},{8,72},{12,76},{16,80},{20,84},{24,88},{28,92},{32,9... | collective-permute-start | bytes 1769480 | tf_op jit(solution)/shard_map/ppermute | solution.py:483
  165.2 52.7 %collective-permute-start.21 = (bf16[576,512]{1,0:T(8,128)(2,1)S(1)}, bf16[576,512]{1,0:T(8,128)(2,1)}, u32[]{:S(2)}, u32[]{:S(2)}) collective-permute-start(bf16[576,512]{1,0:T(8,128)(2,1)S(1)} %bitcast.24), channel_id=1, source_target_pairs={{0,64},{4,68},{8,72},{12,76},{16,80},{20,84},{24,88},{28,92},{32,9... | collective-permute-start | bytes 1769480 | tf_op jit(solution)/shard_map/ppermute | solution.py:483

commit v6 on v5

--- a/solution.py
+++ b/solution.py
@@ -12,7 +12,7 @@
 
 GROUP = 8
 CHUNKS = (1, 2, 2, 2, 1)
-SPANS = ((0, 1), (1, 2), (3, 5))
+SPANS = ((0, 3), (3, 5))
 ORDER = (
     ("extract", 0),
     ("extract", 1),
@@ -20,9 +20,8 @@
     ("tables", 0),
     ("advect", 1),
     ("physics", 0),
-    ("extract", 2),
+    ("physics", 1),
     ("advect", 2),
-    ("physics", 1),
     ("advect", 3),
     ("physics", 2),
     ("advect", 4),
@@ -35,7 +34,7 @@
     ("choose", 4),
 )
 CAP = 256
-P_BLOCK = 16
+P_BLOCK = 32
 F32 = jnp.float32
 BF16 = jnp.bfloat16
 
@@ -192,18 +191,19 @@
                         )
                     )
             for lat in range(2):
-                spot = pl.multiple_of(k * 128 + (lat * 64 + t * 8), 16)
-                made[pl.ds(spot, 16), :] = jnp.concatenate(results[lat], axis=0)
+                for part in range(2):
+                    spot = ((lat * GROUP + t + part) * levels + k) * 8
+                    made[pl.ds(pl.multiple_of(spot, 8), 8), :] = results[lat][part]
         return carry
 
     lax.fori_loop(0, levels, body, 0)
     for shift, out in enumerate(outs):
         tile = 2 * lax.rem(place_ref[0] + shift, 4)
         for t, lat, half in itertools.product(range(GROUP), range(2), range(2)):
-            start = tile + (lat * 64 + t * 8 + half)
+            start = tile + (lat * GROUP + t) * levels * 8 + half
             column = (2 * lat + half) * 128
             out[0, t * levels : (t + 1) * levels, column : column + 128] = made[
-                pl.ds(start, levels, stride=128), :
+                pl.ds(start, levels, stride=8), :
             ].astype(BF16)
 
 
@@ -268,11 +268,15 @@
     all_ref[...] = rain.astype(F32)
     nothing = jnp.zeros((CAP, 128 - levels), F32)
     wet_ref[...] = jnp.concatenate([crossed(back, rain), nothing], axis=1)
+    gap = jnp.zeros((128 - levels, columns), BF16)
     for piece in range(pieces):
         copies[piece].wait()
-        for k in range(per_piece):
-            picked = crossed(back_ref[...], held[piece, k])
-            turned[pl.ds(k, CAP, stride=per_piece), :] = jnp.concatenate([picked, nothing], axis=1)
+        for k in range(0, per_piece, 2):
+            both = jnp.concatenate([held[piece, k], gap, held[piece, k + 1], gap], axis=0)
+            found = crossed(back_ref[...], both)
+            for part in range(2):
+                lanes = slice(part * 128, (part + 1) * 128)
+                turned[pl.ds(k + part, CAP, stride=per_piece), :] = found[:, lanes]
         spot = piece * per_piece
         small_ref[:, spot : spot + per_piece, :] = (
             turned[...].reshape(CAP, per_piece, 128).astype(BF16)
@@ -341,8 +345,12 @@
                         g, t * part : (t + 1) * part, :
                     ]
 
-    for t in range(tracers):
-        picked[t * CAP : (t + 1) * CAP, :] = crossed(picking_ref[...], columns_in[t])
+    for t in range(0, tracers, 2):
+        both = crossed(picking_ref[...], columns_in[t : t + 2].reshape(256, part0.shape[2]))
+        for part_at in range(2):
+            lanes = slice(part_at * 128, (part_at + 1) * 128)
+            g, row = divmod(t + part_at, GROUP)
+            picked[g, pl.ds(row, CAP, stride=GROUP), :] = both[:, lanes]
 
     rate = jnp.concatenate([rate_ref[first + g] for g in range(groups)], axis=0)
     nothing = jnp.zeros((128 - levels, 128), BF16)
@@ -350,30 +358,37 @@
     def contract(block, carry):
         for inner in range(P_BLOCK):
             p = block * P_BLOCK + inner
-            mine = picked[pl.ds(p, tracers, stride=CAP), :].astype(BF16)
+            spot = pl.ds(pl.multiple_of(p * GROUP, GROUP), GROUP)
+            mine = jnp.concatenate([picked[g, spot, :] for g in range(groups)], axis=0).astype(BF16)
             matrix = jnp.concatenate([matrix_ref[p], nothing], axis=0)
             wet = wet_ref[pl.ds(p, tracers, stride=0), :]
-            mixed[pl.ds(p, tracers, stride=CAP), :] = crossed(mine, matrix) * jnp.exp(-rate * wet)
+            washed = crossed(mine, matrix) * jnp.exp(-rate * wet)
+            for g in range(groups):
+                mixed[g, spot, :] = washed[g * GROUP : (g + 1) * GROUP]
         return carry
 
     lax.fori_loop(0, CAP // P_BLOCK, contract, 0)
 
-    def finish(block, carry):
-        for inner in range(2):
-            t = block * 2 + inner
-            spot = pl.multiple_of(t * CAP, CAP)
-            spread = lax.dot_general(
-                mixed[pl.ds(spot, CAP), :].astype(BF16),
-                back_ref[...],
-                (((0,), (0,)), ((), ())),
-                preferred_element_type=F32,
-            )[:levels]
-            plain = product(columns_in[t, :levels], placing_ref[...])
-            scav = scav_ref[first * GROUP + t]
-            out_ref[t] = (spread + plain * jnp.exp(-scav * rain_ref[...])).astype(BF16)
-        return carry
-
-    lax.fori_loop(0, tracers // 2, finish, 0)
+    for g in range(groups):
+
+        def finish(block, carry, g=g):
+            row = block * 2
+            at = g * GROUP + row
+            both = columns_in[pl.ds(at, 2)].reshape(256, columns_in.shape[2])
+            plain = product(both, placing_ref[...])
+            for inner in range(2):
+                spread = lax.dot_general(
+                    mixed[g, pl.ds(row + inner, CAP, stride=GROUP), :].astype(BF16),
+                    back_ref[...],
+                    (((0,), (0,)), ((), ())),
+                    preferred_element_type=F32,
+                )[:levels]
+                scav = scav_ref[first * GROUP + at + inner]
+                dry = plain[inner * 128 : inner * 128 + levels]
+                out_ref[at + inner] = (spread + dry * jnp.exp(-scav * rain_ref[...])).astype(BF16)
+            return carry
+
+        lax.fori_loop(0, GROUP // 2, finish, 0)
 
 
 def physics(place, scav, parts, made, rates, first, groups, after):
@@ -394,14 +409,14 @@
         out_specs=whole_block(tracers, levels, columns, once=True),
         scratch_shapes=[
             pltpu.VMEM((tracers, 128, columns), BF16),
-            pltpu.VMEM((tracers * CAP, 128), F32),
-            pltpu.VMEM((tracers * CAP, 128), F32),
+            pltpu.VMEM((groups, CAP * GROUP, 128), F32),
+            pltpu.VMEM((groups, CAP * GROUP, 128), F32),
         ],
         out_shape=jax.ShapeDtypeStruct((tracers, levels, columns), BF16),
         cost_estimate=pl.CostEstimate(
             flops=flops, bytes_accessed=groups * 1200000 + 6500000, transcendentals=0
         ),
-        compiler_params=pltpu.CompilerParams(vmem_limit_bytes=(9 + 8 * groups) << 20),
+        compiler_params=pltpu.CompilerParams(vmem_limit_bytes=(12 + 4 * groups) << 20),
         name="physics",
     )(place, scav, *parts, *operands, rates, *after)
 

time: 224 us -> 213 us (0.951)
  the two profiles are of different devices: /device:TPU:97 before, /device:TPU:0 now
where the time goes in v6:
time: 213 us; the launch traced here: 212 us
  Pallas kernels  96.5 us (45%)
  starting transfers between devices  50.6 us (24%)
  waiting for transfers between devices  49.3 us (23%)
  local copies, waits for them, and re-layouts  15.5 us (7%)
    ppermute x5, waiting for transfers between devices, paired(): lax.ppermute(value, axis, [(i, i ^ count // 2) for i in range(count)])  42 us
    pallas_call x5, Pallas kernels, physics(): pl.pallas_call(functools.partial(physics_kernel, first=first), grid=(1,),...  41.3 us
    pallas_call x5, Pallas kernels, advect(): pl.pallas_call(advect_kernel, grid=(groups,), in_specs=[pl.BlockSpec(memo...  24.2 us
    ppermute x15, starting transfers between devices, turned(): lax.ppermute(value, axis, [(i, (i + steps) % count) for i in range(count)])  23.2 us
    ppermute x5, starting transfers between devices, paired(): lax.ppermute(value, axis, [(i, i ^ count // 2) for i in range(count)])  17.1 us
    pallas_call x5, Pallas kernels, choose(): pl.pallas_call(functools.partial(choose_kernel, first=first * rows), in_s...  14 us
    unnamed x54, local copies, waits for them, and re-layouts  13.4 us
    ppermute x4, starting transfers between devices, shifted(): return lax.ppermute(value, axis, pairs)  10.3 us
  transfers between devices with their start and end apart: 24, of which 5 were waited for; matrix products, arithmetic and copies ran while one was open for 1% of the time, Pallas kernels for 40%

profile of v6, /device:TPU:0, one launch (start us, length us, event | category | flops | bytes accessed | tf_op | source)
XLA Modules:
  0.0 212.5 jit_solution(9015067534113183416)
XLA Ops:
  0.0 4.1 %extract.2 = (bf16[3,1152,128]{2,1,0:T(8,128)(2,1)S(1)}, bf16[3,1296,128]{2,1,0:T(8,128)(2,1)}, f32[4,144,128]{2,1,0:T(8,128)S(1)}) custom-call(bf16[256,256]{1,0:T(8,128)(2,1)} %constant.31.clone.apart_ref, bf16[288,288]{1,0:T(8,128)(2,1)} %constant.32.clone.face_move_ref, bf16[64,18,16,128]{3,2,1,0:T(8,128)(2,1)} %bitcast.34, ...), custom_call_target="tpu_custom_call" | custom-call | flops 3000000 | bytes 3600000 | tf_op jit(solution)/shard_map/extract/pallas_call | solution.py:108
  4.1 1.3 collective-permute-start.2
  5.4 4.0 %collective-permute-start.3 = (bf16[3,1152,128]{2,1,0:T(8,128)(2,1)S(1)}, bf16[3,1152,128]{2,1,0:T(8,128)(2,1)}, u32[]{:S(2)}, u32[]{:S(2)}) collective-permute-start(bf16[3,1152,128]{2,1,0:T(8,128)(2,1)S(1)} %get-tuple-element.36.refs_0_.north_ref), channel_id=1, source_target_pairs={{0,4},{4,8},{8,12},{12,16},{16,20},{20,24},{24,28},{28,32},{32,36}... | collective-permute-start | bytes 2654216 | tf_op jit(solution)/shard_map/ppermute | solution.py:488
  9.4 5.3 %extract.3 = (bf16[5,1152,128]{2,1,0:T(8,128)(2,1)S(1)}, bf16[5,1152,128]{2,1,0:T(8,128)(2,1)}) custom-call(bf16[256,256]{1,0:T(8,128)(2,1)} %constant.31.clone.apart_ref, bf16[288,288]{1,0:T(8,128)(2,1)} %constant.32.clone.face_move_ref, bf16[64,18,16,128]{3,2,1,0:T(8,128)(2,1)} %bitcast.35, bf16[18,16,128]{2,1,0:T(8,128)(2,1)} %bitcast.37, ...), custom_call_target="tpu_custom_call" | custom-call | flops 5000000 | bytes 6000000 | tf_op jit(solution)/shard_map/extract/pallas_call | solution.py:108
  14.7 3.8 %collective-permute-start = (bf16[5,1152,128]{2,1,0:T(8,128)(2,1)S(1)}, bf16[5,1152,128]{2,1,0:T(8,128)(2,1)}, u32[]{:S(2)}, u32[]{:S(2)}) collective-permute-start(bf16[5,1152,128]{2,1,0:T(8,128)(2,1)S(1)} %get-tuple-element.38.refs_0_.north_ref), channel_id=1, source_target_pairs={{0,4},{4,8},{8,12},{12,16},{16,20},{20,24},{24,28},{28,32},{32,36}... | collective-permute-start | bytes 4423688 | tf_op jit(solution)/shard_map/ppermute | solution.py:488
  18.5 1.3 collective-permute-start.1
  19.8 1.0 copy-done.6
  20.8 3.2 %advect.5 = (bf16[1,144,512]{2,1,0:T(8,128)(2,1)S(1)}, bf16[1,144,512]{2,1,0:T(8,128)(2,1)S(1)}, bf16[1,144,512]{2,1,0:T(8,128)(2,1)S(1)}, bf16[1,144,512]{2,1,0:T(8,128)(2,1)S(1)}) custom-call(s32[1]{0:T(128)} %bitcast.place_ref, bf16[3,1296,128]{2,1,0:T(8,128)(2,1)} %get-tuple-element.40.south_ref, ...), custom_call_target="tpu_custom_call" | custom-call | flops 10000000 | bytes 2000000 | tf_op jit(solution)/shard_map/advect/pallas_call | solution.py:214
  24.0 1.6 collective-permute-start.7
  25.7 2.9 %collective-permute-start.8 = (bf16[1,144,512]{2,1,0:T(8,128)(2,1)S(1)}, bf16[1,144,512]{2,1,0:T(8,128)(2,1)S(1)}, u32[]{:S(2)}, u32[]{:S(2)}) collective-permute-start(bf16[1,144,512]{2,1,0:T(8,128)(2,1)S(1)} %get-tuple-element.53), channel_id=1, source_target_pairs={{0,2},{1,3},{2,0},{3,1},{4,6},{5,7},{6,4},{7,5},{8,10},{9,11},{10,... | collective-permute-start | bytes 442376 | tf_op jit(solution)/shard_map/ppermute | solution.py:493
  28.6 1.3 collective-permute-start.9
  29.9 7.5 %tables.1 = (bf16[256,72,128]{2,1,0:T(8,128)(2,1)S(1)}, bf16[512,512]{1,0:T(8,128)(2,1)S(1)}, bf16[256,512]{1,0:T(8,128)(2,1)S(1)}, bf16[256,512]{1,0:T(8,128)(2...) custom-call(bf16[72,72,512]{2,1,0:T(8,128)(2,1)} %matrix_ref.1, s32[1,512]{1,0:T(1,128)} %bitcast.40, ...), custom_call_target="tpu_custom_call" | custom-call | flops 2415919104 | bytes 12000000 | tf_op jit(solution)/shard_map/tables/pallas_call | solution.py:301
  37.4 0.0 copy-start
  37.5 6.6 %advect.6 = (bf16[2,144,512]{2,1,0:T(8,128)(2,1)S(1)}, bf16[2,144,512]{2,1,0:T(8,128)(2,1)}, bf16[2,144,512]{2,1,0:T(8,128)(2,1)}, bf16[2,144,512]{2,1,0:T(8,128)(2,1)}) custom-call(s32[1]{0:T(128)} %bitcast.place_ref, bf16[3,1296,128]{2,1,0:T(8,128)(2,1)} %get-tuple-element.40.south_ref, bf16[3,1152,128]{2,1,0:T(8,128)(2,1)S(1)} %copy-done.4, ...), custom_call_target="tpu_custom_call" | custom-call | flops 20000000 | bytes 4000000 | tf_op jit(solution)/shard_map/advect/pallas_call | solution.py:214
  44.2 0.7 copy-done.15
  44.9 0.7 copy-done.19
  45.6 0.7 collective-permute-start.4
  46.3 0.7 copy-done.21
  46.9 0.8 collective-permute-start.5
  47.7 0.6 copy-done.23
  48.4 1.9 collective-permute-start.6
  50.3 0.7 broadcast_in_dim.7
  50.9 0.7 broadcast_in_dim.8.rate_ref
  51.7 2.3 %copy-done.1 = bf16[256,72,128]{2,1,0:T(8,128)(2,1)S(1)} copy-done((bf16[256,72,128]{2,1,0:T(8,128)(2,1)S(1)}, bf16[256,72,128]{2,1,0:T(8,128)(2,1)}, u32[]{:S(2)}) %copy-start.1) | copy-done | bytes 4718616
  54.0 0.9 copy-done.9
  55.0 0.9 copy-done.11
  55.9 0.9 copy-done.14
  56.8 1.0 copy-done.16
  57.8 0.9 copy-done.18
  58.7 0.9 copy-done.20
  59.6 0.9 copy-done.22
  60.5 0.9 copy-done.24
  61.4 7.2 %physics.5 = bf16[8,72,512]{2,1,0:T(8,128)(2,1)} custom-call(s32[1]{0:T(128)} %bitcast.place_ref, f32[64]{0:T(128)S(1)} %copy-done.25, bf16[1,144,512]{2,1,0:T(8,128)(2,1)S(1)} %copy-done.18, bf16[1,144,512]{2,1,0:T(8,128)(2,1)S(1)} %copy-done.20, bf16[1,144,512]{2,1,0:T(8,128)(2,1)S(1)} %copy-done.22, bf16[1,144,512]{2,1,0:T(8,128)(2,1)S(1)} %copy-done.24, ...), custom_call_target="tpu_custom_call" | custom-call | flops 754974720 | bytes 7700000 | tf_op jit(solution)/shard_map/physics/pallas_call | solution.py:402
  68.6 10.2 %physics.6 = bf16[16,72,512]{2,1,0:T(8,128)(2,1)} custom-call(s32[1]{0:T(128)} %bitcast.place_ref, f32[64]{0:T(128)S(1)} %copy-done.25, bf16[2,144,512]{2,1,0:T(8,128)(2,1)S(1)} %copy-done.16, bf16[2,144,512]{2,1,0:T(8,128)(2,1)} %collective-permute-done.4.part1, bf16[2,144,512]{2,1,0:T(8,128)(2,1)} %collective-permute-done.5.part2, ...), custom_call_target="tpu_custom_call" | custom-call | flops 1509949440 | bytes 8900000 | tf_op jit(solution)/shard_map/physics/pallas_call | solution.py:402
  78.8 5.5 %advect.7 = (bf16[2,144,512]{2,1,0:T(8,128)(2,1)S(1)}, bf16[2,144,512]{2,1,0:T(8,128)(2,1)S(1)}, bf16[2,144,512]{2,1,0:T(8,128)(2,1)S(1)}, bf16[2,144,512]{2,1,0:T(8,128)(2,1)S(1)}) custom-call(s32[1]{0:T(128)} %bitcast.place_ref, bf16[5,1152,128]{2,1,0:T(8,128)(2,1)} %get-tuple-element.37.south_ref, ...), custom_call_target="tpu_custom_call" | custom-call | flops 20000000 | bytes 4000000 | tf_op jit(solution)/shard_map/advect/pallas_call | solution.py:214
  84.3 0.8 collective-permute-start.10
  85.1 2.2 %collective-permute-start.11 = (bf16[2,144,512]{2,1,0:T(8,128)(2,1)S(1)}, bf16[2,144,512]{2,1,0:T(8,128)(2,1)S(1)}, u32[]{:S(2)}, u32[]{:S(2)}) collective-permute-start(bf16[2,144,512]{2,1,0:T(8,128)(2,1)S(1)} %get-tuple-element.57), channel_id=1, source_target_pairs={{0,2},{1,3},{2,0},{3,1},{4,6},{5,7},{6,4},{7,5},{8,10},{9,11},{10,... | collective-permute-start | bytes 884744 | tf_op jit(solution)/shard_map/ppermute | solution.py:493
  87.3 2.5 %collective-permute-start.12 = (bf16[2,144,512]{2,1,0:T(8,128)(2,1)S(1)}, bf16[2,144,512]{2,1,0:T(8,128)(2,1)S(1)}, u32[]{:S(2)}, u32[]{:S(2)}) collective-permute-start(bf16[2,144,512]{2,1,0:T(8,128)(2,1)S(1)} %get-tuple-element.58), channel_id=1, source_target_pairs={{0,3},{1,0},{2,1},{3,2},{4,7},{5,4},{6,5},{7,6},{8,11},{9,8},{10,9... | collective-permute-start | bytes 884744 | tf_op jit(solution)/shard_map/ppermute | solution.py:493
  89.8 5.5 %advect.8 = (bf16[2,144,512]{2,1,0:T(8,128)(2,1)S(1)}, bf16[2,144,512]{2,1,0:T(8,128)(2,1)S(1)}, bf16[2,144,512]{2,1,0:T(8,128)(2,1)S(1)}, bf16[2,144,512]{2,1,0:T(8,128)(2,1)S(1)}) custom-call(s32[1]{0:T(128)} %bitcast.place_ref, bf16[5,1152,128]{2,1,0:T(8,128)(2,1)} %get-tuple-element.37.south_ref, ...), custom_call_target="tpu_custom_call" | custom-call | flops 20000000 | bytes 4000000 | tf_op jit(solution)/shard_map/advect/pallas_call | solution.py:214
  95.4 0.1 collective-permute-start.16
  95.4 1.5 collective-permute-start.17
  96.9 3.3 %collective-permute-done.10.part1 = bf16[2,144,512]{2,1,0:T(8,128)(2,1)S(1)} collective-permute-done((bf16[2,144,512]{2,1,0:T(8,128)(2,1)S(1)}, bf16[2,144,512]{2,1,0:T(8,128)(2,1)S(1)}, u32[]{:S(2)}, u32[]{:S(2)}) %collective-permute-start.10) | collective-permute-done | bytes 294944 | tf_op jit(solution)/shard_map/ppermute | solution.py:493
  100.2 1.3 collective-permute-done.11.part2
  101.5 7.9 %collective-permute-start.22 = (bf16[1152,512]{1,0:T(8,128)(2,1)}, bf16[1152,512]{1,0:T(8,128)(2,1)}, u32[]{:S(2)}, u32[]{:S(2)}) collective-permute-start(bf16[1152,512]{1,0:T(8,128)(2,1)} %bitcast.19.refs_0_.own_ref), channel_id=1, source_target_pairs={{0,64},{4,68},{8,72},{12,76},{16,80},{20,84},{24,88},{28,92},{32,9... | collective-permute-start | bytes 3538952 | tf_op jit(solution)/shard_map/ppermute | solution.py:498
  109.4 9.3 %physics.7 = bf16[16,72,512]{2,1,0:T(8,128)(2,1)} custom-call(s32[1]{0:T(128)} %bitcast.place_ref, f32[64]{0:T(128)S(1)} %copy-done.25, bf16[2,144,512]{2,1,0:T(8,128)(2,1)S(1)} %get-tuple-element.55.refs_0_.part0, bf16[2,144,512]{2,1,0:T(8,128)(2,1)S(1)} %collective-permute-done.10.part1, bf16[2,144,512]{2,1,0:T(8,128)(2,1)S(1)} %collective-permute-done.11.part2, ...), custom_call_target="tpu_custom_call" | custom-call | flops 1509949440 | bytes 8900000 | tf_op jit(solution)/shard_map/physics/pallas_call | solution.py:402
  118.7 2.6 %collective-permute-start.21 = (bf16[1152,512]{1,0:T(8,128)(2,1)}, bf16[1152,512]{1,0:T(8,128)(2,1)}, u32[]{:S(2)}, u32[]{:S(2)}) collective-permute-start(bf16[1152,512]{1,0:T(8,128)(2,1)} %bitcast.20.refs_0_.own_ref), channel_id=1, source_target_pairs={{0,64},{4,68},{8,72},{12,76},{16,80},{20,84},{24,88},{28,92},{32,9... | collective-permute-start | bytes 3538952 | tf_op jit(solution)/shard_map/ppermute | solution.py:498
  121.4 3.3 %advect.9 = (bf16[1,144,512]{2,1,0:T(8,128)(2,1)S(1)}, bf16[1,144,512]{2,1,0:T(8,128)(2,1)S(1)}, bf16[1,144,512]{2,1,0:T(8,128)(2,1)S(1)}, bf16[1,144,512]{2,1,0:T(8,128)(2,1)S(1)}) custom-call(s32[1]{0:T(128)} %bitcast.place_ref, bf16[5,1152,128]{2,1,0:T(8,128)(2,1)} %get-tuple-element.37.south_ref, ...), custom_call_target="tpu_custom_call" | custom-call | flops 10000000 | bytes 2000000 | tf_op jit(solution)/shard_map/advect/pallas_call | solution.py:214
  124.7 8.3 %physics.8 = bf16[16,72,512]{2,1,0:T(8,128)(2,1)S(1)} custom-call(s32[1]{0:T(128)} %bitcast.place_ref, f32[64]{0:T(128)S(1)} %copy-done.25, bf16[2,144,512]{2,1,0:T(8,128)(2,1)S(1)} %get-tuple-element.59.refs_0_.part0, bf16[2,144,512]{2,1,0:T(8,128)(2,1)S(1)} %collective-permute-done.16.part1, bf16[2,144,512]{2,1,0:T(8,128)(2,1)S(1)} %collective-permute-done.17.part2, ...), custom_call_target="tpu_custom_call" | custom-call | flops 1509949440 | bytes 8900000 | tf_op jit(solution)/shard_map/physics/pallas_call | solution.py:402
  133.0 1.0 collective-permute-start.20
  134.0 0.9 collective-permute-start.13
  134.9 3.9 %collective-permute-start.14 = (bf16[1,144,512]{2,1,0:T(8,128)(2,1)S(1)}, bf16[1,144,512]{2,1,0:T(8,128)(2,1)S(1)}, u32[]{:S(2)}, u32[]{:S(2)}) collective-permute-start(bf16[1,144,512]{2,1,0:T(8,128)(2,1)S(1)} %get-tuple-element.62), channel_id=1, source_target_pairs={{0,2},{1,3},{2,0},{3,1},{4,6},{5,7},{6,4},{7,5},{8,10},{9,11},{10,... | collective-permute-start | bytes 442376 | tf_op jit(solution)/shard_map/ppermute | solution.py:493
  138.8 1.7 collective-permute-done.13.part1
  140.5 2.0 collective-permute-start.15
  142.5 1.0 collective-permute-done.14.part2
  143.5 3.4 %collective-permute-start.23 = (bf16[576,512]{1,0:T(8,128)(2,1)}, bf16[576,512]{1,0:T(8,128)(2,1)}, u32[]{:S(2)}, u32[]{:S(2)}) collective-permute-start(bf16[576,512]{1,0:T(8,128)(2,1)} %bitcast.18.refs_0_.own_ref), channel_id=1, source_target_pairs={{0,64},{4,68},{8,72},{12,76},{16,80},{20,84},{24,88},{28,92},{32,9... | collective-permute-start | bytes 1769480 | tf_op jit(solution)/shard_map/ppermute | solution.py:498
  147.0 6.3 %physics.9 = bf16[8,72,512]{2,1,0:T(8,128)(2,1)S(1)} custom-call(s32[1]{0:T(128)} %bitcast.place_ref, f32[64]{0:T(128)S(1)} %copy-done.25, bf16[1,144,512]{2,1,0:T(8,128)(2,1)S(1)} %get-tuple-element.60.refs_0_.part0, bf16[1,144,512]{2,1,0:T(8,128)(2,1)S(1)} %collective-permute-done.13.part1, bf16[1,144,512]{2,1,0:T(8,128)(2,1)S(1)} %collective-permute-done.14.part2, ...), custom_call_target="tpu_custom_call" | custom-call | flops 754974720 | bytes 7700000 | tf_op jit(solution)/shard_map/physics/pallas_call | solution.py:402
  153.3 2.2 %collective-permute-start.19 = (bf16[576,512]{1,0:T(8,128)(2,1)S(1)}, bf16[576,512]{1,0:T(8,128)(2,1)S(1)}, u32[]{:S(2)}, u32[]{:S(2)}) collective-permute-start(bf16[576,512]{1,0:T(8,128)(2,1)S(1)} %bitcast.24), channel_id=1, source_target_pairs={{0,64},{4,68},{8,72},{12,76},{16,80},{20,84},{24,88},{28,92},{32,9... | collective-permute-start | bytes 1769480 | tf_op jit(solution)/shard_map/ppermute | solution.py:498
  155.5 0.7 dynamic_slice.3.flag_ref
  156.2 42.0 %collective-permute-done.23.partner_ref = bf16[576,512]{1,0:T(8,128)(2,1)} collective-permute-done((bf16[576,512]{1,0:T(8,128)(2,1)}, bf16[576,512]{1,0:T(8,128)(2,1)}, u32[]{:S(2)}, u32[]{:S(2)}) %collective-permute-start.23) | collective-permute-done | bytes 589856 | tf_op jit(solution)/shard_map/ppermute | solution.py:498
  198.2 2.6 %choose.5.refs_0_ = bf16[4608,512]{1,0:T(8,128)(2,1)} custom-call(s32[1]{0:T(128)} %dynamic_slice.3.flag_ref, bf16[576,512]{1,0:T(8,128)(2,1)} %bitcast.18.refs_0_.own_ref, bf16[576,512]{1,0:T(8,128)(2,1)} %collective-permute-done.23.partner_ref, bf16[576,512]{1,0:T(8,128)(2,1)S(1)} %bitcast.25), custom_call_target="tpu_custom_call" | custom-call | bytes 1200000 | tf_op jit(solution)/shard_map/choose/pallas_call | solution.py:466
  200.8 2.9 %choose.6.refs_0_ = bf16[4608,512]{1,0:T(8,128)(2,1)} custom-call(s32[1]{0:T(128)} %dynamic_slice.3.flag_ref, bf16[1152,512]{1,0:T(8,128)(2,1)} %bitcast.19.refs_0_.own_ref, bf16[1152,512]{1,0:T(8,128)(2,1)} %collective-permute-done.22.partner_ref, bf16[4608,512]{1,0:T(8,128)(2,1)} %choose.5.refs_0_, ...), custom_call_target="tpu_custom_call", output_to_operand_aliasing={{}: (3, {})} | custom-call | bytes 2400000 | tf_op jit(solution)/shard_map/choose/pallas_call | solution.py:466
  203.7 2.9 %choose.7.refs_0_ = bf16[4608,512]{1,0:T(8,128)(2,1)} custom-call(s32[1]{0:T(128)} %dynamic_slice.3.flag_ref, bf16[1152,512]{1,0:T(8,128)(2,1)} %bitcast.20.refs_0_.own_ref, bf16[1152,512]{1,0:T(8,128)(2,1)} %collective-permute-done.21.partner_ref, bf16[4608,512]{1,0:T(8,128)(2,1)} %choose.6.refs_0_, ...), custom_call_target="tpu_custom_call", output_to_operand_aliasing={{}: (3, {})} | custom-call | bytes 2400000 | tf_op jit(solution)/shard_map/choose/pallas_call | solution.py:466
  206.6 3.4 %choose.8.refs_0_ = bf16[4608,512]{1,0:T(8,128)(2,1)} custom-call(s32[1]{0:T(128)} %dynamic_slice.3.flag_ref, bf16[1152,512]{1,0:T(8,128)(2,1)S(1)} %bitcast.33, bf16[1152,512]{1,0:T(8,128)(2,1)} %collective-permute-done.20.partner_ref, bf16[4608,512]{1,0:T(8,128)(2,1)} %choose.7.refs_0_, bf16[576,512]{1,0:T(8,128)(2,1)S(1)} %bitcast.28), custom_call_target="tpu_custom_call", output_to_operand_aliasing={{}: (3, {})} | custom-call | bytes 2400000 | tf_op jit(solution)/shard_map/choose/pallas_call | solution.py:466
  210.0 2.3 %choose.9 = bf16[4608,512]{1,0:T(8,128)(2,1)} custom-call(s32[1]{0:T(128)} %dynamic_slice.3.flag_ref, bf16[576,512]{1,0:T(8,128)(2,1)S(1)} %bitcast.29, bf16[576,512]{1,0:T(8,128)(2,1)S(1)} %collective-permute-done.19.partner_ref, bf16[4608,512]{1,0:T(8,128)(2,1)} %choose.8.refs_0_, bf16[576,512]{1,0:T(8,128)(2,1)S(1)} %bitcast.30), custom_call_target="tpu_custom_call", output_to_operand_aliasing={{}: (3, {})} | custom-call | bytes 1200000 | tf_op jit(solution)/shard_map/choose/pallas_call | solution.py:466
  (59 shorter events, 0.1 us)
Async XLA Ops:
  4.1 10.6 %copy-start.5 = (f32[4,144,128]{2,1,0:T(8,128)}, f32[4,144,128]{2,1,0:T(8,128)S(1)}, u32[]{:S(2)}) copy-start(f32[4,144,128]{2,1,0:T(8,128)S(1)} %get-tuple-element.39.faces_ref) | copy-start | bytes 884740
  4.1 15.7 %copy-start.3 = (bf16[3,1152,128]{2,1,0:T(8,128)(2,1)}, bf16[3,1152,128]{2,1,0:T(8,128)(2,1)S(1)}, u32[]{:S(2)}) copy-start(bf16[3,1152,128]{2,1,0:T(8,128)(2,1)S(1)} %get-tuple-element.36.refs_0_.north_ref) | copy-start | bytes 2654212
  4.1 15.7 %collective-permute-start.2 = (bf16[3,1296,128]{2,1,0:T(8,128)(2,1)}, bf16[3,1296,128]{2,1,0:T(8,128)(2,1)S(1)}, u32[]{:S(2)}, u32[]{:S(2)}) collective-permute-start(bf16[3,1296,128]{2,1,0:T(8,128)(2,1)} %get-tuple-element.40.south_ref), channel_id=1, source_target_pairs={{4,0},{8,4},{12,8},{16,12},{20,16},{24,20},{28,24},{32,28},{36,32}... | collective-permute-start | bytes 2985992 | tf_op jit(solution)/shard_map/ppermute | solution.py:488
  5.4 14.4 %collective-permute-start.3 = (bf16[3,1152,128]{2,1,0:T(8,128)(2,1)S(1)}, bf16[3,1152,128]{2,1,0:T(8,128)(2,1)}, u32[]{:S(2)}, u32[]{:S(2)}) collective-permute-start(bf16[3,1152,128]{2,1,0:T(8,128)(2,1)S(1)} %get-tuple-element.36.refs_0_.north_ref), channel_id=1, source_target_pairs={{0,4},{4,8},{8,12},{12,16},{16,20},{20,24},{24,28},{28,32},{32,36}... | collective-permute-start | bytes 2654216 | tf_op jit(solution)/shard_map/ppermute | solution.py:488
  14.7 64.0 %collective-permute-start = (bf16[5,1152,128]{2,1,0:T(8,128)(2,1)S(1)}, bf16[5,1152,128]{2,1,0:T(8,128)(2,1)}, u32[]{:S(2)}, u32[]{:S(2)}) collective-permute-start(bf16[5,1152,128]{2,1,0:T(8,128)(2,1)S(1)} %get-tuple-element.38.refs_0_.north_ref), channel_id=1, source_target_pairs={{0,4},{4,8},{8,12},{12,16},{16,20},{20,24},{24,28},{28,32},{32,36}... | collective-permute-start | bytes 4423688 | tf_op jit(solution)/shard_map/ppermute | solution.py:488
  18.5 60.3 %collective-permute-start.1 = (bf16[5,1152,128]{2,1,0:T(8,128)(2,1)}, bf16[5,1152,128]{2,1,0:T(8,128)(2,1)}, u32[]{:S(2)}, u32[]{:S(2)}) collective-permute-start(bf16[5,1152,128]{2,1,0:T(8,128)(2,1)} %get-tuple-element.37.south_ref), channel_id=1, source_target_pairs={{4,0},{8,4},{12,8},{16,12},{20,16},{24,20},{28,24},{32,28},{36,32}... | collective-permute-start | bytes 4423688 | tf_op jit(solution)/shard_map/ppermute | solution.py:488
  19.8 1.0 copy-start.6
  24.0 13.4 %copy-start.17 = (bf16[1,144,512]{2,1,0:T(8,128)(2,1)}, bf16[1,144,512]{2,1,0:T(8,128)(2,1)S(1)}, u32[]{:S(2)}) copy-start(bf16[1,144,512]{2,1,0:T(8,128)(2,1)S(1)} %get-tuple-element.41.refs_0_.part0) | copy-start | bytes 442372
  24.0 20.9 %collective-permute-start.7 = (bf16[1,144,512]{2,1,0:T(8,128)(2,1)S(1)}, bf16[1,144,512]{2,1,0:T(8,128)(2,1)S(1)}, u32[]{:S(2)}, u32[]{:S(2)}) collective-permute-start(bf16[1,144,512]{2,1,0:T(8,128)(2,1)S(1)} %get-tuple-element.52), channel_id=1, source_target_pairs={{0,1},{1,2},{2,3},{3,0},{4,5},{5,6},{6,7},{7,4},{8,9},{9,10},{10,1... | collective-permute-start | bytes 442376 | tf_op jit(solution)/shard_map/ppermute | solution.py:493
  25.7 20.6 %collective-permute-start.8 = (bf16[1,144,512]{2,1,0:T(8,128)(2,1)S(1)}, bf16[1,144,512]{2,1,0:T(8,128)(2,1)S(1)}, u32[]{:S(2)}, u32[]{:S(2)}) collective-permute-start(bf16[1,144,512]{2,1,0:T(8,128)(2,1)S(1)} %get-tuple-element.53), channel_id=1, source_target_pairs={{0,2},{1,3},{2,0},{3,1},{4,6},{5,7},{6,4},{7,5},{8,10},{9,11},{10,... | collective-permute-start | bytes 442376 | tf_op jit(solution)/shard_map/ppermute | solution.py:493
  28.6 19.2 %collective-permute-start.9 = (bf16[1,144,512]{2,1,0:T(8,128)(2,1)S(1)}, bf16[1,144,512]{2,1,0:T(8,128)(2,1)S(1)}, u32[]{:S(2)}, u32[]{:S(2)}) collective-permute-start(bf16[1,144,512]{2,1,0:T(8,128)(2,1)S(1)} %get-tuple-element.54), channel_id=1, source_target_pairs={{0,3},{1,0},{2,1},{3,2},{4,7},{5,4},{6,5},{7,6},{8,11},{9,8},{10,9... | collective-permute-start | bytes 442376 | tf_op jit(solution)/shard_map/ppermute | solution.py:493
  29.9 7.6 %copy-start.4 = (bf16[3,1152,128]{2,1,0:T(8,128)(2,1)S(1)}, bf16[3,1152,128]{2,1,0:T(8,128)(2,1)}, u32[]{:S(2)}) copy-start(bf16[3,1152,128]{2,1,0:T(8,128)(2,1)} %copy-done.3) | copy-start | bytes 2654212
  29.9 7.6 %copy-start.7 = (f32[4,144,128]{2,1,0:T(8,128)S(1)}, f32[4,144,128]{2,1,0:T(8,128)}, u32[]{:S(2)}) copy-start(f32[4,144,128]{2,1,0:T(8,128)} %copy-done.5) | copy-start | bytes 884740
  37.4 6.7 %copy-start = (bf16[256,72,128]{2,1,0:T(8,128)(2,1)}, bf16[256,72,128]{2,1,0:T(8,128)(2,1)S(1)}, u32[]{:S(2)}) copy-start(bf16[256,72,128]{2,1,0:T(8,128)(2,1)S(1)} %get-tuple-element.49.matrix_ref) | copy-start | bytes 14155780
  37.4 6.7 %copy-start.8 = (bf16[256,512]{1,0:T(8,128)(2,1)}, bf16[256,512]{1,0:T(8,128)(2,1)S(1)}, u32[]{:S(2)}) copy-start(bf16[256,512]{1,0:T(8,128)(2,1)S(1)} %get-tuple-element.48.back_ref) | copy-start | bytes 786436
  37.5 6.7 %copy-start.10 = (f32[72,512]{1,0:T(8,128)}, f32[72,512]{1,0:T(8,128)S(1)}, u32[]{:S(2)}) copy-start(f32[72,512]{1,0:T(8,128)S(1)} %get-tuple-element.50.rain_ref) | copy-start | bytes 442372
  37.5 6.7 %copy-start.13 = (f32[256,128]{1,0:T(8,128)}, f32[256,128]{1,0:T(8,128)S(1)}, u32[]{:S(2)}) copy-start(f32[256,128]{1,0:T(8,128)S(1)} %get-tuple-element.51.wet_ref) | copy-start | bytes 393220
  37.5 12.8 %copy-start.25 = (f32[64]{0:T(128)S(1)}, f32[64]{0:T(128)}, u32[]{:S(2)}) copy-start(f32[64]{0:T(128)} %scav_ref.9) | copy-start | bytes 772
  44.2 0.7 copy-start.15
  44.9 0.7 copy-start.19
  45.6 23.0 %collective-permute-start.4 = (bf16[2,144,512]{2,1,0:T(8,128)(2,1)}, bf16[2,144,512]{2,1,0:T(8,128)(2,1)}, u32[]{:S(2)}, u32[]{:S(2)}) collective-permute-start(bf16[2,144,512]{2,1,0:T(8,128)(2,1)} %get-tuple-element.44), channel_id=1, source_target_pairs={{0,1},{1,2},{2,3},{3,0},{4,5},{5,6},{6,7},{7,4},{8,9},{9,10},{10,1... | collective-permute-start | bytes 884744 | tf_op jit(solution)/shard_map/ppermute | solution.py:493
  46.3 0.7 copy-start.21
  46.9 21.6 %collective-permute-start.5 = (bf16[2,144,512]{2,1,0:T(8,128)(2,1)}, bf16[2,144,512]{2,1,0:T(8,128)(2,1)}, u32[]{:S(2)}, u32[]{:S(2)}) collective-permute-start(bf16[2,144,512]{2,1,0:T(8,128)(2,1)} %get-tuple-element.45), channel_id=1, source_target_pairs={{0,2},{1,3},{2,0},{3,1},{4,6},{5,7},{6,4},{7,5},{8,10},{9,11},{10,... | collective-permute-start | bytes 884744 | tf_op jit(solution)/shard_map/ppermute | solution.py:493
  47.7 0.7 copy-start.23
  48.4 20.2 %collective-permute-start.6 = (bf16[2,144,512]{2,1,0:T(8,128)(2,1)}, bf16[2,144,512]{2,1,0:T(8,128)(2,1)}, u32[]{:S(2)}, u32[]{:S(2)}) collective-permute-start(bf16[2,144,512]{2,1,0:T(8,128)(2,1)} %get-tuple-element.46), channel_id=1, source_target_pairs={{0,3},{1,0},{2,1},{3,2},{4,7},{5,4},{6,5},{7,6},{8,11},{9,8},{10,9... | collective-permute-start | bytes 884744 | tf_op jit(solution)/shard_map/ppermute | solution.py:493
  51.7 2.3 %copy-start.1 = (bf16[256,72,128]{2,1,0:T(8,128)(2,1)S(1)}, bf16[256,72,128]{2,1,0:T(8,128)(2,1)}, u32[]{:S(2)}) copy-start(bf16[256,72,128]{2,1,0:T(8,128)(2,1)} %copy-done) | copy-start | bytes 14155780
  54.0 0.9 copy-start.9
  55.0 0.9 copy-start.11
  55.9 0.9 copy-start.14
  56.8 1.0 copy-start.16
  57.7 0.9 copy-start.18
  58.7 0.9 copy-start.20
  59.6 0.9 copy-start.22
  60.5 0.9 copy-start.24
  61.4 7.2 %copy-start.2 = (bf16[256,72,128]{2,1,0:T(8,128)(2,1)S(1)}, bf16[256,72,128]{2,1,0:T(8,128)(2,1)}, u32[]{:S(2)}) copy-start(bf16[256,72,128]{2,1,0:T(8,128)(2,1)} %copy-done) | copy-start | bytes 14155780
  84.3 15.9 %collective-permute-start.10 = (bf16[2,144,512]{2,1,0:T(8,128)(2,1)S(1)}, bf16[2,144,512]{2,1,0:T(8,128)(2,1)S(1)}, u32[]{:S(2)}, u32[]{:S(2)}) collective-permute-start(bf16[2,144,512]{2,1,0:T(8,128)(2,1)S(1)} %get-tuple-element.56), channel_id=1, source_target_pairs={{0,1},{1,2},{2,3},{3,0},{4,5},{5,6},{6,7},{7,4},{8,9},{9,10},{10,1... | collective-permute-start | bytes 884744 | tf_op jit(solution)/shard_map/ppermute | solution.py:493
  85.1 16.4 %collective-permute-start.11 = (bf16[2,144,512]{2,1,0:T(8,128)(2,1)S(1)}, bf16[2,144,512]{2,1,0:T(8,128)(2,1)S(1)}, u32[]{:S(2)}, u32[]{:S(2)}) collective-permute-start(bf16[2,144,512]{2,1,0:T(8,128)(2,1)S(1)} %get-tuple-element.57), channel_id=1, source_target_pairs={{0,2},{1,3},{2,0},{3,1},{4,6},{5,7},{6,4},{7,5},{8,10},{9,11},{10,... | collective-permute-start | bytes 884744 | tf_op jit(solution)/shard_map/ppermute | solution.py:493
  87.3 22.1 %collective-permute-start.12 = (bf16[2,144,512]{2,1,0:T(8,128)(2,1)S(1)}, bf16[2,144,512]{2,1,0:T(8,128)(2,1)S(1)}, u32[]{:S(2)}, u32[]{:S(2)}) collective-permute-start(bf16[2,144,512]{2,1,0:T(8,128)(2,1)S(1)} %get-tuple-element.58), channel_id=1, source_target_pairs={{0,3},{1,0},{2,1},{3,2},{4,7},{5,4},{6,5},{7,6},{8,11},{9,8},{10,9... | collective-permute-start | bytes 884744 | tf_op jit(solution)/shard_map/ppermute | solution.py:493
  95.4 29.3 %collective-permute-start.16 = (bf16[2,144,512]{2,1,0:T(8,128)(2,1)S(1)}, bf16[2,144,512]{2,1,0:T(8,128)(2,1)S(1)}, u32[]{:S(2)}, u32[]{:S(2)}) collective-permute-start(bf16[2,144,512]{2,1,0:T(8,128)(2,1)S(1)} %get-tuple-element.64), channel_id=1, source_target_pairs={{0,1},{1,2},{2,3},{3,0},{4,5},{5,6},{6,7},{7,4},{8,9},{9,10},{10,1... | collective-permute-start | bytes 884744 | tf_op jit(solution)/shard_map/ppermute | solution.py:493
  95.4 29.2 %collective-permute-start.17 = (bf16[2,144,512]{2,1,0:T(8,128)(2,1)S(1)}, bf16[2,144,512]{2,1,0:T(8,128)(2,1)S(1)}, u32[]{:S(2)}, u32[]{:S(2)}) collective-permute-start(bf16[2,144,512]{2,1,0:T(8,128)(2,1)S(1)} %get-tuple-element.65), channel_id=1, source_target_pairs={{0,2},{1,3},{2,0},{3,1},{4,6},{5,7},{6,4},{7,5},{8,10},{9,11},{10,... | collective-permute-start | bytes 884744 | tf_op jit(solution)/shard_map/ppermute | solution.py:493
  100.2 24.5 %collective-permute-start.18 = (bf16[2,144,512]{2,1,0:T(8,128)(2,1)S(1)}, bf16[2,144,512]{2,1,0:T(8,128)(2,1)S(1)}, u32[]{:S(2)}, u32[]{:S(2)}) collective-permute-start(bf16[2,144,512]{2,1,0:T(8,128)(2,1)S(1)} %get-tuple-element.66), channel_id=1, source_target_pairs={{0,3},{1,0},{2,1},{3,2},{4,7},{5,4},{6,5},{7,6},{8,11},{9,8},{10,9... | collective-permute-start | bytes 884744 | tf_op jit(solution)/shard_map/ppermute | solution.py:493
  101.5 99.3 %collective-permute-start.22 = (bf16[1152,512]{1,0:T(8,128)(2,1)}, bf16[1152,512]{1,0:T(8,128)(2,1)}, u32[]{:S(2)}, u32[]{:S(2)}) collective-permute-start(bf16[1152,512]{1,0:T(8,128)(2,1)} %bitcast.19.refs_0_.own_ref), channel_id=1, source_target_pairs={{0,64},{4,68},{8,72},{12,76},{16,80},{20,84},{24,88},{28,92},{32,9... | collective-permute-start | bytes 3538952 | tf_op jit(solution)/shard_map/ppermute | solution.py:498
  118.7 84.9 %collective-permute-start.21 = (bf16[1152,512]{1,0:T(8,128)(2,1)}, bf16[1152,512]{1,0:T(8,128)(2,1)}, u32[]{:S(2)}, u32[]{:S(2)}) collective-permute-start(bf16[1152,512]{1,0:T(8,128)(2,1)} %bitcast.20.refs_0_.own_ref), channel_id=1, source_target_pairs={{0,64},{4,68},{8,72},{12,76},{16,80},{20,84},{24,88},{28,92},{32,9... | collective-permute-start | bytes 3538952 | tf_op jit(solution)/shard_map/ppermute | solution.py:498
  124.7 22.3 %copy-start.12 = (f32[72,512]{1,0:T(8,128)S(1)}, f32[72,512]{1,0:T(8,128)}, u32[]{:S(2)}) copy-start(f32[72,512]{1,0:T(8,128)} %copy-done.10) | copy-start | bytes 442372
  133.0 73.5 %collective-permute-start.20 = (bf16[1152,512]{1,0:T(8,128)(2,1)S(1)}, bf16[1152,512]{1,0:T(8,128)(2,1)}, u32[]{:S(2)}, u32[]{:S(2)}) collective-permute-start(bf16[1152,512]{1,0:T(8,128)(2,1)S(1)} %bitcast.31), channel_id=1, source_target_pairs={{0,64},{4,68},{8,72},{12,76},{16,80},{20,84},{24,88},{28,92},{32,9... | collective-permute-start | bytes 3538952 | tf_op jit(solution)/shard_map/ppermute | solution.py:498
  134.0 6.5 %collective-permute-start.13 = (bf16[1,144,512]{2,1,0:T(8,128)(2,1)S(1)}, bf16[1,144,512]{2,1,0:T(8,128)(2,1)S(1)}, u32[]{:S(2)}, u32[]{:S(2)}) collective-permute-start(bf16[1,144,512]{2,1,0:T(8,128)(2,1)S(1)} %get-tuple-element.61), channel_id=1, source_target_pairs={{0,1},{1,2},{2,3},{3,0},{4,5},{5,6},{6,7},{7,4},{8,9},{9,10},{10,1... | collective-permute-start | bytes 442376 | tf_op jit(solution)/shard_map/ppermute | solution.py:493
  134.9 8.6 %collective-permute-start.14 = (bf16[1,144,512]{2,1,0:T(8,128)(2,1)S(1)}, bf16[1,144,512]{2,1,0:T(8,128)(2,1)S(1)}, u32[]{:S(2)}, u32[]{:S(2)}) collective-permute-start(bf16[1,144,512]{2,1,0:T(8,128)(2,1)S(1)} %get-tuple-element.62), channel_id=1, source_target_pairs={{0,2},{1,3},{2,0},{3,1},{4,6},{5,7},{6,4},{7,5},{8,10},{9,11},{10,... | collective-permute-start | bytes 442376 | tf_op jit(solution)/shard_map/ppermute | solution.py:493
  140.5 15.0 %copy-start.26 = (s32[64]{0:T(128)S(1)}, s32[64]{0:T(128)}, u32[]{:S(2)}) copy-start(s32[64]{0:T(128)} %param.19) | copy-start | bytes 772
  140.5 6.5 %collective-permute-start.15 = (bf16[1,144,512]{2,1,0:T(8,128)(2,1)S(1)}, bf16[1,144,512]{2,1,0:T(8,128)(2,1)S(1)}, u32[]{:S(2)}, u32[]{:S(2)}) collective-permute-start(bf16[1,144,512]{2,1,0:T(8,128)(2,1)S(1)} %get-tuple-element.63), channel_id=1, source_target_pairs={{0,3},{1,0},{2,1},{3,2},{4,7},{5,4},{6,5},{7,6},{8,11},{9,8},{10,9... | collective-permute-start | bytes 442376 | tf_op jit(solution)/shard_map/ppermute | solution.py:493
  143.5 54.7 %collective-permute-start.23 = (bf16[576,512]{1,0:T(8,128)(2,1)}, bf16[576,512]{1,0:T(8,128)(2,1)}, u32[]{:S(2)}, u32[]{:S(2)}) collective-permute-start(bf16[576,512]{1,0:T(8,128)(2,1)} %bitcast.18.refs_0_.own_ref), channel_id=1, source_target_pairs={{0,64},{4,68},{8,72},{12,76},{16,80},{20,84},{24,88},{28,92},{32,9... | collective-permute-start | bytes 1769480 | tf_op jit(solution)/shard_map/ppermute | solution.py:498
  153.3 56.6 %collective-permute-start.19 = (bf16[576,512]{1,0:T(8,128)(2,1)S(1)}, bf16[576,512]{1,0:T(8,128)(2,1)S(1)}, u32[]{:S(2)}, u32[]{:S(2)}) collective-permute-start(bf16[576,512]{1,0:T(8,128)(2,1)S(1)} %bitcast.24), channel_id=1, source_target_pairs={{0,64},{4,68},{8,72},{12,76},{16,80},{20,84},{24,88},{28,92},{32,9... | collective-permute-start | bytes 1769480 | tf_op jit(solution)/shard_map/ppermute | solution.py:498

commit v7 on v6

--- a/solution.py
+++ b/solution.py
@@ -325,7 +325,7 @@
 
 def physics_kernel(
     place_ref, scav_ref, part0, part1, part2, part3, placing_ref, picking_ref, back_ref,
-    matrix_ref, rain_ref, wet_ref, rate_ref, *refs, first
+    matrix_ref, rain_ref, wet_ref, *refs, first
 ):
     out_ref, columns_in, picked, mixed = refs[-4:]
     groups = part0.shape[0]
@@ -352,7 +352,14 @@
             g, row = divmod(t + part_at, GROUP)
             picked[g, pl.ds(row, CAP, stride=GROUP), :] = both[:, lanes]
 
-    rate = jnp.concatenate([rate_ref[first + g] for g in range(groups)], axis=0)
+    row = lax.broadcasted_iota(jnp.int32, (GROUP, 128), 0)
+    rates = []
+    for g in range(groups):
+        rate = jnp.zeros((GROUP, 128), F32)
+        for t in range(GROUP):
+            rate = jnp.where(row == t, scav_ref[(first + g) * GROUP + t], rate)
+        rates.append(rate)
+    rate = jnp.concatenate(rates, axis=0)
     nothing = jnp.zeros((128 - levels, 128), BF16)
 
     def contract(block, carry):
@@ -391,7 +398,7 @@
         lax.fori_loop(0, GROUP // 2, finish, 0)
 
 
-def physics(place, scav, parts, made, rates, first, groups, after):
+def physics(place, scav, parts, made, first, groups, after):
     matrix, placing, picking, back, wet, rain = made
     columns = parts[0].shape[2]
     levels = rain.shape[0]
@@ -404,7 +411,6 @@
         grid=(1,),
         in_specs=[scalars, scalars]
         + [whole_block(*x.shape, once=True) for x in (*parts, *operands)]
-        + [whole_block(*rates.shape)]
         + [pl.BlockSpec(memory_space=pl.ANY)] * len(after),
         out_specs=whole_block(tracers, levels, columns, once=True),
         scratch_shapes=[
@@ -418,10 +424,10 @@
         ),
         compiler_params=pltpu.CompilerParams(vmem_limit_bytes=(12 + 4 * groups) << 20),
         name="physics",
-    )(place, scav, *parts, *operands, rates, *after)
-
-
-def choose_kernel(flag_ref, own_ref, partner_ref, *refs, first):
+    )(place, scav, *parts, *operands, *after)
+
+
+def choose_kernel(pair_ref, flag_ref, own_ref, partner_ref, *refs, first):
     out_ref, held, in_sems, out_sems = refs[-4:]
     pieces, rows = held.shape[:2]
 
@@ -444,28 +450,30 @@
         for copy in outs:
             copy.wait()
 
-    @pl.when(flag_ref[0] > 0)
+    flag = flag_ref[pair_ref[0]]
+
+    @pl.when(flag > 0)
     def _():
         copied_from(partner_ref)
 
-    @pl.when(flag_ref[0] <= 0)
+    @pl.when(flag <= 0)
     def _():
         copied_from(own_ref)
 
 
-def choose(flag, own, partner, whole, shape, first, groups, after):
+def choose(pair, flag, own, partner, whole, shape, first, groups, after):
     rows = shape[0] // sum(CHUNKS)
     pieces = 4 * groups
     operands = [own, partner]
     aliases = {}
     if whole is not None:
         operands.append(whole)
-        aliases = {3: 0}
+        aliases = {4: 0}
     operands += after
     anywhere = pl.BlockSpec(memory_space=pl.ANY)
     return pl.pallas_call(
         functools.partial(choose_kernel, first=first * rows),
-        in_specs=[pl.BlockSpec(memory_space=pltpu.SMEM)] + [anywhere] * len(operands),
+        in_specs=[pl.BlockSpec(memory_space=pltpu.SMEM)] * 2 + [anywhere] * len(operands),
         out_specs=anywhere,
         scratch_shapes=[
             pltpu.VMEM((pieces, rows * groups // pieces, shape[1]), BF16),
@@ -479,7 +487,7 @@
         ),
         compiler_params=pltpu.CompilerParams(vmem_limit_bytes=8 << 20),
         name="choose",
-    )(flag, *operands)
+    )(pair, flag, *operands)
 
 
 def shifted(value, axis, steps):
@@ -522,11 +530,7 @@
     levels, columns = rain.shape
     lev_place = lax.axis_index("lev")
     pair_index = lax.axis_index("lat") % (n_lat // 2) * n_lev + lev_place
-    flag = lax.dynamic_slice_in_dim(pair_flag, pair_index, 1)
-    rates = jnp.broadcast_to(
-        scav_rate.reshape(tracers // GROUP, GROUP, 1), (tracers // GROUP, GROUP, 128)
-    )
-
+    pair = pair_index.astype(jnp.int32).reshape(1)
     in_hbm = functools.partial(pltpu.with_memory_space_constraint, memory_space=pltpu.HBM)
     q = in_hbm(tiled_rows(tracer_dyn))
     lat, lon = in_hbm(tiled_rows(courant_lat)), in_hbm(tiled_rows(courant_lon))
@@ -569,7 +573,7 @@
             sections[number] = parts
         elif kind == "physics":
             own = physics(
-                place, scav_rate, sections[number], made, rates,
+                place, scav_rate, sections[number], made,
                 firsts[number], CHUNKS[number], after,
             )
             own = own.reshape(-1, columns)
@@ -577,7 +581,7 @@
             partners[number] = paired(own, "lat")
         else:
             out = choose(
-                flag, owns[number], partners[number], out, (tracers * levels, columns),
+                pair, pair_flag, owns[number], partners[number], out, (tracers * levels, columns),
                 firsts[number], CHUNKS[number], after,
             )
     return out.reshape(tracers, levels, columns)

time: 213 us -> 202 us (0.948)
  the two profiles are of different devices: /device:TPU:0 before, /device:TPU:100 now
where the time goes in v7:
time: 202 us; the launch traced here: 201 us
  Pallas kernels  92.6 us (46%)
  waiting for transfers between devices  63.3 us (31%)
  starting transfers between devices  44 us (22%)
    ppermute x5, waiting for transfers between devices, paired(): lax.ppermute(value, axis, [(i, i ^ count // 2) for i in range(count)])  45.7 us
    pallas_call x5, Pallas kernels, physics(): pl.pallas_call(functools.partial(physics_kernel, first=first), grid=(1,),...  40 us
    ppermute x15, starting transfers between devices, turned(): lax.ppermute(value, axis, [(i, (i + steps) % count) for i in range(count)])  23.3 us
    pallas_call x5, Pallas kernels, advect(): pl.pallas_call(advect_kernel, grid=(groups,), in_specs=[pl.BlockSpec(memo...  23.1 us
    ppermute x15, waiting for transfers between devices, turned(): lax.ppermute(value, axis, [(i, (i + steps) % count) for i in range(count)])  17.6 us
    pallas_call x5, Pallas kernels, choose(): pl.pallas_call(functools.partial(choose_kernel, first=first * rows), in_s...  12.7 us
    ppermute x4, starting transfers between devices, shifted(): return lax.ppermute(value, axis, pairs)  11.3 us
    pallas_call x2, Pallas kernels, extract(): pl.pallas_call(functools.partial(extract_kernel, faces_too=faces_too), gr...  9.44 us
  transfers between devices with their start and end apart: 24, of which 7 were waited for; matrix products, arithmetic and copies ran while one was open for 0% of the time, Pallas kernels for 40%

profile of v7, /device:TPU:100, one launch (start us, length us, event | category | flops | bytes accessed | tf_op | source)
XLA Modules:
  0.0 201.3 jit_solution(17715805992250068072)
XLA Ops:
  0.0 4.1 %extract.2 = (bf16[3,1152,128]{2,1,0:T(8,128)(2,1)S(1)}, bf16[3,1296,128]{2,1,0:T(8,128)(2,1)}, f32[4,144,128]{2,1,0:T(8,128)S(1)}) custom-call(bf16[256,256]{1,0:T(8,128)(2,1)} %constant.28.clone.apart_ref, bf16[288,288]{1,0:T(8,128)(2,1)} %constant.29.clone.face_move_ref, bf16[64,18,16,128]{3,2,1,0:T(8,128)(2,1)} %bitcast.38, ...), custom_call_target="tpu_custom_call" | custom-call | flops 3000000 | bytes 3600000 | tf_op jit(solution)/shard_map/extract/pallas_call | solution.py:108
  4.1 1.9 collective-permute-start.2
  6.0 2.4 %collective-permute-start.3 = (bf16[3,1152,128]{2,1,0:T(8,128)(2,1)S(1)}, bf16[3,1152,128]{2,1,0:T(8,128)(2,1)}, u32[]{:S(2)}, u32[]{:S(2)}) collective-permute-start(bf16[3,1152,128]{2,1,0:T(8,128)(2,1)S(1)} %get-tuple-element.36.refs_0_.north_ref), channel_id=1, source_target_pairs={{0,4},{4,8},{8,12},{12,16},{16,20},{20,24},{24,28},{28,32},{32,36}... | collective-permute-start | bytes 2654216 | tf_op jit(solution)/shard_map/ppermute | solution.py:496
  8.4 5.3 %extract.3 = (bf16[5,1152,128]{2,1,0:T(8,128)(2,1)S(1)}, bf16[5,1152,128]{2,1,0:T(8,128)(2,1)}) custom-call(bf16[256,256]{1,0:T(8,128)(2,1)} %constant.28.clone.apart_ref, bf16[288,288]{1,0:T(8,128)(2,1)} %constant.29.clone.face_move_ref, bf16[64,18,16,128]{3,2,1,0:T(8,128)(2,1)} %bitcast.39, bf16[18,16,128]{2,1,0:T(8,128)(2,1)} %bitcast.41, ...), custom_call_target="tpu_custom_call" | custom-call | flops 5000000 | bytes 6000000 | tf_op jit(solution)/shard_map/extract/pallas_call | solution.py:108
  13.8 5.1 %collective-permute-start = (bf16[5,1152,128]{2,1,0:T(8,128)(2,1)S(1)}, bf16[5,1152,128]{2,1,0:T(8,128)(2,1)}, u32[]{:S(2)}, u32[]{:S(2)}) collective-permute-start(bf16[5,1152,128]{2,1,0:T(8,128)(2,1)S(1)} %get-tuple-element.38.refs_0_.north_ref), channel_id=1, source_target_pairs={{0,4},{4,8},{8,12},{12,16},{16,20},{20,24},{24,28},{28,32},{32,36}... | collective-permute-start | bytes 4423688 | tf_op jit(solution)/shard_map/ppermute | solution.py:496
  18.9 1.9 collective-permute-start.1
  20.8 0.0 collective-permute-done.3.low_ref
  20.8 0.0 collective-permute-done.2.high_ref.above_ref
  20.8 1.0 copy-done.1
  21.8 3.2 %advect.5 = (bf16[1,144,512]{2,1,0:T(8,128)(2,1)S(1)}, bf16[1,144,512]{2,1,0:T(8,128)(2,1)S(1)}, bf16[1,144,512]{2,1,0:T(8,128)(2,1)S(1)}, bf16[1,144,512]{2,1,0:T(8,128)(2,1)S(1)}) custom-call(s32[1]{0:T(128)} %bitcast.1.place_ref, bf16[3,1296,128]{2,1,0:T(8,128)(2,1)} %get-tuple-element.40.south_ref, ...), custom_call_target="tpu_custom_call" | custom-call | flops 10000000 | bytes 2000000 | tf_op jit(solution)/shard_map/advect/pallas_call | solution.py:214
  25.0 1.6 collective-permute-start.7
  26.7 2.9 %collective-permute-start.8 = (bf16[1,144,512]{2,1,0:T(8,128)(2,1)S(1)}, bf16[1,144,512]{2,1,0:T(8,128)(2,1)S(1)}, u32[]{:S(2)}, u32[]{:S(2)}) collective-permute-start(bf16[1,144,512]{2,1,0:T(8,128)(2,1)S(1)} %get-tuple-element.53), channel_id=1, source_target_pairs={{0,2},{1,3},{2,0},{3,1},{4,6},{5,7},{6,4},{7,5},{8,10},{9,11},{10,... | collective-permute-start | bytes 442376 | tf_op jit(solution)/shard_map/ppermute | solution.py:501
  29.6 1.3 collective-permute-start.9
  30.9 7.4 %tables.1 = (bf16[256,72,128]{2,1,0:T(8,128)(2,1)S(1)}, bf16[512,512]{1,0:T(8,128)(2,1)S(1)}, bf16[256,512]{1,0:T(8,128)(2,1)S(1)}, bf16[256,512]{1,0:T(8,128)(2...) custom-call(bf16[72,72,512]{2,1,0:T(8,128)(2,1)} %matrix_ref.1, s32[1,512]{1,0:T(1,128)} %bitcast.44, ...), custom_call_target="tpu_custom_call" | custom-call | flops 2415919104 | bytes 12000000 | tf_op jit(solution)/shard_map/tables/pallas_call | solution.py:301
  38.3 0.0 copy-start.3
  38.3 5.5 %advect.6 = (bf16[2,144,512]{2,1,0:T(8,128)(2,1)S(1)}, bf16[2,144,512]{2,1,0:T(8,128)(2,1)S(1)}, bf16[2,144,512]{2,1,0:T(8,128)(2,1)S(1)}, bf16[2,144,512]{2,1,0:T(8,128)(2,1)S(1)}) custom-call(s32[1]{0:T(128)} %bitcast.1.place_ref, bf16[3,1296,128]{2,1,0:T(8,128)(2,1)} %get-tuple-element.40.south_ref, ...), custom_call_target="tpu_custom_call" | custom-call | flops 20000000 | bytes 4000000 | tf_op jit(solution)/shard_map/advect/pallas_call | solution.py:214
  43.8 0.0 collective-permute-done.7.part1
  43.8 0.8 collective-permute-start.4
  44.6 0.0 collective-permute-done.8.part2
  44.6 0.8 collective-permute-start.5
  45.4 0.0 collective-permute-done.9.part3
  45.4 2.0 collective-permute-start.6
  47.4 6.4 %physics.5 = bf16[8,72,512]{2,1,0:T(8,128)(2,1)S(1)} custom-call(s32[1]{0:T(128)} %bitcast.1.place_ref, f32[64]{0:T(128)S(1)} %copy-done.3, bf16[1,144,512]{2,1,0:T(8,128)(2,1)S(1)} %get-tuple-element.41.refs_0_.part0, bf16[1,144,512]{2,1,0:T(8,128)(2,1)S(1)} %collective-permute-done.7.part1, bf16[1,144,512]{2,1,0:T(8,128)(2,1)S(1)} %collective-permute-done.8.part2, ...), custom_call_target="tpu_custom_call" | custom-call | flops 754974720 | bytes 7700000 | tf_op jit(solution)/shard_map/physics/pallas_call | solution.py:409
  53.8 6.7 %collective-permute-done.4.part1 = bf16[2,144,512]{2,1,0:T(8,128)(2,1)S(1)} collective-permute-done((bf16[2,144,512]{2,1,0:T(8,128)(2,1)S(1)}, bf16[2,144,512]{2,1,0:T(8,128)(2,1)S(1)}, u32[]{:S(2)}, u32[]{:S(2)}) %collective-permute-start.4) | collective-permute-done | bytes 294944 | tf_op jit(solution)/shard_map/ppermute | solution.py:501
  60.5 0.0 collective-permute-done.5.part2
  60.5 0.6 collective-permute-done.6.part3
  61.1 9.5 %physics.6 = bf16[16,72,512]{2,1,0:T(8,128)(2,1)} custom-call(s32[1]{0:T(128)} %bitcast.1.place_ref, f32[64]{0:T(128)S(1)} %copy-done.3, bf16[2,144,512]{2,1,0:T(8,128)(2,1)S(1)} %get-tuple-element.43.refs_0_.part0, bf16[2,144,512]{2,1,0:T(8,128)(2,1)S(1)} %collective-permute-done.4.part1, bf16[2,144,512]{2,1,0:T(8,128)(2,1)S(1)} %collective-permute-done.5.part2, ...), custom_call_target="tpu_custom_call" | custom-call | flops 1509949440 | bytes 8900000 | tf_op jit(solution)/shard_map/physics/pallas_call | solution.py:409
  70.7 0.0 collective-permute-done.low_ref
  70.7 0.0 collective-permute-done.1.high_ref
  70.7 5.5 %advect.7 = (bf16[2,144,512]{2,1,0:T(8,128)(2,1)S(1)}, bf16[2,144,512]{2,1,0:T(8,128)(2,1)S(1)}, bf16[2,144,512]{2,1,0:T(8,128)(2,1)S(1)}, bf16[2,144,512]{2,1,0:T(8,128)(2,1)S(1)}) custom-call(s32[1]{0:T(128)} %bitcast.1.place_ref, bf16[5,1152,128]{2,1,0:T(8,128)(2,1)} %get-tuple-element.37.south_ref, ...), custom_call_target="tpu_custom_call" | custom-call | flops 20000000 | bytes 4000000 | tf_op jit(solution)/shard_map/advect/pallas_call | solution.py:214
  76.2 0.5 collective-permute-start.10
  76.7 3.6 %collective-permute-start.11 = (bf16[2,144,512]{2,1,0:T(8,128)(2,1)S(1)}, bf16[2,144,512]{2,1,0:T(8,128)(2,1)S(1)}, u32[]{:S(2)}, u32[]{:S(2)}) collective-permute-start(bf16[2,144,512]{2,1,0:T(8,128)(2,1)S(1)} %get-tuple-element.57), channel_id=1, source_target_pairs={{0,2},{1,3},{2,0},{3,1},{4,6},{5,7},{6,4},{7,5},{8,10},{9,11},{10,... | collective-permute-start | bytes 884744 | tf_op jit(solution)/shard_map/ppermute | solution.py:501
  80.3 0.0 collective-permute-start.12
  80.3 5.5 %advect.8 = (bf16[2,144,512]{2,1,0:T(8,128)(2,1)S(1)}, bf16[2,144,512]{2,1,0:T(8,128)(2,1)S(1)}, bf16[2,144,512]{2,1,0:T(8,128)(2,1)S(1)}, bf16[2,144,512]{2,1,0:T(8,128)(2,1)S(1)}) custom-call(s32[1]{0:T(128)} %bitcast.1.place_ref, bf16[5,1152,128]{2,1,0:T(8,128)(2,1)} %get-tuple-element.37.south_ref, ...), custom_call_target="tpu_custom_call" | custom-call | flops 20000000 | bytes 4000000 | tf_op jit(solution)/shard_map/advect/pallas_call | solution.py:214
  85.8 2.1 %collective-permute-start.16 = (bf16[2,144,512]{2,1,0:T(8,128)(2,1)S(1)}, bf16[2,144,512]{2,1,0:T(8,128)(2,1)S(1)}, u32[]{:S(2)}, u32[]{:S(2)}) collective-permute-start(bf16[2,144,512]{2,1,0:T(8,128)(2,1)S(1)} %get-tuple-element.64), channel_id=1, source_target_pairs={{0,1},{1,2},{2,3},{3,0},{4,5},{5,6},{6,7},{7,4},{8,9},{9,10},{10,1... | collective-permute-start | bytes 884744 | tf_op jit(solution)/shard_map/ppermute | solution.py:501
  87.9 0.2 collective-permute-start.17
  88.1 0.0 collective-permute-done.10.part1
  88.1 2.6 %collective-permute-start.18 = (bf16[2,144,512]{2,1,0:T(8,128)(2,1)S(1)}, bf16[2,144,512]{2,1,0:T(8,128)(2,1)S(1)}, u32[]{:S(2)}, u32[]{:S(2)}) collective-permute-start(bf16[2,144,512]{2,1,0:T(8,128)(2,1)S(1)} %get-tuple-element.66), channel_id=1, source_target_pairs={{0,3},{1,0},{2,1},{3,2},{4,7},{5,4},{6,5},{7,6},{8,11},{9,8},{10,9... | collective-permute-start | bytes 884744 | tf_op jit(solution)/shard_map/ppermute | solution.py:501
  90.7 3.8 %collective-permute-done.11.part2 = bf16[2,144,512]{2,1,0:T(8,128)(2,1)S(1)} collective-permute-done((bf16[2,144,512]{2,1,0:T(8,128)(2,1)S(1)}, bf16[2,144,512]{2,1,0:T(8,128)(2,1)S(1)}, u32[]{:S(2)}, u32[]{:S(2)}) %collective-permute-start.11) | collective-permute-done | bytes 294944 | tf_op jit(solution)/shard_map/ppermute | solution.py:501
  94.5 0.5 collective-permute-start.22
  95.0 0.0 collective-permute-done.12.part3
  95.0 9.4 %physics.7 = bf16[16,72,512]{2,1,0:T(8,128)(2,1)} custom-call(s32[1]{0:T(128)} %bitcast.1.place_ref, f32[64]{0:T(128)S(1)} %copy-done.3, bf16[2,144,512]{2,1,0:T(8,128)(2,1)S(1)} %get-tuple-element.55.refs_0_.part0, bf16[2,144,512]{2,1,0:T(8,128)(2,1)S(1)} %collective-permute-done.10.part1, bf16[2,144,512]{2,1,0:T(8,128)(2,1)S(1)} %collective-permute-done.11.part2, ...), custom_call_target="tpu_custom_call" | custom-call | flops 1509949440 | bytes 8900000 | tf_op jit(solution)/shard_map/physics/pallas_call | solution.py:409
  104.4 3.0 %collective-permute-start.21 = (bf16[1152,512]{1,0:T(8,128)(2,1)}, bf16[1152,512]{1,0:T(8,128)(2,1)}, u32[]{:S(2)}, u32[]{:S(2)}) collective-permute-start(bf16[1152,512]{1,0:T(8,128)(2,1)} %bitcast.21.refs_0_.own_ref), channel_id=1, source_target_pairs={{0,64},{4,68},{8,72},{12,76},{16,80},{20,84},{24,88},{28,92},{32,9... | collective-permute-start | bytes 3538952 | tf_op jit(solution)/shard_map/ppermute | solution.py:506
  107.4 3.3 %advect.9 = (bf16[1,144,512]{2,1,0:T(8,128)(2,1)S(1)}, bf16[1,144,512]{2,1,0:T(8,128)(2,1)S(1)}, bf16[1,144,512]{2,1,0:T(8,128)(2,1)S(1)}, bf16[1,144,512]{2,1,0:T(8,128)(2,1)S(1)}) custom-call(s32[1]{0:T(128)} %bitcast.1.place_ref, bf16[5,1152,128]{2,1,0:T(8,128)(2,1)} %get-tuple-element.37.south_ref, ...), custom_call_target="tpu_custom_call" | custom-call | flops 10000000 | bytes 2000000 | tf_op jit(solution)/shard_map/advect/pallas_call | solution.py:214
  110.7 0.0 collective-permute-done.16.part1
  110.8 8.4 %physics.8 = bf16[16,72,512]{2,1,0:T(8,128)(2,1)S(1)} custom-call(s32[1]{0:T(128)} %bitcast.1.place_ref, f32[64]{0:T(128)S(1)} %copy-done.3, bf16[2,144,512]{2,1,0:T(8,128)(2,1)S(1)} %get-tuple-element.59.refs_0_.part0, bf16[2,144,512]{2,1,0:T(8,128)(2,1)S(1)} %collective-permute-done.16.part1, bf16[2,144,512]{2,1,0:T(8,128)(2,1)S(1)} %collective-permute-done.17.part2, ...), custom_call_target="tpu_custom_call" | custom-call | flops 1509949440 | bytes 8900000 | tf_op jit(solution)/shard_map/physics/pallas_call | solution.py:409
  119.1 0.6 collective-permute-start.20
  119.7 0.1 collective-permute-start.13
  119.9 3.6 %collective-permute-start.14 = (bf16[1,144,512]{2,1,0:T(8,128)(2,1)S(1)}, bf16[1,144,512]{2,1,0:T(8,128)(2,1)S(1)}, u32[]{:S(2)}, u32[]{:S(2)}) collective-permute-start(bf16[1,144,512]{2,1,0:T(8,128)(2,1)S(1)} %get-tuple-element.62), channel_id=1, source_target_pairs={{0,2},{1,3},{2,0},{3,1},{4,6},{5,7},{6,4},{7,5},{8,10},{9,11},{10,... | collective-permute-start | bytes 442376 | tf_op jit(solution)/shard_map/ppermute | solution.py:501
  123.5 4.0 %collective-permute-done.13.part1 = bf16[1,144,512]{2,1,0:T(8,128)(2,1)S(1)} collective-permute-done((bf16[1,144,512]{2,1,0:T(8,128)(2,1)S(1)}, bf16[1,144,512]{2,1,0:T(8,128)(2,1)S(1)}, u32[]{:S(2)}, u32[]{:S(2)}) %collective-permute-start.13) | collective-permute-done | bytes 147488 | tf_op jit(solution)/shard_map/ppermute | solution.py:501
  127.5 1.1 collective-permute-start.15
  128.6 1.0 collective-permute-done.14.part2
  129.6 1.6 collective-permute-start.23
  131.2 1.4 collective-permute-done.15.part3
  132.6 6.4 %physics.9 = bf16[8,72,512]{2,1,0:T(8,128)(2,1)S(1)} custom-call(s32[1]{0:T(128)} %bitcast.1.place_ref, f32[64]{0:T(128)S(1)} %copy-done.3, bf16[1,144,512]{2,1,0:T(8,128)(2,1)S(1)} %get-tuple-element.60.refs_0_.part0, bf16[1,144,512]{2,1,0:T(8,128)(2,1)S(1)} %collective-permute-done.13.part1, bf16[1,144,512]{2,1,0:T(8,128)(2,1)S(1)} %collective-permute-done.14.part2, ...), custom_call_target="tpu_custom_call" | custom-call | flops 754974720 | bytes 7700000 | tf_op jit(solution)/shard_map/physics/pallas_call | solution.py:409
  139.0 3.7 %collective-permute-start.19 = (bf16[576,512]{1,0:T(8,128)(2,1)S(1)}, bf16[576,512]{1,0:T(8,128)(2,1)S(1)}, u32[]{:S(2)}, u32[]{:S(2)}) collective-permute-start(bf16[576,512]{1,0:T(8,128)(2,1)S(1)} %bitcast.25), channel_id=1, source_target_pairs={{0,64},{4,68},{8,72},{12,76},{16,80},{20,84},{24,88},{28,92},{32,9... | collective-permute-start | bytes 1769480 | tf_op jit(solution)/shard_map/ppermute | solution.py:506
  142.7 45.7 %collective-permute-done.23.partner_ref = bf16[576,512]{1,0:T(8,128)(2,1)} collective-permute-done((bf16[576,512]{1,0:T(8,128)(2,1)S(1)}, bf16[576,512]{1,0:T(8,128)(2,1)}, u32[]{:S(2)}, u32[]{:S(2)}) %collective-permute-start.23) | collective-permute-done | bytes 589856 | tf_op jit(solution)/shard_map/ppermute | solution.py:506
  188.4 2.4 %choose.5.refs_0_ = bf16[4608,512]{1,0:T(8,128)(2,1)} custom-call(s32[1]{0:T(128)} %bitcast.pair_ref, s32[64]{0:T(128)S(1)} %copy-done.4, bf16[576,512]{1,0:T(8,128)(2,1)S(1)} %bitcast.37, bf16[576,512]{1,0:T(8,128)(2,1)} %collective-permute-done.23.partner_ref, bf16[576,512]{1,0:T(8,128)(2,1)S(1)} %bitcast.26), custom_call_target="tpu_custom_call" | custom-call | bytes 1200000 | tf_op jit(solution)/shard_map/choose/pallas_call | solution.py:474
  190.8 2.7 %choose.6.refs_0_ = bf16[4608,512]{1,0:T(8,128)(2,1)} custom-call(s32[1]{0:T(128)} %bitcast.pair_ref, s32[64]{0:T(128)S(1)} %copy-done.4, bf16[1152,512]{1,0:T(8,128)(2,1)} %bitcast.20.refs_0_.own_ref, bf16[1152,512]{1,0:T(8,128)(2,1)} %collective-permute-done.22.partner_ref, bf16[4608,512]{1,0:T(8,128)(2,1)} %choose.5.refs_0_, ...), custom_call_target="tpu_custom_call", output_to_operand_aliasing={{}: (4, {})} | custom-call | bytes 2400000 | tf_op jit(solution)/shard_map/choose/pallas_call | solution.py:474
  193.5 0.0 collective-permute-done.21.partner_ref
  193.5 2.7 %choose.7.refs_0_ = bf16[4608,512]{1,0:T(8,128)(2,1)} custom-call(s32[1]{0:T(128)} %bitcast.pair_ref, s32[64]{0:T(128)S(1)} %copy-done.4, bf16[1152,512]{1,0:T(8,128)(2,1)} %bitcast.21.refs_0_.own_ref, bf16[1152,512]{1,0:T(8,128)(2,1)} %collective-permute-done.21.partner_ref, bf16[4608,512]{1,0:T(8,128)(2,1)} %choose.6.refs_0_, ...), custom_call_target="tpu_custom_call", output_to_operand_aliasing={{}: (4, {})} | custom-call | bytes 2400000 | tf_op jit(solution)/shard_map/choose/pallas_call | solution.py:474
  196.2 2.7 %choose.8.refs_0_ = bf16[4608,512]{1,0:T(8,128)(2,1)} custom-call(s32[1]{0:T(128)} %bitcast.pair_ref, s32[64]{0:T(128)S(1)} %copy-done.4, bf16[1152,512]{1,0:T(8,128)(2,1)S(1)} %bitcast.34, bf16[1152,512]{1,0:T(8,128)(2,1)} %collective-permute-done.20.partner_ref, bf16[4608,512]{1,0:T(8,128)(2,1)} %choose.7.refs_0_, ...), custom_call_target="tpu_custom_call", output_to_operand_aliasing={{}: (4, {})} | custom-call | bytes 2400000 | tf_op jit(solution)/shard_map/choose/pallas_call | solution.py:474
  198.9 0.0 collective-permute-done.19.partner_ref
  198.9 2.2 %choose.9 = bf16[4608,512]{1,0:T(8,128)(2,1)} custom-call(s32[1]{0:T(128)} %bitcast.pair_ref, s32[64]{0:T(128)S(1)} %copy-done.4, bf16[576,512]{1,0:T(8,128)(2,1)S(1)} %bitcast.30, bf16[576,512]{1,0:T(8,128)(2,1)S(1)} %collective-permute-done.19.partner_ref, bf16[4608,512]{1,0:T(8,128)(2,1)} %choose.8.refs_0_, ...), custom_call_target="tpu_custom_call", output_to_operand_aliasing={{}: (4, {})} | custom-call | bytes 1200000 | tf_op jit(solution)/shard_map/choose/pallas_call | solution.py:474
  (12 shorter events, 0.0 us)
Async XLA Ops:
  4.1 9.7 %copy-start = (f32[4,144,128]{2,1,0:T(8,128)}, f32[4,144,128]{2,1,0:T(8,128)S(1)}, u32[]{:S(2)}) copy-start(f32[4,144,128]{2,1,0:T(8,128)S(1)} %get-tuple-element.39.faces_ref) | copy-start | bytes 884740
  4.1 16.7 %collective-permute-start.2 = (bf16[3,1296,128]{2,1,0:T(8,128)(2,1)}, bf16[3,1296,128]{2,1,0:T(8,128)(2,1)S(1)}, u32[]{:S(2)}, u32[]{:S(2)}) collective-permute-start(bf16[3,1296,128]{2,1,0:T(8,128)(2,1)} %get-tuple-element.40.south_ref), channel_id=1, source_target_pairs={{4,0},{8,4},{12,8},{16,12},{20,16},{24,20},{28,24},{32,28},{36,32}... | collective-permute-start | bytes 2985992 | tf_op jit(solution)/shard_map/ppermute | solution.py:496
  6.0 14.8 %collective-permute-start.3 = (bf16[3,1152,128]{2,1,0:T(8,128)(2,1)S(1)}, bf16[3,1152,128]{2,1,0:T(8,128)(2,1)}, u32[]{:S(2)}, u32[]{:S(2)}) collective-permute-start(bf16[3,1152,128]{2,1,0:T(8,128)(2,1)S(1)} %get-tuple-element.36.refs_0_.north_ref), channel_id=1, source_target_pairs={{0,4},{4,8},{8,12},{12,16},{16,20},{20,24},{24,28},{28,32},{32,36}... | collective-permute-start | bytes 2654216 | tf_op jit(solution)/shard_map/ppermute | solution.py:496
  13.8 56.9 %collective-permute-start = (bf16[5,1152,128]{2,1,0:T(8,128)(2,1)S(1)}, bf16[5,1152,128]{2,1,0:T(8,128)(2,1)}, u32[]{:S(2)}, u32[]{:S(2)}) collective-permute-start(bf16[5,1152,128]{2,1,0:T(8,128)(2,1)S(1)} %get-tuple-element.38.refs_0_.north_ref), channel_id=1, source_target_pairs={{0,4},{4,8},{8,12},{12,16},{16,20},{20,24},{24,28},{28,32},{32,36}... | collective-permute-start | bytes 4423688 | tf_op jit(solution)/shard_map/ppermute | solution.py:496
  18.9 51.8 %collective-permute-start.1 = (bf16[5,1152,128]{2,1,0:T(8,128)(2,1)}, bf16[5,1152,128]{2,1,0:T(8,128)(2,1)}, u32[]{:S(2)}, u32[]{:S(2)}) collective-permute-start(bf16[5,1152,128]{2,1,0:T(8,128)(2,1)} %get-tuple-element.37.south_ref), channel_id=1, source_target_pairs={{4,0},{8,4},{12,8},{16,12},{20,16},{24,20},{28,24},{32,28},{36,32}... | collective-permute-start | bytes 4423688 | tf_op jit(solution)/shard_map/ppermute | solution.py:496
  20.8 1.0 copy-start.1
  25.0 18.8 %collective-permute-start.7 = (bf16[1,144,512]{2,1,0:T(8,128)(2,1)S(1)}, bf16[1,144,512]{2,1,0:T(8,128)(2,1)S(1)}, u32[]{:S(2)}, u32[]{:S(2)}) collective-permute-start(bf16[1,144,512]{2,1,0:T(8,128)(2,1)S(1)} %get-tuple-element.52), channel_id=1, source_target_pairs={{0,1},{1,2},{2,3},{3,0},{4,5},{5,6},{6,7},{7,4},{8,9},{9,10},{10,1... | collective-permute-start | bytes 442376 | tf_op jit(solution)/shard_map/ppermute | solution.py:501
  26.7 17.9 %collective-permute-start.8 = (bf16[1,144,512]{2,1,0:T(8,128)(2,1)S(1)}, bf16[1,144,512]{2,1,0:T(8,128)(2,1)S(1)}, u32[]{:S(2)}, u32[]{:S(2)}) collective-permute-start(bf16[1,144,512]{2,1,0:T(8,128)(2,1)S(1)} %get-tuple-element.53), channel_id=1, source_target_pairs={{0,2},{1,3},{2,0},{3,1},{4,6},{5,7},{6,4},{7,5},{8,10},{9,11},{10,... | collective-permute-start | bytes 442376 | tf_op jit(solution)/shard_map/ppermute | solution.py:501
  29.6 15.8 %collective-permute-start.9 = (bf16[1,144,512]{2,1,0:T(8,128)(2,1)S(1)}, bf16[1,144,512]{2,1,0:T(8,128)(2,1)S(1)}, u32[]{:S(2)}, u32[]{:S(2)}) collective-permute-start(bf16[1,144,512]{2,1,0:T(8,128)(2,1)S(1)} %get-tuple-element.54), channel_id=1, source_target_pairs={{0,3},{1,0},{2,1},{3,2},{4,7},{5,4},{6,5},{7,6},{8,11},{9,8},{10,9... | collective-permute-start | bytes 442376 | tf_op jit(solution)/shard_map/ppermute | solution.py:501
  30.9 7.4 %copy-start.2 = (f32[4,144,128]{2,1,0:T(8,128)S(1)}, f32[4,144,128]{2,1,0:T(8,128)}, u32[]{:S(2)}) copy-start(f32[4,144,128]{2,1,0:T(8,128)} %copy-done) | copy-start | bytes 884740
  38.3 9.1 %copy-start.3 = (f32[64]{0:T(128)S(1)}, f32[64]{0:T(128)}, u32[]{:S(2)}) copy-start(f32[64]{0:T(128)} %scav_ref.9) | copy-start | bytes 772
  43.8 16.7 %collective-permute-start.4 = (bf16[2,144,512]{2,1,0:T(8,128)(2,1)S(1)}, bf16[2,144,512]{2,1,0:T(8,128)(2,1)S(1)}, u32[]{:S(2)}, u32[]{:S(2)}) collective-permute-start(bf16[2,144,512]{2,1,0:T(8,128)(2,1)S(1)} %get-tuple-element.44), channel_id=1, source_target_pairs={{0,1},{1,2},{2,3},{3,0},{4,5},{5,6},{6,7},{7,4},{8,9},{9,10},{10,1... | collective-permute-start | bytes 884744 | tf_op jit(solution)/shard_map/ppermute | solution.py:501
  44.6 15.9 %collective-permute-start.5 = (bf16[2,144,512]{2,1,0:T(8,128)(2,1)S(1)}, bf16[2,144,512]{2,1,0:T(8,128)(2,1)S(1)}, u32[]{:S(2)}, u32[]{:S(2)}) collective-permute-start(bf16[2,144,512]{2,1,0:T(8,128)(2,1)S(1)} %get-tuple-element.45), channel_id=1, source_target_pairs={{0,2},{1,3},{2,0},{3,1},{4,6},{5,7},{6,4},{7,5},{8,10},{9,11},{10,... | collective-permute-start | bytes 884744 | tf_op jit(solution)/shard_map/ppermute | solution.py:501
  45.4 15.7 %collective-permute-start.6 = (bf16[2,144,512]{2,1,0:T(8,128)(2,1)S(1)}, bf16[2,144,512]{2,1,0:T(8,128)(2,1)S(1)}, u32[]{:S(2)}, u32[]{:S(2)}) collective-permute-start(bf16[2,144,512]{2,1,0:T(8,128)(2,1)S(1)} %get-tuple-element.46), channel_id=1, source_target_pairs={{0,3},{1,0},{2,1},{3,2},{4,7},{5,4},{6,5},{7,6},{8,11},{9,8},{10,9... | collective-permute-start | bytes 884744 | tf_op jit(solution)/shard_map/ppermute | solution.py:501
  76.2 11.9 %collective-permute-start.10 = (bf16[2,144,512]{2,1,0:T(8,128)(2,1)S(1)}, bf16[2,144,512]{2,1,0:T(8,128)(2,1)S(1)}, u32[]{:S(2)}, u32[]{:S(2)}) collective-permute-start(bf16[2,144,512]{2,1,0:T(8,128)(2,1)S(1)} %get-tuple-element.56), channel_id=1, source_target_pairs={{0,1},{1,2},{2,3},{3,0},{4,5},{5,6},{6,7},{7,4},{8,9},{9,10},{10,1... | collective-permute-start | bytes 884744 | tf_op jit(solution)/shard_map/ppermute | solution.py:501
  76.7 17.8 %collective-permute-start.11 = (bf16[2,144,512]{2,1,0:T(8,128)(2,1)S(1)}, bf16[2,144,512]{2,1,0:T(8,128)(2,1)S(1)}, u32[]{:S(2)}, u32[]{:S(2)}) collective-permute-start(bf16[2,144,512]{2,1,0:T(8,128)(2,1)S(1)} %get-tuple-element.57), channel_id=1, source_target_pairs={{0,2},{1,3},{2,0},{3,1},{4,6},{5,7},{6,4},{7,5},{8,10},{9,11},{10,... | collective-permute-start | bytes 884744 | tf_op jit(solution)/shard_map/ppermute | solution.py:501
  80.3 14.7 %collective-permute-start.12 = (bf16[2,144,512]{2,1,0:T(8,128)(2,1)S(1)}, bf16[2,144,512]{2,1,0:T(8,128)(2,1)S(1)}, u32[]{:S(2)}, u32[]{:S(2)}) collective-permute-start(bf16[2,144,512]{2,1,0:T(8,128)(2,1)S(1)} %get-tuple-element.58), channel_id=1, source_target_pairs={{0,3},{1,0},{2,1},{3,2},{4,7},{5,4},{6,5},{7,6},{8,11},{9,8},{10,9... | collective-permute-start | bytes 884744 | tf_op jit(solution)/shard_map/ppermute | solution.py:501
  85.8 24.9 %collective-permute-start.16 = (bf16[2,144,512]{2,1,0:T(8,128)(2,1)S(1)}, bf16[2,144,512]{2,1,0:T(8,128)(2,1)S(1)}, u32[]{:S(2)}, u32[]{:S(2)}) collective-permute-start(bf16[2,144,512]{2,1,0:T(8,128)(2,1)S(1)} %get-tuple-element.64), channel_id=1, source_target_pairs={{0,1},{1,2},{2,3},{3,0},{4,5},{5,6},{6,7},{7,4},{8,9},{9,10},{10,1... | collective-permute-start | bytes 884744 | tf_op jit(solution)/shard_map/ppermute | solution.py:501
  87.9 22.8 %collective-permute-start.17 = (bf16[2,144,512]{2,1,0:T(8,128)(2,1)S(1)}, bf16[2,144,512]{2,1,0:T(8,128)(2,1)S(1)}, u32[]{:S(2)}, u32[]{:S(2)}) collective-permute-start(bf16[2,144,512]{2,1,0:T(8,128)(2,1)S(1)} %get-tuple-element.65), channel_id=1, source_target_pairs={{0,2},{1,3},{2,0},{3,1},{4,6},{5,7},{6,4},{7,5},{8,10},{9,11},{10,... | collective-permute-start | bytes 884744 | tf_op jit(solution)/shard_map/ppermute | solution.py:501
  88.1 22.6 %collective-permute-start.18 = (bf16[2,144,512]{2,1,0:T(8,128)(2,1)S(1)}, bf16[2,144,512]{2,1,0:T(8,128)(2,1)S(1)}, u32[]{:S(2)}, u32[]{:S(2)}) collective-permute-start(bf16[2,144,512]{2,1,0:T(8,128)(2,1)S(1)} %get-tuple-element.66), channel_id=1, source_target_pairs={{0,3},{1,0},{2,1},{3,2},{4,7},{5,4},{6,5},{7,6},{8,11},{9,8},{10,9... | collective-permute-start | bytes 884744 | tf_op jit(solution)/shard_map/ppermute | solution.py:501
  94.5 96.3 %collective-permute-start.22 = (bf16[1152,512]{1,0:T(8,128)(2,1)}, bf16[1152,512]{1,0:T(8,128)(2,1)}, u32[]{:S(2)}, u32[]{:S(2)}) collective-permute-start(bf16[1152,512]{1,0:T(8,128)(2,1)} %bitcast.20.refs_0_.own_ref), channel_id=1, source_target_pairs={{0,64},{4,68},{8,72},{12,76},{16,80},{20,84},{24,88},{28,92},{32,9... | collective-permute-start | bytes 3538952 | tf_op jit(solution)/shard_map/ppermute | solution.py:506
  104.4 89.1 %collective-permute-start.21 = (bf16[1152,512]{1,0:T(8,128)(2,1)}, bf16[1152,512]{1,0:T(8,128)(2,1)}, u32[]{:S(2)}, u32[]{:S(2)}) collective-permute-start(bf16[1152,512]{1,0:T(8,128)(2,1)} %bitcast.21.refs_0_.own_ref), channel_id=1, source_target_pairs={{0,64},{4,68},{8,72},{12,76},{16,80},{20,84},{24,88},{28,92},{32,9... | collective-permute-start | bytes 3538952 | tf_op jit(solution)/shard_map/ppermute | solution.py:506
  119.1 77.1 %collective-permute-start.20 = (bf16[1152,512]{1,0:T(8,128)(2,1)S(1)}, bf16[1152,512]{1,0:T(8,128)(2,1)}, u32[]{:S(2)}, u32[]{:S(2)}) collective-permute-start(bf16[1152,512]{1,0:T(8,128)(2,1)S(1)} %bitcast.32), channel_id=1, source_target_pairs={{0,64},{4,68},{8,72},{12,76},{16,80},{20,84},{24,88},{28,92},{32,9... | collective-permute-start | bytes 3538952 | tf_op jit(solution)/shard_map/ppermute | solution.py:506
  119.7 7.7 %collective-permute-start.13 = (bf16[1,144,512]{2,1,0:T(8,128)(2,1)S(1)}, bf16[1,144,512]{2,1,0:T(8,128)(2,1)S(1)}, u32[]{:S(2)}, u32[]{:S(2)}) collective-permute-start(bf16[1,144,512]{2,1,0:T(8,128)(2,1)S(1)} %get-tuple-element.61), channel_id=1, source_target_pairs={{0,1},{1,2},{2,3},{3,0},{4,5},{5,6},{6,7},{7,4},{8,9},{9,10},{10,1... | collective-permute-start | bytes 442376 | tf_op jit(solution)/shard_map/ppermute | solution.py:501
  119.9 9.7 %collective-permute-start.14 = (bf16[1,144,512]{2,1,0:T(8,128)(2,1)S(1)}, bf16[1,144,512]{2,1,0:T(8,128)(2,1)S(1)}, u32[]{:S(2)}, u32[]{:S(2)}) collective-permute-start(bf16[1,144,512]{2,1,0:T(8,128)(2,1)S(1)} %get-tuple-element.62), channel_id=1, source_target_pairs={{0,2},{1,3},{2,0},{3,1},{4,6},{5,7},{6,4},{7,5},{8,10},{9,11},{10,... | collective-permute-start | bytes 442376 | tf_op jit(solution)/shard_map/ppermute | solution.py:501
  127.5 60.9 %copy-start.4 = (s32[64]{0:T(128)S(1)}, s32[64]{0:T(128)}, u32[]{:S(2)}) copy-start(s32[64]{0:T(128)} %flag_ref.9) | copy-start | bytes 772
  127.5 5.1 %collective-permute-start.15 = (bf16[1,144,512]{2,1,0:T(8,128)(2,1)S(1)}, bf16[1,144,512]{2,1,0:T(8,128)(2,1)S(1)}, u32[]{:S(2)}, u32[]{:S(2)}) collective-permute-start(bf16[1,144,512]{2,1,0:T(8,128)(2,1)S(1)} %get-tuple-element.63), channel_id=1, source_target_pairs={{0,3},{1,0},{2,1},{3,2},{4,7},{5,4},{6,5},{7,6},{8,11},{9,8},{10,9... | collective-permute-start | bytes 442376 | tf_op jit(solution)/shard_map/ppermute | solution.py:501
  129.6 58.8 %collective-permute-start.23 = (bf16[576,512]{1,0:T(8,128)(2,1)S(1)}, bf16[576,512]{1,0:T(8,128)(2,1)}, u32[]{:S(2)}, u32[]{:S(2)}) collective-permute-start(bf16[576,512]{1,0:T(8,128)(2,1)S(1)} %bitcast.36), channel_id=1, source_target_pairs={{0,64},{4,68},{8,72},{12,76},{16,80},{20,84},{24,88},{28,92},{32,9... | collective-permute-start | bytes 1769480 | tf_op jit(solution)/shard_map/ppermute | solution.py:506
  139.0 59.9 %collective-permute-start.19 = (bf16[576,512]{1,0:T(8,128)(2,1)S(1)}, bf16[576,512]{1,0:T(8,128)(2,1)S(1)}, u32[]{:S(2)}, u32[]{:S(2)}) collective-permute-start(bf16[576,512]{1,0:T(8,128)(2,1)S(1)} %bitcast.25), channel_id=1, source_target_pairs={{0,64},{4,68},{8,72},{12,76},{16,80},{20,84},{24,88},{28,92},{32,9... | collective-permute-start | bytes 1769480 | tf_op jit(solution)/shard_map/ppermute | solution.py:506

commit v8 on v7

--- a/solution.py
+++ b/solution.py
@@ -11,17 +11,17 @@
 
 
 GROUP = 8
-CHUNKS = (1, 2, 2, 2, 1)
-SPANS = ((0, 3), (3, 5))
+CHUNKS = (2, 1, 2, 2, 1)
+SPANS = ((0, 2), (2, 6))
 ORDER = (
     ("extract", 0),
     ("extract", 1),
     ("advect", 0),
     ("tables", 0),
+    ("physics", 0),
     ("advect", 1),
-    ("physics", 0),
+    ("advect", 2),
     ("physics", 1),
-    ("advect", 2),
     ("advect", 3),
     ("physics", 2),
     ("advect", 4),
@@ -327,7 +327,7 @@
     place_ref, scav_ref, part0, part1, part2, part3, placing_ref, picking_ref, back_ref,
     matrix_ref, rain_ref, wet_ref, *refs, first
 ):
-    out_ref, columns_in, picked, mixed = refs[-4:]
+    out_ref, columns_in, picked, mixed, results, sems = refs[-6:]
     groups = part0.shape[0]
     levels = rain_ref.shape[0]
     part = part0.shape[1] // GROUP
@@ -392,10 +392,15 @@
                 )[:levels]
                 scav = scav_ref[first * GROUP + at + inner]
                 dry = plain[inner * 128 : inner * 128 + levels]
-                out_ref[at + inner] = (spread + dry * jnp.exp(-scav * rain_ref[...])).astype(BF16)
+                t = at + inner
+                results[t] = (spread + dry * jnp.exp(-scav * rain_ref[...])).astype(BF16)
+                pltpu.make_async_copy(results.at[t], out_ref.at[t], sems.at[t]).start()
             return carry
 
         lax.fori_loop(0, GROUP // 2, finish, 0)
+
+    for t in range(tracers):
+        pltpu.make_async_copy(results.at[t], out_ref.at[t], sems.at[t]).wait()
 
 
 def physics(place, scav, parts, made, first, groups, after):
@@ -412,11 +417,13 @@
         in_specs=[scalars, scalars]
         + [whole_block(*x.shape, once=True) for x in (*parts, *operands)]
         + [pl.BlockSpec(memory_space=pl.ANY)] * len(after),
-        out_specs=whole_block(tracers, levels, columns, once=True),
+        out_specs=pl.BlockSpec(memory_space=pl.ANY),
         scratch_shapes=[
             pltpu.VMEM((tracers, 128, columns), BF16),
             pltpu.VMEM((groups, CAP * GROUP, 128), F32),
             pltpu.VMEM((groups, CAP * GROUP, 128), F32),
+            pltpu.VMEM((tracers, levels, columns), BF16),
+            pltpu.SemaphoreType.DMA((tracers,)),
         ],
         out_shape=jax.ShapeDtypeStruct((tracers, levels, columns), BF16),
         cost_estimate=pl.CostEstimate(

time: 202 us -> 225 us (1.11)
  the two profiles are of different devices: /device:TPU:100 before, /device:TPU:97 now
where the time goes in v8:
time: 225 us; the launch traced here: 222 us
  Pallas kernels  96.3 us (43%)
  waiting for transfers between devices  88.5 us (39%)
  starting transfers between devices  35.5 us (16%)
    pallas_call x5, Pallas kernels, physics(): pl.pallas_call(functools.partial(physics_kernel, first=first), grid=(1,),...  44.7 us
    ppermute x5, waiting for transfers between devices, paired(): lax.ppermute(value, axis, [(i, i ^ count // 2) for i in range(count)])  42.4 us
    ppermute x4, waiting for transfers between devices, shifted(): return lax.ppermute(value, axis, pairs)  23.3 us
    pallas_call x5, Pallas kernels, advect(): pl.pallas_call(advect_kernel, grid=(groups,), in_specs=[pl.BlockSpec(memo...  23 us
    ppermute x15, waiting for transfers between devices, turned(): lax.ppermute(value, axis, [(i, (i + steps) % count) for i in range(count)])  22.9 us
    ppermute x15, starting transfers between devices, turned(): lax.ppermute(value, axis, [(i, (i + steps) % count) for i in range(count)])  17 us
    pallas_call x5, Pallas kernels, choose(): pl.pallas_call(functools.partial(choose_kernel, first=first * rows), in_s...  13.2 us
    ppermute x4, starting transfers between devices, shifted(): return lax.ppermute(value, axis, pairs)  12.2 us
  transfers between devices with their start and end apart: 24, of which 9 were waited for; matrix products, arithmetic and copies ran while one was open for 0% of the time, Pallas kernels for 35%

profile of v8, /device:TPU:97, one launch (start us, length us, event | category | flops | bytes accessed | tf_op | source)
XLA Modules:
  0.0 221.8 jit_solution(10296838297487558961)
XLA Ops:
  0.0 3.0 %extract.2 = (bf16[2,1152,128]{2,1,0:T(8,128)(2,1)}, bf16[2,1296,128]{2,1,0:T(8,128)(2,1)}, f32[4,144,128]{2,1,0:T(8,128)S(1)}) custom-call(bf16[256,256]{1,0:T(8,128)(2,1)} %constant.28.clone.apart_ref, bf16[288,288]{1,0:T(8,128)(2,1)} %constant.29.clone.face_move_ref, bf16[64,18,16,128]{3,2,1,0:T(8,128)(2,1)} %bitcast.35, bf16[18,16,128]{2,1,0:T(8,128)(2,1)} %bitcast.37, ...), custom_call_target="tpu_custom_call" | custom-call | flops 2000000 | bytes 2400000 | tf_op jit(solution)/shard_map/extract/pallas_call | solution.py:108
  3.0 5.0 %extract.3 = (bf16[6,1152,128]{2,1,0:T(8,128)(2,1)S(1)}, bf16[6,1152,128]{2,1,0:T(8,128)(2,1)S(1)}) custom-call(bf16[256,256]{1,0:T(8,128)(2,1)} %constant.28.clone.apart_ref, bf16[288,288]{1,0:T(8,128)(2,1)} %constant.29.clone.face_move_ref, bf16[64,18,16,128]{3,2,1,0:T(8,128)(2,1)} %bitcast.36, bf16[18,16,128]{2,1,0:T(8,128)(2,1)} %bitcast.38, ...), custom_call_target="tpu_custom_call" | custom-call | flops 6000000 | bytes 7200000 | tf_op jit(solution)/shard_map/extract/pallas_call | solution.py:108
  8.0 2.3 %collective-permute-start = (bf16[6,1152,128]{2,1,0:T(8,128)(2,1)S(1)}, bf16[6,1152,128]{2,1,0:T(8,128)(2,1)}, u32[]{:S(2)}, u32[]{:S(2)}) collective-permute-start(bf16[6,1152,128]{2,1,0:T(8,128)(2,1)S(1)} %get-tuple-element.38.refs_0_.north_ref), channel_id=1, source_target_pairs={{0,4},{4,8},{8,12},{12,16},{16,20},{20,24},{24,28},{28,32},{32,36}... | collective-permute-start | bytes 5308424 | tf_op jit(solution)/shard_map/ppermute | solution.py:503
  10.3 2.2 collective-permute-start.1
  12.5 3.6 %collective-permute-start.2 = (bf16[2,1296,128]{2,1,0:T(8,128)(2,1)}, bf16[2,1296,128]{2,1,0:T(8,128)(2,1)}, u32[]{:S(2)}, u32[]{:S(2)}) collective-permute-start(bf16[2,1296,128]{2,1,0:T(8,128)(2,1)} %get-tuple-element.40.south_ref), channel_id=1, source_target_pairs={{4,0},{8,4},{12,8},{16,12},{20,16},{24,20},{28,24},{32,28},{36,32}... | collective-permute-start | bytes 1990664 | tf_op jit(solution)/shard_map/ppermute | solution.py:503
  16.2 4.0 %collective-permute-start.3 = (bf16[2,1152,128]{2,1,0:T(8,128)(2,1)}, bf16[2,1152,128]{2,1,0:T(8,128)(2,1)}, u32[]{:S(2)}, u32[]{:S(2)}) collective-permute-start(bf16[2,1152,128]{2,1,0:T(8,128)(2,1)} %get-tuple-element.36.refs_0_.north_ref), channel_id=1, source_target_pairs={{0,4},{4,8},{8,12},{12,16},{16,20},{20,24},{24,28},{28,32},{32,36}... | collective-permute-start | bytes 1769480 | tf_op jit(solution)/shard_map/ppermute | solution.py:503
  20.2 16.0 %collective-permute-done.3.low_ref = bf16[2,1152,128]{2,1,0:T(8,128)(2,1)} collective-permute-done((bf16[2,1152,128]{2,1,0:T(8,128)(2,1)}, bf16[2,1152,128]{2,1,0:T(8,128)(2,1)}, u32[]{:S(2)}, u32[]{:S(2)}) %collective-permute-start.3) | collective-permute-done | bytes 589856 | tf_op jit(solution)/shard_map/ppermute | solution.py:503
  36.2 7.3 %collective-permute-done.2.high_ref.above_ref = bf16[2,1296,128]{2,1,0:T(8,128)(2,1)} collective-permute-done((bf16[2,1296,128]{2,1,0:T(8,128)(2,1)}, bf16[2,1296,128]{2,1,0:T(8,128)(2,1)}, u32[]{:S(2)}, u32[]{:S(2)}) %collective-permute-start.2) | collective-permute-done | bytes 663584 | tf_op jit(solution)/shard_map/ppermute | solution.py:503
  43.5 1.0 copy-done.1
  44.5 5.6 %advect.5 = (bf16[2,144,512]{2,1,0:T(8,128)(2,1)S(1)}, bf16[2,144,512]{2,1,0:T(8,128)(2,1)S(1)}, bf16[2,144,512]{2,1,0:T(8,128)(2,1)S(1)}, bf16[2,144,512]{2,1,0:T(8,128)(2,1)S(1)}) custom-call(s32[1]{0:T(128)} %bitcast.1.place_ref, bf16[2,1296,128]{2,1,0:T(8,128)(2,1)} %get-tuple-element.40.south_ref, ...), custom_call_target="tpu_custom_call" | custom-call | flops 20000000 | bytes 4000000 | tf_op jit(solution)/shard_map/advect/pallas_call | solution.py:214
  50.1 1.4 collective-permute-start.4
  51.5 2.6 %collective-permute-start.5 = (bf16[2,144,512]{2,1,0:T(8,128)(2,1)S(1)}, bf16[2,144,512]{2,1,0:T(8,128)(2,1)S(1)}, u32[]{:S(2)}, u32[]{:S(2)}) collective-permute-start(bf16[2,144,512]{2,1,0:T(8,128)(2,1)S(1)} %get-tuple-element.43), channel_id=1, source_target_pairs={{0,2},{1,3},{2,0},{3,1},{4,6},{5,7},{6,4},{7,5},{8,10},{9,11},{10,... | collective-permute-start | bytes 884744 | tf_op jit(solution)/shard_map/ppermute | solution.py:508
  54.1 1.1 collective-permute-start.6
  55.2 7.4 %tables.1 = (bf16[256,72,128]{2,1,0:T(8,128)(2,1)S(1)}, bf16[512,512]{1,0:T(8,128)(2,1)S(1)}, bf16[256,512]{1,0:T(8,128)(2,1)S(1)}, bf16[256,512]{1,0:T(8,128)(2...) custom-call(bf16[72,72,512]{2,1,0:T(8,128)(2,1)} %matrix_ref.1, s32[1,512]{1,0:T(1,128)} %bitcast.41, ...), custom_call_target="tpu_custom_call" | custom-call | flops 2415919104 | bytes 12000000 | tf_op jit(solution)/shard_map/tables/pallas_call | solution.py:301
  62.6 0.0 collective-permute-done.4.part1
  62.6 3.5 %collective-permute-done.5.part2 = bf16[2,144,512]{2,1,0:T(8,128)(2,1)S(1)} collective-permute-done((bf16[2,144,512]{2,1,0:T(8,128)(2,1)S(1)}, bf16[2,144,512]{2,1,0:T(8,128)(2,1)S(1)}, u32[]{:S(2)}, u32[]{:S(2)}) %collective-permute-start.5) | collective-permute-done | bytes 294944 | tf_op jit(solution)/shard_map/ppermute | solution.py:508
  66.2 0.0 collective-permute-done.6.part3
  66.2 9.2 %physics.5 = bf16[16,72,512]{2,1,0:T(8,128)(2,1)} custom-call(s32[1]{0:T(128)} %bitcast.1.place_ref, f32[64]{0:T(128)S(1)} %copy-done.3, bf16[2,144,512]{2,1,0:T(8,128)(2,1)S(1)} %get-tuple-element.41.refs_0_.part0, bf16[2,144,512]{2,1,0:T(8,128)(2,1)S(1)} %collective-permute-done.4.part1, bf16[2,144,512]{2,1,0:T(8,128)(2,1)S(1)} %collective-permute-done.5.part2, ...), custom_call_target="tpu_custom_call" | custom-call | flops 1509949440 | bytes 8900000 | tf_op jit(solution)/shard_map/physics/pallas_call | solution.py:414
  75.3 0.0 collective-permute-done.low_ref
  75.4 0.0 collective-permute-done.1.high_ref
  75.4 3.2 %advect.6 = (bf16[1,144,512]{2,1,0:T(8,128)(2,1)S(1)}, bf16[1,144,512]{2,1,0:T(8,128)(2,1)S(1)}, bf16[1,144,512]{2,1,0:T(8,128)(2,1)S(1)}, bf16[1,144,512]{2,1,0:T(8,128)(2,1)S(1)}) custom-call(s32[1]{0:T(128)} %bitcast.1.place_ref, bf16[6,1152,128]{2,1,0:T(8,128)(2,1)S(1)} %get-tuple-element.37.south_ref, ...), custom_call_target="tpu_custom_call" | custom-call | flops 10000000 | bytes 2000000 | tf_op jit(solution)/shard_map/advect/pallas_call | solution.py:214
  78.6 5.5 %advect.7 = (bf16[2,144,512]{2,1,0:T(8,128)(2,1)S(1)}, bf16[2,144,512]{2,1,0:T(8,128)(2,1)S(1)}, bf16[2,144,512]{2,1,0:T(8,128)(2,1)S(1)}, bf16[2,144,512]{2,1,0:T(8,128)(2,1)S(1)}) custom-call(s32[1]{0:T(128)} %bitcast.1.place_ref, bf16[6,1152,128]{2,1,0:T(8,128)(2,1)S(1)} %get-tuple-element.37.south_ref, ...), custom_call_target="tpu_custom_call" | custom-call | flops 20000000 | bytes 4000000 | tf_op jit(solution)/shard_map/advect/pallas_call | solution.py:214
  84.1 1.4 collective-permute-start.7
  85.5 0.9 collective-permute-start.10
  86.4 1.6 collective-permute-start.11
  88.0 1.6 collective-permute-start.12
  89.6 0.9 collective-permute-start.8
  90.5 6.9 %collective-permute-done.10.part1 = bf16[1,144,512]{2,1,0:T(8,128)(2,1)S(1)} collective-permute-done((bf16[1,144,512]{2,1,0:T(8,128)(2,1)S(1)}, bf16[1,144,512]{2,1,0:T(8,128)(2,1)S(1)}, u32[]{:S(2)}, u32[]{:S(2)}) %collective-permute-start.10) | collective-permute-done | bytes 147488 | tf_op jit(solution)/shard_map/ppermute | solution.py:508
  97.4 0.3 collective-permute-start.9
  97.7 2.9 %collective-permute-done.11.part2 = bf16[1,144,512]{2,1,0:T(8,128)(2,1)S(1)} collective-permute-done((bf16[1,144,512]{2,1,0:T(8,128)(2,1)S(1)}, bf16[1,144,512]{2,1,0:T(8,128)(2,1)S(1)}, u32[]{:S(2)}, u32[]{:S(2)}) %collective-permute-start.11) | collective-permute-done | bytes 147488 | tf_op jit(solution)/shard_map/ppermute | solution.py:508
  100.6 0.0 collective-permute-done.12.part3
  100.6 7.1 %physics.6 = bf16[8,72,512]{2,1,0:T(8,128)(2,1)} custom-call(s32[1]{0:T(128)} %bitcast.1.place_ref, f32[64]{0:T(128)S(1)} %copy-done.3, bf16[1,144,512]{2,1,0:T(8,128)(2,1)S(1)} %get-tuple-element.51.refs_0_.part0, bf16[1,144,512]{2,1,0:T(8,128)(2,1)S(1)} %collective-permute-done.10.part1, bf16[1,144,512]{2,1,0:T(8,128)(2,1)S(1)} %collective-permute-done.11.part2, ...), custom_call_target="tpu_custom_call" | custom-call | flops 754974720 | bytes 7700000 | tf_op jit(solution)/shard_map/physics/pallas_call | solution.py:414
  107.6 5.5 %advect.8 = (bf16[2,144,512]{2,1,0:T(8,128)(2,1)S(1)}, bf16[2,144,512]{2,1,0:T(8,128)(2,1)S(1)}, bf16[2,144,512]{2,1,0:T(8,128)(2,1)S(1)}, bf16[2,144,512]{2,1,0:T(8,128)(2,1)S(1)}) custom-call(s32[1]{0:T(128)} %bitcast.1.place_ref, bf16[6,1152,128]{2,1,0:T(8,128)(2,1)S(1)} %get-tuple-element.37.south_ref, ...), custom_call_target="tpu_custom_call" | custom-call | flops 20000000 | bytes 4000000 | tf_op jit(solution)/shard_map/advect/pallas_call | solution.py:214
  113.1 0.1 collective-permute-start.16
  113.2 1.4 collective-permute-start.17
  114.6 0.0 collective-permute-done.7.part1
  114.6 2.0 collective-permute-start.18
  116.6 0.0 collective-permute-done.8.part2
  116.6 2.7 %collective-permute-start.23 = (bf16[1152,512]{1,0:T(8,128)(2,1)}, bf16[1152,512]{1,0:T(8,128)(2,1)}, u32[]{:S(2)}, u32[]{:S(2)}) collective-permute-start(bf16[1152,512]{1,0:T(8,128)(2,1)} %bitcast.19.refs_0_.own_ref), channel_id=1, source_target_pairs={{0,64},{4,68},{8,72},{12,76},{16,80},{20,84},{24,88},{28,92},{32,9... | collective-permute-start | bytes 3538952 | tf_op jit(solution)/shard_map/ppermute | solution.py:513
  119.3 0.0 collective-permute-done.9.part3
  119.3 9.1 %physics.7 = bf16[16,72,512]{2,1,0:T(8,128)(2,1)} custom-call(s32[1]{0:T(128)} %bitcast.1.place_ref, f32[64]{0:T(128)S(1)} %copy-done.3, bf16[2,144,512]{2,1,0:T(8,128)(2,1)S(1)} %get-tuple-element.52.refs_0_.part0, bf16[2,144,512]{2,1,0:T(8,128)(2,1)S(1)} %collective-permute-done.7.part1, bf16[2,144,512]{2,1,0:T(8,128)(2,1)S(1)} %collective-permute-done.8.part2, ...), custom_call_target="tpu_custom_call" | custom-call | flops 1509949440 | bytes 8900000 | tf_op jit(solution)/shard_map/physics/pallas_call | solution.py:414
  128.5 0.3 collective-permute-start.21
  128.8 3.2 %advect.9 = (bf16[1,144,512]{2,1,0:T(8,128)(2,1)S(1)}, bf16[1,144,512]{2,1,0:T(8,128)(2,1)S(1)}, bf16[1,144,512]{2,1,0:T(8,128)(2,1)S(1)}, bf16[1,144,512]{2,1,0:T(8,128)(2,1)S(1)}) custom-call(s32[1]{0:T(128)} %bitcast.1.place_ref, bf16[6,1152,128]{2,1,0:T(8,128)(2,1)S(1)} %get-tuple-element.37.south_ref, ...), custom_call_target="tpu_custom_call" | custom-call | flops 10000000 | bytes 2000000 | tf_op jit(solution)/shard_map/advect/pallas_call | solution.py:214
  132.0 0.0 collective-permute-done.17.part2
  132.0 0.0 collective-permute-done.18.part3
  132.0 11.4 %physics.8 = bf16[16,72,512]{2,1,0:T(8,128)(2,1)S(1)} custom-call(s32[1]{0:T(128)} %bitcast.1.place_ref, f32[64]{0:T(128)S(1)} %copy-done.3, bf16[2,144,512]{2,1,0:T(8,128)(2,1)S(1)} %get-tuple-element.59.refs_0_.part0, bf16[2,144,512]{2,1,0:T(8,128)(2,1)S(1)} %collective-permute-done.16.part1, bf16[2,144,512]{2,1,0:T(8,128)(2,1)S(1)} %collective-permute-done.17.part2, ...), custom_call_target="tpu_custom_call" | custom-call | flops 1509949440 | bytes 8900000 | tf_op jit(solution)/shard_map/physics/pallas_call | solution.py:414
  143.4 2.8 %collective-permute-start.20 = (bf16[1152,512]{1,0:T(8,128)(2,1)S(1)}, bf16[1152,512]{1,0:T(8,128)(2,1)S(1)}, u32[]{:S(2)}, u32[]{:S(2)}) collective-permute-start(bf16[1152,512]{1,0:T(8,128)(2,1)S(1)} %bitcast.32), channel_id=1, source_target_pairs={{0,64},{4,68},{8,72},{12,76},{16,80},{20,84},{24,88},{28,92},{32,9... | collective-permute-start | bytes 3538952 | tf_op jit(solution)/shard_map/ppermute | solution.py:513
  146.3 0.0 collective-permute-start.13
  146.3 1.8 collective-permute-start.14
  148.1 5.4 %collective-permute-done.13.part1 = bf16[1,144,512]{2,1,0:T(8,128)(2,1)S(1)} collective-permute-done((bf16[1,144,512]{2,1,0:T(8,128)(2,1)S(1)}, bf16[1,144,512]{2,1,0:T(8,128)(2,1)S(1)}, u32[]{:S(2)}, u32[]{:S(2)}) %collective-permute-start.13) | collective-permute-done | bytes 147488 | tf_op jit(solution)/shard_map/ppermute | solution.py:508
  153.5 0.0 collective-permute-start.15
  153.5 0.0 collective-permute-done.14.part2
  153.5 0.2 collective-permute-start.22
  153.6 4.2 %collective-permute-done.15.part3 = bf16[1,144,512]{2,1,0:T(8,128)(2,1)S(1)} collective-permute-done((bf16[1,144,512]{2,1,0:T(8,128)(2,1)S(1)}, bf16[1,144,512]{2,1,0:T(8,128)(2,1)S(1)}, u32[]{:S(2)}, u32[]{:S(2)}) %collective-permute-start.15) | collective-permute-done | bytes 147488 | tf_op jit(solution)/shard_map/ppermute | solution.py:508
  157.8 7.9 %physics.9 = bf16[8,72,512]{2,1,0:T(8,128)(2,1)S(1)} custom-call(s32[1]{0:T(128)} %bitcast.1.place_ref, f32[64]{0:T(128)S(1)} %copy-done.3, bf16[1,144,512]{2,1,0:T(8,128)(2,1)S(1)} %get-tuple-element.60.refs_0_.part0, bf16[1,144,512]{2,1,0:T(8,128)(2,1)S(1)} %collective-permute-done.13.part1, bf16[1,144,512]{2,1,0:T(8,128)(2,1)S(1)} %collective-permute-done.14.part2, ...), custom_call_target="tpu_custom_call" | custom-call | flops 754974720 | bytes 7700000 | tf_op jit(solution)/shard_map/physics/pallas_call | solution.py:414
  165.8 0.3 collective-permute-start.19
  166.0 2.7 %choose.5.refs_0_ = bf16[4608,512]{1,0:T(8,128)(2,1)} custom-call(s32[1]{0:T(128)} %bitcast.pair_ref, s32[64]{0:T(128)S(1)} %copy-done.4, bf16[1152,512]{1,0:T(8,128)(2,1)} %bitcast.19.refs_0_.own_ref, bf16[1152,512]{1,0:T(8,128)(2,1)} %collective-permute-done.23.partner_ref, bf16[576,512]{1,0:T(8,128)(2,1)S(1)} %bitcast.26), custom_call_target="tpu_custom_call" | custom-call | bytes 2400000 | tf_op jit(solution)/shard_map/choose/pallas_call | solution.py:481
  168.7 38.2 %collective-permute-done.22.partner_ref = bf16[576,512]{1,0:T(8,128)(2,1)} collective-permute-done((bf16[576,512]{1,0:T(8,128)(2,1)}, bf16[576,512]{1,0:T(8,128)(2,1)}, u32[]{:S(2)}, u32[]{:S(2)}) %collective-permute-start.22) | collective-permute-done | bytes 589856 | tf_op jit(solution)/shard_map/ppermute | solution.py:513
  206.9 2.4 %choose.6.refs_0_ = bf16[4608,512]{1,0:T(8,128)(2,1)} custom-call(s32[1]{0:T(128)} %bitcast.pair_ref, s32[64]{0:T(128)S(1)} %copy-done.4, bf16[576,512]{1,0:T(8,128)(2,1)} %bitcast.20.refs_0_.own_ref, bf16[576,512]{1,0:T(8,128)(2,1)} %collective-permute-done.22.partner_ref, bf16[4608,512]{1,0:T(8,128)(2,1)} %choose.5.refs_0_, ...), custom_call_target="tpu_custom_call", output_to_operand_aliasing={{}: (4, {})} | custom-call | bytes 1200000 | tf_op jit(solution)/shard_map/choose/pallas_call | solution.py:481
  209.3 0.0 collective-permute-done.21.partner_ref
  209.3 2.7 %choose.7.refs_0_ = bf16[4608,512]{1,0:T(8,128)(2,1)} custom-call(s32[1]{0:T(128)} %bitcast.pair_ref, s32[64]{0:T(128)S(1)} %copy-done.4, bf16[1152,512]{1,0:T(8,128)(2,1)} %bitcast.21.refs_0_.own_ref, bf16[1152,512]{1,0:T(8,128)(2,1)} %collective-permute-done.21.partner_ref, bf16[4608,512]{1,0:T(8,128)(2,1)} %choose.6.refs_0_, ...), custom_call_target="tpu_custom_call", output_to_operand_aliasing={{}: (4, {})} | custom-call | bytes 2400000 | tf_op jit(solution)/shard_map/choose/pallas_call | solution.py:481
  212.0 3.2 %choose.8.refs_0_ = bf16[4608,512]{1,0:T(8,128)(2,1)} custom-call(s32[1]{0:T(128)} %bitcast.pair_ref, s32[64]{0:T(128)S(1)} %copy-done.4, bf16[1152,512]{1,0:T(8,128)(2,1)S(1)} %bitcast.34, bf16[1152,512]{1,0:T(8,128)(2,1)S(1)} %collective-permute-done.20.partner_ref, bf16[4608,512]{1,0:T(8,128)(2,1)} %choose.7.refs_0_, ...), custom_call_target="tpu_custom_call", output_to_operand_aliasing={{}: (4, {})} | custom-call | bytes 2400000 | tf_op jit(solution)/shard_map/choose/pallas_call | solution.py:481
  215.2 4.2 %collective-permute-done.19.partner_ref = bf16[576,512]{1,0:T(8,128)(2,1)S(1)} collective-permute-done((bf16[576,512]{1,0:T(8,128)(2,1)S(1)}, bf16[576,512]{1,0:T(8,128)(2,1)S(1)}, u32[]{:S(2)}, u32[]{:S(2)}) %collective-permute-start.19) | collective-permute-done | bytes 589856 | tf_op jit(solution)/shard_map/ppermute | solution.py:513
  219.4 2.2 choose.9
  (12 shorter events, 0.0 us)
Async XLA Ops:
  3.0 5.0 %copy-start = (f32[4,144,128]{2,1,0:T(8,128)}, f32[4,144,128]{2,1,0:T(8,128)S(1)}, u32[]{:S(2)}) copy-start(f32[4,144,128]{2,1,0:T(8,128)S(1)} %get-tuple-element.39.faces_ref) | copy-start | bytes 884740
  8.0 67.3 %collective-permute-start = (bf16[6,1152,128]{2,1,0:T(8,128)(2,1)S(1)}, bf16[6,1152,128]{2,1,0:T(8,128)(2,1)}, u32[]{:S(2)}, u32[]{:S(2)}) collective-permute-start(bf16[6,1152,128]{2,1,0:T(8,128)(2,1)S(1)} %get-tuple-element.38.refs_0_.north_ref), channel_id=1, source_target_pairs={{0,4},{4,8},{8,12},{12,16},{16,20},{20,24},{24,28},{28,32},{32,36}... | collective-permute-start | bytes 5308424 | tf_op jit(solution)/shard_map/ppermute | solution.py:503
  10.3 65.0 %collective-permute-start.1 = (bf16[6,1152,128]{2,1,0:T(8,128)(2,1)S(1)}, bf16[6,1152,128]{2,1,0:T(8,128)(2,1)}, u32[]{:S(2)}, u32[]{:S(2)}) collective-permute-start(bf16[6,1152,128]{2,1,0:T(8,128)(2,1)S(1)} %get-tuple-element.37.south_ref), channel_id=1, source_target_pairs={{4,0},{8,4},{12,8},{16,12},{20,16},{24,20},{28,24},{32,28},{36,32}... | collective-permute-start | bytes 5308424 | tf_op jit(solution)/shard_map/ppermute | solution.py:503
  12.5 31.0 %collective-permute-start.2 = (bf16[2,1296,128]{2,1,0:T(8,128)(2,1)}, bf16[2,1296,128]{2,1,0:T(8,128)(2,1)}, u32[]{:S(2)}, u32[]{:S(2)}) collective-permute-start(bf16[2,1296,128]{2,1,0:T(8,128)(2,1)} %get-tuple-element.40.south_ref), channel_id=1, source_target_pairs={{4,0},{8,4},{12,8},{16,12},{20,16},{24,20},{28,24},{32,28},{36,32}... | collective-permute-start | bytes 1990664 | tf_op jit(solution)/shard_map/ppermute | solution.py:503
  16.2 20.0 %collective-permute-start.3 = (bf16[2,1152,128]{2,1,0:T(8,128)(2,1)}, bf16[2,1152,128]{2,1,0:T(8,128)(2,1)}, u32[]{:S(2)}, u32[]{:S(2)}) collective-permute-start(bf16[2,1152,128]{2,1,0:T(8,128)(2,1)} %get-tuple-element.36.refs_0_.north_ref), channel_id=1, source_target_pairs={{0,4},{4,8},{8,12},{12,16},{16,20},{20,24},{24,28},{28,32},{32,36}... | collective-permute-start | bytes 1769480 | tf_op jit(solution)/shard_map/ppermute | solution.py:503
  43.5 1.0 copy-start.1
  50.1 12.5 %collective-permute-start.4 = (bf16[2,144,512]{2,1,0:T(8,128)(2,1)S(1)}, bf16[2,144,512]{2,1,0:T(8,128)(2,1)S(1)}, u32[]{:S(2)}, u32[]{:S(2)}) collective-permute-start(bf16[2,144,512]{2,1,0:T(8,128)(2,1)S(1)} %get-tuple-element.42), channel_id=1, source_target_pairs={{0,1},{1,2},{2,3},{3,0},{4,5},{5,6},{6,7},{7,4},{8,9},{9,10},{10,1... | collective-permute-start | bytes 884744 | tf_op jit(solution)/shard_map/ppermute | solution.py:508
  51.5 14.7 %collective-permute-start.5 = (bf16[2,144,512]{2,1,0:T(8,128)(2,1)S(1)}, bf16[2,144,512]{2,1,0:T(8,128)(2,1)S(1)}, u32[]{:S(2)}, u32[]{:S(2)}) collective-permute-start(bf16[2,144,512]{2,1,0:T(8,128)(2,1)S(1)} %get-tuple-element.43), channel_id=1, source_target_pairs={{0,2},{1,3},{2,0},{3,1},{4,6},{5,7},{6,4},{7,5},{8,10},{9,11},{10,... | collective-permute-start | bytes 884744 | tf_op jit(solution)/shard_map/ppermute | solution.py:508
  54.1 12.0 %collective-permute-start.6 = (bf16[2,144,512]{2,1,0:T(8,128)(2,1)S(1)}, bf16[2,144,512]{2,1,0:T(8,128)(2,1)S(1)}, u32[]{:S(2)}, u32[]{:S(2)}) collective-permute-start(bf16[2,144,512]{2,1,0:T(8,128)(2,1)S(1)} %get-tuple-element.44), channel_id=1, source_target_pairs={{0,3},{1,0},{2,1},{3,2},{4,7},{5,4},{6,5},{7,6},{8,11},{9,8},{10,9... | collective-permute-start | bytes 884744 | tf_op jit(solution)/shard_map/ppermute | solution.py:508
  55.2 11.0 %copy-start.3 = (f32[64]{0:T(128)S(1)}, f32[64]{0:T(128)}, u32[]{:S(2)}) copy-start(f32[64]{0:T(128)} %scav_ref.9) | copy-start | bytes 772
  66.2 9.2 %copy-start.2 = (f32[4,144,128]{2,1,0:T(8,128)S(1)}, f32[4,144,128]{2,1,0:T(8,128)}, u32[]{:S(2)}) copy-start(f32[4,144,128]{2,1,0:T(8,128)} %copy-done) | copy-start | bytes 884740
  84.1 30.5 %collective-permute-start.7 = (bf16[2,144,512]{2,1,0:T(8,128)(2,1)S(1)}, bf16[2,144,512]{2,1,0:T(8,128)(2,1)S(1)}, u32[]{:S(2)}, u32[]{:S(2)}) collective-permute-start(bf16[2,144,512]{2,1,0:T(8,128)(2,1)S(1)} %get-tuple-element.53), channel_id=1, source_target_pairs={{0,1},{1,2},{2,3},{3,0},{4,5},{5,6},{6,7},{7,4},{8,9},{9,10},{10,1... | collective-permute-start | bytes 884744 | tf_op jit(solution)/shard_map/ppermute | solution.py:508
  85.5 11.9 %collective-permute-start.10 = (bf16[1,144,512]{2,1,0:T(8,128)(2,1)S(1)}, bf16[1,144,512]{2,1,0:T(8,128)(2,1)S(1)}, u32[]{:S(2)}, u32[]{:S(2)}) collective-permute-start(bf16[1,144,512]{2,1,0:T(8,128)(2,1)S(1)} %get-tuple-element.56), channel_id=1, source_target_pairs={{0,1},{1,2},{2,3},{3,0},{4,5},{5,6},{6,7},{7,4},{8,9},{9,10},{10,1... | collective-permute-start | bytes 442376 | tf_op jit(solution)/shard_map/ppermute | solution.py:508
  86.4 14.2 %collective-permute-start.11 = (bf16[1,144,512]{2,1,0:T(8,128)(2,1)S(1)}, bf16[1,144,512]{2,1,0:T(8,128)(2,1)S(1)}, u32[]{:S(2)}, u32[]{:S(2)}) collective-permute-start(bf16[1,144,512]{2,1,0:T(8,128)(2,1)S(1)} %get-tuple-element.57), channel_id=1, source_target_pairs={{0,2},{1,3},{2,0},{3,1},{4,6},{5,7},{6,4},{7,5},{8,10},{9,11},{10,... | collective-permute-start | bytes 442376 | tf_op jit(solution)/shard_map/ppermute | solution.py:508
  88.0 12.6 %collective-permute-start.12 = (bf16[1,144,512]{2,1,0:T(8,128)(2,1)S(1)}, bf16[1,144,512]{2,1,0:T(8,128)(2,1)S(1)}, u32[]{:S(2)}, u32[]{:S(2)}) collective-permute-start(bf16[1,144,512]{2,1,0:T(8,128)(2,1)S(1)} %get-tuple-element.58), channel_id=1, source_target_pairs={{0,3},{1,0},{2,1},{3,2},{4,7},{5,4},{6,5},{7,6},{8,11},{9,8},{10,9... | collective-permute-start | bytes 442376 | tf_op jit(solution)/shard_map/ppermute | solution.py:508
  89.6 27.0 %collective-permute-start.8 = (bf16[2,144,512]{2,1,0:T(8,128)(2,1)S(1)}, bf16[2,144,512]{2,1,0:T(8,128)(2,1)S(1)}, u32[]{:S(2)}, u32[]{:S(2)}) collective-permute-start(bf16[2,144,512]{2,1,0:T(8,128)(2,1)S(1)} %get-tuple-element.54), channel_id=1, source_target_pairs={{0,2},{1,3},{2,0},{3,1},{4,6},{5,7},{6,4},{7,5},{8,10},{9,11},{10,... | collective-permute-start | bytes 884744 | tf_op jit(solution)/shard_map/ppermute | solution.py:508
  97.4 21.9 %collective-permute-start.9 = (bf16[2,144,512]{2,1,0:T(8,128)(2,1)S(1)}, bf16[2,144,512]{2,1,0:T(8,128)(2,1)S(1)}, u32[]{:S(2)}, u32[]{:S(2)}) collective-permute-start(bf16[2,144,512]{2,1,0:T(8,128)(2,1)S(1)} %get-tuple-element.55), channel_id=1, source_target_pairs={{0,3},{1,0},{2,1},{3,2},{4,7},{5,4},{6,5},{7,6},{8,11},{9,8},{10,9... | collective-permute-start | bytes 884744 | tf_op jit(solution)/shard_map/ppermute | solution.py:508
  113.1 18.9 %collective-permute-start.16 = (bf16[2,144,512]{2,1,0:T(8,128)(2,1)S(1)}, bf16[2,144,512]{2,1,0:T(8,128)(2,1)S(1)}, u32[]{:S(2)}, u32[]{:S(2)}) collective-permute-start(bf16[2,144,512]{2,1,0:T(8,128)(2,1)S(1)} %get-tuple-element.64), channel_id=1, source_target_pairs={{0,1},{1,2},{2,3},{3,0},{4,5},{5,6},{6,7},{7,4},{8,9},{9,10},{10,1... | collective-permute-start | bytes 884744 | tf_op jit(solution)/shard_map/ppermute | solution.py:508
  113.2 18.8 %collective-permute-start.17 = (bf16[2,144,512]{2,1,0:T(8,128)(2,1)S(1)}, bf16[2,144,512]{2,1,0:T(8,128)(2,1)S(1)}, u32[]{:S(2)}, u32[]{:S(2)}) collective-permute-start(bf16[2,144,512]{2,1,0:T(8,128)(2,1)S(1)} %get-tuple-element.65), channel_id=1, source_target_pairs={{0,2},{1,3},{2,0},{3,1},{4,6},{5,7},{6,4},{7,5},{8,10},{9,11},{10,... | collective-permute-start | bytes 884744 | tf_op jit(solution)/shard_map/ppermute | solution.py:508
  114.6 17.4 %collective-permute-start.18 = (bf16[2,144,512]{2,1,0:T(8,128)(2,1)S(1)}, bf16[2,144,512]{2,1,0:T(8,128)(2,1)S(1)}, u32[]{:S(2)}, u32[]{:S(2)}) collective-permute-start(bf16[2,144,512]{2,1,0:T(8,128)(2,1)S(1)} %get-tuple-element.66), channel_id=1, source_target_pairs={{0,3},{1,0},{2,1},{3,2},{4,7},{5,4},{6,5},{7,6},{8,11},{9,8},{10,9... | collective-permute-start | bytes 884744 | tf_op jit(solution)/shard_map/ppermute | solution.py:508
  116.6 49.5 %collective-permute-start.23 = (bf16[1152,512]{1,0:T(8,128)(2,1)}, bf16[1152,512]{1,0:T(8,128)(2,1)}, u32[]{:S(2)}, u32[]{:S(2)}) collective-permute-start(bf16[1152,512]{1,0:T(8,128)(2,1)} %bitcast.19.refs_0_.own_ref), channel_id=1, source_target_pairs={{0,64},{4,68},{8,72},{12,76},{16,80},{20,84},{24,88},{28,92},{32,9... | collective-permute-start | bytes 3538952 | tf_op jit(solution)/shard_map/ppermute | solution.py:513
  128.5 80.8 %collective-permute-start.21 = (bf16[1152,512]{1,0:T(8,128)(2,1)}, bf16[1152,512]{1,0:T(8,128)(2,1)}, u32[]{:S(2)}, u32[]{:S(2)}) collective-permute-start(bf16[1152,512]{1,0:T(8,128)(2,1)} %bitcast.21.refs_0_.own_ref), channel_id=1, source_target_pairs={{0,64},{4,68},{8,72},{12,76},{16,80},{20,84},{24,88},{28,92},{32,9... | collective-permute-start | bytes 3538952 | tf_op jit(solution)/shard_map/ppermute | solution.py:513
  143.4 68.6 %collective-permute-start.20 = (bf16[1152,512]{1,0:T(8,128)(2,1)S(1)}, bf16[1152,512]{1,0:T(8,128)(2,1)S(1)}, u32[]{:S(2)}, u32[]{:S(2)}) collective-permute-start(bf16[1152,512]{1,0:T(8,128)(2,1)S(1)} %bitcast.32), channel_id=1, source_target_pairs={{0,64},{4,68},{8,72},{12,76},{16,80},{20,84},{24,88},{28,92},{32,9... | collective-permute-start | bytes 3538952 | tf_op jit(solution)/shard_map/ppermute | solution.py:513
  146.3 7.2 %collective-permute-start.13 = (bf16[1,144,512]{2,1,0:T(8,128)(2,1)S(1)}, bf16[1,144,512]{2,1,0:T(8,128)(2,1)S(1)}, u32[]{:S(2)}, u32[]{:S(2)}) collective-permute-start(bf16[1,144,512]{2,1,0:T(8,128)(2,1)S(1)} %get-tuple-element.61), channel_id=1, source_target_pairs={{0,1},{1,2},{2,3},{3,0},{4,5},{5,6},{6,7},{7,4},{8,9},{9,10},{10,1... | collective-permute-start | bytes 442376 | tf_op jit(solution)/shard_map/ppermute | solution.py:508
  146.3 7.2 %collective-permute-start.14 = (bf16[1,144,512]{2,1,0:T(8,128)(2,1)S(1)}, bf16[1,144,512]{2,1,0:T(8,128)(2,1)S(1)}, u32[]{:S(2)}, u32[]{:S(2)}) collective-permute-start(bf16[1,144,512]{2,1,0:T(8,128)(2,1)S(1)} %get-tuple-element.62), channel_id=1, source_target_pairs={{0,2},{1,3},{2,0},{3,1},{4,6},{5,7},{6,4},{7,5},{8,10},{9,11},{10,... | collective-permute-start | bytes 442376 | tf_op jit(solution)/shard_map/ppermute | solution.py:508
  153.5 12.6 %copy-start.4 = (s32[64]{0:T(128)S(1)}, s32[64]{0:T(128)}, u32[]{:S(2)}) copy-start(s32[64]{0:T(128)} %flag_ref.9) | copy-start | bytes 772
  153.5 4.4 %collective-permute-start.15 = (bf16[1,144,512]{2,1,0:T(8,128)(2,1)S(1)}, bf16[1,144,512]{2,1,0:T(8,128)(2,1)S(1)}, u32[]{:S(2)}, u32[]{:S(2)}) collective-permute-start(bf16[1,144,512]{2,1,0:T(8,128)(2,1)S(1)} %get-tuple-element.63), channel_id=1, source_target_pairs={{0,3},{1,0},{2,1},{3,2},{4,7},{5,4},{6,5},{7,6},{8,11},{9,8},{10,9... | collective-permute-start | bytes 442376 | tf_op jit(solution)/shard_map/ppermute | solution.py:508
  153.5 53.4 %collective-permute-start.22 = (bf16[576,512]{1,0:T(8,128)(2,1)}, bf16[576,512]{1,0:T(8,128)(2,1)}, u32[]{:S(2)}, u32[]{:S(2)}) collective-permute-start(bf16[576,512]{1,0:T(8,128)(2,1)} %bitcast.20.refs_0_.own_ref), channel_id=1, source_target_pairs={{0,64},{4,68},{8,72},{12,76},{16,80},{20,84},{24,88},{28,92},{32,9... | collective-permute-start | bytes 1769480 | tf_op jit(solution)/shard_map/ppermute | solution.py:513
  165.8 53.7 %collective-permute-start.19 = (bf16[576,512]{1,0:T(8,128)(2,1)S(1)}, bf16[576,512]{1,0:T(8,128)(2,1)S(1)}, u32[]{:S(2)}, u32[]{:S(2)}) collective-permute-start(bf16[576,512]{1,0:T(8,128)(2,1)S(1)} %bitcast.25), channel_id=1, source_target_pairs={{0,64},{4,68},{8,72},{12,76},{16,80},{20,84},{24,88},{28,92},{32,9... | collective-permute-start | bytes 1769480 | tf_op jit(solution)/shard_map/ppermute | solution.py:513

commit v9 on v8

--- a/solution.py
+++ b/solution.py
@@ -12,14 +12,14 @@
 
 GROUP = 8
 CHUNKS = (2, 1, 2, 2, 1)
-SPANS = ((0, 2), (2, 6))
+SPANS = ((0, 3), (3, 5))
 ORDER = (
     ("extract", 0),
     ("extract", 1),
     ("advect", 0),
     ("tables", 0),
+    ("advect", 1),
     ("physics", 0),
-    ("advect", 1),
     ("advect", 2),
     ("physics", 1),
     ("advect", 3),
@@ -34,6 +34,7 @@
     ("choose", 4),
 )
 CAP = 256
+STREAMS = 4
 P_BLOCK = 32
 F32 = jnp.float32
 BF16 = jnp.bfloat16
@@ -58,8 +59,9 @@
     return jnp.dot(a, b, preferred_element_type=F32)
 
 
-def two_levels(q_ref, pair):
-    return q_ref[:, 2 * pair : 2 * pair + 2].reshape(2 * GROUP * 16, 128)
+def two_levels(q_refs, pair):
+    rows = [q_ref[:, 2 * pair : 2 * pair + 2].reshape(-1, 128) for q_ref in q_refs]
+    return jnp.concatenate(rows, axis=0)
 
 
 def moved_rows(move, blocks):
@@ -71,12 +73,13 @@
     return moved
 
 
-def extract_kernel(apart_ref, face_move_ref, q_ref, lat_ref, lon_ref, *refs, faces_too):
+def extract_kernel(apart_ref, face_move_ref, lat_ref, lon_ref, *refs, faces_too):
+    q_refs = refs[:STREAMS]
     outs = refs[-3:] if faces_too else refs[-2:]
     north_ref, south_ref = outs[:2]
-    levels = q_ref.shape[1]
+    levels = q_refs[0].shape[1]
     rows = levels * GROUP * 8
-    blocks = [two_levels(q_ref, pair) for pair in range(levels // 2)]
+    blocks = [two_levels(q_refs, pair) for pair in range(levels // 2)]
     for pair, apart in enumerate(moved_rows(apart_ref[...], blocks)):
         for k in range(2):
             spot = pair * 128 + k * 64
@@ -111,9 +114,15 @@
         in_specs=[
             whole_block(*apart.shape),
             whole_block(*face_move.shape),
-            pl.BlockSpec((GROUP, levels, 16, 128), lambda g: (g + first, 0, 0, 0)),
             whole_block(*lat.shape),
             whole_block(*lon.shape),
+        ]
+        + [
+            pl.BlockSpec(
+                (GROUP // STREAMS, levels, 16, 128),
+                lambda g, i=i: ((g + first) * STREAMS + i, 0, 0, 0),
+            )
+            for i in range(STREAMS)
         ]
         + [pl.BlockSpec(memory_space=pl.ANY)] * len(after),
         out_specs=[
@@ -131,7 +140,7 @@
         ),
         compiler_params=pltpu.CompilerParams(vmem_limit_bytes=7 << 20),
         name="extract",
-    )(apart, face_move, q, lat, lon, *after)
+    )(apart, face_move, lat, lon, *[q] * STREAMS, *after)
 
 
 def beside(x, lane, toward_east):
@@ -417,7 +426,7 @@
         in_specs=[scalars, scalars]
         + [whole_block(*x.shape, once=True) for x in (*parts, *operands)]
         + [pl.BlockSpec(memory_space=pl.ANY)] * len(after),
-        out_specs=pl.BlockSpec(memory_space=pl.ANY),
+        out_specs=pl.BlockSpec(memory_space=pltpu.HBM),
         scratch_shapes=[
             pltpu.VMEM((tracers, 128, columns), BF16),
             pltpu.VMEM((groups, CAP * GROUP, 128), F32),
@@ -434,9 +443,23 @@
     )(place, scav, *parts, *operands, *after)
 
 
-def choose_kernel(pair_ref, flag_ref, own_ref, partner_ref, *refs, first):
+def choose_kernel(pair_ref, flag_ref, own_ref, partner_ref, *refs, first, near):
     out_ref, held, in_sems, out_sems = refs[-4:]
     pieces, rows = held.shape[:2]
+
+    def copied_at_once(source):
+        outs = [
+            pltpu.make_async_copy(
+                source.at[pl.ds(i * rows, rows)],
+                out_ref.at[pl.ds(first + i * rows, rows)],
+                out_sems.at[i],
+            )
+            for i in range(pieces)
+        ]
+        for copy in outs:
+            copy.start()
+        for copy in outs:
+            copy.wait()
 
     def copied_from(source):
         ins = [
@@ -461,14 +484,16 @@
 
     @pl.when(flag > 0)
     def _():
-        copied_from(partner_ref)
-
-    @pl.when(flag <= 0)
-    def _():
-        copied_from(own_ref)
-
-
-def choose(pair, flag, own, partner, whole, shape, first, groups, after):
+        (copied_at_once if near else copied_from)(partner_ref)
+
+    if not near:
+
+        @pl.when(flag <= 0)
+        def _():
+            copied_from(own_ref)
+
+
+def choose(pair, flag, own, partner, whole, shape, first, groups, after, near=False):
     rows = shape[0] // sum(CHUNKS)
     pieces = 4 * groups
     operands = [own, partner]
@@ -479,8 +504,10 @@
     operands += after
     anywhere = pl.BlockSpec(memory_space=pl.ANY)
     return pl.pallas_call(
-        functools.partial(choose_kernel, first=first * rows),
-        in_specs=[pl.BlockSpec(memory_space=pltpu.SMEM)] * 2 + [anywhere] * len(operands),
+        functools.partial(choose_kernel, first=first * rows, near=near),
+        in_specs=[pl.BlockSpec(memory_space=pltpu.SMEM)] * 2
+        + [anywhere, pl.BlockSpec(memory_space=pltpu.VMEM) if near else anywhere]
+        + [anywhere] * (len(operands) - 2),
         out_specs=anywhere,
         scratch_shapes=[
             pltpu.VMEM((pieces, rows * groups // pieces, shape[1]), BF16),
@@ -587,10 +614,14 @@
             last = owns[number] = own
             partners[number] = paired(own, "lat")
         else:
-            out = choose(
-                pair, pair_flag, owns[number], partners[number], out, (tracers * levels, columns),
-                firsts[number], CHUNKS[number], after,
-            )
+            where = ((tracers * levels, columns), firsts[number], CHUNKS[number], after)
+            if number + 1 < len(CHUNKS):
+                out = choose(pair, pair_flag, owns[number], partners[number], out, *where)
+            else:
+                out = choose(pair, pair_flag, owns[number], owns[number], out, *where)
+                out = choose(
+                    pair, pair_flag, owns[number], partners[number], out, *where, near=True
+                )
     return out.reshape(tracers, levels, columns)
 
 

time: 225 us -> 226 us (level)
  the two profiles are of different devices: /device:TPU:97 before, /device:TPU:6 now
where the time goes in v9:
time: 226 us; the launch traced here: 225 us
  Pallas kernels  100 us (44%)
  waiting for transfers between devices  79.6 us (35%)
  starting transfers between devices  43.8 us (19%)
    pallas_call x5, Pallas kernels, physics(): pl.pallas_call(functools.partial(physics_kernel, first=first), grid=(1,),...  45.6 us
    ppermute x5, waiting for transfers between devices, paired(): lax.ppermute(value, axis, [(i, i ^ count // 2) for i in range(count)])  38.9 us
    ppermute x4, waiting for transfers between devices, shifted(): return lax.ppermute(value, axis, pairs)  23.4 us
    pallas_call x5, Pallas kernels, advect(): pl.pallas_call(advect_kernel, grid=(groups,), in_specs=[pl.BlockSpec(memo...  23.1 us
    ppermute x15, starting transfers between devices, turned(): lax.ppermute(value, axis, [(i, (i + steps) % count) for i in range(count)])  22.3 us
    ppermute x15, waiting for transfers between devices, turned(): lax.ppermute(value, axis, [(i, (i + steps) % count) for i in range(count)])  17.3 us
    pallas_call x6, Pallas kernels, choose(): pl.pallas_call(functools.partial(choose_kernel, first=first * rows, near=...  14.1 us
    ppermute x4, starting transfers between devices, shifted(): return lax.ppermute(value, axis, pairs)  12.1 us
  transfers between devices with their start and end apart: 24, of which 8 were waited for; matrix products, arithmetic and copies ran while one was open for 0% of the time, Pallas kernels for 37%

profile of v9, /device:TPU:6, one launch (start us, length us, event | category | flops | bytes accessed | tf_op | source)
XLA Modules:
  0.0 225.1 jit_solution(13930129476771018861)
XLA Ops:
  0.0 4.4 %extract.2 = (bf16[3,1152,128]{2,1,0:T(8,128)(2,1)S(1)}, bf16[3,1296,128]{2,1,0:T(8,128)(2,1)}, f32[4,144,128]{2,1,0:T(8,128)S(1)}) custom-call(bf16[256,256]{1,0:T(8,128)(2,1)} %constant.28.clone.apart_ref, bf16[288,288]{1,0:T(8,128)(2,1)} %constant.29.clone.face_move_ref, bf16[18,16,128]{2,1,0:T(8,128)(2,1)} %bitcast.49, bf16[18,16,128]{2,1,0:T(8,128)(2,1)} %bitcast.51, ...), custom_call_target="tpu_custom_call" | custom-call | flops 3000000 | bytes 3600000 | tf_op jit(solution)/shard_map/extract/pallas_call | solution.py:111
  4.4 5.6 %extract.3 = (bf16[5,1152,128]{2,1,0:T(8,128)(2,1)S(1)}, bf16[5,1152,128]{2,1,0:T(8,128)(2,1)}) custom-call(bf16[256,256]{1,0:T(8,128)(2,1)} %constant.28.clone.apart_ref, bf16[288,288]{1,0:T(8,128)(2,1)} %constant.29.clone.face_move_ref, bf16[18,16,128]{2,1,0:T(8,128)(2,1)} %bitcast.50, bf16[18,16,128]{2,1,0:T(8,128)(2,1)} %bitcast.52, ...), custom_call_target="tpu_custom_call" | custom-call | flops 5000000 | bytes 6000000 | tf_op jit(solution)/shard_map/extract/pallas_call | solution.py:111
  10.0 1.9 collective-permute-start
  11.9 5.8 %collective-permute-start.1 = (bf16[5,1152,128]{2,1,0:T(8,128)(2,1)}, bf16[5,1152,128]{2,1,0:T(8,128)(2,1)}, u32[]{:S(2)}, u32[]{:S(2)}) collective-permute-start(bf16[5,1152,128]{2,1,0:T(8,128)(2,1)} %get-tuple-element.37.south_ref), channel_id=1, source_target_pairs={{4,0},{8,4},{12,8},{16,12},{20,16},{24,20},{28,24},{32,28},{36,32}... | collective-permute-start | bytes 4423688 | tf_op jit(solution)/shard_map/ppermute | solution.py:530
  17.7 2.5 %collective-permute-start.2 = (bf16[3,1296,128]{2,1,0:T(8,128)(2,1)}, bf16[3,1296,128]{2,1,0:T(8,128)(2,1)S(1)}, u32[]{:S(2)}, u32[]{:S(2)}) collective-permute-start(bf16[3,1296,128]{2,1,0:T(8,128)(2,1)} %get-tuple-element.40.south_ref), channel_id=1, source_target_pairs={{4,0},{8,4},{12,8},{16,12},{20,16},{24,20},{28,24},{32,28},{36,32}... | collective-permute-start | bytes 2985992 | tf_op jit(solution)/shard_map/ppermute | solution.py:530
  20.2 1.9 collective-permute-start.3
  22.1 20.3 %collective-permute-done.3.low_ref = bf16[3,1152,128]{2,1,0:T(8,128)(2,1)} collective-permute-done((bf16[3,1152,128]{2,1,0:T(8,128)(2,1)S(1)}, bf16[3,1152,128]{2,1,0:T(8,128)(2,1)}, u32[]{:S(2)}, u32[]{:S(2)}) %collective-permute-start.3) | collective-permute-done | bytes 884768 | tf_op jit(solution)/shard_map/ppermute | solution.py:530
  42.4 3.2 %collective-permute-done.2.high_ref.above_ref = bf16[3,1296,128]{2,1,0:T(8,128)(2,1)S(1)} collective-permute-done((bf16[3,1296,128]{2,1,0:T(8,128)(2,1)}, bf16[3,1296,128]{2,1,0:T(8,128)(2,1)S(1)}, u32[]{:S(2)}, u32[]{:S(2)}) %collective-permute-start.2) | collective-permute-done | bytes 995360 | tf_op jit(solution)/shard_map/ppermute | solution.py:530
  45.5 1.0 copy-done.1
  46.5 5.5 %advect.5 = (bf16[2,144,512]{2,1,0:T(8,128)(2,1)S(1)}, bf16[2,144,512]{2,1,0:T(8,128)(2,1)S(1)}, bf16[2,144,512]{2,1,0:T(8,128)(2,1)S(1)}, bf16[2,144,512]{2,1,0:T(8,128)(2,1)S(1)}) custom-call(s32[1]{0:T(128)} %bitcast.1.place_ref, bf16[3,1296,128]{2,1,0:T(8,128)(2,1)} %get-tuple-element.40.south_ref, ...), custom_call_target="tpu_custom_call" | custom-call | flops 20000000 | bytes 4000000 | tf_op jit(solution)/shard_map/advect/pallas_call | solution.py:223
  52.0 1.6 collective-permute-start.4
  53.6 2.9 %collective-permute-start.5 = (bf16[2,144,512]{2,1,0:T(8,128)(2,1)S(1)}, bf16[2,144,512]{2,1,0:T(8,128)(2,1)S(1)}, u32[]{:S(2)}, u32[]{:S(2)}) collective-permute-start(bf16[2,144,512]{2,1,0:T(8,128)(2,1)S(1)} %get-tuple-element.43), channel_id=1, source_target_pairs={{0,2},{1,3},{2,0},{3,1},{4,6},{5,7},{6,4},{7,5},{8,10},{9,11},{10,... | collective-permute-start | bytes 884744 | tf_op jit(solution)/shard_map/ppermute | solution.py:535
  56.5 1.3 collective-permute-start.6
  57.9 7.5 %tables.1 = (bf16[256,72,128]{2,1,0:T(8,128)(2,1)S(1)}, bf16[512,512]{1,0:T(8,128)(2,1)S(1)}, bf16[256,512]{1,0:T(8,128)(2,1)S(1)}, bf16[256,512]{1,0:T(8,128)(2...) custom-call(bf16[72,72,512]{2,1,0:T(8,128)(2,1)} %matrix_ref.1, s32[1,512]{1,0:T(1,128)} %bitcast.53, ...), custom_call_target="tpu_custom_call" | custom-call | flops 2415919104 | bytes 12000000 | tf_op jit(solution)/shard_map/tables/pallas_call | solution.py:310
  65.4 0.0 copy-start.4
  65.4 3.2 %advect.6 = (bf16[1,144,512]{2,1,0:T(8,128)(2,1)S(1)}, bf16[1,144,512]{2,1,0:T(8,128)(2,1)S(1)}, bf16[1,144,512]{2,1,0:T(8,128)(2,1)S(1)}, bf16[1,144,512]{2,1,0:T(8,128)(2,1)S(1)}) custom-call(s32[1]{0:T(128)} %bitcast.1.place_ref, bf16[3,1296,128]{2,1,0:T(8,128)(2,1)} %get-tuple-element.40.south_ref, ...), custom_call_target="tpu_custom_call" | custom-call | flops 10000000 | bytes 2000000 | tf_op jit(solution)/shard_map/advect/pallas_call | solution.py:223
  68.6 0.0 collective-permute-done.4.part1
  68.6 1.1 collective-permute-done.5.part2
  69.7 9.2 %physics.5 = bf16[16,72,512]{2,1,0:T(8,128)(2,1)} custom-call(s32[1]{0:T(128)} %bitcast.1.place_ref, f32[64]{0:T(128)S(1)} %copy-done.4, bf16[2,144,512]{2,1,0:T(8,128)(2,1)S(1)} %get-tuple-element.41.refs_0_.part0, bf16[2,144,512]{2,1,0:T(8,128)(2,1)S(1)} %collective-permute-done.4.part1, bf16[2,144,512]{2,1,0:T(8,128)(2,1)S(1)} %collective-permute-done.5.part2, ...), custom_call_target="tpu_custom_call" | custom-call | flops 1509949440 | bytes 8900000 | tf_op jit(solution)/shard_map/physics/pallas_call | solution.py:423
  78.9 0.0 collective-permute-done.1.high_ref
  78.9 5.5 %advect.7 = (bf16[2,144,512]{2,1,0:T(8,128)(2,1)S(1)}, bf16[2,144,512]{2,1,0:T(8,128)(2,1)S(1)}, bf16[2,144,512]{2,1,0:T(8,128)(2,1)S(1)}, bf16[2,144,512]{2,1,0:T(8,128)(2,1)S(1)}) custom-call(s32[1]{0:T(128)} %bitcast.1.place_ref, bf16[5,1152,128]{2,1,0:T(8,128)(2,1)} %get-tuple-element.37.south_ref, ...), custom_call_target="tpu_custom_call" | custom-call | flops 20000000 | bytes 4000000 | tf_op jit(solution)/shard_map/advect/pallas_call | solution.py:223
  84.4 1.3 collective-permute-start.7
  85.7 1.3 collective-permute-start.10
  87.0 2.2 collective-permute-start.11
  89.2 1.6 collective-permute-start.12
  90.8 1.1 collective-permute-start.8
  91.9 5.1 %collective-permute-done.10.part1 = bf16[1,144,512]{2,1,0:T(8,128)(2,1)S(1)} collective-permute-done((bf16[1,144,512]{2,1,0:T(8,128)(2,1)S(1)}, bf16[1,144,512]{2,1,0:T(8,128)(2,1)S(1)}, u32[]{:S(2)}, u32[]{:S(2)}) %collective-permute-start.10) | collective-permute-done | bytes 147488 | tf_op jit(solution)/shard_map/ppermute | solution.py:535
  97.0 2.7 %collective-permute-start.9 = (bf16[2,144,512]{2,1,0:T(8,128)(2,1)S(1)}, bf16[2,144,512]{2,1,0:T(8,128)(2,1)S(1)}, u32[]{:S(2)}, u32[]{:S(2)}) collective-permute-start(bf16[2,144,512]{2,1,0:T(8,128)(2,1)S(1)} %get-tuple-element.55), channel_id=1, source_target_pairs={{0,3},{1,0},{2,1},{3,2},{4,7},{5,4},{6,5},{7,6},{8,11},{9,8},{10,9... | collective-permute-start | bytes 884744 | tf_op jit(solution)/shard_map/ppermute | solution.py:535
  99.7 2.6 %collective-permute-done.11.part2 = bf16[1,144,512]{2,1,0:T(8,128)(2,1)S(1)} collective-permute-done((bf16[1,144,512]{2,1,0:T(8,128)(2,1)S(1)}, bf16[1,144,512]{2,1,0:T(8,128)(2,1)S(1)}, u32[]{:S(2)}, u32[]{:S(2)}) %collective-permute-start.11) | collective-permute-done | bytes 147488 | tf_op jit(solution)/shard_map/ppermute | solution.py:535
  102.3 0.0 collective-permute-done.12.part3
  102.3 7.9 %physics.6 = bf16[8,72,512]{2,1,0:T(8,128)(2,1)S(1)} custom-call(s32[1]{0:T(128)} %bitcast.1.place_ref, f32[64]{0:T(128)S(1)} %copy-done.4, bf16[1,144,512]{2,1,0:T(8,128)(2,1)S(1)} %get-tuple-element.51.refs_0_.part0, bf16[1,144,512]{2,1,0:T(8,128)(2,1)S(1)} %collective-permute-done.10.part1, bf16[1,144,512]{2,1,0:T(8,128)(2,1)S(1)} %collective-permute-done.11.part2, ...), custom_call_target="tpu_custom_call" | custom-call | flops 754974720 | bytes 7700000 | tf_op jit(solution)/shard_map/physics/pallas_call | solution.py:423
  110.2 5.5 %advect.8 = (bf16[2,144,512]{2,1,0:T(8,128)(2,1)S(1)}, bf16[2,144,512]{2,1,0:T(8,128)(2,1)S(1)}, bf16[2,144,512]{2,1,0:T(8,128)(2,1)S(1)}, bf16[2,144,512]{2,1,0:T(8,128)(2,1)S(1)}) custom-call(s32[1]{0:T(128)} %bitcast.1.place_ref, bf16[5,1152,128]{2,1,0:T(8,128)(2,1)} %get-tuple-element.37.south_ref, ...), custom_call_target="tpu_custom_call" | custom-call | flops 20000000 | bytes 4000000 | tf_op jit(solution)/shard_map/advect/pallas_call | solution.py:223
  115.8 0.1 collective-permute-start.16
  115.9 2.6 %collective-permute-start.17 = (bf16[2,144,512]{2,1,0:T(8,128)(2,1)S(1)}, bf16[2,144,512]{2,1,0:T(8,128)(2,1)S(1)}, u32[]{:S(2)}, u32[]{:S(2)}) collective-permute-start(bf16[2,144,512]{2,1,0:T(8,128)(2,1)S(1)} %get-tuple-element.65), channel_id=1, source_target_pairs={{0,2},{1,3},{2,0},{3,1},{4,6},{5,7},{6,4},{7,5},{8,10},{9,11},{10,... | collective-permute-start | bytes 884744 | tf_op jit(solution)/shard_map/ppermute | solution.py:535
  118.5 0.0 collective-permute-done.7.part1
  118.5 1.2 collective-permute-start.18
  119.6 0.0 collective-permute-done.8.part2
  119.6 1.4 collective-permute-start.23
  121.0 0.0 collective-permute-done.9.part3
  121.0 9.2 %physics.7 = bf16[16,72,512]{2,1,0:T(8,128)(2,1)} custom-call(s32[1]{0:T(128)} %bitcast.1.place_ref, f32[64]{0:T(128)S(1)} %copy-done.4, bf16[2,144,512]{2,1,0:T(8,128)(2,1)S(1)} %get-tuple-element.52.refs_0_.part0, bf16[2,144,512]{2,1,0:T(8,128)(2,1)S(1)} %collective-permute-done.7.part1, bf16[2,144,512]{2,1,0:T(8,128)(2,1)S(1)} %collective-permute-done.8.part2, ...), custom_call_target="tpu_custom_call" | custom-call | flops 1509949440 | bytes 8900000 | tf_op jit(solution)/shard_map/physics/pallas_call | solution.py:423
  130.2 2.2 collective-permute-start.21
  132.4 3.3 %advect.9 = (bf16[1,144,512]{2,1,0:T(8,128)(2,1)S(1)}, bf16[1,144,512]{2,1,0:T(8,128)(2,1)S(1)}, bf16[1,144,512]{2,1,0:T(8,128)(2,1)S(1)}, bf16[1,144,512]{2,1,0:T(8,128)(2,1)S(1)}) custom-call(s32[1]{0:T(128)} %bitcast.1.place_ref, bf16[5,1152,128]{2,1,0:T(8,128)(2,1)} %get-tuple-element.37.south_ref, ...), custom_call_target="tpu_custom_call" | custom-call | flops 10000000 | bytes 2000000 | tf_op jit(solution)/shard_map/advect/pallas_call | solution.py:223
  135.7 0.0 collective-permute-done.16.part1
  135.7 0.0 collective-permute-done.17.part2
  135.7 11.4 %physics.8 = bf16[16,72,512]{2,1,0:T(8,128)(2,1)S(1)} custom-call(s32[1]{0:T(128)} %bitcast.1.place_ref, f32[64]{0:T(128)S(1)} %copy-done.4, bf16[2,144,512]{2,1,0:T(8,128)(2,1)S(1)} %get-tuple-element.59.refs_0_.part0, bf16[2,144,512]{2,1,0:T(8,128)(2,1)S(1)} %collective-permute-done.16.part1, bf16[2,144,512]{2,1,0:T(8,128)(2,1)S(1)} %collective-permute-done.17.part2, ...), custom_call_target="tpu_custom_call" | custom-call | flops 1509949440 | bytes 8900000 | tf_op jit(solution)/shard_map/physics/pallas_call | solution.py:423
  147.2 1.5 collective-permute-start.20
  148.7 0.9 collective-permute-start.13
  149.5 1.5 collective-permute-start.14
  151.1 5.5 %collective-permute-done.13.part1 = bf16[1,144,512]{2,1,0:T(8,128)(2,1)S(1)} collective-permute-done((bf16[1,144,512]{2,1,0:T(8,128)(2,1)S(1)}, bf16[1,144,512]{2,1,0:T(8,128)(2,1)S(1)}, u32[]{:S(2)}, u32[]{:S(2)}) %collective-permute-start.13) | collective-permute-done | bytes 147488 | tf_op jit(solution)/shard_map/ppermute | solution.py:535
  156.6 0.0 collective-permute-start.15
  156.6 0.0 collective-permute-done.14.part2
  156.6 2.2 collective-permute-start.22
  158.8 2.9 %collective-permute-done.15.part3 = bf16[1,144,512]{2,1,0:T(8,128)(2,1)S(1)} collective-permute-done((bf16[1,144,512]{2,1,0:T(8,128)(2,1)S(1)}, bf16[1,144,512]{2,1,0:T(8,128)(2,1)S(1)}, u32[]{:S(2)}, u32[]{:S(2)}) %collective-permute-start.15) | collective-permute-done | bytes 147488 | tf_op jit(solution)/shard_map/ppermute | solution.py:535
  161.7 7.9 %physics.9 = bf16[8,72,512]{2,1,0:T(8,128)(2,1)S(1)} custom-call(s32[1]{0:T(128)} %bitcast.1.place_ref, f32[64]{0:T(128)S(1)} %copy-done.4, bf16[1,144,512]{2,1,0:T(8,128)(2,1)S(1)} %get-tuple-element.60.refs_0_.part0, bf16[1,144,512]{2,1,0:T(8,128)(2,1)S(1)} %collective-permute-done.13.part1, bf16[1,144,512]{2,1,0:T(8,128)(2,1)S(1)} %collective-permute-done.14.part2, ...), custom_call_target="tpu_custom_call" | custom-call | flops 754974720 | bytes 7700000 | tf_op jit(solution)/shard_map/physics/pallas_call | solution.py:423
  169.7 2.2 collective-permute-start.19
  171.9 0.0 collective-permute-done.23.partner_ref
  171.9 2.7 %choose.6.refs_0_ = bf16[4608,512]{1,0:T(8,128)(2,1)} custom-call(s32[1]{0:T(128)} %bitcast.pair_ref, s32[64]{0:T(128)S(1)} %copy-done.3, bf16[1152,512]{1,0:T(8,128)(2,1)} %bitcast.19.refs_0_.own_ref, bf16[1152,512]{1,0:T(8,128)(2,1)} %collective-permute-done.23.partner_ref, bf16[576,512]{1,0:T(8,128)(2,1)S(1)} %bitcast.26), custom_call_target="tpu_custom_call" | custom-call | bytes 2400000 | tf_op jit(solution)/shard_map/choose/pallas_call | solution.py:506
  174.6 38.9 %collective-permute-done.22.partner_ref = bf16[576,512]{1,0:T(8,128)(2,1)} collective-permute-done((bf16[576,512]{1,0:T(8,128)(2,1)S(1)}, bf16[576,512]{1,0:T(8,128)(2,1)}, u32[]{:S(2)}, u32[]{:S(2)}) %collective-permute-start.22) | collective-permute-done | bytes 589856 | tf_op jit(solution)/shard_map/ppermute | solution.py:540
  213.5 2.4 %choose.7.refs_0_ = bf16[4608,512]{1,0:T(8,128)(2,1)} custom-call(s32[1]{0:T(128)} %bitcast.pair_ref, s32[64]{0:T(128)S(1)} %copy-done.3, bf16[576,512]{1,0:T(8,128)(2,1)S(1)} %bitcast.40, bf16[576,512]{1,0:T(8,128)(2,1)} %collective-permute-done.22.partner_ref, bf16[4608,512]{1,0:T(8,128)(2,1)} %choose.6.refs_0_, ...), custom_call_target="tpu_custom_call", output_to_operand_aliasing={{}: (4, {})} | custom-call | bytes 1200000 | tf_op jit(solution)/shard_map/choose/pallas_call | solution.py:506
  215.9 2.7 %choose.8.refs_0_ = bf16[4608,512]{1,0:T(8,128)(2,1)} custom-call(s32[1]{0:T(128)} %bitcast.pair_ref, s32[64]{0:T(128)S(1)} %copy-done.3, bf16[1152,512]{1,0:T(8,128)(2,1)} %bitcast.21.refs_0_.own_ref, bf16[1152,512]{1,0:T(8,128)(2,1)} %collective-permute-done.21.partner_ref, bf16[4608,512]{1,0:T(8,128)(2,1)} %choose.7.refs_0_, ...), custom_call_target="tpu_custom_call", output_to_operand_aliasing={{}: (4, {})} | custom-call | bytes 2400000 | tf_op jit(solution)/shard_map/choose/pallas_call | solution.py:506
  218.6 0.0 collective-permute-done.20.partner_ref
  218.6 2.7 %choose.9.refs_0_ = bf16[4608,512]{1,0:T(8,128)(2,1)} custom-call(s32[1]{0:T(128)} %bitcast.pair_ref, s32[64]{0:T(128)S(1)} %copy-done.3, bf16[1152,512]{1,0:T(8,128)(2,1)S(1)} %bitcast.37, bf16[1152,512]{1,0:T(8,128)(2,1)} %collective-permute-done.20.partner_ref, bf16[4608,512]{1,0:T(8,128)(2,1)} %choose.8.refs_0_, ...), custom_call_target="tpu_custom_call", output_to_operand_aliasing={{}: (4, {})} | custom-call | bytes 2400000 | tf_op jit(solution)/shard_map/choose/pallas_call | solution.py:506
  221.3 2.2 choose.10.refs_0_
  223.5 1.4 choose.11
  (13 shorter events, 0.0 us)
Async XLA Ops:
  4.4 5.6 %copy-start = (f32[4,144,128]{2,1,0:T(8,128)}, f32[4,144,128]{2,1,0:T(8,128)S(1)}, u32[]{:S(2)}) copy-start(f32[4,144,128]{2,1,0:T(8,128)S(1)} %get-tuple-element.39.faces_ref) | copy-start | bytes 884740
  10.0 68.9 %collective-permute-start = (bf16[5,1152,128]{2,1,0:T(8,128)(2,1)S(1)}, bf16[5,1152,128]{2,1,0:T(8,128)(2,1)}, u32[]{:S(2)}, u32[]{:S(2)}) collective-permute-start(bf16[5,1152,128]{2,1,0:T(8,128)(2,1)S(1)} %get-tuple-element.38.refs_0_.north_ref), channel_id=1, source_target_pairs={{0,4},{4,8},{8,12},{12,16},{16,20},{20,24},{24,28},{28,32},{32,36}... | collective-permute-start | bytes 4423688 | tf_op jit(solution)/shard_map/ppermute | solution.py:530
  11.9 67.0 %collective-permute-start.1 = (bf16[5,1152,128]{2,1,0:T(8,128)(2,1)}, bf16[5,1152,128]{2,1,0:T(8,128)(2,1)}, u32[]{:S(2)}, u32[]{:S(2)}) collective-permute-start(bf16[5,1152,128]{2,1,0:T(8,128)(2,1)} %get-tuple-element.37.south_ref), channel_id=1, source_target_pairs={{4,0},{8,4},{12,8},{16,12},{20,16},{24,20},{28,24},{32,28},{36,32}... | collective-permute-start | bytes 4423688 | tf_op jit(solution)/shard_map/ppermute | solution.py:530
  17.7 27.8 %collective-permute-start.2 = (bf16[3,1296,128]{2,1,0:T(8,128)(2,1)}, bf16[3,1296,128]{2,1,0:T(8,128)(2,1)S(1)}, u32[]{:S(2)}, u32[]{:S(2)}) collective-permute-start(bf16[3,1296,128]{2,1,0:T(8,128)(2,1)} %get-tuple-element.40.south_ref), channel_id=1, source_target_pairs={{4,0},{8,4},{12,8},{16,12},{20,16},{24,20},{28,24},{32,28},{36,32}... | collective-permute-start | bytes 2985992 | tf_op jit(solution)/shard_map/ppermute | solution.py:530
  20.2 22.2 %collective-permute-start.3 = (bf16[3,1152,128]{2,1,0:T(8,128)(2,1)S(1)}, bf16[3,1152,128]{2,1,0:T(8,128)(2,1)}, u32[]{:S(2)}, u32[]{:S(2)}) collective-permute-start(bf16[3,1152,128]{2,1,0:T(8,128)(2,1)S(1)} %get-tuple-element.36.refs_4_.north_ref), channel_id=1, source_target_pairs={{0,4},{4,8},{8,12},{12,16},{16,20},{20,24},{24,28},{28,32},{32,36}... | collective-permute-start | bytes 2654216 | tf_op jit(solution)/shard_map/ppermute | solution.py:530
  45.5 1.0 copy-start.1
  52.0 16.7 %collective-permute-start.4 = (bf16[2,144,512]{2,1,0:T(8,128)(2,1)S(1)}, bf16[2,144,512]{2,1,0:T(8,128)(2,1)S(1)}, u32[]{:S(2)}, u32[]{:S(2)}) collective-permute-start(bf16[2,144,512]{2,1,0:T(8,128)(2,1)S(1)} %get-tuple-element.42), channel_id=1, source_target_pairs={{0,1},{1,2},{2,3},{3,0},{4,5},{5,6},{6,7},{7,4},{8,9},{9,10},{10,1... | collective-permute-start | bytes 884744 | tf_op jit(solution)/shard_map/ppermute | solution.py:535
  53.6 16.1 %collective-permute-start.5 = (bf16[2,144,512]{2,1,0:T(8,128)(2,1)S(1)}, bf16[2,144,512]{2,1,0:T(8,128)(2,1)S(1)}, u32[]{:S(2)}, u32[]{:S(2)}) collective-permute-start(bf16[2,144,512]{2,1,0:T(8,128)(2,1)S(1)} %get-tuple-element.43), channel_id=1, source_target_pairs={{0,2},{1,3},{2,0},{3,1},{4,6},{5,7},{6,4},{7,5},{8,10},{9,11},{10,... | collective-permute-start | bytes 884744 | tf_op jit(solution)/shard_map/ppermute | solution.py:535
  56.5 13.2 %collective-permute-start.6 = (bf16[2,144,512]{2,1,0:T(8,128)(2,1)S(1)}, bf16[2,144,512]{2,1,0:T(8,128)(2,1)S(1)}, u32[]{:S(2)}, u32[]{:S(2)}) collective-permute-start(bf16[2,144,512]{2,1,0:T(8,128)(2,1)S(1)} %get-tuple-element.44), channel_id=1, source_target_pairs={{0,3},{1,0},{2,1},{3,2},{4,7},{5,4},{6,5},{7,6},{8,11},{9,8},{10,9... | collective-permute-start | bytes 884744 | tf_op jit(solution)/shard_map/ppermute | solution.py:535
  57.9 7.5 %copy-start.2 = (f32[4,144,128]{2,1,0:T(8,128)S(1)}, f32[4,144,128]{2,1,0:T(8,128)}, u32[]{:S(2)}) copy-start(f32[4,144,128]{2,1,0:T(8,128)} %copy-done) | copy-start | bytes 884740
  65.4 4.3 %copy-start.4 = (f32[64]{0:T(128)S(1)}, f32[64]{0:T(128)}, u32[]{:S(2)}) copy-start(f32[64]{0:T(128)} %scav_ref.9) | copy-start | bytes 772
  84.4 34.0 %collective-permute-start.7 = (bf16[2,144,512]{2,1,0:T(8,128)(2,1)S(1)}, bf16[2,144,512]{2,1,0:T(8,128)(2,1)S(1)}, u32[]{:S(2)}, u32[]{:S(2)}) collective-permute-start(bf16[2,144,512]{2,1,0:T(8,128)(2,1)S(1)} %get-tuple-element.53), channel_id=1, source_target_pairs={{0,1},{1,2},{2,3},{3,0},{4,5},{5,6},{6,7},{7,4},{8,9},{9,10},{10,1... | collective-permute-start | bytes 884744 | tf_op jit(solution)/shard_map/ppermute | solution.py:535
  85.7 11.3 %collective-permute-start.10 = (bf16[1,144,512]{2,1,0:T(8,128)(2,1)S(1)}, bf16[1,144,512]{2,1,0:T(8,128)(2,1)S(1)}, u32[]{:S(2)}, u32[]{:S(2)}) collective-permute-start(bf16[1,144,512]{2,1,0:T(8,128)(2,1)S(1)} %get-tuple-element.56), channel_id=1, source_target_pairs={{0,1},{1,2},{2,3},{3,0},{4,5},{5,6},{6,7},{7,4},{8,9},{9,10},{10,1... | collective-permute-start | bytes 442376 | tf_op jit(solution)/shard_map/ppermute | solution.py:535
  87.0 15.3 %collective-permute-start.11 = (bf16[1,144,512]{2,1,0:T(8,128)(2,1)S(1)}, bf16[1,144,512]{2,1,0:T(8,128)(2,1)S(1)}, u32[]{:S(2)}, u32[]{:S(2)}) collective-permute-start(bf16[1,144,512]{2,1,0:T(8,128)(2,1)S(1)} %get-tuple-element.57), channel_id=1, source_target_pairs={{0,2},{1,3},{2,0},{3,1},{4,6},{5,7},{6,4},{7,5},{8,10},{9,11},{10,... | collective-permute-start | bytes 442376 | tf_op jit(solution)/shard_map/ppermute | solution.py:535
  89.2 13.1 %collective-permute-start.12 = (bf16[1,144,512]{2,1,0:T(8,128)(2,1)S(1)}, bf16[1,144,512]{2,1,0:T(8,128)(2,1)S(1)}, u32[]{:S(2)}, u32[]{:S(2)}) collective-permute-start(bf16[1,144,512]{2,1,0:T(8,128)(2,1)S(1)} %get-tuple-element.58), channel_id=1, source_target_pairs={{0,3},{1,0},{2,1},{3,2},{4,7},{5,4},{6,5},{7,6},{8,11},{9,8},{10,9... | collective-permute-start | bytes 442376 | tf_op jit(solution)/shard_map/ppermute | solution.py:535
  90.8 28.9 %collective-permute-start.8 = (bf16[2,144,512]{2,1,0:T(8,128)(2,1)S(1)}, bf16[2,144,512]{2,1,0:T(8,128)(2,1)S(1)}, u32[]{:S(2)}, u32[]{:S(2)}) collective-permute-start(bf16[2,144,512]{2,1,0:T(8,128)(2,1)S(1)} %get-tuple-element.54), channel_id=1, source_target_pairs={{0,2},{1,3},{2,0},{3,1},{4,6},{5,7},{6,4},{7,5},{8,10},{9,11},{10,... | collective-permute-start | bytes 884744 | tf_op jit(solution)/shard_map/ppermute | solution.py:535
  97.0 24.0 %collective-permute-start.9 = (bf16[2,144,512]{2,1,0:T(8,128)(2,1)S(1)}, bf16[2,144,512]{2,1,0:T(8,128)(2,1)S(1)}, u32[]{:S(2)}, u32[]{:S(2)}) collective-permute-start(bf16[2,144,512]{2,1,0:T(8,128)(2,1)S(1)} %get-tuple-element.55), channel_id=1, source_target_pairs={{0,3},{1,0},{2,1},{3,2},{4,7},{5,4},{6,5},{7,6},{8,11},{9,8},{10,9... | collective-permute-start | bytes 884744 | tf_op jit(solution)/shard_map/ppermute | solution.py:535
  115.8 19.9 %collective-permute-start.16 = (bf16[2,144,512]{2,1,0:T(8,128)(2,1)S(1)}, bf16[2,144,512]{2,1,0:T(8,128)(2,1)S(1)}, u32[]{:S(2)}, u32[]{:S(2)}) collective-permute-start(bf16[2,144,512]{2,1,0:T(8,128)(2,1)S(1)} %get-tuple-element.64), channel_id=1, source_target_pairs={{0,1},{1,2},{2,3},{3,0},{4,5},{5,6},{6,7},{7,4},{8,9},{9,10},{10,1... | collective-permute-start | bytes 884744 | tf_op jit(solution)/shard_map/ppermute | solution.py:535
  115.9 19.9 %collective-permute-start.17 = (bf16[2,144,512]{2,1,0:T(8,128)(2,1)S(1)}, bf16[2,144,512]{2,1,0:T(8,128)(2,1)S(1)}, u32[]{:S(2)}, u32[]{:S(2)}) collective-permute-start(bf16[2,144,512]{2,1,0:T(8,128)(2,1)S(1)} %get-tuple-element.65), channel_id=1, source_target_pairs={{0,2},{1,3},{2,0},{3,1},{4,6},{5,7},{6,4},{7,5},{8,10},{9,11},{10,... | collective-permute-start | bytes 884744 | tf_op jit(solution)/shard_map/ppermute | solution.py:535
  118.5 17.3 %collective-permute-start.18 = (bf16[2,144,512]{2,1,0:T(8,128)(2,1)S(1)}, bf16[2,144,512]{2,1,0:T(8,128)(2,1)S(1)}, u32[]{:S(2)}, u32[]{:S(2)}) collective-permute-start(bf16[2,144,512]{2,1,0:T(8,128)(2,1)S(1)} %get-tuple-element.66), channel_id=1, source_target_pairs={{0,3},{1,0},{2,1},{3,2},{4,7},{5,4},{6,5},{7,6},{8,11},{9,8},{10,9... | collective-permute-start | bytes 884744 | tf_op jit(solution)/shard_map/ppermute | solution.py:535
  119.6 52.2 %collective-permute-start.23 = (bf16[1152,512]{1,0:T(8,128)(2,1)}, bf16[1152,512]{1,0:T(8,128)(2,1)}, u32[]{:S(2)}, u32[]{:S(2)}) collective-permute-start(bf16[1152,512]{1,0:T(8,128)(2,1)} %bitcast.19.refs_0_.own_ref), channel_id=1, source_target_pairs={{0,64},{4,68},{8,72},{12,76},{16,80},{20,84},{24,88},{28,92},{32,9... | collective-permute-start | bytes 3538952 | tf_op jit(solution)/shard_map/ppermute | solution.py:540
  130.2 85.7 %collective-permute-start.21 = (bf16[1152,512]{1,0:T(8,128)(2,1)}, bf16[1152,512]{1,0:T(8,128)(2,1)}, u32[]{:S(2)}, u32[]{:S(2)}) collective-permute-start(bf16[1152,512]{1,0:T(8,128)(2,1)} %bitcast.21.refs_0_.own_ref), channel_id=1, source_target_pairs={{0,64},{4,68},{8,72},{12,76},{16,80},{20,84},{24,88},{28,92},{32,9... | collective-permute-start | bytes 3538952 | tf_op jit(solution)/shard_map/ppermute | solution.py:540
  147.2 71.4 %collective-permute-start.20 = (bf16[1152,512]{1,0:T(8,128)(2,1)S(1)}, bf16[1152,512]{1,0:T(8,128)(2,1)}, u32[]{:S(2)}, u32[]{:S(2)}) collective-permute-start(bf16[1152,512]{1,0:T(8,128)(2,1)S(1)} %bitcast.35), channel_id=1, source_target_pairs={{0,64},{4,68},{8,72},{12,76},{16,80},{20,84},{24,88},{28,92},{32,9... | collective-permute-start | bytes 3538952 | tf_op jit(solution)/shard_map/ppermute | solution.py:540
  148.7 7.9 %collective-permute-start.13 = (bf16[1,144,512]{2,1,0:T(8,128)(2,1)S(1)}, bf16[1,144,512]{2,1,0:T(8,128)(2,1)S(1)}, u32[]{:S(2)}, u32[]{:S(2)}) collective-permute-start(bf16[1,144,512]{2,1,0:T(8,128)(2,1)S(1)} %get-tuple-element.61), channel_id=1, source_target_pairs={{0,1},{1,2},{2,3},{3,0},{4,5},{5,6},{6,7},{7,4},{8,9},{9,10},{10,1... | collective-permute-start | bytes 442376 | tf_op jit(solution)/shard_map/ppermute | solution.py:535
  149.5 7.1 %collective-permute-start.14 = (bf16[1,144,512]{2,1,0:T(8,128)(2,1)S(1)}, bf16[1,144,512]{2,1,0:T(8,128)(2,1)S(1)}, u32[]{:S(2)}, u32[]{:S(2)}) collective-permute-start(bf16[1,144,512]{2,1,0:T(8,128)(2,1)S(1)} %get-tuple-element.62), channel_id=1, source_target_pairs={{0,2},{1,3},{2,0},{3,1},{4,6},{5,7},{6,4},{7,5},{8,10},{9,11},{10,... | collective-permute-start | bytes 442376 | tf_op jit(solution)/shard_map/ppermute | solution.py:535
  156.6 15.3 %copy-start.3 = (s32[64]{0:T(128)S(1)}, s32[64]{0:T(128)}, u32[]{:S(2)}) copy-start(s32[64]{0:T(128)} %flag_ref.11) | copy-start | bytes 772
  156.6 5.1 %collective-permute-start.15 = (bf16[1,144,512]{2,1,0:T(8,128)(2,1)S(1)}, bf16[1,144,512]{2,1,0:T(8,128)(2,1)S(1)}, u32[]{:S(2)}, u32[]{:S(2)}) collective-permute-start(bf16[1,144,512]{2,1,0:T(8,128)(2,1)S(1)} %get-tuple-element.63), channel_id=1, source_target_pairs={{0,3},{1,0},{2,1},{3,2},{4,7},{5,4},{6,5},{7,6},{8,11},{9,8},{10,9... | collective-permute-start | bytes 442376 | tf_op jit(solution)/shard_map/ppermute | solution.py:535
  156.6 56.9 %collective-permute-start.22 = (bf16[576,512]{1,0:T(8,128)(2,1)S(1)}, bf16[576,512]{1,0:T(8,128)(2,1)}, u32[]{:S(2)}, u32[]{:S(2)}) collective-permute-start(bf16[576,512]{1,0:T(8,128)(2,1)S(1)} %bitcast.39), channel_id=1, source_target_pairs={{0,64},{4,68},{8,72},{12,76},{16,80},{20,84},{24,88},{28,92},{32,9... | collective-permute-start | bytes 1769480 | tf_op jit(solution)/shard_map/ppermute | solution.py:540
  169.7 53.8 %collective-permute-start.19 = (bf16[576,512]{1,0:T(8,128)(2,1)S(1)}, bf16[576,512]{1,0:T(8,128)(2,1)S(1)}, u32[]{:S(2)}, u32[]{:S(2)}) collective-permute-start(bf16[576,512]{1,0:T(8,128)(2,1)S(1)} %bitcast.25), channel_id=1, source_target_pairs={{0,64},{4,68},{8,72},{12,76},{16,80},{20,84},{24,88},{28,92},{32,9... | collective-permute-start | bytes 1769480 | tf_op jit(solution)/shard_map/ppermute | solution.py:540

commit v10 on v9

--- a/solution.py
+++ b/solution.py
@@ -234,7 +234,7 @@
         ]
         + [pl.BlockSpec(memory_space=pl.ANY)] * len(after),
         out_specs=[pl.BlockSpec((1, rows, 512), lambda g: (g, 0, 0))] * 4,
-        scratch_shapes=[pltpu.VMEM((levels * 128, 128), F32)],
+        scratch_shapes=[pltpu.VMEM((levels * 128 + 64, 128), F32)],
         out_shape=[jax.ShapeDtypeStruct((groups, rows, 512), BF16)] * 4,
         cost_estimate=pl.CostEstimate(
             flops=groups * 10**7, bytes_accessed=groups * 2000000, transcendentals=0
@@ -276,7 +276,8 @@
     rain = rain_ref[...]
     all_ref[...] = rain.astype(F32)
     nothing = jnp.zeros((CAP, 128 - levels), F32)
-    wet_ref[...] = jnp.concatenate([crossed(back, rain), nothing], axis=1)
+    wet_ref[:CAP] = jnp.concatenate([crossed(back, rain), nothing], axis=1)
+    wet_ref[CAP:] = jnp.zeros((16, 128), F32)
     gap = jnp.zeros((128 - levels, columns), BF16)
     for piece in range(pieces):
         copies[piece].wait()
@@ -288,7 +289,7 @@
                 turned[pl.ds(k + part, CAP, stride=per_piece), :] = found[:, lanes]
         spot = piece * per_piece
         small_ref[:, spot : spot + per_piece, :] = (
-            turned[...].reshape(CAP, per_piece, 128).astype(BF16)
+            turned[: CAP * per_piece].reshape(CAP, per_piece, 128).astype(BF16)
         )
 
 
@@ -304,7 +305,7 @@
         ((columns, columns), BF16),
         ((CAP, columns), BF16),
         ((CAP, columns), BF16),
-        ((CAP, 128), F32),
+        ((CAP + 16, 128), F32),
         ((levels, columns), F32),
     ]
     return pl.pallas_call(
@@ -321,7 +322,7 @@
         out_shape=[jax.ShapeDtypeStruct(*x) for x in shapes],
         scratch_shapes=[
             pltpu.VMEM((levels // per_piece, per_piece, levels, columns), BF16),
-            pltpu.VMEM((CAP * per_piece, 128), F32),
+            pltpu.VMEM((CAP * per_piece + 8, 128), F32),
             pltpu.SemaphoreType.DMA((levels // per_piece,)),
         ],
         cost_estimate=pl.CostEstimate(
@@ -429,8 +430,8 @@
         out_specs=pl.BlockSpec(memory_space=pltpu.HBM),
         scratch_shapes=[
             pltpu.VMEM((tracers, 128, columns), BF16),
-            pltpu.VMEM((groups, CAP * GROUP, 128), F32),
-            pltpu.VMEM((groups, CAP * GROUP, 128), F32),
+            pltpu.VMEM((groups, CAP * GROUP + 8, 128), F32),
+            pltpu.VMEM((groups, CAP * GROUP + 8, 128), F32),
             pltpu.VMEM((tracers, levels, columns), BF16),
             pltpu.SemaphoreType.DMA((tracers,)),
         ],

time: 226 us -> 226 us (level)
  no operation moved by 1% of the time
where the time goes in v10:
time: 226 us; the launch traced here: 225 us
  Pallas kernels  100 us (44%)
  waiting for transfers between devices  79.8 us (35%)
  starting transfers between devices  43.8 us (19%)
    pallas_call x5, Pallas kernels, physics(): pl.pallas_call(functools.partial(physics_kernel, first=first), grid=(1,),...  45.3 us
    ppermute x5, waiting for transfers between devices, paired(): lax.ppermute(value, axis, [(i, i ^ count // 2) for i in range(count)])  39.1 us
    ppermute x4, waiting for transfers between devices, shifted(): return lax.ppermute(value, axis, pairs)  23.4 us
    pallas_call x5, Pallas kernels, advect(): pl.pallas_call(advect_kernel, grid=(groups,), in_specs=[pl.BlockSpec(memo...  23.1 us
    ppermute x15, starting transfers between devices, turned(): lax.ppermute(value, axis, [(i, (i + steps) % count) for i in range(count)])  22.3 us
    ppermute x15, waiting for transfers between devices, turned(): lax.ppermute(value, axis, [(i, (i + steps) % count) for i in range(count)])  17.3 us
    pallas_call x6, Pallas kernels, choose(): pl.pallas_call(functools.partial(choose_kernel, first=first * rows, near=...  14.1 us
    ppermute x4, starting transfers between devices, shifted(): return lax.ppermute(value, axis, pairs)  12.1 us
  transfers between devices with their start and end apart: 24, of which 8 were waited for; matrix products, arithmetic and copies ran while one was open for 0% of the time, Pallas kernels for 37%

profile of v10, /device:TPU:6, one launch (start us, length us, event | category | flops | bytes accessed | tf_op | source)
XLA Modules:
  0.0 225.0 jit_solution(10285814962408806893)
XLA Ops:
  0.0 4.4 %extract.2 = (bf16[3,1152,128]{2,1,0:T(8,128)(2,1)S(1)}, bf16[3,1296,128]{2,1,0:T(8,128)(2,1)}, f32[4,144,128]{2,1,0:T(8,128)S(1)}) custom-call(bf16[256,256]{1,0:T(8,128)(2,1)} %constant.28.clone.apart_ref, bf16[288,288]{1,0:T(8,128)(2,1)} %constant.29.clone.face_move_ref, bf16[18,16,128]{2,1,0:T(8,128)(2,1)} %bitcast.49, bf16[18,16,128]{2,1,0:T(8,128)(2,1)} %bitcast.51, ...), custom_call_target="tpu_custom_call" | custom-call | flops 3000000 | bytes 3600000 | tf_op jit(solution)/shard_map/extract/pallas_call | solution.py:111
  4.4 5.6 %extract.3 = (bf16[5,1152,128]{2,1,0:T(8,128)(2,1)S(1)}, bf16[5,1152,128]{2,1,0:T(8,128)(2,1)}) custom-call(bf16[256,256]{1,0:T(8,128)(2,1)} %constant.28.clone.apart_ref, bf16[288,288]{1,0:T(8,128)(2,1)} %constant.29.clone.face_move_ref, bf16[18,16,128]{2,1,0:T(8,128)(2,1)} %bitcast.50, bf16[18,16,128]{2,1,0:T(8,128)(2,1)} %bitcast.52, ...), custom_call_target="tpu_custom_call" | custom-call | flops 5000000 | bytes 6000000 | tf_op jit(solution)/shard_map/extract/pallas_call | solution.py:111
  10.0 1.9 collective-permute-start
  11.9 5.8 %collective-permute-start.1 = (bf16[5,1152,128]{2,1,0:T(8,128)(2,1)}, bf16[5,1152,128]{2,1,0:T(8,128)(2,1)}, u32[]{:S(2)}, u32[]{:S(2)}) collective-permute-start(bf16[5,1152,128]{2,1,0:T(8,128)(2,1)} %get-tuple-element.37.south_ref), channel_id=1, source_target_pairs={{4,0},{8,4},{12,8},{16,12},{20,16},{24,20},{28,24},{32,28},{36,32}... | collective-permute-start | bytes 4423688 | tf_op jit(solution)/shard_map/ppermute | solution.py:531
  17.7 2.5 %collective-permute-start.2 = (bf16[3,1296,128]{2,1,0:T(8,128)(2,1)}, bf16[3,1296,128]{2,1,0:T(8,128)(2,1)S(1)}, u32[]{:S(2)}, u32[]{:S(2)}) collective-permute-start(bf16[3,1296,128]{2,1,0:T(8,128)(2,1)} %get-tuple-element.40.south_ref), channel_id=1, source_target_pairs={{4,0},{8,4},{12,8},{16,12},{20,16},{24,20},{28,24},{32,28},{36,32}... | collective-permute-start | bytes 2985992 | tf_op jit(solution)/shard_map/ppermute | solution.py:531
  20.2 1.9 collective-permute-start.3
  22.1 20.3 %collective-permute-done.3.low_ref = bf16[3,1152,128]{2,1,0:T(8,128)(2,1)} collective-permute-done((bf16[3,1152,128]{2,1,0:T(8,128)(2,1)S(1)}, bf16[3,1152,128]{2,1,0:T(8,128)(2,1)}, u32[]{:S(2)}, u32[]{:S(2)}) %collective-permute-start.3) | collective-permute-done | bytes 884768 | tf_op jit(solution)/shard_map/ppermute | solution.py:531
  42.4 3.2 %collective-permute-done.2.high_ref.above_ref = bf16[3,1296,128]{2,1,0:T(8,128)(2,1)S(1)} collective-permute-done((bf16[3,1296,128]{2,1,0:T(8,128)(2,1)}, bf16[3,1296,128]{2,1,0:T(8,128)(2,1)S(1)}, u32[]{:S(2)}, u32[]{:S(2)}) %collective-permute-start.2) | collective-permute-done | bytes 995360 | tf_op jit(solution)/shard_map/ppermute | solution.py:531
  45.5 1.0 copy-done.1
  46.5 5.5 %advect.5 = (bf16[2,144,512]{2,1,0:T(8,128)(2,1)S(1)}, bf16[2,144,512]{2,1,0:T(8,128)(2,1)S(1)}, bf16[2,144,512]{2,1,0:T(8,128)(2,1)S(1)}, bf16[2,144,512]{2,1,0:T(8,128)(2,1)S(1)}) custom-call(s32[1]{0:T(128)} %bitcast.1.place_ref, bf16[3,1296,128]{2,1,0:T(8,128)(2,1)} %get-tuple-element.40.south_ref, ...), custom_call_target="tpu_custom_call" | custom-call | flops 20000000 | bytes 4000000 | tf_op jit(solution)/shard_map/advect/pallas_call | solution.py:223
  52.0 1.6 collective-permute-start.4
  53.6 2.9 %collective-permute-start.5 = (bf16[2,144,512]{2,1,0:T(8,128)(2,1)S(1)}, bf16[2,144,512]{2,1,0:T(8,128)(2,1)S(1)}, u32[]{:S(2)}, u32[]{:S(2)}) collective-permute-start(bf16[2,144,512]{2,1,0:T(8,128)(2,1)S(1)} %get-tuple-element.43), channel_id=1, source_target_pairs={{0,2},{1,3},{2,0},{3,1},{4,6},{5,7},{6,4},{7,5},{8,10},{9,11},{10,... | collective-permute-start | bytes 884744 | tf_op jit(solution)/shard_map/ppermute | solution.py:536
  56.5 1.3 collective-permute-start.6
  57.9 7.5 %tables.1 = (bf16[256,72,128]{2,1,0:T(8,128)(2,1)S(1)}, bf16[512,512]{1,0:T(8,128)(2,1)S(1)}, bf16[256,512]{1,0:T(8,128)(2,1)S(1)}, bf16[256,512]{1,0:T(8,128)(2...) custom-call(bf16[72,72,512]{2,1,0:T(8,128)(2,1)} %matrix_ref.1, s32[1,512]{1,0:T(1,128)} %bitcast.53, ...), custom_call_target="tpu_custom_call" | custom-call | flops 2415919104 | bytes 12000000 | tf_op jit(solution)/shard_map/tables/pallas_call | solution.py:311
  65.3 0.0 copy-start.4
  65.3 3.2 %advect.6 = (bf16[1,144,512]{2,1,0:T(8,128)(2,1)S(1)}, bf16[1,144,512]{2,1,0:T(8,128)(2,1)S(1)}, bf16[1,144,512]{2,1,0:T(8,128)(2,1)S(1)}, bf16[1,144,512]{2,1,0:T(8,128)(2,1)S(1)}) custom-call(s32[1]{0:T(128)} %bitcast.1.place_ref, bf16[3,1296,128]{2,1,0:T(8,128)(2,1)} %get-tuple-element.40.south_ref, ...), custom_call_target="tpu_custom_call" | custom-call | flops 10000000 | bytes 2000000 | tf_op jit(solution)/shard_map/advect/pallas_call | solution.py:223
  68.6 0.0 collective-permute-done.4.part1
  68.6 1.1 collective-permute-done.5.part2
  69.7 0.0 collective-permute-done.6.part3
  69.7 9.1 %physics.5 = bf16[16,72,512]{2,1,0:T(8,128)(2,1)} custom-call(s32[1]{0:T(128)} %bitcast.1.place_ref, f32[64]{0:T(128)S(1)} %copy-done.4, bf16[2,144,512]{2,1,0:T(8,128)(2,1)S(1)} %get-tuple-element.41.refs_0_.part0, bf16[2,144,512]{2,1,0:T(8,128)(2,1)S(1)} %collective-permute-done.4.part1, bf16[2,144,512]{2,1,0:T(8,128)(2,1)S(1)} %collective-permute-done.5.part2, ...), custom_call_target="tpu_custom_call" | custom-call | flops 1509949440 | bytes 8900000 | tf_op jit(solution)/shard_map/physics/pallas_call | solution.py:424
  78.8 0.0 collective-permute-done.low_ref
  78.8 0.0 collective-permute-done.1.high_ref
  78.8 5.5 %advect.7 = (bf16[2,144,512]{2,1,0:T(8,128)(2,1)S(1)}, bf16[2,144,512]{2,1,0:T(8,128)(2,1)S(1)}, bf16[2,144,512]{2,1,0:T(8,128)(2,1)S(1)}, bf16[2,144,512]{2,1,0:T(8,128)(2,1)S(1)}) custom-call(s32[1]{0:T(128)} %bitcast.1.place_ref, bf16[5,1152,128]{2,1,0:T(8,128)(2,1)} %get-tuple-element.37.south_ref, ...), custom_call_target="tpu_custom_call" | custom-call | flops 20000000 | bytes 4000000 | tf_op jit(solution)/shard_map/advect/pallas_call | solution.py:223
  84.4 1.3 collective-permute-start.7
  85.7 1.3 collective-permute-start.10
  87.0 2.2 collective-permute-start.11
  89.2 1.6 collective-permute-start.12
  90.7 1.1 collective-permute-start.8
  91.9 5.1 %collective-permute-done.10.part1 = bf16[1,144,512]{2,1,0:T(8,128)(2,1)S(1)} collective-permute-done((bf16[1,144,512]{2,1,0:T(8,128)(2,1)S(1)}, bf16[1,144,512]{2,1,0:T(8,128)(2,1)S(1)}, u32[]{:S(2)}, u32[]{:S(2)}) %collective-permute-start.10) | collective-permute-done | bytes 147488 | tf_op jit(solution)/shard_map/ppermute | solution.py:536
  97.0 2.7 %collective-permute-start.9 = (bf16[2,144,512]{2,1,0:T(8,128)(2,1)S(1)}, bf16[2,144,512]{2,1,0:T(8,128)(2,1)S(1)}, u32[]{:S(2)}, u32[]{:S(2)}) collective-permute-start(bf16[2,144,512]{2,1,0:T(8,128)(2,1)S(1)} %get-tuple-element.55), channel_id=1, source_target_pairs={{0,3},{1,0},{2,1},{3,2},{4,7},{5,4},{6,5},{7,6},{8,11},{9,8},{10,9... | collective-permute-start | bytes 884744 | tf_op jit(solution)/shard_map/ppermute | solution.py:536
  99.7 2.6 %collective-permute-done.11.part2 = bf16[1,144,512]{2,1,0:T(8,128)(2,1)S(1)} collective-permute-done((bf16[1,144,512]{2,1,0:T(8,128)(2,1)S(1)}, bf16[1,144,512]{2,1,0:T(8,128)(2,1)S(1)}, u32[]{:S(2)}, u32[]{:S(2)}) %collective-permute-start.11) | collective-permute-done | bytes 147488 | tf_op jit(solution)/shard_map/ppermute | solution.py:536
  102.3 0.0 collective-permute-done.12.part3
  102.3 7.9 %physics.6 = bf16[8,72,512]{2,1,0:T(8,128)(2,1)S(1)} custom-call(s32[1]{0:T(128)} %bitcast.1.place_ref, f32[64]{0:T(128)S(1)} %copy-done.4, bf16[1,144,512]{2,1,0:T(8,128)(2,1)S(1)} %get-tuple-element.51.refs_0_.part0, bf16[1,144,512]{2,1,0:T(8,128)(2,1)S(1)} %collective-permute-done.10.part1, bf16[1,144,512]{2,1,0:T(8,128)(2,1)S(1)} %collective-permute-done.11.part2, ...), custom_call_target="tpu_custom_call" | custom-call | flops 754974720 | bytes 7700000 | tf_op jit(solution)/shard_map/physics/pallas_call | solution.py:424
  110.1 5.5 %advect.8 = (bf16[2,144,512]{2,1,0:T(8,128)(2,1)S(1)}, bf16[2,144,512]{2,1,0:T(8,128)(2,1)S(1)}, bf16[2,144,512]{2,1,0:T(8,128)(2,1)S(1)}, bf16[2,144,512]{2,1,0:T(8,128)(2,1)S(1)}) custom-call(s32[1]{0:T(128)} %bitcast.1.place_ref, bf16[5,1152,128]{2,1,0:T(8,128)(2,1)} %get-tuple-element.37.south_ref, ...), custom_call_target="tpu_custom_call" | custom-call | flops 20000000 | bytes 4000000 | tf_op jit(solution)/shard_map/advect/pallas_call | solution.py:223
  115.7 0.1 collective-permute-start.16
  115.8 2.6 %collective-permute-start.17 = (bf16[2,144,512]{2,1,0:T(8,128)(2,1)S(1)}, bf16[2,144,512]{2,1,0:T(8,128)(2,1)S(1)}, u32[]{:S(2)}, u32[]{:S(2)}) collective-permute-start(bf16[2,144,512]{2,1,0:T(8,128)(2,1)S(1)} %get-tuple-element.65), channel_id=1, source_target_pairs={{0,2},{1,3},{2,0},{3,1},{4,6},{5,7},{6,4},{7,5},{8,10},{9,11},{10,... | collective-permute-start | bytes 884744 | tf_op jit(solution)/shard_map/ppermute | solution.py:536
  118.4 0.0 collective-permute-done.7.part1
  118.4 1.2 collective-permute-start.18
  119.5 0.0 collective-permute-done.8.part2
  119.5 1.4 collective-permute-start.23
  120.9 0.0 collective-permute-done.9.part3
  120.9 9.1 %physics.7 = bf16[16,72,512]{2,1,0:T(8,128)(2,1)} custom-call(s32[1]{0:T(128)} %bitcast.1.place_ref, f32[64]{0:T(128)S(1)} %copy-done.4, bf16[2,144,512]{2,1,0:T(8,128)(2,1)S(1)} %get-tuple-element.52.refs_0_.part0, bf16[2,144,512]{2,1,0:T(8,128)(2,1)S(1)} %collective-permute-done.7.part1, bf16[2,144,512]{2,1,0:T(8,128)(2,1)S(1)} %collective-permute-done.8.part2, ...), custom_call_target="tpu_custom_call" | custom-call | flops 1509949440 | bytes 8900000 | tf_op jit(solution)/shard_map/physics/pallas_call | solution.py:424
  130.1 2.2 collective-permute-start.21
  132.3 3.3 %advect.9 = (bf16[1,144,512]{2,1,0:T(8,128)(2,1)S(1)}, bf16[1,144,512]{2,1,0:T(8,128)(2,1)S(1)}, bf16[1,144,512]{2,1,0:T(8,128)(2,1)S(1)}, bf16[1,144,512]{2,1,0:T(8,128)(2,1)S(1)}) custom-call(s32[1]{0:T(128)} %bitcast.1.place_ref, bf16[5,1152,128]{2,1,0:T(8,128)(2,1)} %get-tuple-element.37.south_ref, ...), custom_call_target="tpu_custom_call" | custom-call | flops 10000000 | bytes 2000000 | tf_op jit(solution)/shard_map/advect/pallas_call | solution.py:223
  135.6 0.0 collective-permute-done.16.part1
  135.6 0.0 collective-permute-done.18.part3
  135.6 11.4 %physics.8 = bf16[16,72,512]{2,1,0:T(8,128)(2,1)S(1)} custom-call(s32[1]{0:T(128)} %bitcast.1.place_ref, f32[64]{0:T(128)S(1)} %copy-done.4, bf16[2,144,512]{2,1,0:T(8,128)(2,1)S(1)} %get-tuple-element.59.refs_0_.part0, bf16[2,144,512]{2,1,0:T(8,128)(2,1)S(1)} %collective-permute-done.16.part1, bf16[2,144,512]{2,1,0:T(8,128)(2,1)S(1)} %collective-permute-done.17.part2, ...), custom_call_target="tpu_custom_call" | custom-call | flops 1509949440 | bytes 8900000 | tf_op jit(solution)/shard_map/physics/pallas_call | solution.py:424
  147.0 1.5 collective-permute-start.20
  148.5 0.9 collective-permute-start.13
  149.3 1.5 collective-permute-start.14
  150.9 5.5 %collective-permute-done.13.part1 = bf16[1,144,512]{2,1,0:T(8,128)(2,1)S(1)} collective-permute-done((bf16[1,144,512]{2,1,0:T(8,128)(2,1)S(1)}, bf16[1,144,512]{2,1,0:T(8,128)(2,1)S(1)}, u32[]{:S(2)}, u32[]{:S(2)}) %collective-permute-start.13) | collective-permute-done | bytes 147488 | tf_op jit(solution)/shard_map/ppermute | solution.py:536
  156.4 2.2 collective-permute-start.22
  158.6 2.9 %collective-permute-done.15.part3 = bf16[1,144,512]{2,1,0:T(8,128)(2,1)S(1)} collective-permute-done((bf16[1,144,512]{2,1,0:T(8,128)(2,1)S(1)}, bf16[1,144,512]{2,1,0:T(8,128)(2,1)S(1)}, u32[]{:S(2)}, u32[]{:S(2)}) %collective-permute-start.15) | collective-permute-done | bytes 147488 | tf_op jit(solution)/shard_map/ppermute | solution.py:536
  161.6 7.9 %physics.9 = bf16[8,72,512]{2,1,0:T(8,128)(2,1)S(1)} custom-call(s32[1]{0:T(128)} %bitcast.1.place_ref, f32[64]{0:T(128)S(1)} %copy-done.4, bf16[1,144,512]{2,1,0:T(8,128)(2,1)S(1)} %get-tuple-element.60.refs_0_.part0, bf16[1,144,512]{2,1,0:T(8,128)(2,1)S(1)} %collective-permute-done.13.part1, bf16[1,144,512]{2,1,0:T(8,128)(2,1)S(1)} %collective-permute-done.14.part2, ...), custom_call_target="tpu_custom_call" | custom-call | flops 754974720 | bytes 7700000 | tf_op jit(solution)/shard_map/physics/pallas_call | solution.py:424
  169.4 2.2 collective-permute-start.19
  171.6 2.7 %choose.6.refs_0_ = bf16[4608,512]{1,0:T(8,128)(2,1)} custom-call(s32[1]{0:T(128)} %bitcast.pair_ref, s32[64]{0:T(128)S(1)} %copy-done.3, bf16[1152,512]{1,0:T(8,128)(2,1)} %bitcast.19.refs_0_.own_ref, bf16[1152,512]{1,0:T(8,128)(2,1)} %collective-permute-done.23.partner_ref, bf16[576,512]{1,0:T(8,128)(2,1)S(1)} %bitcast.26), custom_call_target="tpu_custom_call" | custom-call | bytes 2400000 | tf_op jit(solution)/shard_map/choose/pallas_call | solution.py:507
  174.3 39.1 %collective-permute-done.22.partner_ref = bf16[576,512]{1,0:T(8,128)(2,1)} collective-permute-done((bf16[576,512]{1,0:T(8,128)(2,1)S(1)}, bf16[576,512]{1,0:T(8,128)(2,1)}, u32[]{:S(2)}, u32[]{:S(2)}) %collective-permute-start.22) | collective-permute-done | bytes 589856 | tf_op jit(solution)/shard_map/ppermute | solution.py:541
  213.4 2.4 %choose.7.refs_0_ = bf16[4608,512]{1,0:T(8,128)(2,1)} custom-call(s32[1]{0:T(128)} %bitcast.pair_ref, s32[64]{0:T(128)S(1)} %copy-done.3, bf16[576,512]{1,0:T(8,128)(2,1)S(1)} %bitcast.40, bf16[576,512]{1,0:T(8,128)(2,1)} %collective-permute-done.22.partner_ref, bf16[4608,512]{1,0:T(8,128)(2,1)} %choose.6.refs_0_, ...), custom_call_target="tpu_custom_call", output_to_operand_aliasing={{}: (4, {})} | custom-call | bytes 1200000 | tf_op jit(solution)/shard_map/choose/pallas_call | solution.py:507
  215.8 0.0 collective-permute-done.21.partner_ref
  215.8 2.7 %choose.8.refs_0_ = bf16[4608,512]{1,0:T(8,128)(2,1)} custom-call(s32[1]{0:T(128)} %bitcast.pair_ref, s32[64]{0:T(128)S(1)} %copy-done.3, bf16[1152,512]{1,0:T(8,128)(2,1)} %bitcast.21.refs_0_.own_ref, bf16[1152,512]{1,0:T(8,128)(2,1)} %collective-permute-done.21.partner_ref, bf16[4608,512]{1,0:T(8,128)(2,1)} %choose.7.refs_0_, ...), custom_call_target="tpu_custom_call", output_to_operand_aliasing={{}: (4, {})} | custom-call | bytes 2400000 | tf_op jit(solution)/shard_map/choose/pallas_call | solution.py:507
  218.5 2.7 %choose.9.refs_0_ = bf16[4608,512]{1,0:T(8,128)(2,1)} custom-call(s32[1]{0:T(128)} %bitcast.pair_ref, s32[64]{0:T(128)S(1)} %copy-done.3, bf16[1152,512]{1,0:T(8,128)(2,1)S(1)} %bitcast.37, bf16[1152,512]{1,0:T(8,128)(2,1)} %collective-permute-done.20.partner_ref, bf16[4608,512]{1,0:T(8,128)(2,1)} %choose.8.refs_0_, ...), custom_call_target="tpu_custom_call", output_to_operand_aliasing={{}: (4, {})} | custom-call | bytes 2400000 | tf_op jit(solution)/shard_map/choose/pallas_call | solution.py:507
  221.2 2.2 choose.10.refs_0_
  223.4 0.0 collective-permute-done.19.partner_ref
  223.4 1.4 choose.11
  (13 shorter events, 0.0 us)
Async XLA Ops:
  4.4 5.6 %copy-start = (f32[4,144,128]{2,1,0:T(8,128)}, f32[4,144,128]{2,1,0:T(8,128)S(1)}, u32[]{:S(2)}) copy-start(f32[4,144,128]{2,1,0:T(8,128)S(1)} %get-tuple-element.39.faces_ref) | copy-start | bytes 884740
  10.0 68.8 %collective-permute-start = (bf16[5,1152,128]{2,1,0:T(8,128)(2,1)S(1)}, bf16[5,1152,128]{2,1,0:T(8,128)(2,1)}, u32[]{:S(2)}, u32[]{:S(2)}) collective-permute-start(bf16[5,1152,128]{2,1,0:T(8,128)(2,1)S(1)} %get-tuple-element.38.refs_0_.north_ref), channel_id=1, source_target_pairs={{0,4},{4,8},{8,12},{12,16},{16,20},{20,24},{24,28},{28,32},{32,36}... | collective-permute-start | bytes 4423688 | tf_op jit(solution)/shard_map/ppermute | solution.py:531
  11.9 66.9 %collective-permute-start.1 = (bf16[5,1152,128]{2,1,0:T(8,128)(2,1)}, bf16[5,1152,128]{2,1,0:T(8,128)(2,1)}, u32[]{:S(2)}, u32[]{:S(2)}) collective-permute-start(bf16[5,1152,128]{2,1,0:T(8,128)(2,1)} %get-tuple-element.37.south_ref), channel_id=1, source_target_pairs={{4,0},{8,4},{12,8},{16,12},{20,16},{24,20},{28,24},{32,28},{36,32}... | collective-permute-start | bytes 4423688 | tf_op jit(solution)/shard_map/ppermute | solution.py:531
  17.7 27.8 %collective-permute-start.2 = (bf16[3,1296,128]{2,1,0:T(8,128)(2,1)}, bf16[3,1296,128]{2,1,0:T(8,128)(2,1)S(1)}, u32[]{:S(2)}, u32[]{:S(2)}) collective-permute-start(bf16[3,1296,128]{2,1,0:T(8,128)(2,1)} %get-tuple-element.40.south_ref), channel_id=1, source_target_pairs={{4,0},{8,4},{12,8},{16,12},{20,16},{24,20},{28,24},{32,28},{36,32}... | collective-permute-start | bytes 2985992 | tf_op jit(solution)/shard_map/ppermute | solution.py:531
  20.2 22.2 %collective-permute-start.3 = (bf16[3,1152,128]{2,1,0:T(8,128)(2,1)S(1)}, bf16[3,1152,128]{2,1,0:T(8,128)(2,1)}, u32[]{:S(2)}, u32[]{:S(2)}) collective-permute-start(bf16[3,1152,128]{2,1,0:T(8,128)(2,1)S(1)} %get-tuple-element.36.refs_4_.north_ref), channel_id=1, source_target_pairs={{0,4},{4,8},{8,12},{12,16},{16,20},{20,24},{24,28},{28,32},{32,36}... | collective-permute-start | bytes 2654216 | tf_op jit(solution)/shard_map/ppermute | solution.py:531
  45.5 1.0 copy-start.1
  52.0 16.6 %collective-permute-start.4 = (bf16[2,144,512]{2,1,0:T(8,128)(2,1)S(1)}, bf16[2,144,512]{2,1,0:T(8,128)(2,1)S(1)}, u32[]{:S(2)}, u32[]{:S(2)}) collective-permute-start(bf16[2,144,512]{2,1,0:T(8,128)(2,1)S(1)} %get-tuple-element.42), channel_id=1, source_target_pairs={{0,1},{1,2},{2,3},{3,0},{4,5},{5,6},{6,7},{7,4},{8,9},{9,10},{10,1... | collective-permute-start | bytes 884744 | tf_op jit(solution)/shard_map/ppermute | solution.py:536
  53.6 16.1 %collective-permute-start.5 = (bf16[2,144,512]{2,1,0:T(8,128)(2,1)S(1)}, bf16[2,144,512]{2,1,0:T(8,128)(2,1)S(1)}, u32[]{:S(2)}, u32[]{:S(2)}) collective-permute-start(bf16[2,144,512]{2,1,0:T(8,128)(2,1)S(1)} %get-tuple-element.43), channel_id=1, source_target_pairs={{0,2},{1,3},{2,0},{3,1},{4,6},{5,7},{6,4},{7,5},{8,10},{9,11},{10,... | collective-permute-start | bytes 884744 | tf_op jit(solution)/shard_map/ppermute | solution.py:536
  56.5 13.2 %collective-permute-start.6 = (bf16[2,144,512]{2,1,0:T(8,128)(2,1)S(1)}, bf16[2,144,512]{2,1,0:T(8,128)(2,1)S(1)}, u32[]{:S(2)}, u32[]{:S(2)}) collective-permute-start(bf16[2,144,512]{2,1,0:T(8,128)(2,1)S(1)} %get-tuple-element.44), channel_id=1, source_target_pairs={{0,3},{1,0},{2,1},{3,2},{4,7},{5,4},{6,5},{7,6},{8,11},{9,8},{10,9... | collective-permute-start | bytes 884744 | tf_op jit(solution)/shard_map/ppermute | solution.py:536
  57.9 7.5 %copy-start.2 = (f32[4,144,128]{2,1,0:T(8,128)S(1)}, f32[4,144,128]{2,1,0:T(8,128)}, u32[]{:S(2)}) copy-start(f32[4,144,128]{2,1,0:T(8,128)} %copy-done) | copy-start | bytes 884740
  65.3 4.4 %copy-start.4 = (f32[64]{0:T(128)S(1)}, f32[64]{0:T(128)}, u32[]{:S(2)}) copy-start(f32[64]{0:T(128)} %scav_ref.9) | copy-start | bytes 772
  84.4 34.0 %collective-permute-start.7 = (bf16[2,144,512]{2,1,0:T(8,128)(2,1)S(1)}, bf16[2,144,512]{2,1,0:T(8,128)(2,1)S(1)}, u32[]{:S(2)}, u32[]{:S(2)}) collective-permute-start(bf16[2,144,512]{2,1,0:T(8,128)(2,1)S(1)} %get-tuple-element.53), channel_id=1, source_target_pairs={{0,1},{1,2},{2,3},{3,0},{4,5},{5,6},{6,7},{7,4},{8,9},{9,10},{10,1... | collective-permute-start | bytes 884744 | tf_op jit(solution)/shard_map/ppermute | solution.py:536
  85.7 11.3 %collective-permute-start.10 = (bf16[1,144,512]{2,1,0:T(8,128)(2,1)S(1)}, bf16[1,144,512]{2,1,0:T(8,128)(2,1)S(1)}, u32[]{:S(2)}, u32[]{:S(2)}) collective-permute-start(bf16[1,144,512]{2,1,0:T(8,128)(2,1)S(1)} %get-tuple-element.56), channel_id=1, source_target_pairs={{0,1},{1,2},{2,3},{3,0},{4,5},{5,6},{6,7},{7,4},{8,9},{9,10},{10,1... | collective-permute-start | bytes 442376 | tf_op jit(solution)/shard_map/ppermute | solution.py:536
  87.0 15.3 %collective-permute-start.11 = (bf16[1,144,512]{2,1,0:T(8,128)(2,1)S(1)}, bf16[1,144,512]{2,1,0:T(8,128)(2,1)S(1)}, u32[]{:S(2)}, u32[]{:S(2)}) collective-permute-start(bf16[1,144,512]{2,1,0:T(8,128)(2,1)S(1)} %get-tuple-element.57), channel_id=1, source_target_pairs={{0,2},{1,3},{2,0},{3,1},{4,6},{5,7},{6,4},{7,5},{8,10},{9,11},{10,... | collective-permute-start | bytes 442376 | tf_op jit(solution)/shard_map/ppermute | solution.py:536
  89.2 13.1 %collective-permute-start.12 = (bf16[1,144,512]{2,1,0:T(8,128)(2,1)S(1)}, bf16[1,144,512]{2,1,0:T(8,128)(2,1)S(1)}, u32[]{:S(2)}, u32[]{:S(2)}) collective-permute-start(bf16[1,144,512]{2,1,0:T(8,128)(2,1)S(1)} %get-tuple-element.58), channel_id=1, source_target_pairs={{0,3},{1,0},{2,1},{3,2},{4,7},{5,4},{6,5},{7,6},{8,11},{9,8},{10,9... | collective-permute-start | bytes 442376 | tf_op jit(solution)/shard_map/ppermute | solution.py:536
  90.7 28.8 %collective-permute-start.8 = (bf16[2,144,512]{2,1,0:T(8,128)(2,1)S(1)}, bf16[2,144,512]{2,1,0:T(8,128)(2,1)S(1)}, u32[]{:S(2)}, u32[]{:S(2)}) collective-permute-start(bf16[2,144,512]{2,1,0:T(8,128)(2,1)S(1)} %get-tuple-element.54), channel_id=1, source_target_pairs={{0,2},{1,3},{2,0},{3,1},{4,6},{5,7},{6,4},{7,5},{8,10},{9,11},{10,... | collective-permute-start | bytes 884744 | tf_op jit(solution)/shard_map/ppermute | solution.py:536
  97.0 24.0 %collective-permute-start.9 = (bf16[2,144,512]{2,1,0:T(8,128)(2,1)S(1)}, bf16[2,144,512]{2,1,0:T(8,128)(2,1)S(1)}, u32[]{:S(2)}, u32[]{:S(2)}) collective-permute-start(bf16[2,144,512]{2,1,0:T(8,128)(2,1)S(1)} %get-tuple-element.55), channel_id=1, source_target_pairs={{0,3},{1,0},{2,1},{3,2},{4,7},{5,4},{6,5},{7,6},{8,11},{9,8},{10,9... | collective-permute-start | bytes 884744 | tf_op jit(solution)/shard_map/ppermute | solution.py:536
  115.7 19.9 %collective-permute-start.16 = (bf16[2,144,512]{2,1,0:T(8,128)(2,1)S(1)}, bf16[2,144,512]{2,1,0:T(8,128)(2,1)S(1)}, u32[]{:S(2)}, u32[]{:S(2)}) collective-permute-start(bf16[2,144,512]{2,1,0:T(8,128)(2,1)S(1)} %get-tuple-element.64), channel_id=1, source_target_pairs={{0,1},{1,2},{2,3},{3,0},{4,5},{5,6},{6,7},{7,4},{8,9},{9,10},{10,1... | collective-permute-start | bytes 884744 | tf_op jit(solution)/shard_map/ppermute | solution.py:536
  115.8 19.8 %collective-permute-start.17 = (bf16[2,144,512]{2,1,0:T(8,128)(2,1)S(1)}, bf16[2,144,512]{2,1,0:T(8,128)(2,1)S(1)}, u32[]{:S(2)}, u32[]{:S(2)}) collective-permute-start(bf16[2,144,512]{2,1,0:T(8,128)(2,1)S(1)} %get-tuple-element.65), channel_id=1, source_target_pairs={{0,2},{1,3},{2,0},{3,1},{4,6},{5,7},{6,4},{7,5},{8,10},{9,11},{10,... | collective-permute-start | bytes 884744 | tf_op jit(solution)/shard_map/ppermute | solution.py:536
  118.4 17.2 %collective-permute-start.18 = (bf16[2,144,512]{2,1,0:T(8,128)(2,1)S(1)}, bf16[2,144,512]{2,1,0:T(8,128)(2,1)S(1)}, u32[]{:S(2)}, u32[]{:S(2)}) collective-permute-start(bf16[2,144,512]{2,1,0:T(8,128)(2,1)S(1)} %get-tuple-element.66), channel_id=1, source_target_pairs={{0,3},{1,0},{2,1},{3,2},{4,7},{5,4},{6,5},{7,6},{8,11},{9,8},{10,9... | collective-permute-start | bytes 884744 | tf_op jit(solution)/shard_map/ppermute | solution.py:536
  119.5 52.1 %collective-permute-start.23 = (bf16[1152,512]{1,0:T(8,128)(2,1)}, bf16[1152,512]{1,0:T(8,128)(2,1)}, u32[]{:S(2)}, u32[]{:S(2)}) collective-permute-start(bf16[1152,512]{1,0:T(8,128)(2,1)} %bitcast.19.refs_0_.own_ref), channel_id=1, source_target_pairs={{0,64},{4,68},{8,72},{12,76},{16,80},{20,84},{24,88},{28,92},{32,9... | collective-permute-start | bytes 3538952 | tf_op jit(solution)/shard_map/ppermute | solution.py:541
  130.1 85.7 %collective-permute-start.21 = (bf16[1152,512]{1,0:T(8,128)(2,1)}, bf16[1152,512]{1,0:T(8,128)(2,1)}, u32[]{:S(2)}, u32[]{:S(2)}) collective-permute-start(bf16[1152,512]{1,0:T(8,128)(2,1)} %bitcast.21.refs_0_.own_ref), channel_id=1, source_target_pairs={{0,64},{4,68},{8,72},{12,76},{16,80},{20,84},{24,88},{28,92},{32,9... | collective-permute-start | bytes 3538952 | tf_op jit(solution)/shard_map/ppermute | solution.py:541
  147.0 71.5 %collective-permute-start.20 = (bf16[1152,512]{1,0:T(8,128)(2,1)S(1)}, bf16[1152,512]{1,0:T(8,128)(2,1)}, u32[]{:S(2)}, u32[]{:S(2)}) collective-permute-start(bf16[1152,512]{1,0:T(8,128)(2,1)S(1)} %bitcast.35), channel_id=1, source_target_pairs={{0,64},{4,68},{8,72},{12,76},{16,80},{20,84},{24,88},{28,92},{32,9... | collective-permute-start | bytes 3538952 | tf_op jit(solution)/shard_map/ppermute | solution.py:541
  148.5 7.9 %collective-permute-start.13 = (bf16[1,144,512]{2,1,0:T(8,128)(2,1)S(1)}, bf16[1,144,512]{2,1,0:T(8,128)(2,1)S(1)}, u32[]{:S(2)}, u32[]{:S(2)}) collective-permute-start(bf16[1,144,512]{2,1,0:T(8,128)(2,1)S(1)} %get-tuple-element.61), channel_id=1, source_target_pairs={{0,1},{1,2},{2,3},{3,0},{4,5},{5,6},{6,7},{7,4},{8,9},{9,10},{10,1... | collective-permute-start | bytes 442376 | tf_op jit(solution)/shard_map/ppermute | solution.py:536
  149.3 7.1 %collective-permute-start.14 = (bf16[1,144,512]{2,1,0:T(8,128)(2,1)S(1)}, bf16[1,144,512]{2,1,0:T(8,128)(2,1)S(1)}, u32[]{:S(2)}, u32[]{:S(2)}) collective-permute-start(bf16[1,144,512]{2,1,0:T(8,128)(2,1)S(1)} %get-tuple-element.62), channel_id=1, source_target_pairs={{0,2},{1,3},{2,0},{3,1},{4,6},{5,7},{6,4},{7,5},{8,10},{9,11},{10,... | collective-permute-start | bytes 442376 | tf_op jit(solution)/shard_map/ppermute | solution.py:536
  156.4 15.2 %copy-start.3 = (s32[64]{0:T(128)S(1)}, s32[64]{0:T(128)}, u32[]{:S(2)}) copy-start(s32[64]{0:T(128)} %flag_ref.11) | copy-start | bytes 772
  156.4 5.1 %collective-permute-start.15 = (bf16[1,144,512]{2,1,0:T(8,128)(2,1)S(1)}, bf16[1,144,512]{2,1,0:T(8,128)(2,1)S(1)}, u32[]{:S(2)}, u32[]{:S(2)}) collective-permute-start(bf16[1,144,512]{2,1,0:T(8,128)(2,1)S(1)} %get-tuple-element.63), channel_id=1, source_target_pairs={{0,3},{1,0},{2,1},{3,2},{4,7},{5,4},{6,5},{7,6},{8,11},{9,8},{10,9... | collective-permute-start | bytes 442376 | tf_op jit(solution)/shard_map/ppermute | solution.py:536
  156.4 57.0 %collective-permute-start.22 = (bf16[576,512]{1,0:T(8,128)(2,1)S(1)}, bf16[576,512]{1,0:T(8,128)(2,1)}, u32[]{:S(2)}, u32[]{:S(2)}) collective-permute-start(bf16[576,512]{1,0:T(8,128)(2,1)S(1)} %bitcast.39), channel_id=1, source_target_pairs={{0,64},{4,68},{8,72},{12,76},{16,80},{20,84},{24,88},{28,92},{32,9... | collective-permute-start | bytes 1769480 | tf_op jit(solution)/shard_map/ppermute | solution.py:541
  169.4 54.0 %collective-permute-start.19 = (bf16[576,512]{1,0:T(8,128)(2,1)S(1)}, bf16[576,512]{1,0:T(8,128)(2,1)S(1)}, u32[]{:S(2)}, u32[]{:S(2)}) collective-permute-start(bf16[576,512]{1,0:T(8,128)(2,1)S(1)} %bitcast.25), channel_id=1, source_target_pairs={{0,64},{4,68},{8,72},{12,76},{16,80},{20,84},{24,88},{28,92},{32,9... | collective-permute-start | bytes 1769480 | tf_op jit(solution)/shard_map/ppermute | solution.py:541
